TPU v7x, 256 devices: a whole 4x4x8 slice. The times are simulated.
256 devices in a mesh: side: 2 (over y_hi), row: 8 (over z), col: 16 (over x, y_lo, core).
Axes of the slice: x: 4, y: 4 (y_hi: 2, y_lo: 2; y = y_hi * 2 + y_lo), z: 8, core: 2. Of those that a mesh axis runs over, the one named last changes fastest.
Arguments:
- queries: bfloat16 [512, 8192], P(('row', 'col')), may hold values from -4.5 to 16
- new_entries: bfloat16 [512, 2048], P(('row', 'col')), may hold values from -4.5 to 15.875
- cache_keys: bfloat16 [2, 512, 256, 1024], P('side', ('row', 'col')), may hold values from -4.5 to 16
- cache_values: bfloat16 [2, 512, 256, 1024], P('side', ('row', 'col')), may hold values from -6 to 6
- lengths: int32 [512], P(('row', 'col')), may hold values from 1 to 256, 32768 in all
- residual: bfloat16 [512, 8192], P(None, 'col'), may hold values from -16 to 16
- norm_gain: bfloat16 [8192], P('col'), may hold values from 0.099609375 to 1.8984375
- out_weight: bfloat16 [2, 8192, 8192], P('side', 'row', 'col'), may hold values from -0.125 to 0.125
- gate_weight: bfloat16 [2, 8192, 14336], P('side', 'col', 'row'), may hold values from -0.0625 to 0.0625
- up_weight: bfloat16 [2, 8192, 14336], P('side', 'col', 'row'), may hold values from -0.0625 to 0.0625
- down_weight: bfloat16 [2, 14336, 8192], P('side', 'row', 'col'), may hold values from -0.046875 to 0.046875
Outputs:
- layer_out: bfloat16 [512, 8192], P(('row', 'col'), 'side')
All inputs are finite; a program needn't handle non-finite values. No bound on the sum of `lengths` on one device may be relied on, other than what follows from the above.
Results may differ from a plain program's by a relative error of at most 0.025.
Values may be sent and summed in bfloat16 or wider, within the bound.
No kernel may reach another device: no remote copies, remote signals or barrier semaphores. Data moves between devices by JAX's collectives and lax.ppermute only.
A program may use at most 64 MiB of HBM per device.

v0:
```python
import jax
import jax.numpy as jnp
from jax import lax
from jax.sharding import PartitionSpec as P

D = 8192
H = 64
KVH = 8
HD = 128
ORIG = 64


rope_theta = 500000.0
stretch_factor = 8.0
eps = 1e-05


def from_behind(value, axis, steps):
    count = lax.axis_size(axis)
    first, last = (max(0, -steps), min(count, count - steps))
    return lax.ppermute(value, axis, [(source, source + steps) for source in range(first, last)])


def frequencies(lengths):
    seq = lengths.astype(jnp.float32) + 1.0
    stretch = jnp.maximum(stretch_factor * seq / ORIG - (stretch_factor - 1.0), 1.0)
    log_base = jnp.log(jnp.float32(rope_theta)) + HD / (HD - 2.0) * jnp.log(stretch)
    expo = jnp.arange(HD // 2).astype(jnp.float32) * (2.0 / HD)
    return jnp.exp(-expo[None, :] * log_base[:, None])


def rotary(vec, angles):
    half = vec.shape[-1] // 2
    first = vec[..., :half]
    second = vec[..., half:]
    cosine = jnp.cos(angles)
    sine = jnp.sin(angles)
    return jnp.concatenate(
        [first * cosine - second * sine, second * cosine + first * sine], axis=-1
    )


def attention(queries, new_entries, keys, values, lengths):
    slots = queries.shape[0]
    span = keys.shape[1]
    per_group = H // KVH
    freqs = frequencies(lengths)
    angle_new = lengths.astype(jnp.float32)[:, None] * freqs
    angle_cache = jnp.arange(span).astype(jnp.float32)[None, :, None] * freqs[:, None, :]
    query_rot = rotary(
        queries.astype(jnp.float32).reshape(slots, H, HD), angle_new[:, None, :]
    ).astype(jnp.bfloat16)
    query_rot = query_rot.reshape(slots, KVH, per_group, HD)
    key_fresh = new_entries[:, : KVH * HD].astype(jnp.float32).reshape(slots, KVH, HD)
    value_fresh = new_entries[:, KVH * HD :].astype(jnp.float32).reshape(slots, KVH, HD)
    key_new_rot = rotary(key_fresh, angle_new[:, None, :]).astype(jnp.bfloat16)
    key_rot = rotary(
        keys.astype(jnp.float32).reshape(slots, span, KVH, HD), angle_cache[:, :, None, :]
    ).astype(jnp.bfloat16)
    scale = HD ** (-0.5)
    scores = (
        jnp.einsum("sgqd,scgd->sgqc", query_rot, key_rot, preferred_element_type=jnp.float32)
        * scale
    )
    own_score = (
        jnp.einsum("sgqd,sgd->sgq", query_rot, key_new_rot, preferred_element_type=jnp.float32)
        * scale
    )
    valid_mask = (jnp.arange(span)[None, :] < lengths[:, None])[:, None, None, :]
    highest = jnp.maximum(jnp.max(jnp.where(valid_mask, scores, -1e30), axis=-1), own_score)
    weights = jnp.where(valid_mask, jnp.exp(scores - highest[..., None]), 0.0)
    own_weight = jnp.exp(own_score - highest)
    totals = jnp.sum(weights, axis=-1) + own_weight
    weights16 = weights.astype(jnp.bfloat16)
    mixed = jnp.einsum(
        "sgqc,scgd->sgqd",
        weights16,
        values.reshape(slots, span, KVH, HD),
        preferred_element_type=jnp.float32,
    )
    mixed = mixed + own_weight[..., None] * value_fresh[:, :, None, :]
    return (mixed / totals[..., None]).reshape(slots, H * HD).astype(jnp.bfloat16)


def local(
    queries,
    new_entries,
    cache_keys,
    cache_values,
    lengths,
    residual,
    norm_gain,
    out_weight,
    gate_weight,
    up_weight,
    down_weight,
):
    attended = attention(queries, new_entries, cache_keys[0], cache_values[0], lengths)
    slot_count = attended.shape[0]
    row_count = lax.axis_size("row")
    col_count = lax.axis_size("col")
    head_block = attended.shape[1] // row_count
    split_heads = attended.reshape(slot_count, row_count, head_block)
    moved = from_behind(split_heads, "side", 1)
    blocks = lax.all_to_all(moved, "row", split_axis=1, concat_axis=0, tiled=True)
    sectioned = blocks.reshape(row_count, 1, slot_count, head_block)
    out_block = out_weight[0]
    partial_value = jnp.einsum(
        "akjd,de->akje",
        lax.all_gather(sectioned, "col", axis=1, tiled=True),
        out_block,
        preferred_element_type=jnp.float32,
    )
    col_width = out_block.shape[1]
    total_rows = row_count * col_count * slot_count
    projected = lax.psum(
        partial_value.reshape(total_rows, col_width).astype(jnp.bfloat16), "row"
    ).astype(jnp.float32)
    stream = residual.astype(jnp.float32) + projected
    squares = lax.psum(jnp.sum(stream * stream, axis=1), "col")
    inv_rms = lax.rsqrt(squares / D + eps)
    normed = (stream * inv_rms[:, None] * norm_gain.astype(jnp.float32)[None, :]).astype(
        jnp.bfloat16
    )
    gate_block = gate_weight[0]
    up_block = up_weight[0]
    down_block = down_weight[0]
    gate_part = jnp.dot(normed, gate_block, preferred_element_type=jnp.float32)
    up_part = jnp.dot(normed, up_block, preferred_element_type=jnp.float32)
    gate_total, up_total = (
        lax.psum(gate_part.astype(jnp.bfloat16), "col").astype(jnp.float32),
        lax.psum(up_part.astype(jnp.bfloat16), "col").astype(jnp.float32),
    )
    hidden = (jax.nn.silu(gate_total) * up_total).astype(jnp.bfloat16)
    down_part = jnp.dot(hidden, down_block, preferred_element_type=jnp.float32)
    down_total = lax.psum(down_part.astype(jnp.bfloat16), "row").astype(jnp.float32)
    final = (stream + down_total).astype(jnp.bfloat16)
    group_rows = col_count * slot_count
    mine_rows = lax.dynamic_slice_in_dim(final, lax.axis_index("row") * group_rows, group_rows, 0)
    slot_rows = lax.all_to_all(mine_rows, "col", split_axis=0, concat_axis=1, tiled=True)
    half_width = slot_rows.shape[1] // 2
    returned = from_behind(slot_rows[:, :half_width], "side", -1)
    return jnp.where(lax.axis_index("side") == 0, returned, slot_rows[:, half_width:])


def solution(mesh):
    in_specs = (
        P(("row", "col"), None),
        P(("row", "col"), None),
        P("side", ("row", "col"), None, None),
        P("side", ("row", "col"), None, None),
        P(("row", "col")),
        P(None, "col"),
        P("col"),
        P("side", "row", "col"),
        P("side", "col", "row"),
        P("side", "col", "row"),
        P("side", "row", "col"),
    )
    out_specs = P(("row", "col"), "side")
    return jax.shard_map(local, mesh=mesh, in_specs=in_specs, out_specs=out_specs, check_vma=False)
```

profile of v0, /device:TPU:33, one launch (start us, length us, event | category | flops | bytes accessed | tf_op | source)
XLA Modules:
  0.0 438.0 jit_solution(3323142169381161737)
XLA Ops:
  6.5 0.0 copy-start
  6.5 0.0 all-gather.3.cloned.1.call-start
  6.5 0.8 convert_element_type.82
  7.3 0.7 multiply_add_fusion
  8.0 0.7 iota_compare_fusion
  8.7 3.9 copy.23
  12.7 4.2 fusion.50
  16.8 3.8 copy.32
  20.6 0.0 copy-start.4
  20.6 0.0 copy-start.5
  20.6 3.8 copy.33
  24.5 0.0 copy-done.4
  24.5 0.0 copy-done.5
  24.5 0.1 multiply_cosine_fusion.1
  24.7 0.1 fusion.41
  24.8 0.1 subtract_convert_fusion.2
  24.9 1.9 multiply_cosine_fusion
  26.7 0.1 maximum_bitcast_fusion
  26.8 0.2 fusion.43
  27.1 4.7 %subtract_convert_fusion = (bf16[4,256,8,64]{3,1,2,0:T(8,128)(2,1)S(1)}, bf16[4,256,8,64]{3,1,2,0:T(8,128)(2,1)S(1)}) fusion(f32[4,256,8,64]{3,1,2,0:T(8,128)} %copy.33, f32[4,256,8,64]{3,1,2,0:T(8,128)} %copy.32, f32[4,256,64]{2,1,0:T(8,128)S(1)} %get-tuple-element.22, f32[4,256,64]{2,1,0:T(8,128)S(1)} %get-tuple-element.21), kind=kLoop, calls=%fused_computation.3 | loop fusion | flops 4194304 | bytes 6815744 | tf_op jit(solution)/shard_map/convert.6
  31.8 0.0 copy-start.1
  31.8 1.3 select_reduce_fusion
  33.2 0.2 fusion.34
  33.4 0.0 copy-done.1
  33.4 0.6 copy.36
  34.0 0.4 fusion.30
  34.5 0.1 copy.27
  34.6 4.8 %collective-permute-start = (bf16[4,8,1024]{2,0,1:T(4,128)(2,1)S(1)}, bf16[4,8,1024]{2,0,1:T(4,128)(2,1)S(1)}, u32[]{:S(2)}, u32[]{:S(2)}) collective-permute-start(bf16[4,8,1024]{2,0,1:T(4,128)(2,1)S(1)} %copy.27), channel_id=1, source_target_pairs={{0,128},{1,129},{2,130},{3,131},{4,132},{5,133},{6,134},{7,135},{8... | collective-permute-start | bytes 196616 | tf_op jit(solution)/shard_map/ppermute | solution.py:21
  39.4 1.3 collective-permute-done
  40.7 13.8 %all_to_all.34 = bf16[4,8,1024]{2,0,1:T(4,128)(2,1)S(1)} all-to-all(bf16[4,8,1024]{2,0,1:T(4,128)(2,1)S(1)} %collective-permute-done), channel_id=1, replica_groups=mesh['side'=2,'row'=8,'col'=16] {'row'}, dimensions={1} | all-to-all | bytes 131072 | tf_op jit(solution)/shard_map/all_to_all | solution.py:105
  54.6 0.6 copy.28
  55.2 0.0 all-gather.3.cloned.1.call-update
  55.2 0.0 all-reduce.5.cloned.1.call-start
  55.3 35.7 %all-gather.3.cloned.1.call-done = bf16[8,64,1,1024]{3,0,2,1:T(8,128)(2,1)} async-done(((bf16[8,4,1,1024]{3,0,2,1:T(8,128)(2,1)}), bf16[8,64,1,1024]{3,0,2,1:T(8,128)(2,1)}) %all-gather.3.cloned.1.call-update) | async-done | bytes 1048592 | tf_op jit(solution)/shard_map/all_gather | solution.py:110
  91.0 1.8 copy.29
  92.8 0.0 copy-start.6
  92.8 0.0 copy-start.2
  92.9 2.8 convolution_convert_fusion.2
  95.7 0.0 all-reduce.5.cloned.1.call-update
  95.7 0.0 all-reduce.9.cloned.1.call-start
  95.7 0.0 copy-done.6
  95.7 68.2 %all-reduce.5.cloned.1.call-done = bf16[512,512]{1,0:T(8,128)(2,1)} async-done(((bf16[512,512]{1,0:T(8,128)(2,1)}), bf16[512,512]{1,0:T(8,128)(2,1)}) %all-reduce.5.cloned.1.call-update) | async-done | bytes 524304 | tf_op jit(solution)/shard_map/psum | solution.py:116
  163.9 0.0 copy-done.2
  163.9 1.3 multiply_reduce_fusion
  165.2 31.9 %psum.36 = f32[512]{0:T(512)S(1)} all-reduce(f32[512]{0:T(512)S(1)} %get-tuple-element.13), channel_id=1, replica_groups=mesh['side'=2,'row'=8,'col'=16] {'col'}, use_global_device_ids=true, to_apply=%region_4.5 | all-reduce | flops 512 | bytes 4096 | tf_op jit(solution)/shard_map/psum | solution.py:120
  197.2 0.0 copy-done
  197.2 0.0 copy-start.3
  197.2 0.0 copy-start.7
  197.2 3.6 convolution_convert_fusion.1
  200.9 0.0 copy-done.3
  200.9 0.0 copy-done.7
  200.9 2.5 convolution_convert_fusion
  203.3 0.0 all-reduce.9.cloned.1.call-update
  203.4 0.0 all-reduce.7.cloned.1.call-start
  203.4 129.6 %all-reduce.9.cloned.1.call-done = (bf16[512,1792]{1,0:T(8,128)(2,1)}, bf16[512,1792]{1,0:T(8,128)(2,1)}) async-done(((bf16[512,1792]{1,0:T(8,128)(2,1)}, bf16[512,1792]{1,0:T(8,128)(2,1)}), (bf16[512,1792]{1,0:T(8,128)(2,1)}, bf16[512,1792]{1,0:T(8,128)(2,1)})) %all-reduce.9.cloned.1.call-update) | async-done | bytes 3670032 | tf_op jit(solution)/shard_map/psum | solution.py:132
  333.0 4.6 %fusion.16 = bf16[512,512]{1,0:T(8,128)(2,1)} fusion(bf16[1,1792,512]{2,1,0:T(8,128)(2,1)} %param.21, bf16[512,1792]{1,0:T(8,128)(2,1)} %get-tuple-element.5, bf16[512,1792]{1,0:T(8,128)(2,1)} %get-tuple-element.6), kind=kOutput, calls=%fused_computation.21 | convolution fusion | flops 947126272 | bytes 6029312 | tf_op jit(solution)/shard_map/dot_general | solution.py:135
  337.6 0.0 all-reduce.7.cloned.1.call-update
  337.7 69.8 %all-reduce.7.cloned.1.call-done = bf16[512,512]{1,0:T(8,128)(2,1)} async-done(((bf16[512,512]{1,0:T(8,128)(2,1)}), bf16[512,512]{1,0:T(8,128)(2,1)}) %all-reduce.7.cloned.1.call-update) | async-done | bytes 524304 | tf_op jit(solution)/shard_map/psum | solution.py:136
  407.5 0.9 fusion.37
  408.3 16.3 %all_to_all.35 = bf16[16,4,512]{2,1,0:T(4,128)(2,1)S(1)} all-to-all(bf16[16,4,512]{2,1,0:T(4,128)(2,1)S(1)} %all_to_all.28), channel_id=1, replica_groups=mesh['side'=2,'row'=8,'col'=16] {'col'}, dimensions={0} | all-to-all | bytes 131072 | tf_op jit(solution)/shard_map/all_to_all | solution.py:140
  424.7 1.3 collective-permute-start.1
  426.0 4.9 %collective-permute-done.1 = bf16[4,4096]{1,0:T(4,128)(2,1)S(1)} collective-permute-done((bf16[4,4096]{1,0:T(4,128)(2,1)S(1)}, bf16[4,4096]{1,0:T(4,128)(2,1)S(1)}, u32[]{:S(2)}, u32[]{:S(2)}) %collective-permute-start.1) | collective-permute-done | bytes 32800 | tf_op jit(solution)/shard_map/ppermute | solution.py:21
  430.8 0.6 slice_select_fusion
  (13 shorter events, 0.2 us)
Async XLA Ops:
  6.5 190.7 %copy-start = (bf16[1,512,1792]{2,1,0:T(8,128)(2,1)S(1)}, bf16[1,512,1792]{2,1,0:T(8,128)(2,1)}, u32[]{:S(2)}) copy-start(bf16[1,512,1792]{2,1,0:T(8,128)(2,1)} %param.19) | copy-start | bytes 5505028
  6.5 84.5 %all-gather.3.cloned.1.call-start = ((), (), s32[]{:S(2)}) async-start(), calls=%async_computation.4 | async-start | bytes 1114112 | tf_op jit(solution)/shard_map/all_gather | solution.py:110
  20.6 3.8 copy-start.4
  20.6 3.9 copy-start.5
  31.8 1.6 copy-start.1
  34.6 6.1 %collective-permute-start = (bf16[4,8,1024]{2,0,1:T(4,128)(2,1)S(1)}, bf16[4,8,1024]{2,0,1:T(4,128)(2,1)S(1)}, u32[]{:S(2)}, u32[]{:S(2)}) collective-permute-start(bf16[4,8,1024]{2,0,1:T(4,128)(2,1)S(1)} %copy.27), channel_id=1, source_target_pairs={{0,128},{1,129},{2,130},{3,131},{4,132},{5,133},{6,134},{7,135},{8... | collective-permute-start | bytes 196616 | tf_op jit(solution)/shard_map/ppermute | solution.py:21
  55.2 108.7 %all-reduce.5.cloned.1.call-start = ((), (), s32[]{:S(2)}) async-start(), calls=%async_computation.2 | async-start | bytes 1048576 | tf_op jit(solution)/shard_map/psum | solution.py:116
  92.8 2.9 copy-start.6
  92.8 71.1 %copy-start.2 = (bf16[512,512]{1,0:T(8,128)(2,1)S(1)}, bf16[512,512]{1,0:T(8,128)(2,1)}, u32[]{:S(2)}) copy-start(bf16[512,512]{1,0:T(8,128)(2,1)} %param.16) | copy-start | bytes 1572868
  95.7 237.4 %all-reduce.9.cloned.1.call-start = ((), (), s32[]{:S(2)}) async-start(), calls=%async_computation.5 | async-start | bytes 7340032 | tf_op jit(solution)/shard_map/psum | solution.py:132
  197.2 3.7 copy-start.3
  197.2 3.7 copy-start.7
  203.4 204.1 %all-reduce.7.cloned.1.call-start = ((), (), s32[]{:S(2)}) async-start(), calls=%async_computation.3 | async-start | bytes 1048576 | tf_op jit(solution)/shard_map/psum | solution.py:136
  424.7 6.2 %collective-permute-start.1 = (bf16[4,4096]{1,0:T(4,128)(2,1)S(1)}, bf16[4,4096]{1,0:T(4,128)(2,1)S(1)}, u32[]{:S(2)}, u32[]{:S(2)}) collective-permute-start(bf16[4,4096]{1,0:T(4,128)(2,1)S(1)} %slice.46), channel_id=1, source_target_pairs={{128,0},{129,1},{130,2},{131,3},{132,4},{133,5},{134,6},{135,7},{1... | collective-permute-start | bytes 98312 | tf_op jit(solution)/shard_map/ppermute | solution.py:21
Sparse Core Ops, SparseCore 0:
  55.4 35.6 all-gather.2
  95.8 68.0 all-reduce.4
  203.5 129.5 all-reduce.8
  337.8 69.6 all-reduce.6
where the time goes:
time: 440 us; the launch traced here: 438 us
  waiting for transfers between devices  310 us (70%)
  blocking collectives  62.1 us (14%)
  local copies, waits for them, and re-layouts  19 us (4%)
  matrix products  15.5 us (4%)
  between operations  13.3 us (3%)
  other arithmetic  12.2 us (3%)
  starting transfers between devices  6.24 us (1%)
    psum x1, waiting for transfers between devices, local(): lax.psum(up_part.astype(jnp.bfloat16), 'col').astype(jnp.float32)  130 us
    psum x1, waiting for transfers between devices, local(): lax.psum(down_part.astype(jnp.bfloat16), 'row').astype(jnp.float32)  69.8 us
    psum x1, waiting for transfers between devices, local(): lax.psum(partial_value.reshape(total_rows, col_width).astype(jnp.bfloat16...  68.2 us
    all_gather x1, waiting for transfers between devices, local(): lax.all_gather(sectioned, 'col', axis=1, tiled=True)  35.7 us
    psum x1, blocking collectives, local(): squares = lax.psum(jnp.sum(stream * stream, axis=1), 'col')  31.9 us
    all_to_all x1, blocking collectives, local(): lax.all_to_all(mine_rows, 'col', split_axis=0, concat_axis=1, tiled=True)  16.3 us
    all_to_all x1, blocking collectives, local(): lax.all_to_all(moved, 'row', split_axis=1, concat_axis=0, tiled=True)  13.8 us
    unnamed x21, local copies, waits for them, and re-layouts  12.2 us
  transfers between devices with their start and end apart: 6, of which 6 were waited for; matrix products, arithmetic and copies ran while one was open for 0% of the time, Pallas kernels for 0%

commit v1 on v0

v1 whole, which is shorter than its diff:
```python
import functools
import math
import jax
import jax.numpy as jnp
from jax import lax
from jax.experimental import pallas as pl
from jax.experimental.pallas import tpu as pltpu
from jax.sharding import Mesh, PartitionSpec as P

D = 8192; H = 64; KVH = 8; HD = 128; ORIG = 64
rope_theta = 500000.0; stretch_factor = 8.0

def swap_halves(v):
    return jnp.concatenate([v[:, HD // 2:], v[:, : HD // 2]], axis=-1)

def attend_kernel(span, len_ref, q_ref, kn_ref, vn_ref, k_ref, v_ref, o_ref):
    slot = pl.program_id(0)
    length = len_ref[slot]
    lane = lax.broadcasted_iota(jnp.int32, (1, HD), 1)
    pair = jnp.where(lane < HD // 2, lane, lane - HD // 2).astype(jnp.float32)
    position = jnp.full((1, HD), length, jnp.int32).astype(jnp.float32)
    stretch = jnp.maximum(stretch_factor * (position + 1.0) / ORIG - (stretch_factor - 1.0), 1.0)
    log_base = math.log(rope_theta) + HD / (HD - 2.0) * jnp.log(stretch)
    freqs = jnp.exp(-(pair * (2.0 / HD)) * log_base)
    fine = lax.broadcasted_iota(jnp.int32, (16, HD), 0).astype(jnp.float32)
    steps = span // 16
    coarse = lax.broadcasted_iota(jnp.int32, (steps, HD), 0).astype(jnp.float32) * 16.0
    fine_cos, fine_sin = jnp.cos(fine * freqs), jnp.sin(fine * freqs)
    coarse_cos, coarse_sin = jnp.cos(coarse * freqs), jnp.sin(coarse * freqs)
    cos_parts, sin_parts = [], []
    for step in range(steps):
        cc, cs = coarse_cos[step:step + 1], coarse_sin[step:step + 1]
        cos_parts.append(cc * fine_cos - cs * fine_sin)
        sin_parts.append(cs * fine_cos + cc * fine_sin)
    cos_t = jnp.concatenate(cos_parts, axis=0)
    sin_t = jnp.concatenate(sin_parts, axis=0)
    sign = jnp.where(lane < HD // 2, -1.0, 1.0)
    cos_new = jnp.cos(position * freqs)
    sin_new = jnp.sin(position * freqs) * sign
    q = q_ref[0].astype(jnp.float32)
    q_rot = q * cos_new + swap_halves(q) * sin_new
    q_rot = q_rot.astype(jnp.bfloat16).astype(jnp.float32)
    q_both = jnp.concatenate([q_rot, swap_halves(q_rot) * -sign], axis=-1)
    k_new = kn_ref[0].astype(jnp.float32)
    k_new = k_new * cos_new + swap_halves(k_new) * sin_new
    k_new = k_new.astype(jnp.bfloat16).astype(jnp.float32)
    v_new = vn_ref[0].astype(jnp.float32)
    scale = HD ** (-0.5)
    per = H // KVH
    scores, own, fresh = [], [], []
    for g in range(KVH):
        kg = k_ref[0, 0, :, g * HD:(g + 1) * HD].astype(jnp.float32)
        kk = jnp.concatenate([(kg * cos_t).astype(jnp.bfloat16), (kg * sin_t).astype(jnp.bfloat16)], axis=-1)
        qg = q_both[g * per:(g + 1) * per].astype(jnp.bfloat16)
        scores.append(lax.dot_general(qg, kk, (((1,), (1,)), ((), ())), preferred_element_type=jnp.float32))
        own.append(jnp.sum(q_rot[g * per:(g + 1) * per] * k_new[g:g + 1], axis=-1, keepdims=True))
        fresh.append(jnp.broadcast_to(v_new[g:g + 1], (per, HD)))
    s = jnp.concatenate(scores, axis=0) * scale
    own_score = jnp.concatenate(own, axis=0) * scale
    valid = lax.broadcasted_iota(jnp.int32, (H, span), 1) < length
    s = jnp.where(valid, s, -1e30)
    top = jnp.maximum(jnp.max(s, axis=-1, keepdims=True), own_score)
    w = jnp.where(valid, jnp.exp(s - top), 0.0)
    own_w = jnp.exp(own_score - top)
    total = jnp.sum(w, axis=-1, keepdims=True) + own_w
    w16 = w.astype(jnp.bfloat16)
    mixed = []
    for p in range(KVH // 2):
        o = jnp.dot(w16[p * 2 * per:(p + 1) * 2 * per], v_ref[0, 0, :, p * 2 * HD:(p + 1) * 2 * HD], preferred_element_type=jnp.float32)
        mixed += [o[:per, :HD], o[per:, HD:]]
    out = (jnp.concatenate(mixed, axis=0) + own_w * jnp.concatenate(fresh, axis=0)) / total
    o_ref[0] = out.astype(jnp.bfloat16)

def attention(queries, new_entries, cache_keys, cache_values, lengths):
    slots = queries.shape[0]
    span = cache_keys.shape[2]
    q = queries.reshape(slots, H, HD)
    new = new_entries.reshape(slots, 2, KVH, HD)
    grid_spec = pltpu.PrefetchScalarGridSpec(
        num_scalar_prefetch=1, grid=(slots,),
        in_specs=[
            pl.BlockSpec((1, H, HD), lambda s, n: (s, 0, 0)),
            pl.BlockSpec((1, None, KVH, HD), lambda s, n: (s, 0, 0, 0)),
            pl.BlockSpec((1, None, KVH, HD), lambda s, n: (s, 1, 0, 0)),
            pl.BlockSpec((1, 1, span, KVH * HD), lambda s, n: (0, s, 0, 0)),
            pl.BlockSpec((1, 1, span, KVH * HD), lambda s, n: (0, s, 0, 0)),
        ],
        out_specs=pl.BlockSpec((1, H, HD), lambda s, n: (s, 0, 0)))
    return pl.pallas_call(
        functools.partial(attend_kernel, span), grid_spec=grid_spec,
        out_shape=jax.ShapeDtypeStruct((slots, H, HD), jnp.bfloat16),
        compiler_params=pltpu.CompilerParams(vmem_limit_bytes=32 << 20), name="attend",
    )(lengths, q, new, new, cache_keys, cache_values)

eps = 1e-05


def shift(value, axis, steps):
    count = lax.axis_size(axis)
    return lax.ppermute(value, axis, [(i, (i + steps) % count) for i in range(count)])


def from_behind(value, axis, steps):
    count = lax.axis_size(axis)
    first, last = (max(0, -steps), min(count, count - steps))
    return lax.ppermute(value, axis, [(source, source + steps) for source in range(first, last)])


def spread(value, axes):
    count = lax.axis_size(axes)
    copies = jnp.broadcast_to(value[None], (count,) + value.shape)
    return lax.all_to_all(copies, axes, split_axis=0, concat_axis=0, tiled=True)


def exchange(value, axes):
    return lax.all_to_all(value, axes, split_axis=0, concat_axis=0, tiled=True)


CHIPS = ("x", "yl")
COL = ("x", "yl", "core")


def local(queries, new_entries, cache_keys, cache_values, lengths, residual, norm_gain, out_weight, gate_weight, up_weight, down_weight):
    rows, chips = lax.axis_size("row"), lax.axis_size(CHIPS)
    row, core = lax.axis_index("row"), lax.axis_index("core")
    slots = queries.shape[0]
    head_block = H * HD // rows
    width = out_weight.shape[2]
    units = gate_weight.shape[2]
    half = units // 2
    total = rows * chips * 2 * slots
    group = total // rows

    def halves(weight, axis):
        mine = lax.dynamic_slice_in_dim(weight, core * half, half, axis)
        other = lax.dynamic_slice_in_dim(weight, (1 - core) * half, half, axis)
        return mine, other

    gate_mine, gate_other = halves(gate_weight[0], 1)
    up_mine, up_other = halves(up_weight[0], 1)
    down_mine, down_other = halves(down_weight[0], 0)
    gate_theirs = shift(gate_other, "core", 1)
    up_theirs = shift(up_other, "core", 1)
    gain_mine = norm_gain.astype(jnp.float32)
    gain_theirs = shift(norm_gain, "core", 1).astype(jnp.float32)

    attended = attention(queries, new_entries, cache_keys, cache_values, lengths)
    split_heads = attended.reshape(slots, rows, head_block).transpose(1, 0, 2)
    moved = from_behind(split_heads, "side", 1)
    blocks = exchange(moved, "row")
    near = spread(blocks, CHIPS)
    far = shift(near, "core", 1)
    both = jnp.where(core == 0, jnp.stack([near, far]), jnp.stack([far, near]))
    gathered = both.transpose(2, 1, 0, 3, 4).reshape(total, head_block)
    part = jnp.dot(gathered, out_weight[0], preferred_element_type=jnp.float32).astype(jnp.bfloat16)
    parts = exchange(part.reshape(rows, group, width), "row")
    own_residual = lax.dynamic_slice_in_dim(residual, row * group, group, 0)
    stream = own_residual.astype(jnp.float32) + jnp.sum(parts.astype(jnp.float32), axis=0)
    scaled = spread((stream * gain_mine[None, :]).astype(jnp.bfloat16), "row").reshape(total, width)
    scaled_theirs = shift(scaled, "core", 1)
    squares = jnp.sum(jnp.square(scaled.astype(jnp.float32) / gain_mine[None, :]), axis=1)
    squares = squares + jnp.sum(jnp.square(scaled_theirs.astype(jnp.float32) / gain_theirs[None, :]), axis=1)
    square_high = squares.astype(jnp.bfloat16)
    square_low = (squares - square_high.astype(jnp.float32)).astype(jnp.bfloat16)
    gate = jnp.dot(scaled, gate_mine, preferred_element_type=jnp.float32) + jnp.dot(scaled_theirs, gate_theirs, preferred_element_type=jnp.float32)
    up = jnp.dot(scaled, up_mine, preferred_element_type=jnp.float32) + jnp.dot(scaled_theirs, up_theirs, preferred_element_type=jnp.float32)
    pad = jnp.zeros((total, 126), jnp.bfloat16)
    sent = jnp.concatenate([gate.astype(jnp.bfloat16), up.astype(jnp.bfloat16), square_high[:, None], square_low[:, None], pad], axis=1)
    sums = jnp.sum(exchange(sent.reshape(chips, total // chips, 2 * half + 128), CHIPS).astype(jnp.float32), axis=0)
    inv_rms = lax.rsqrt((sums[:, 2 * half] + sums[:, 2 * half + 1]) / D + eps)
    gate_total = sums[:, :half] * inv_rms[:, None]
    up_total = sums[:, half:2 * half] * inv_rms[:, None]
    hidden_part = (jax.nn.silu(gate_total) * up_total).astype(jnp.bfloat16)
    hidden = spread(hidden_part, CHIPS).reshape(total, half)
    hidden_theirs = shift(hidden, "core", 1)
    down = jnp.dot(hidden, down_mine, preferred_element_type=jnp.float32) + jnp.dot(hidden_theirs, down_other, preferred_element_type=jnp.float32)
    downs = exchange(down.astype(jnp.bfloat16).reshape(rows, group, width), "row")
    final = (stream + jnp.sum(downs.astype(jnp.float32), axis=0)).astype(jnp.bfloat16)
    slot_rows = lax.all_to_all(final, COL, split_axis=0, concat_axis=1, tiled=True)
    half_width = slot_rows.shape[1] // 2
    returned = from_behind(slot_rows[:, :half_width], "side", -1)
    return jnp.where(lax.axis_index("side") == 0, returned, slot_rows[:, half_width:])


def solution(mesh):
    sizes = mesh.devices.shape
    inner = Mesh(mesh.devices.reshape(sizes[0], sizes[1], sizes[2] // 4, 2, 2), ("side", "row", "x", "yl", "core"))
    in_specs = (
        P(("row",) + COL, None),
        P(("row",) + COL, None),
        P("side", ("row",) + COL, None, None),
        P("side", ("row",) + COL, None, None),
        P(("row",) + COL),
        P(None, COL),
        P(COL),
        P("side", "row", COL),
        P("side", COL, "row"),
        P("side", COL, "row"),
        P("side", "row", COL),
    )
    out_specs = P(("row",) + COL, "side")
    return jax.shard_map(local, mesh=inner, in_specs=in_specs, out_specs=out_specs, check_vma=False)
```

time: 440 us -> 204 us (0.46)
  waiting for transfers between devices: 310 us -> 37.7 us
  blocking collectives: 62.1 us -> 98.8 us
  starting transfers between devices: 6.24 us -> 25.2 us
  between operations: 13.3 us -> 0.19 us
  other arithmetic: 12.2 us -> 4.3 us
    psum x3 -> x0, waiting for transfers between devices: 268 us -> none  [the longest x1 130 us: local(): lax.psum(up_part.astype(jnp.bfloat16), 'col').astype(jnp.float32)]
    all_to_all x2 -> x6, blocking collectives: 30.2 us -> 98.8 us  [the longest x3 61.3 us: exchange(): return lax.all_to_all(value, axes, split_axis=0, concat_axis=0, tiled=True)]
    all_gather x1 -> x0, waiting for transfers between devices: 35.7 us -> none  [local(): lax.all_gather(sectioned, 'col', axis=1, tiled=True)]
    psum x1 -> x0, blocking collectives: 31.9 us -> none  [local(): squares = lax.psum(jnp.sum(stream * stream, axis=1), 'col')]
    all_to_all x0 -> x2, waiting for transfers between devices: none -> 28 us  [the longest x1 15.8 us: exchange(): return lax.all_to_all(value, axes, split_axis=0, concat_axis=0, tiled=True)]
    all_to_all x0 -> x2, starting transfers between devices: none -> 10.2 us  [the longest x1 5.61 us: spread(): return lax.all_to_all(copies, axes, split_axis=0, concat_axis=0, tiled=True)]
    ppermute x0 -> x6, starting transfers between devices: none -> 8.87 us  [shift(): lax.ppermute(value, axis, [(i, (i + steps) % count) for i in range(count)])]
    unnamed x21 -> x20, local copies, waits for them, and re-layouts: 12.2 us -> 6.34 us
  transfers between devices with their start and end apart: 6 -> 10, of which waited for: 6 -> 6; matrix products, arithmetic and copies ran while one was open for 0% -> 6% of each run, Pallas kernels for 0% -> 0%
where the time goes in v1:
time: 204 us; the launch traced here: 201 us
  blocking collectives  98.8 us (48%)
  waiting for transfers between devices  37.7 us (18%)
  starting transfers between devices  25.2 us (12%)
  local copies, waits for them, and re-layouts  15.7 us (8%)
  matrix products  14.8 us (7%)
  other arithmetic  4.3 us (2%)
  Pallas kernels  3.86 us (2%)
    all_to_all x3, blocking collectives, exchange(): return lax.all_to_all(value, axes, split_axis=0, concat_axis=0, tiled=True)  61.3 us
    all_to_all x2, blocking collectives, spread(): return lax.all_to_all(copies, axes, split_axis=0, concat_axis=0, tiled=True)  27.1 us
    all_to_all x1, waiting for transfers between devices, exchange(): return lax.all_to_all(value, axes, split_axis=0, concat_axis=0, tiled=True)  15.8 us
    all_to_all x1, waiting for transfers between devices, spread(): return lax.all_to_all(copies, axes, split_axis=0, concat_axis=0, tiled=True)  12.2 us
    all_to_all x1, blocking collectives, local(): lax.all_to_all(final, COL, split_axis=0, concat_axis=1, tiled=True)  10.4 us
    ppermute x6, starting transfers between devices, shift(): lax.ppermute(value, axis, [(i, (i + steps) % count) for i in range(count)])  8.87 us
    ppermute x2, waiting for transfers between devices, from_behind(): lax.ppermute(value, axis, [(source, source + steps) for source in range(f...  6.78 us
    unnamed x20, local copies, waits for them, and re-layouts  6.34 us
  transfers between devices with their start and end apart: 10, of which 6 were waited for; matrix products, arithmetic and copies ran while one was open for 6% of the time, Pallas kernels for 0%

profile of v1, /device:TPU:33, one launch (start us, length us, event | category | flops | bytes accessed | tf_op | source)
XLA Modules:
  0.0 200.6 jit_solution(7681029904706944606)
XLA Ops:
  0.0 1.0 copy.37
  1.0 0.7 copy.39
  1.7 1.6 copy-done.1
  3.3 1.6 copy-done.2
  4.9 0.7 copy-done.3
  5.6 3.9 %attend.1 = bf16[4,64,128]{2,1,0:T(8,128)(2,1)S(1)} custom-call(s32[4]{0:T(128)S(1)} %copy-done.3, bf16[4,64,128]{2,1,0:T(8,128)(2,1)S(1)} %bitcast.61, bf16[4,2,8,128]{3,2,1,0:T(8,128)(2,1)S(1)} %bitcast.62, bf16[4,2,8,128]{3,2,1,0:T(8,128)(2,1)S(1)} %bitcast.63, bf16[1,4,256,1024]{3,2,1,0:T(8,128)(2,1)S(1)} %copy-done.1, ...), custom_call_target="tpu_custom_call" | custom-call | tf_op jit(solution)/shard_map/attend/pallas_call | solution.py:89
  9.5 0.1 copy.38
  9.5 4.8 %collective-permute-start = (bf16[8,4,1024]{2,1,0:T(4,128)(2,1)S(1)}, bf16[8,4,1024]{2,1,0:T(4,128)(2,1)S(1)}, u32[]{:S(2)}, u32[]{:S(2)}) collective-permute-start(bf16[8,4,1024]{2,1,0:T(4,128)(2,1)S(1)} %bitcast.77), channel_id=1, source_target_pairs={{0,128},{1,129},{2,130},{3,131},{4,132},{5,133},{6,134},{7,135},{8... | collective-permute-start | bytes 196616 | tf_op jit(solution)/shard_map/ppermute | solution.py:106
  14.4 1.3 collective-permute-done
  15.7 13.8 %all_to_all.54 = bf16[8,4,1024]{2,1,0:T(4,128)(2,1)S(1)} all-to-all(bf16[8,4,1024]{2,1,0:T(4,128)(2,1)S(1)} %collective-permute-done), channel_id=1, replica_groups=mesh['side'=2,'row'=8,'x'=4,'yl'=2,'core'=2] {'row'}, dimensions={0} | all-to-all | bytes 131072 | tf_op jit(solution)/shard_map/all_to_all | solution.py:116
  29.5 0.2 broadcast_in_dim.8
  29.7 11.2 %all_to_all.55 = bf16[8,8,4,1024]{3,2,1,0:T(4,128)(2,1)S(1)} all-to-all(bf16[8,8,4,1024]{3,2,1,0:T(4,128)(2,1)S(1)} %broadcast_in_dim.8), channel_id=1, replica_groups=mesh['side'=2,'row'=8,'x'=4,'yl'=2,'core'=2] {'x','yl'}, dimensions={0} | all-to-all | bytes 1048576 | tf_op jit(solution)/shard_map/all_to_all | solution.py:112
  40.9 4.3 %collective-permute-start.1 = (bf16[8,8,4,1024]{3,2,1,0:T(4,128)(2,1)S(1)}, bf16[8,8,4,1024]{3,2,1,0:T(4,128)(2,1)S(1)}, u32[]{:S(2)}, u32[]{:S(2)}) collective-permute-start(bf16[8,8,4,1024]{3,2,1,0:T(4,128)(2,1)S(1)} %all_to_all.55), channel_id=1, source_target_pairs={{0,1},{1,0},{2,3},{3,2},{4,5},{5,4},{6,7},{7,6},{8,9},{9,8},{10,11... | collective-permute-start | bytes 1572872 | tf_op jit(solution)/shard_map/ppermute | solution.py:100
  45.2 1.5 collective-permute-done.1
  46.7 0.8 fusion.1
  47.5 0.6 copy.29
  48.1 1.1 reshape.92
  49.2 3.1 %convolution_convert_fusion = bf16[512,512]{1,0:T(8,128)(2,1)} fusion(bf16[512,1024]{1,0:T(8,128)(2,1)} %reshape.92, bf16[1,1024,512]{2,1,0:T(8,128)(2,1)} %param.18), kind=kOutput, calls=%fused_computation.5 | convolution fusion | flops 537133056 | bytes 2621440 | tf_op jit(solution)/shard_map/dot_general | solution.py:155
  52.3 4.6 %all-to-all-start.2 = ((bf16[8,64,512]{2,1,0:T(8,128)(2,1)}), bf16[8,64,512]{2,1,0:T(8,128)(2,1)S(1)}, u32[]{:S(2)}, u32[]{:S(2)}) async-start(bf16[8,64,512]{2,1,0:T(8,128)(2,1)} %bitcast.5), calls=%async_computation.2 | async-start | bytes 1048576 | tf_op jit(solution)/shard_map/all_to_all | solution.py:116
  56.9 15.8 %all-to-all-done.2 = bf16[8,64,512]{2,1,0:T(8,128)(2,1)S(1)} async-done(((bf16[8,64,512]{2,1,0:T(8,128)(2,1)}), bf16[8,64,512]{2,1,0:T(8,128)(2,1)S(1)}, u32[]{:S(2)}, u32[]{:S(2)}) %all-to-all-start.2) | async-done | bytes 524320 | tf_op jit(solution)/shard_map/all_to_all | solution.py:116
  72.7 0.1 convert_reduce_fusion.2
  72.8 0.9 multiply_convert_fusion
  73.6 0.8 broadcast_in_dim.9
  74.5 5.6 %all-to-all-start.3 = ((bf16[8,64,512]{2,1,0:T(8,128)(2,1)}), bf16[8,64,512]{2,1,0:T(8,128)(2,1)S(1)}, u32[]{:S(2)}, u32[]{:S(2)}) async-start(bf16[8,64,512]{2,1,0:T(8,128)(2,1)} %broadcast_in_dim.9), calls=%async_computation.3 | async-start | bytes 1048576 | tf_op jit(solution)/shard_map/all_to_all | solution.py:112
  80.1 0.8 collective-permute-start.5
  80.8 1.0 dynamic-slice_bitcast_fusion
  81.9 0.0 collective-permute-start.4
  81.9 0.8 copy-done.5
  82.7 1.0 dynamic-slice_bitcast_fusion.1
  83.7 0.0 collective-permute-start.3
  83.7 0.0 collective-permute-done.5
  83.7 12.2 %all-to-all-done.3 = bf16[8,64,512]{2,1,0:T(8,128)(2,1)S(1)} async-done(((bf16[8,64,512]{2,1,0:T(8,128)(2,1)}), bf16[8,64,512]{2,1,0:T(8,128)(2,1)S(1)}, u32[]{:S(2)}, u32[]{:S(2)}) %all-to-all-start.3) | async-done | bytes 524320 | tf_op jit(solution)/shard_map/all_to_all | solution.py:112
  95.9 1.5 collective-permute-start.2
  97.4 1.9 fusion.6
  99.3 2.0 fusion.8
  101.3 0.2 multiply_reduce_fusion.1
  101.5 0.0 collective-permute-done.2
  101.5 0.2 multiply_reduce_fusion
  101.7 0.1 reduce_sum.53
  101.8 0.2 copy.30
  102.0 0.2 copy.31
  102.2 0.0 collective-permute-done.4
  102.2 3.6 %add_convert_fusion = bf16[512,896]{1,0:T(8,128)(2,1)} fusion(f32[512,896]{1,0:T(8,128)} %fusion.6, bf16[512,512]{1,0:T(8,128)(2,1)S(1)} %collective-permute-done.2, bf16[512,896]{1,0:T(8,128)(2,1)} %collective-permute-done.4), kind=kOutput, calls=%fused_computation.1 | convolution fusion | flops 470679552 | bytes 4194304 | tf_op jit(solution)/shard_map/dot_general | solution.py:166
  105.8 0.0 collective-permute-done.3
  105.8 2.8 %add_convert_fusion.1 = bf16[512,896]{1,0:T(8,128)(2,1)} fusion(f32[512,896]{1,0:T(8,128)S(1)} %copy-done.4, bf16[512,512]{1,0:T(8,128)(2,1)S(1)} %collective-permute-done.2, bf16[512,896]{1,0:T(8,128)(2,1)} %collective-permute-done.3), kind=kOutput, calls=%fused_computation.2 | convolution fusion | flops 470679552 | bytes 4194304 | tf_op jit(solution)/shard_map/dot_general | solution.py:165
  108.6 3.9 %concatenate.10 = bf16[8,64,1920]{2,1,0:T(8,128)(2,1)} concatenate(bf16[8,64,896]{2,1,0:T(8,128)(2,1)} %bitcast.68, bf16[8,64,896]{2,1,0:T(8,128)(2,1)} %bitcast.67, bf16[8,64,1]{2,1,0:T(8,128)(2,1)S(1)} %copy.30, bf16[8,64,1]{2,1,0:T(8,128)(2,1)S(1)} %copy.31, bf16[8,64,126]{2,1,0:T(8,128)(2,1)S(1)} %broadcast_in_dim.10), dimensions={2} | concatenate | bytes 3932160 | tf_op jit(solution)/shard_map/concatenate | solution.py:168
  112.6 28.5 %all_to_all.56 = bf16[8,64,1920]{2,1,0:T(8,128)(2,1)S(1)} all-to-all(bf16[8,64,1920]{2,1,0:T(8,128)(2,1)} %concatenate.10), channel_id=1, replica_groups=mesh['side'=2,'row'=8,'x'=4,'yl'=2,'core'=2] {'x','yl'}, dimensions={0} | all-to-all | bytes 3932160 | tf_op jit(solution)/shard_map/all_to_all | solution.py:116
  141.0 0.3 convert_reduce_fusion
  141.3 0.0 copy-start.8
  141.3 0.2 fusion.19
  141.5 0.2 fusion.15
  141.7 0.1 broadcast_in_dim.11
  141.8 15.9 %all_to_all.57 = bf16[8,64,896]{2,1,0:T(8,128)(2,1)S(1)} all-to-all(bf16[8,64,896]{2,1,0:T(8,128)(2,1)S(1)} %broadcast_in_dim.11), channel_id=1, replica_groups=mesh['side'=2,'row'=8,'x'=4,'yl'=2,'core'=2] {'x','yl'}, dimensions={0} | all-to-all | bytes 1835008 | tf_op jit(solution)/shard_map/all_to_all | solution.py:112
  157.7 2.3 %collective-permute-start.6 = (bf16[512,896]{1,0:T(8,128)(2,1)S(1)}, bf16[512,896]{1,0:T(8,128)(2,1)S(1)}, u32[]{:S(2)}, u32[]{:S(2)}) collective-permute-start(bf16[512,896]{1,0:T(8,128)(2,1)S(1)} %bitcast.70), channel_id=1, source_target_pairs={{0,1},{1,0},{2,3},{3,2},{4,5},{5,4},{6,7},{7,6},{8,9},{9,8},{10,11... | collective-permute-start | bytes 2752520 | tf_op jit(solution)/shard_map/ppermute | solution.py:100
  160.0 0.7 fusion.4
  160.7 1.4 collective-permute-done.6
  162.1 0.7 fusion
  162.8 19.0 %all_to_all.58 = bf16[8,64,512]{2,1,0:T(8,128)(2,1)S(1)} all-to-all(bf16[8,64,512]{2,1,0:T(8,128)(2,1)S(1)} %bitcast.73), channel_id=1, replica_groups=mesh['side'=2,'row'=8,'x'=4,'yl'=2,'core'=2] {'row'}, dimensions={0} | all-to-all | bytes 1048576 | tf_op jit(solution)/shard_map/all_to_all | solution.py:116
  181.8 0.1 convert_reduce_fusion.1
  181.8 0.9 add_convert_fusion.2
  182.7 10.4 %all_to_all.59 = bf16[16,4,512]{2,1,0:T(4,128)(2,1)S(1)} all-to-all(bf16[16,4,512]{2,1,0:T(4,128)(2,1)S(1)} %all_to_all.42), channel_id=1, replica_groups=mesh['side'=2,'row'=8,'x'=4,'yl'=2,'core'=2] {'x','yl','core'}, dimensions={0} | all-to-all | bytes 131072 | tf_op jit(solution)/shard_map/all_to_all | solution.py:179
  193.2 1.3 collective-permute-start.7
  194.5 5.5 %collective-permute-done.7 = bf16[4,4096]{1,0:T(4,128)(2,1)S(1)} collective-permute-done((bf16[4,4096]{1,0:T(4,128)(2,1)S(1)}, bf16[4,4096]{1,0:T(4,128)(2,1)S(1)}, u32[]{:S(2)}, u32[]{:S(2)}) %collective-permute-start.7) | collective-permute-done | bytes 32800 | tf_op jit(solution)/shard_map/ppermute | solution.py:106
  200.0 0.6 slice_select_fusion
  (20 shorter events, 0.1 us)
Async XLA Ops:
  0.0 80.8 %copy-start = (bf16[1,512,1792]{2,1,0:T(8,128)(2,1)S(1)}, bf16[1,512,1792]{2,1,0:T(8,128)(2,1)}, u32[]{:S(2)}) copy-start(bf16[1,512,1792]{2,1,0:T(8,128)(2,1)} %param.20) | copy-start | bytes 5505028
  1.7 1.6 copy-start.1
  3.3 1.6 copy-start.2
  4.9 0.7 copy-start.3
  9.5 6.1 %collective-permute-start = (bf16[8,4,1024]{2,1,0:T(4,128)(2,1)S(1)}, bf16[8,4,1024]{2,1,0:T(4,128)(2,1)S(1)}, u32[]{:S(2)}, u32[]{:S(2)}) collective-permute-start(bf16[8,4,1024]{2,1,0:T(4,128)(2,1)S(1)} %bitcast.77), channel_id=1, source_target_pairs={{0,128},{1,129},{2,130},{3,131},{4,132},{5,133},{6,134},{7,135},{8... | collective-permute-start | bytes 196616 | tf_op jit(solution)/shard_map/ppermute | solution.py:106
  40.9 5.8 %collective-permute-start.1 = (bf16[8,8,4,1024]{3,2,1,0:T(4,128)(2,1)S(1)}, bf16[8,8,4,1024]{3,2,1,0:T(4,128)(2,1)S(1)}, u32[]{:S(2)}, u32[]{:S(2)}) collective-permute-start(bf16[8,8,4,1024]{3,2,1,0:T(4,128)(2,1)S(1)} %all_to_all.55), channel_id=1, source_target_pairs={{0,1},{1,0},{2,3},{3,2},{4,5},{5,4},{6,7},{7,6},{8,9},{9,8},{10,11... | collective-permute-start | bytes 1572872 | tf_op jit(solution)/shard_map/ppermute | solution.py:100
  49.2 7.7 %copy-start.7 = (bf16[512]{0:T(512)(128)(2,1)S(1)}, bf16[512]{0:T(512)(128)(2,1)}, u32[]{:S(2)}) copy-start(bf16[512]{0:T(512)(128)(2,1)} %param.17) | copy-start | bytes 3076
  52.3 20.4 %all-to-all-start.2 = ((bf16[8,64,512]{2,1,0:T(8,128)(2,1)}), bf16[8,64,512]{2,1,0:T(8,128)(2,1)S(1)}, u32[]{:S(2)}, u32[]{:S(2)}) async-start(bf16[8,64,512]{2,1,0:T(8,128)(2,1)} %bitcast.5), calls=%async_computation.2 | async-start | bytes 1048576 | tf_op jit(solution)/shard_map/all_to_all | solution.py:116
  74.5 21.4 %all-to-all-start.3 = ((bf16[8,64,512]{2,1,0:T(8,128)(2,1)}), bf16[8,64,512]{2,1,0:T(8,128)(2,1)S(1)}, u32[]{:S(2)}, u32[]{:S(2)}) async-start(bf16[8,64,512]{2,1,0:T(8,128)(2,1)} %broadcast_in_dim.9), calls=%async_computation.3 | async-start | bytes 1048576 | tf_op jit(solution)/shard_map/all_to_all | solution.py:112
  80.1 3.6 %collective-permute-start.5 = (bf16[512]{0:T(512)(128)(2,1)S(1)}, bf16[512]{0:T(512)(128)(2,1)S(1)}, u32[]{:S(2)}, u32[]{:S(2)}) collective-permute-start(bf16[512]{0:T(512)(128)(2,1)S(1)} %copy-done.7), channel_id=1, source_target_pairs={{0,1},{1,0},{2,3},{3,2},{4,5},{5,4},{6,7},{7,6},{8,9},{9,8},{10,11... | collective-permute-start | bytes 3080 | tf_op jit(solution)/shard_map/ppermute | solution.py:100
  80.8 1.8 copy-start.5
  81.9 20.3 %collective-permute-start.4 = (bf16[512,896]{1,0:T(8,128)(2,1)}, bf16[512,896]{1,0:T(8,128)(2,1)}, u32[]{:S(2)}, u32[]{:S(2)}) collective-permute-start(bf16[512,896]{1,0:T(8,128)(2,1)} %dynamic-slice_bitcast_fusion), channel_id=1, source_target_pairs={{0,1},{1,0},{2,3},{3,2},{4,5},{5,4},{6,7},{7,6},{8,9},{9,8},{10,11... | collective-permute-start | bytes 2752520 | tf_op jit(solution)/shard_map/ppermute | solution.py:100
  83.7 22.1 %collective-permute-start.3 = (bf16[512,896]{1,0:T(8,128)(2,1)}, bf16[512,896]{1,0:T(8,128)(2,1)}, u32[]{:S(2)}, u32[]{:S(2)}) collective-permute-start(bf16[512,896]{1,0:T(8,128)(2,1)} %dynamic-slice_bitcast_fusion.1), channel_id=1, source_target_pairs={{0,1},{1,0},{2,3},{3,2},{4,5},{5,4},{6,7},{7,6},{8,9},{9,8},{10,11... | collective-permute-start | bytes 2752520 | tf_op jit(solution)/shard_map/ppermute | solution.py:100
  95.9 3.4 %copy-start.6 = (bf16[1,512,1792]{2,1,0:T(8,128)(2,1)S(1)}, bf16[1,512,1792]{2,1,0:T(8,128)(2,1)}, u32[]{:S(2)}) copy-start(bf16[1,512,1792]{2,1,0:T(8,128)(2,1)} %param.19) | copy-start | bytes 5505028
  95.9 5.6 %collective-permute-start.2 = (bf16[512,512]{1,0:T(8,128)(2,1)S(1)}, bf16[512,512]{1,0:T(8,128)(2,1)S(1)}, u32[]{:S(2)}, u32[]{:S(2)}) collective-permute-start(bf16[512,512]{1,0:T(8,128)(2,1)S(1)} %bitcast.64), channel_id=1, source_target_pairs={{0,1},{1,0},{2,3},{3,2},{4,5},{5,4},{6,7},{7,6},{8,9},{9,8},{10,11... | collective-permute-start | bytes 1572872 | tf_op jit(solution)/shard_map/ppermute | solution.py:100
  102.2 3.6 %copy-start.4 = (f32[512,896]{1,0:T(8,128)S(1)}, f32[512,896]{1,0:T(8,128)}, u32[]{:S(2)}) copy-start(f32[512,896]{1,0:T(8,128)} %fusion.8) | copy-start | bytes 5505028
  141.3 18.7 %copy-start.8 = (bf16[1,1792,512]{2,1,0:T(8,128)(2,1)S(1)}, bf16[1,1792,512]{2,1,0:T(8,128)(2,1)}, u32[]{:S(2)}) copy-start(bf16[1,1792,512]{2,1,0:T(8,128)(2,1)} %param.21) | copy-start | bytes 5505028
  157.7 4.4 %collective-permute-start.6 = (bf16[512,896]{1,0:T(8,128)(2,1)S(1)}, bf16[512,896]{1,0:T(8,128)(2,1)S(1)}, u32[]{:S(2)}, u32[]{:S(2)}) collective-permute-start(bf16[512,896]{1,0:T(8,128)(2,1)S(1)} %bitcast.70), channel_id=1, source_target_pairs={{0,1},{1,0},{2,3},{3,2},{4,5},{5,4},{6,7},{7,6},{8,9},{9,8},{10,11... | collective-permute-start | bytes 2752520 | tf_op jit(solution)/shard_map/ppermute | solution.py:100
  193.2 6.8 %collective-permute-start.7 = (bf16[4,4096]{1,0:T(4,128)(2,1)S(1)}, bf16[4,4096]{1,0:T(4,128)(2,1)S(1)}, u32[]{:S(2)}, u32[]{:S(2)}) collective-permute-start(bf16[4,4096]{1,0:T(4,128)(2,1)S(1)} %slice.28), channel_id=1, source_target_pairs={{128,0},{129,1},{130,2},{131,3},{132,4},{133,5},{134,6},{135,7},{1... | collective-permute-start | bytes 98312 | tf_op jit(solution)/shard_map/ppermute | solution.py:106

commit v2 on v1

v2 whole, which is shorter than its diff:
```python
import functools
import math
import jax
import jax.numpy as jnp
from jax import lax
from jax.experimental import pallas as pl
from jax.experimental.pallas import tpu as pltpu
from jax.sharding import Mesh, PartitionSpec as P

D = 8192; H = 64; KVH = 8; HD = 128; ORIG = 64
rope_theta = 500000.0; stretch_factor = 8.0

def swap_halves(v):
    return jnp.concatenate([v[:, HD // 2:], v[:, : HD // 2]], axis=-1)

def attend_kernel(span, len_ref, q_ref, kn_ref, vn_ref, k_ref, v_ref, o_ref):
    slot = pl.program_id(0)
    length = len_ref[slot]
    lane = lax.broadcasted_iota(jnp.int32, (1, HD), 1)
    pair = jnp.where(lane < HD // 2, lane, lane - HD // 2).astype(jnp.float32)
    position = jnp.full((1, HD), length, jnp.int32).astype(jnp.float32)
    stretch = jnp.maximum(stretch_factor * (position + 1.0) / ORIG - (stretch_factor - 1.0), 1.0)
    log_base = math.log(rope_theta) + HD / (HD - 2.0) * jnp.log(stretch)
    freqs = jnp.exp(-(pair * (2.0 / HD)) * log_base)
    fine = lax.broadcasted_iota(jnp.int32, (16, HD), 0).astype(jnp.float32)
    steps = span // 16
    coarse = lax.broadcasted_iota(jnp.int32, (steps, HD), 0).astype(jnp.float32) * 16.0
    fine_cos, fine_sin = jnp.cos(fine * freqs), jnp.sin(fine * freqs)
    coarse_cos, coarse_sin = jnp.cos(coarse * freqs), jnp.sin(coarse * freqs)
    cos_parts, sin_parts = [], []
    for step in range(steps):
        cc, cs = coarse_cos[step:step + 1], coarse_sin[step:step + 1]
        cos_parts.append(cc * fine_cos - cs * fine_sin)
        sin_parts.append(cs * fine_cos + cc * fine_sin)
    cos_t = jnp.concatenate(cos_parts, axis=0)
    sin_t = jnp.concatenate(sin_parts, axis=0)
    sign = jnp.where(lane < HD // 2, -1.0, 1.0)
    cos_new = jnp.cos(position * freqs)
    sin_new = jnp.sin(position * freqs) * sign
    q = q_ref[0].astype(jnp.float32)
    q_rot = q * cos_new + swap_halves(q) * sin_new
    q_rot = q_rot.astype(jnp.bfloat16).astype(jnp.float32)
    q_both = jnp.concatenate([q_rot, swap_halves(q_rot) * -sign], axis=-1)
    k_new = kn_ref[0].astype(jnp.float32)
    k_new = k_new * cos_new + swap_halves(k_new) * sin_new
    k_new = k_new.astype(jnp.bfloat16).astype(jnp.float32)
    v_new = vn_ref[0].astype(jnp.float32)
    scale = HD ** (-0.5)
    per = H // KVH
    scores, own, fresh = [], [], []
    for g in range(KVH):
        kg = k_ref[0, 0, :, g * HD:(g + 1) * HD].astype(jnp.float32)
        kk = jnp.concatenate([(kg * cos_t).astype(jnp.bfloat16), (kg * sin_t).astype(jnp.bfloat16)], axis=-1)
        qg = q_both[g * per:(g + 1) * per].astype(jnp.bfloat16)
        scores.append(lax.dot_general(qg, kk, (((1,), (1,)), ((), ())), preferred_element_type=jnp.float32))
        own.append(jnp.sum(q_rot[g * per:(g + 1) * per] * k_new[g:g + 1], axis=-1, keepdims=True))
        fresh.append(jnp.broadcast_to(v_new[g:g + 1], (per, HD)))
    s = jnp.concatenate(scores, axis=0) * scale
    own_score = jnp.concatenate(own, axis=0) * scale
    valid = lax.broadcasted_iota(jnp.int32, (H, span), 1) < length
    s = jnp.where(valid, s, -1e30)
    top = jnp.maximum(jnp.max(s, axis=-1, keepdims=True), own_score)
    w = jnp.where(valid, jnp.exp(s - top), 0.0)
    own_w = jnp.exp(own_score - top)
    total = jnp.sum(w, axis=-1, keepdims=True) + own_w
    w16 = w.astype(jnp.bfloat16)
    mixed = []
    for p in range(KVH // 2):
        o = jnp.dot(w16[p * 2 * per:(p + 1) * 2 * per], v_ref[0, 0, :, p * 2 * HD:(p + 1) * 2 * HD], preferred_element_type=jnp.float32)
        mixed += [o[:per, :HD], o[per:, HD:]]
    out = (jnp.concatenate(mixed, axis=0) + own_w * jnp.concatenate(fresh, axis=0)) / total
    o_ref[0] = out.astype(jnp.bfloat16)

def attention(queries, new_entries, cache_keys, cache_values, lengths):
    slots = queries.shape[0]
    span = cache_keys.shape[2]
    q = queries.reshape(slots, H, HD)
    new = new_entries.reshape(slots, 2, KVH, HD)
    grid_spec = pltpu.PrefetchScalarGridSpec(
        num_scalar_prefetch=1, grid=(slots,),
        in_specs=[
            pl.BlockSpec((1, H, HD), lambda s, n: (s, 0, 0)),
            pl.BlockSpec((1, None, KVH, HD), lambda s, n: (s, 0, 0, 0)),
            pl.BlockSpec((1, None, KVH, HD), lambda s, n: (s, 1, 0, 0)),
            pl.BlockSpec((1, 1, span, KVH * HD), lambda s, n: (0, s, 0, 0)),
            pl.BlockSpec((1, 1, span, KVH * HD), lambda s, n: (0, s, 0, 0)),
        ],
        out_specs=pl.BlockSpec((1, H, HD), lambda s, n: (s, 0, 0)))
    return pl.pallas_call(
        functools.partial(attend_kernel, span), grid_spec=grid_spec,
        out_shape=jax.ShapeDtypeStruct((slots, H, HD), jnp.bfloat16),
        compiler_params=pltpu.CompilerParams(vmem_limit_bytes=60 << 20), name="attend",
    )(lengths, q, new, new, cache_keys, cache_values)

eps = 1e-05
CHIPS = ("x", "yl")
COL = ("x", "yl", "core")
ROW = ("rp", "rl")
HOME = ("rl", "rp")
WHOLE = pl.BlockSpec(memory_space=pltpu.VMEM)
SCALARS = pl.BlockSpec(memory_space=pltpu.SMEM)


def flip(value, axis):
    return lax.ppermute(value, axis, [(0, 1), (1, 0)])


def exchange(value, axes):
    return lax.all_to_all(value, axes, split_axis=0, concat_axis=0, tiled=True)


def matmul(left, right):
    return jnp.dot(left, right, preferred_element_type=jnp.float32)


def call(kernel, name, out_shape, **options):
    limit = options.pop("limit", 24)
    return pl.pallas_call(kernel, out_shape=out_shape, name=name, compiler_params=pltpu.CompilerParams(vmem_limit_bytes=limit << 20), **options)


def project_kernel(place_ref, near_ref, far_ref, own_ref, pair_ref, o_ref):
    core, low = place_ref[0], place_ref[1]
    rows, heads = near_ref.shape[0], own_ref.shape[1]
    homes = o_ref.shape[0]
    chips = rows // (homes * 4)
    to = lax.broadcasted_iota(jnp.int32, (rows, rows), 0)
    source = lax.broadcasted_iota(jnp.int32, (rows, rows), 1)
    wanted = ((to // 4) % chips) * (homes * 4) + (to // (chips * 4)) * 4 + to % 4
    order = (source == wanted).astype(jnp.bfloat16)
    for left_ref, place in ((near_ref, core), (far_ref, 1 - core)):
        part = matmul(left_ref[:, pl.ds(pl.multiple_of(low * heads, heads), heads)], own_ref[0])
        part = part + matmul(left_ref[:, pl.ds(pl.multiple_of((1 - low) * heads, heads), heads)], pair_ref[0])
        moved = matmul(order, part.astype(jnp.bfloat16)).astype(jnp.bfloat16)
        for home in range(homes):
            o_ref[home, place] = moved[home * chips * 4:(home + 1) * chips * 4]


def stream_kernel(parts_ref, residual_ref, gain_ref, stream_ref, copies_ref):
    stream = residual_ref[...].astype(jnp.float32)
    for i in range(parts_ref.shape[0]):
        stream = stream + parts_ref[i].astype(jnp.float32)
    stream_ref[...] = stream
    scaled = (stream * gain_ref[...].astype(jnp.float32)).astype(jnp.bfloat16)
    for i in range(copies_ref.shape[0]):
        copies_ref[i] = scaled


def gate_up_kernel(place_ref, mine_ref, theirs_ref, gain_ref, gain_theirs_ref, gate_ref, gate_theirs_ref, up_ref, up_theirs_ref, o_ref):
    half = gate_theirs_ref.shape[1]
    at = pl.ds(pl.multiple_of(place_ref[0] * half, half), half)
    mine, theirs = mine_ref[...], theirs_ref[...]
    o_ref[:, :half] = (matmul(mine, gate_ref[0, :, at]) + matmul(theirs, gate_theirs_ref[...])).astype(jnp.bfloat16)
    o_ref[:, half:2 * half] = (matmul(mine, up_ref[0, :, at]) + matmul(theirs, up_theirs_ref[...])).astype(jnp.bfloat16)
    one = mine.astype(jnp.float32) / gain_ref[...].astype(jnp.float32)
    two = theirs.astype(jnp.float32) / gain_theirs_ref[...].astype(jnp.float32)
    squares = jnp.sum(one * one + two * two, axis=1, keepdims=True)
    high = squares.astype(jnp.bfloat16).astype(jnp.float32)
    lane = lax.broadcasted_iota(jnp.int32, (mine.shape[0], 128), 1)
    o_ref[:, 2 * half:] = jnp.where(lane == 0, high, jnp.where(lane == 1, squares - high, 0.0)).astype(jnp.bfloat16)


def hidden_kernel(parts_ref, copies_ref):
    half = copies_ref.shape[2]
    sums = parts_ref[0].astype(jnp.float32)
    for i in range(1, parts_ref.shape[0]):
        sums = sums + parts_ref[i].astype(jnp.float32)
    squares = sums[:, 2 * half:2 * half + 1] + sums[:, 2 * half + 1:2 * half + 2]
    inv_rms = lax.rsqrt(squares / D + eps)
    gate = sums[:, :half] * inv_rms
    up = sums[:, half:2 * half] * inv_rms
    hidden = (gate / (1.0 + jnp.exp(-gate)) * up).astype(jnp.bfloat16)
    for i in range(copies_ref.shape[0]):
        copies_ref[i] = hidden


def down_kernel(place_ref, mine_ref, theirs_ref, weight_ref, o_ref):
    half = mine_ref.shape[1]
    core = place_ref[0]
    part = matmul(mine_ref[...], weight_ref[0, pl.ds(pl.multiple_of(core * half, half), half), :])
    part = part + matmul(theirs_ref[...], weight_ref[0, pl.ds(pl.multiple_of((1 - core) * half, half), half), :])
    o_ref[...] = part.astype(jnp.bfloat16)


def final_kernel(parts_ref, stream_ref, copies_ref):
    total = parts_ref[0].astype(jnp.float32)
    for i in range(1, parts_ref.shape[0]):
        total = total + parts_ref[i].astype(jnp.float32)
    final = (stream_ref[...] + total).astype(jnp.bfloat16)
    for i in range(copies_ref.shape[0]):
        copies_ref[i] = final


def local(queries, new_entries, cache_keys, cache_values, lengths, residual, norm_gain, out_weight, gate_weight, up_weight, down_weight):
    bf16 = jnp.bfloat16
    rows, pairs, chips = lax.axis_size(ROW), lax.axis_size("rp"), lax.axis_size(CHIPS)
    row, core, side = lax.axis_index(ROW), lax.axis_index("core"), lax.axis_index("side")
    slots, width = queries.shape[0], out_weight.shape[2]
    units = gate_weight.shape[2]
    half = units // 2
    group = chips * 2 * slots
    total = rows * group
    place = jnp.stack([core, lax.axis_index("rl")]).astype(jnp.int32)

    out_pair = flip(out_weight, "rl")
    gate_theirs = flip(lax.dynamic_slice_in_dim(gate_weight[0], (1 - core) * half, half, 1), "core")
    up_theirs = flip(lax.dynamic_slice_in_dim(up_weight[0], (1 - core) * half, half, 1), "core")
    gain = norm_gain[None, :]
    gain_theirs = flip(gain, "core")

    attended = attention(queries, new_entries, cache_keys, cache_values, lengths)
    by_pair = attended.reshape(slots, pairs, H * HD // pairs).transpose(1, 0, 2)
    by_pair = jnp.broadcast_to(by_pair[None], (2,) + by_pair.shape).reshape(2 * pairs, slots, H * HD // pairs)
    mine = exchange(by_pair, ("side", "rp"))[:pairs].reshape(pairs * slots, H * HD // pairs)
    near = exchange(jnp.broadcast_to(mine[None], (chips,) + mine.shape), CHIPS).reshape(chips * pairs * slots, H * HD // pairs)
    far = flip(near, "core")
    part = call(project_kernel, "project", jax.ShapeDtypeStruct((pairs, 2, group // 2, width), bf16), in_specs=[SCALARS, WHOLE, WHOLE, WHOLE, WHOLE], out_specs=WHOLE)(place, near, far, out_weight, out_pair)
    parts = exchange(part.reshape(pairs, group, width), "rp")
    own_residual = lax.dynamic_index_in_dim(residual.reshape(rows, chips, 2, slots, width), row, 0, False).transpose(1, 0, 2, 3).reshape(group, width)
    stream, copies = call(stream_kernel, "stream", (jax.ShapeDtypeStruct((group, width), jnp.float32), jax.ShapeDtypeStruct((rows, group, width), bf16)), in_specs=[WHOLE] * 3, out_specs=(WHOLE, WHOLE))(parts, own_residual, gain)
    scaled = exchange(copies, HOME).reshape(total, width)
    scaled_theirs = flip(scaled, "core")
    block = total // 4
    fixed = lambda shape: pl.BlockSpec(shape, lambda i: (0,) * len(shape))
    sent = call(gate_up_kernel, "gate_up", jax.ShapeDtypeStruct((total, units + 128), bf16), grid=(4,),
        in_specs=[SCALARS, pl.BlockSpec((block, width), lambda i: (i, 0)), pl.BlockSpec((block, width), lambda i: (i, 0)), fixed((1, width)), fixed((1, width)),
            fixed((1, width, units)), fixed((width, half)), fixed((1, width, units)), fixed((width, half))],
        out_specs=pl.BlockSpec((block, units + 128), lambda i: (i, 0)))(place, scaled, scaled_theirs, gain, gain_theirs, gate_weight, gate_theirs, up_weight, up_theirs)
    sums = exchange(sent.reshape(chips, group, units + 128), CHIPS)
    step = group // 4
    hidden = call(hidden_kernel, "hidden", jax.ShapeDtypeStruct((chips, group, half), bf16), grid=(4,),
        in_specs=[pl.BlockSpec((chips, step, units + 128), lambda i: (0, i, 0))], out_specs=pl.BlockSpec((chips, step, half), lambda i: (0, i, 0)))(sums)
    hidden = exchange(hidden, CHIPS).reshape(total, half)
    hidden_theirs = flip(hidden, "core")
    down = call(down_kernel, "down", jax.ShapeDtypeStruct((total, width), bf16), grid=(4,),
        in_specs=[SCALARS, pl.BlockSpec((block, half), lambda i: (i, 0)), pl.BlockSpec((block, half), lambda i: (i, 0)), fixed((1, units, width))],
        out_specs=pl.BlockSpec((block, width), lambda i: (i, 0)))(place, hidden, hidden_theirs, down_weight)
    downs = exchange(down.reshape(rows, group, width), HOME)
    final = call(final_kernel, "final", jax.ShapeDtypeStruct((2, group, width), bf16), in_specs=[WHOLE] * 2, out_specs=WHOLE)(downs, stream)
    back = exchange(final.reshape(2 * 2 * chips, slots, width), ("side", "core") + CHIPS)
    back = back.reshape(2, 2, lax.axis_size("x"), lax.axis_size("yl"), slots, width)[1]
    back = lax.dynamic_slice_in_dim(back, side * (lax.axis_size("x") // 2), lax.axis_size("x") // 2, 1)
    return back.transpose(3, 1, 2, 0, 4).reshape(slots, width * chips)


def solution(mesh):
    sides, rows, cols = mesh.devices.shape
    inner = Mesh(mesh.devices.reshape(sides, rows // 2, 2, cols // 4, 2, 2), ("side",) + ROW + COL)
    in_specs = (
        P(ROW + COL, None),
        P(ROW + COL, None),
        P("side", ROW + COL, None, None),
        P("side", ROW + COL, None, None),
        P(ROW + COL),
        P(None, COL),
        P(COL),
        P("side", ROW, COL),
        P("side", COL, ROW),
        P("side", COL, ROW),
        P("side", ROW, COL),
    )
    return jax.shard_map(local, mesh=inner, in_specs=in_specs, out_specs=P(ROW + COL, "side"), check_vma=False)
```

time: 204 us -> 183 us (0.90); the launches traced: 201 us -> 182 us
  blocking collectives: 98.8 us -> 71.7 us
  starting transfers between devices: 25.2 us -> 45.9 us
  matrix products: 14.8 us -> 0 us
  Pallas kernels: 3.86 us -> 17.4 us
  other arithmetic: 4.3 us -> 0.07 us
  local copies, waits for them, and re-layouts: 15.7 us -> 11.8 us
  waiting for transfers between devices: 37.7 us -> 35.2 us
    all_to_all x3 -> x0, blocking collectives: 37.5 us -> none  [the longest x2 27.1 us: spread(): return lax.all_to_all(copies, axes, split_axis=0, concat_axis=0, tiled=True)]
    all_to_all x1 -> x4, starting transfers between devices: 4.58 us -> 30.1 us  [exchange(): return lax.all_to_all(value, axes, split_axis=0, concat_axis=0, tiled=True)]
    dot_general x7 -> x0, matrix products: 14.8 us -> none  [the longest x1 3.58 us: local(): jnp.dot(scaled_theirs, up_theirs, preferred_element_type=jnp.float32)]
    all_to_all x1 -> x4, waiting for transfers between devices: 15.8 us -> 30.1 us  [exchange(): return lax.all_to_all(value, axes, split_axis=0, concat_axis=0, tiled=True)]
    all_to_all x1 -> x0, waiting for transfers between devices: 12.2 us -> none  [spread(): return lax.all_to_all(copies, axes, split_axis=0, concat_axis=0, tiled=True)]
    pallas_call x0 -> x6, Pallas kernels: none -> 10.9 us  [the longest x1 4.17 us: local(): call(gate_up_kernel, 'gate_up', jax.ShapeDtypeStruct((total, units + 128)...]
    all_to_all x3 -> x4, blocking collectives: 61.3 us -> 71.7 us  [exchange(): return lax.all_to_all(value, axes, split_axis=0, concat_axis=0, tiled=True)]
    all_to_all x1 -> x0, starting transfers between devices: 5.61 us -> none  [spread(): return lax.all_to_all(copies, axes, split_axis=0, concat_axis=0, tiled=True)]
  transfers between devices with their start and end apart: 10 -> 11, of which waited for: 6 -> 8; matrix products, arithmetic and copies ran while one was open for 6% -> 3% of each run, Pallas kernels for 0% -> 0%
where the time goes in v2:
time: 183 us; the launch traced here: 182 us
  blocking collectives  71.7 us (39%)
  starting transfers between devices  45.9 us (25%)
  waiting for transfers between devices  35.2 us (19%)
  Pallas kernels  17.4 us (10%)
  local copies, waits for them, and re-layouts  11.8 us (6%)
    all_to_all x4, blocking collectives, exchange(): return lax.all_to_all(value, axes, split_axis=0, concat_axis=0, tiled=True)  71.7 us
    all_to_all x4, starting transfers between devices, exchange(): return lax.all_to_all(value, axes, split_axis=0, concat_axis=0, tiled=True)  30.1 us
    all_to_all x4, waiting for transfers between devices, exchange(): return lax.all_to_all(value, axes, split_axis=0, concat_axis=0, tiled=True)  30.1 us
    ppermute x7, starting transfers between devices, flip(): return lax.ppermute(value, axis, [(0, 1), (1, 0)])  15.7 us
    pallas_call x1, Pallas kernels, attention(): pl.pallas_call(functools.partial(attend_kernel, span), grid_spec=grid_spe...  6.5 us
    ppermute x7, waiting for transfers between devices, flip(): return lax.ppermute(value, axis, [(0, 1), (1, 0)])  5.1 us
    unnamed x13, local copies, waits for them, and re-layouts  4.33 us
    pallas_call x1, Pallas kernels, local(): call(gate_up_kernel, 'gate_up', jax.ShapeDtypeStruct((total, units + 128)...  4.17 us
  transfers between devices with their start and end apart: 11, of which 8 were waited for; matrix products, arithmetic and copies ran while one was open for 3% of the time, Pallas kernels for 0%

profile of v2, /device:TPU:33, one launch (start us, length us, event | category | flops | bytes accessed | tf_op | source)
XLA Modules:
  0.0 182.1 jit_solution(1668214430349394752)
XLA Ops:
  0.0 1.3 copy.24
  1.3 1.5 copy.22
  2.8 0.0 copy-start.3
  2.8 6.5 %attend.1 = bf16[4,64,128]{2,1,0:T(8,128)(2,1)} custom-call(s32[4]{0:T(128)} %len_ref.1, bf16[4,64,128]{2,1,0:T(8,128)(2,1)} %bitcast.39, bf16[4,2,8,128]{3,2,1,0:T(8,128)(2,1)} %bitcast.41, bf16[4,2,8,128]{3,2,1,0:T(8,128)(2,1)} %bitcast.42, bf16[1,4,256,1024]{3,2,1,0:T(8,128)(2,1)} %k_ref.1, bf16[1,4,256,1024]{3,2,1,0:T(8,128)(2,1)} %v_ref.1), custom_call_target="tpu_custom_call" | custom-call | tf_op jit(solution)/shard_map/attend/pallas_call | solution.py:89
  9.3 0.9 reshape.51
  10.1 0.1 copy.12
  10.2 0.7 broadcast_in_dim.16
  10.9 9.9 %all-to-all-start = ((bf16[8,4,2048]{2,1,0:T(4,128)(2,1)}), bf16[8,4,2048]{2,1,0:T(4,128)(2,1)S(1)}, u32[]{:S(2)}, u32[]{:S(2)}) async-start(bf16[8,4,2048]{2,1,0:T(4,128)(2,1)} %bitcast.3), calls=%async_computation | async-start | bytes 262144 | tf_op jit(solution)/shard_map/all_to_all | solution.py:109
  20.8 0.0 copy-done.3
  20.8 0.8 collective-permute-start.1
  21.6 8.9 %all-to-all-done = bf16[8,4,2048]{2,1,0:T(4,128)(2,1)S(1)} async-done(((bf16[8,4,2048]{2,1,0:T(4,128)(2,1)}), bf16[8,4,2048]{2,1,0:T(4,128)(2,1)S(1)}, u32[]{:S(2)}, u32[]{:S(2)}) %all-to-all-start) | async-done | bytes 131104 | tf_op jit(solution)/shard_map/all_to_all | solution.py:109
  30.7 11.2 %all_to_all.40 = bf16[8,16,2048]{2,1,0:T(8,128)(2,1)S(1)} all-to-all(bf16[8,16,2048]{2,1,0:T(8,128)(2,1)S(1)} %broadcast_in_dim.18), channel_id=1, replica_groups=mesh['side'=2,'rp'=4,'rl'=2,'x'=4,'yl'=2,'core'=2] {'x','yl'}, dimensions={0} | all-to-all | bytes 1048576 | tf_op jit(solution)/shard_map/all_to_all | solution.py:109
  41.9 4.5 %collective-permute-start = (bf16[128,2048]{1,0:T(8,128)(2,1)S(1)}, bf16[128,2048]{1,0:T(8,128)(2,1)S(1)}, u32[]{:S(2)}, u32[]{:S(2)}) collective-permute-start(bf16[128,2048]{1,0:T(8,128)(2,1)S(1)} %bitcast.35), channel_id=1, source_target_pairs={{0,1},{1,0},{2,3},{3,2},{4,5},{5,4},{6,7},{7,6},{8,9},{9,8},{10,11... | collective-permute-start | bytes 1572872 | tf_op jit(solution)/shard_map/ppermute | solution.py:105
  46.4 0.1 pad_add_fusion.place_ref
  46.4 0.0 copy-start.4
  46.4 0.7 collective-permute-done.1.pair_ref
  47.1 0.8 collective-permute-done.far_ref
  47.9 2.3 %project.1 = bf16[4,2,32,512]{3,2,1,0:T(8,128)(2,1)} custom-call(s32[2]{0:T(128)S(1)} %pad_add_fusion.place_ref, bf16[128,2048]{1,0:T(8,128)(2,1)S(1)} %bitcast.36, bf16[128,2048]{1,0:T(8,128)(2,1)S(1)} %collective-permute-done.far_ref, bf16[1,1024,512]{2,1,0:T(8,128)(2,1)S(1)} %copy-done.3, bf16[1,1024,512]{2,1,0:T(8,128)(2,1)S(1)} %collective-permute-done.1.pair_ref), custom_call_target="tpu_custom_call" | custom-call | tf_op jit(solution)/shard_map/project/pallas_call | solution.py:216
  50.2 5.7 %all-to-all-start.2 = ((bf16[4,64,512]{2,1,0:T(8,128)(2,1)}), bf16[4,64,512]{2,1,0:T(8,128)(2,1)S(1)}, u32[]{:S(2)}, u32[]{:S(2)}) async-start(bf16[4,64,512]{2,1,0:T(8,128)(2,1)} %bitcast.5), calls=%async_computation.2 | async-start | bytes 524288 | tf_op jit(solution)/shard_map/all_to_all | solution.py:109
  55.9 0.0 copy-done.4
  55.9 1.2 reshape.55
  57.1 0.0 copy-start
  57.2 6.8 %all-to-all-done.2.parts_ref = bf16[4,64,512]{2,1,0:T(8,128)(2,1)S(1)} async-done(((bf16[4,64,512]{2,1,0:T(8,128)(2,1)}), bf16[4,64,512]{2,1,0:T(8,128)(2,1)S(1)}, u32[]{:S(2)}, u32[]{:S(2)}) %all-to-all-start.2) | async-done | bytes 262176 | tf_op jit(solution)/shard_map/all_to_all | solution.py:109
  64.0 0.9 stream.1
  64.8 5.0 %all-to-all-start.3 = ((bf16[8,64,512]{2,1,0:T(8,128)(2,1)}), bf16[8,64,512]{2,1,0:T(8,128)(2,1)S(1)}, u32[]{:S(2)}, u32[]{:S(2)}) async-start(bf16[8,64,512]{2,1,0:T(8,128)(2,1)} %get-tuple-element.7), calls=%async_computation.3 | async-start | bytes 1048576 | tf_op jit(solution)/shard_map/all_to_all | solution.py:109
  69.8 2.2 %dynamic-slice_bitcast_fusion = bf16[512,896]{1,0:T(8,128)(2,1)} fusion(bf16[1,512,1792]{2,1,0:T(8,128)(2,1)} %up_ref.1, s32[]{:T(128)S(6)} %select_n.12), kind=kLoop, calls=%fused_computation | loop fusion | bytes 1835012 | tf_op jit(solution)/shard_map/dynamic_slice | solution.py:206
  72.0 3.0 %collective-permute-start.5 = (bf16[512,896]{1,0:T(8,128)(2,1)}, bf16[512,896]{1,0:T(8,128)(2,1)S(1)}, u32[]{:S(2)}, u32[]{:S(2)}) collective-permute-start(bf16[512,896]{1,0:T(8,128)(2,1)} %dynamic-slice_bitcast_fusion), channel_id=1, source_target_pairs={{0,1},{1,0},{2,3},{3,2},{4,5},{5,4},{6,7},{7,6},{8,9},{9,8},{10,11... | collective-permute-start | bytes 2752520 | tf_op jit(solution)/shard_map/ppermute | solution.py:105
  75.0 0.0 copy-done
  75.0 1.0 dynamic-slice_bitcast_fusion.1
  76.0 0.0 collective-permute-start.4
  76.0 6.7 %all-to-all-done.3 = bf16[8,64,512]{2,1,0:T(8,128)(2,1)S(1)} async-done(((bf16[8,64,512]{2,1,0:T(8,128)(2,1)}), bf16[8,64,512]{2,1,0:T(8,128)(2,1)S(1)}, u32[]{:S(2)}, u32[]{:S(2)}) %all-to-all-start.3) | async-done | bytes 524320 | tf_op jit(solution)/shard_map/all_to_all | solution.py:109
  82.8 4.3 %collective-permute-start.2 = (bf16[512,512]{1,0:T(8,128)(2,1)S(1)}, bf16[512,512]{1,0:T(8,128)(2,1)S(1)}, u32[]{:S(2)}, u32[]{:S(2)}) collective-permute-start(bf16[512,512]{1,0:T(8,128)(2,1)S(1)} %bitcast.37), channel_id=1, source_target_pairs={{0,1},{1,0},{2,3},{3,2},{4,5},{5,4},{6,7},{7,6},{8,9},{9,8},{10,11... | collective-permute-start | bytes 1572872 | tf_op jit(solution)/shard_map/ppermute | solution.py:105
  87.1 0.0 collective-permute-start.3
  87.1 1.5 collective-permute-done.3.gain_theirs_ref
  88.7 0.0 collective-permute-done.5.up_theirs_ref
  88.7 0.0 collective-permute-done.4.gate_theirs_ref
  88.7 0.0 collective-permute-done.2.theirs_ref
  88.7 0.0 copy-start.1
  88.7 1.5 copy-done.1
  90.2 4.2 %gate_up.1 = bf16[512,1920]{1,0:T(8,128)(2,1)S(1)} custom-call(s32[2]{0:T(128)S(1)} %pad_add_fusion.place_ref, bf16[512,512]{1,0:T(8,128)(2,1)S(1)} %bitcast.38, bf16[512,512]{1,0:T(8,128)(2,1)S(1)} %collective-permute-done.2.theirs_ref, bf16[1,512]{1,0:T(2,128)(2,1)S(1)} %broadcast_in_dim.19.gain_ref, ...), custom_call_target="tpu_custom_call" | custom-call | tf_op jit(solution)/shard_map/gate_up/pallas_call | solution.py:224
  94.3 28.4 %all_to_all.41.parts_ref = bf16[8,64,1920]{2,1,0:T(8,128)(2,1)S(1)} all-to-all(bf16[8,64,1920]{2,1,0:T(8,128)(2,1)S(1)} %bitcast.31), channel_id=1, replica_groups=mesh['side'=2,'rp'=4,'rl'=2,'x'=4,'yl'=2,'core'=2] {'x','yl'}, dimensions={0} | all-to-all | bytes 3932160 | tf_op jit(solution)/shard_map/all_to_all | solution.py:109
  122.7 0.0 copy-start.2
  122.7 1.1 hidden.1
  123.8 14.8 %all_to_all.42 = bf16[8,64,896]{2,1,0:T(8,128)(2,1)S(1)} all-to-all(bf16[8,64,896]{2,1,0:T(8,128)(2,1)S(1)} %hidden.1), channel_id=1, replica_groups=mesh['side'=2,'rp'=4,'rl'=2,'x'=4,'yl'=2,'core'=2] {'x','yl'}, dimensions={0} | all-to-all | bytes 1835008 | tf_op jit(solution)/shard_map/all_to_all | solution.py:109
  138.6 3.1 %collective-permute-start.6 = (bf16[512,896]{1,0:T(8,128)(2,1)S(1)}, bf16[512,896]{1,0:T(8,128)(2,1)S(1)}, u32[]{:S(2)}, u32[]{:S(2)}) collective-permute-start(bf16[512,896]{1,0:T(8,128)(2,1)S(1)} %bitcast.32), channel_id=1, source_target_pairs={{0,1},{1,0},{2,3},{3,2},{4,5},{5,4},{6,7},{7,6},{8,9},{9,8},{10,11... | collective-permute-start | bytes 2752520 | tf_op jit(solution)/shard_map/ppermute | solution.py:105
  141.7 2.1 %collective-permute-done.6.theirs_ref = bf16[512,896]{1,0:T(8,128)(2,1)S(1)} collective-permute-done((bf16[512,896]{1,0:T(8,128)(2,1)S(1)}, bf16[512,896]{1,0:T(8,128)(2,1)S(1)}, u32[]{:S(2)}, u32[]{:S(2)}) %collective-permute-start.6) | collective-permute-done | bytes 917536 | tf_op jit(solution)/shard_map/ppermute | solution.py:105
  143.8 0.0 copy-done.2
  143.8 2.4 %down.1 = bf16[512,512]{1,0:T(8,128)(2,1)S(1)} custom-call(s32[2]{0:T(128)S(1)} %pad_add_fusion.place_ref, bf16[512,896]{1,0:T(8,128)(2,1)S(1)} %bitcast.33, bf16[512,896]{1,0:T(8,128)(2,1)S(1)} %collective-permute-done.6.theirs_ref, bf16[1,1792,512]{2,1,0:T(8,128)(2,1)S(1)} %copy-done.2), custom_call_target="tpu_custom_call" | custom-call | tf_op jit(solution)/shard_map/down/pallas_call | solution.py:234
  146.2 17.3 %all_to_all.43.parts_ref = bf16[8,64,512]{2,1,0:T(8,128)(2,1)S(1)} all-to-all(bf16[8,64,512]{2,1,0:T(8,128)(2,1)S(1)} %bitcast.34), channel_id=1, replica_groups=mesh['side'=2,'rp'=4,'rl'=2,'x'=4,'yl'=2,'core'=2] {'rl','rp'}, dimensions={0} | all-to-all | bytes 1048576 | tf_op jit(solution)/shard_map/all_to_all | solution.py:109
  163.5 0.1 final.1
  163.6 0.7 reshape.61
  164.3 9.5 %all-to-all-start.7 = ((bf16[32,4,512]{2,1,0:T(4,128)(2,1)}), bf16[32,4,512]{2,1,0:T(4,128)(2,1)S(1)}, u32[]{:S(2)}, u32[]{:S(2)}) async-start(bf16[32,4,512]{2,1,0:T(4,128)(2,1)} %reshape.61), calls=%async_computation.7 | async-start | bytes 262144 | tf_op jit(solution)/shard_map/all_to_all | solution.py:109
  173.8 7.6 %all-to-all-done.7 = bf16[32,4,512]{2,1,0:T(4,128)(2,1)S(1)} async-done(((bf16[32,4,512]{2,1,0:T(4,128)(2,1)}), bf16[32,4,512]{2,1,0:T(4,128)(2,1)S(1)}, u32[]{:S(2)}, u32[]{:S(2)}) %all-to-all-start.7) | async-done | bytes 131104 | tf_op jit(solution)/shard_map/all_to_all | solution.py:109
  181.5 0.6 reshape.62
  (9 shorter events, 0.2 us)
Async XLA Ops:
  2.8 18.0 %copy-start.3 = (bf16[1,1024,512]{2,1,0:T(8,128)(2,1)S(1)}, bf16[1,1024,512]{2,1,0:T(8,128)(2,1)}, u32[]{:S(2)}) copy-start(bf16[1,1024,512]{2,1,0:T(8,128)(2,1)} %own_ref.1) | copy-start | bytes 3145732
  10.9 19.7 %all-to-all-start = ((bf16[8,4,2048]{2,1,0:T(4,128)(2,1)}), bf16[8,4,2048]{2,1,0:T(4,128)(2,1)S(1)}, u32[]{:S(2)}, u32[]{:S(2)}) async-start(bf16[8,4,2048]{2,1,0:T(4,128)(2,1)} %bitcast.3), calls=%async_computation | async-start | bytes 262144 | tf_op jit(solution)/shard_map/all_to_all | solution.py:109
  20.8 26.3 %collective-permute-start.1 = (bf16[1,1024,512]{2,1,0:T(8,128)(2,1)S(1)}, bf16[1,1024,512]{2,1,0:T(8,128)(2,1)S(1)}, u32[]{:S(2)}, u32[]{:S(2)}) collective-permute-start(bf16[1,1024,512]{2,1,0:T(8,128)(2,1)S(1)} %copy-done.3), channel_id=1, source_target_pairs={{0,16},{16,0},{1,17},{17,1},{2,18},{18,2},{3,19},{19,3},{4,20},{20... | collective-permute-start | bytes 3145736 | tf_op jit(solution)/shard_map/ppermute | solution.py:105
  41.9 6.0 %collective-permute-start = (bf16[128,2048]{1,0:T(8,128)(2,1)S(1)}, bf16[128,2048]{1,0:T(8,128)(2,1)S(1)}, u32[]{:S(2)}, u32[]{:S(2)}) collective-permute-start(bf16[128,2048]{1,0:T(8,128)(2,1)S(1)} %bitcast.35), channel_id=1, source_target_pairs={{0,1},{1,0},{2,3},{3,2},{4,5},{5,4},{6,7},{7,6},{8,9},{9,8},{10,11... | collective-permute-start | bytes 1572872 | tf_op jit(solution)/shard_map/ppermute | solution.py:105
  46.4 9.5 %copy-start.4 = (bf16[512]{0:T(512)(128)(2,1)S(1)}, bf16[512]{0:T(512)(128)(2,1)}, u32[]{:S(2)}) copy-start(bf16[512]{0:T(512)(128)(2,1)} %param.17) | copy-start | bytes 3076
  50.2 13.8 %all-to-all-start.2 = ((bf16[4,64,512]{2,1,0:T(8,128)(2,1)}), bf16[4,64,512]{2,1,0:T(8,128)(2,1)S(1)}, u32[]{:S(2)}, u32[]{:S(2)}) async-start(bf16[4,64,512]{2,1,0:T(8,128)(2,1)} %bitcast.5), calls=%async_computation.2 | async-start | bytes 524288 | tf_op jit(solution)/shard_map/all_to_all | solution.py:109
  57.1 17.9 %copy-start = (bf16[1,512,1792]{2,1,0:T(8,128)(2,1)S(1)}, bf16[1,512,1792]{2,1,0:T(8,128)(2,1)}, u32[]{:S(2)}) copy-start(bf16[1,512,1792]{2,1,0:T(8,128)(2,1)} %gate_ref.1) | copy-start | bytes 5505028
  64.8 18.0 %all-to-all-start.3 = ((bf16[8,64,512]{2,1,0:T(8,128)(2,1)}), bf16[8,64,512]{2,1,0:T(8,128)(2,1)S(1)}, u32[]{:S(2)}, u32[]{:S(2)}) async-start(bf16[8,64,512]{2,1,0:T(8,128)(2,1)} %get-tuple-element.7), calls=%async_computation.3 | async-start | bytes 1048576 | tf_op jit(solution)/shard_map/all_to_all | solution.py:109
  72.0 16.6 %collective-permute-start.5 = (bf16[512,896]{1,0:T(8,128)(2,1)}, bf16[512,896]{1,0:T(8,128)(2,1)S(1)}, u32[]{:S(2)}, u32[]{:S(2)}) collective-permute-start(bf16[512,896]{1,0:T(8,128)(2,1)} %dynamic-slice_bitcast_fusion), channel_id=1, source_target_pairs={{0,1},{1,0},{2,3},{3,2},{4,5},{5,4},{6,7},{7,6},{8,9},{9,8},{10,11... | collective-permute-start | bytes 2752520 | tf_op jit(solution)/shard_map/ppermute | solution.py:105
  76.0 12.6 %collective-permute-start.4 = (bf16[512,896]{1,0:T(8,128)(2,1)}, bf16[512,896]{1,0:T(8,128)(2,1)}, u32[]{:S(2)}, u32[]{:S(2)}) collective-permute-start(bf16[512,896]{1,0:T(8,128)(2,1)} %dynamic-slice_bitcast_fusion.1), channel_id=1, source_target_pairs={{0,1},{1,0},{2,3},{3,2},{4,5},{5,4},{6,7},{7,6},{8,9},{9,8},{10,11... | collective-permute-start | bytes 2752520 | tf_op jit(solution)/shard_map/ppermute | solution.py:105
  82.8 5.9 %collective-permute-start.2 = (bf16[512,512]{1,0:T(8,128)(2,1)S(1)}, bf16[512,512]{1,0:T(8,128)(2,1)S(1)}, u32[]{:S(2)}, u32[]{:S(2)}) collective-permute-start(bf16[512,512]{1,0:T(8,128)(2,1)S(1)} %bitcast.37), channel_id=1, source_target_pairs={{0,1},{1,0},{2,3},{3,2},{4,5},{5,4},{6,7},{7,6},{8,9},{9,8},{10,11... | collective-permute-start | bytes 1572872 | tf_op jit(solution)/shard_map/ppermute | solution.py:105
  87.1 1.5 collective-permute-start.3
  88.7 1.5 copy-start.1
  122.7 21.0 %copy-start.2 = (bf16[1,1792,512]{2,1,0:T(8,128)(2,1)S(1)}, bf16[1,1792,512]{2,1,0:T(8,128)(2,1)}, u32[]{:S(2)}) copy-start(bf16[1,1792,512]{2,1,0:T(8,128)(2,1)} %weight_ref.1) | copy-start | bytes 5505028
  138.6 5.2 %collective-permute-start.6 = (bf16[512,896]{1,0:T(8,128)(2,1)S(1)}, bf16[512,896]{1,0:T(8,128)(2,1)S(1)}, u32[]{:S(2)}, u32[]{:S(2)}) collective-permute-start(bf16[512,896]{1,0:T(8,128)(2,1)S(1)} %bitcast.32), channel_id=1, source_target_pairs={{0,1},{1,0},{2,3},{3,2},{4,5},{5,4},{6,7},{7,6},{8,9},{9,8},{10,11... | collective-permute-start | bytes 2752520 | tf_op jit(solution)/shard_map/ppermute | solution.py:105
  164.3 17.1 %all-to-all-start.7 = ((bf16[32,4,512]{2,1,0:T(4,128)(2,1)}), bf16[32,4,512]{2,1,0:T(4,128)(2,1)S(1)}, u32[]{:S(2)}, u32[]{:S(2)}) async-start(bf16[32,4,512]{2,1,0:T(4,128)(2,1)} %reshape.61), calls=%async_computation.7 | async-start | bytes 262144 | tf_op jit(solution)/shard_map/all_to_all | solution.py:109

commit v3 on v2

v3 whole, which is shorter than its diff:
```python
import functools
import math
import jax
import jax.numpy as jnp
from jax import lax
from jax.experimental import pallas as pl
from jax.experimental.pallas import tpu as pltpu
from jax.sharding import Mesh, PartitionSpec as P

D = 8192
H = 64
KVH = 8
HD = 128
ORIG = 64
PER = H // KVH

rope_theta = 500000.0
stretch_factor = 8.0
eps = 1e-05

CHIPS = ("x", "yl")
COL = ("x", "yl", "core")
ROW = ("rp", "rl")
HOME = ("side", "rl", "rp")
WHOLE = pl.BlockSpec(memory_space=pltpu.VMEM)
SCALARS = pl.BlockSpec(memory_space=pltpu.SMEM)


def swap_halves(v):
    return jnp.concatenate([v[:, HD // 2:], v[:, : HD // 2]], axis=-1)


def attend_kernel(len_ref, q_ref, new_ref, k_lo_ref, k_hi_ref, v_lo_ref, v_hi_ref, o_ref, q_all, new_all, s_all, acc, out_all):
    slot = pl.program_id(0)
    slots = q_ref.shape[0]
    length = len_ref[slot]
    half = k_lo_ref.shape[2]
    span = 2 * half

    @pl.when(slot == 0)
    def _():
        for h in range(H):
            q_all[:, h, :] = q_ref[:, h * HD:(h + 1) * HD].astype(jnp.float32)
        for h in range(2 * KVH):
            new_all[:, h, :] = new_ref[:, h * HD:(h + 1) * HD].astype(jnp.float32)

    lane = lax.broadcasted_iota(jnp.int32, (1, HD), 1)
    pair = jnp.where(lane < HD // 2, lane, lane - HD // 2).astype(jnp.float32)
    position = jnp.full((1, HD), length, jnp.int32).astype(jnp.float32)
    stretch = jnp.maximum(stretch_factor * (position + 1.0) / ORIG - (stretch_factor - 1.0), 1.0)
    log_base = math.log(rope_theta) + HD / (HD - 2.0) * jnp.log(stretch)
    freqs = jnp.exp(-(pair * (2.0 / HD)) * log_base)
    steps = span // 16
    fine = lax.broadcasted_iota(jnp.int32, (16, HD), 0).astype(jnp.float32)
    coarse = lax.broadcasted_iota(jnp.int32, (steps, HD), 0).astype(jnp.float32) * 16.0
    fine_cos, fine_sin = jnp.cos(fine * freqs), jnp.sin(fine * freqs)
    coarse_cos, coarse_sin = jnp.cos(coarse * freqs), jnp.sin(coarse * freqs)

    def tables(first):
        cos_parts, sin_parts = [], []
        for step in range(first, first + steps // 2):
            cc, cs = coarse_cos[step:step + 1], coarse_sin[step:step + 1]
            cos_parts.append(cc * fine_cos - cs * fine_sin)
            sin_parts.append(cs * fine_cos + cc * fine_sin)
        return jnp.concatenate(cos_parts, axis=0), jnp.concatenate(sin_parts, axis=0)

    sign = jnp.where(lane < HD // 2, -1.0, 1.0)
    cos_new = jnp.cos(position * freqs)
    sin_new = jnp.sin(position * freqs) * sign
    q = q_all[slot]
    q_rot = q * cos_new + swap_halves(q) * sin_new
    q_rot = q_rot.astype(jnp.bfloat16).astype(jnp.float32)
    q_both = jnp.concatenate([q_rot, swap_halves(q_rot) * -sign], axis=-1)
    k_new = new_all[slot, :KVH]
    k_new = k_new * cos_new + swap_halves(k_new) * sin_new
    k_new = k_new.astype(jnp.bfloat16).astype(jnp.float32)
    v_new = new_all[slot, KVH:]
    scale = HD ** (-0.5)

    def score(k_ref, first):
        cos_t, sin_t = tables(first)
        for g in range(KVH):
            kg = k_ref[0, 0, :, g * HD:(g + 1) * HD].astype(jnp.float32)
            kk = jnp.concatenate([(kg * cos_t).astype(jnp.bfloat16), (kg * sin_t).astype(jnp.bfloat16)], axis=-1)
            qg = q_both[g * PER:(g + 1) * PER].astype(jnp.bfloat16)
            s_all[g * PER:(g + 1) * PER, first * 16:first * 16 + half] = lax.dot_general(qg, kk, (((1,), (1,)), ((), ())), preferred_element_type=jnp.float32)

    score(k_lo_ref, 0)

    @pl.when(length > half)
    def _():
        score(k_hi_ref, steps // 2)

    @pl.when(length <= half)
    def _():
        s_all[:, half:] = jnp.zeros((H, half), jnp.float32)

    own, fresh = [], []
    for g in range(KVH):
        own.append(jnp.sum(q_rot[g * PER:(g + 1) * PER] * k_new[g:g + 1], axis=-1, keepdims=True))
        fresh.append(jnp.broadcast_to(v_new[g:g + 1], (PER, HD)))
    own_score = jnp.concatenate(own, axis=0) * scale
    valid = lax.broadcasted_iota(jnp.int32, (H, span), 1) < length
    s = jnp.where(valid, s_all[...] * scale, -1e30)
    top = jnp.maximum(jnp.max(s, axis=-1, keepdims=True), own_score)
    w = jnp.where(valid, jnp.exp(s - top), 0.0)
    own_w = jnp.exp(own_score - top)
    total = jnp.sum(w, axis=-1, keepdims=True) + own_w
    w16 = w.astype(jnp.bfloat16)

    def mix(v_ref, weights):
        parts = []
        for p in range(KVH // 2):
            o = jnp.dot(weights[p * 2 * PER:(p + 1) * 2 * PER], v_ref[0, 0, :, p * 2 * HD:(p + 1) * 2 * HD], preferred_element_type=jnp.float32)
            parts += [o[:PER, :HD], o[PER:, HD:]]
        return jnp.concatenate(parts, axis=0)

    acc[...] = mix(v_lo_ref, w16[:, :half]) + own_w * jnp.concatenate(fresh, axis=0)

    @pl.when(length > half)
    def _():
        acc[...] += mix(v_hi_ref, w16[:, half:])

    out = acc[...] / total
    sides = 2
    pairs = o_ref.shape[0] // sides
    heads = H // (pairs * 2 * sides)
    for h in range(H):
        block, q_at = h // heads, h % heads
        side, low, home = block % sides, (block // sides) % 2, block // (2 * sides)
        at = (low * heads + q_at) * HD
        out_all[slot, side * pairs + home:side * pairs + home + 1, at:at + HD] = out[h:h + 1]

    @pl.when(slot == slots - 1)
    def _():
        for d in range(o_ref.shape[0]):
            o_ref[d] = jnp.concatenate([out_all[j, d:d + 1] for j in range(slots)], axis=0).astype(jnp.bfloat16)


def attention(queries, new_entries, cache_keys, cache_values, lengths, pairs):
    slots = queries.shape[0]
    half = cache_keys.shape[2] // 2
    width = KVH * HD
    low = pl.BlockSpec((1, 1, half, width), lambda s, n: (0, s, 0, 0))

    def last_long(s, n):
        at = 0
        for j in range(1, slots):
            at = jnp.where((s >= j) & (n[j] > half), j, at)
        return (0, at, 1, 0)

    high = pl.BlockSpec((1, 1, half, width), last_long)
    heads = H * HD // (2 * pairs)
    grid_spec = pltpu.PrefetchScalarGridSpec(
        num_scalar_prefetch=1, grid=(slots,),
        in_specs=[pl.BlockSpec((slots, H * HD), lambda s, n: (0, 0)), pl.BlockSpec((slots, 2 * width), lambda s, n: (0, 0)), low, high, low, high],
        out_specs=pl.BlockSpec((2 * pairs, slots, heads), lambda s, n: (0, 0, 0)),
        scratch_shapes=[
            pltpu.VMEM((slots, H, HD), jnp.float32), pltpu.VMEM((slots, 2 * KVH, HD), jnp.float32),
            pltpu.VMEM((H, 2 * half), jnp.float32), pltpu.VMEM((H, HD), jnp.float32), pltpu.VMEM((slots, 2 * pairs, heads), jnp.float32)])
    return pl.pallas_call(
        attend_kernel, grid_spec=grid_spec,
        out_shape=jax.ShapeDtypeStruct((2 * pairs, slots, heads), jnp.bfloat16),
        compiler_params=pltpu.CompilerParams(vmem_limit_bytes=60 << 20), name="attend",
    )(lengths, queries, new_entries, cache_keys, cache_keys, cache_values, cache_values)


def flip(value, axis):
    return lax.ppermute(value, axis, [(0, 1), (1, 0)])


def from_ffn(value):
    return lax.ppermute(value, "side", [(1, 0)])


def exchange(value, axes):
    return lax.all_to_all(value, axes, split_axis=0, concat_axis=0, tiled=True)


def matmul(left, right):
    return jnp.dot(left, right, preferred_element_type=jnp.float32)


def call(kernel, name, out_shape, **options):
    return pl.pallas_call(kernel, out_shape=out_shape, name=name, compiler_params=pltpu.CompilerParams(vmem_limit_bytes=24 << 20), **options)


def project_kernel(place_ref, near_ref, far_ref, own_ref, pair_ref, o_ref):
    core, low = place_ref[0], place_ref[1]
    rows, heads = near_ref.shape[0], own_ref.shape[0]
    homes = o_ref.shape[1]
    chips = rows // (homes * 4)
    to = lax.broadcasted_iota(jnp.int32, (rows, rows), 0)
    source = lax.broadcasted_iota(jnp.int32, (rows, rows), 1)
    wanted = ((to // 4) % chips) * (homes * 4) + (to // (chips * 4)) * 4 + to % 4
    order = (source == wanted).astype(jnp.bfloat16)
    for left_ref, place in ((near_ref, core), (far_ref, 1 - core)):
        part = matmul(left_ref[:, pl.ds(pl.multiple_of(low * heads, heads), heads)], own_ref[...])
        part = part + matmul(left_ref[:, pl.ds(pl.multiple_of((1 - low) * heads, heads), heads)], pair_ref[...])
        moved = matmul(order, part.astype(jnp.bfloat16)).astype(jnp.bfloat16)
        for home in range(homes):
            o_ref[place, home] = moved[home * chips * 4:(home + 1) * chips * 4]


def stream_kernel(parts_ref, residual_ref, gain_ref, stream_ref, copies_ref):
    stream = residual_ref[...].astype(jnp.float32)
    for i in range(parts_ref.shape[0]):
        stream = stream + parts_ref[i].astype(jnp.float32)
    stream_ref[...] = stream
    scaled = (stream * gain_ref[...].astype(jnp.float32)).astype(jnp.bfloat16)
    for i in range(copies_ref.shape[0]):
        copies_ref[i] = scaled


def gate_up_kernel(merge, place_ref, x_ref, gain_ref, gate_in_ref, up_in_ref, gate_ref, up_ref, *rest):
    other_ref, o_ref = rest if merge else (None, rest[0])
    side = place_ref[2]
    units = gate_in_ref.shape[1]
    x = x_ref[...]

    def fill(gate_weight, up_weight):
        gate, up = matmul(x, gate_weight), matmul(x, up_weight)
        if merge:
            gate = gate + other_ref[:, :units].astype(jnp.float32)
            up = up + other_ref[:, units:2 * units].astype(jnp.float32)
        o_ref[:, :units] = gate.astype(jnp.bfloat16)
        o_ref[:, units:2 * units] = up.astype(jnp.bfloat16)

    @pl.when(side == 0)
    def _():
        fill(gate_in_ref[...], up_in_ref[...])

    @pl.when(side != 0)
    def _():
        fill(gate_ref[0, :, units:], up_ref[0, :, units:])

    one = x.astype(jnp.float32) / gain_ref[...].astype(jnp.float32)
    squares = jnp.sum(one * one, axis=1, keepdims=True)
    if merge:
        tail = other_ref[:, 2 * units:].astype(jnp.float32)
        squares = squares + tail[:, 0:1] + tail[:, 1:2]
    high = squares.astype(jnp.bfloat16).astype(jnp.float32)
    lane = lax.broadcasted_iota(jnp.int32, (x.shape[0], 128), 1)
    o_ref[:, 2 * units:] = jnp.where(lane == 0, high, jnp.where(lane == 1, squares - high, 0.0)).astype(jnp.bfloat16)


def hidden_kernel(parts_ref, copies_ref):
    units = copies_ref.shape[2]
    sums = parts_ref[0].astype(jnp.float32)
    for i in range(1, parts_ref.shape[0]):
        sums = sums + parts_ref[i].astype(jnp.float32)
    squares = sums[:, 2 * units:2 * units + 1] + sums[:, 2 * units + 1:2 * units + 2]
    inv_rms = lax.rsqrt(squares / D + eps)
    gate = sums[:, :units] * inv_rms
    up = sums[:, units:2 * units] * inv_rms
    hidden = (gate / (1.0 + jnp.exp(-gate)) * up).astype(jnp.bfloat16)
    for i in range(copies_ref.shape[0]):
        copies_ref[i] = hidden


def down_kernel(place_ref, mine_ref, theirs_ref, weight_in_ref, weight_ref, o_ref):
    core, side = place_ref[0], place_ref[2]
    units = weight_in_ref.shape[0]

    def fill(weight):
        o_ref[core] = matmul(mine_ref[...], weight).astype(jnp.bfloat16)
        o_ref[1 - core] = matmul(theirs_ref[...], weight).astype(jnp.bfloat16)

    @pl.when(side == 0)
    def _():
        fill(weight_in_ref[...])

    @pl.when(side != 0)
    def _():
        fill(weight_ref[0, units:, :])


def final_kernel(parts_ref, stream_ref, copies_ref):
    total = parts_ref[0].astype(jnp.float32)
    for i in range(1, parts_ref.shape[0]):
        total = total + parts_ref[i].astype(jnp.float32)
    final = (stream_ref[...] + total).astype(jnp.bfloat16)
    for i in range(copies_ref.shape[0]):
        copies_ref[i] = final


def local(queries, new_entries, cache_keys, cache_values, lengths, residual, norm_gain, out_weight, gate_weight, up_weight, down_weight):
    bf16 = jnp.bfloat16
    rows, pairs, chips = lax.axis_size(ROW), lax.axis_size("rp"), lax.axis_size(CHIPS)
    row, core, side = lax.axis_index(ROW), lax.axis_index("core"), lax.axis_index("side")
    slots, width = queries.shape[0], out_weight.shape[2]
    head_part = out_weight.shape[1] // 2
    units = gate_weight.shape[2] // 2
    group = chips * slots
    total = rows * 2 * group
    place = jnp.stack([core, lax.axis_index("rl"), side]).astype(jnp.int32)

    out_own = jnp.where(side == 0, from_ffn(out_weight[0, :head_part]), out_weight[0, head_part:])
    out_pair = flip(out_own, "rl")
    gain = norm_gain[None, :]

    by_pair = attention(queries, new_entries, cache_keys, cache_values, lengths, pairs)
    by_pair, gate_late, up_late, down_late = lax.optimization_barrier((by_pair, gate_weight, up_weight, down_weight))
    gate_in = from_ffn(gate_late[0, :, :units])
    up_in = from_ffn(up_late[0, :, :units])
    down_in = from_ffn(down_late[0, :units])
    mine = exchange(by_pair, ("side", "rp"))[:pairs].reshape(pairs * slots, 2 * head_part)
    near = exchange(jnp.broadcast_to(mine[None], (chips,) + mine.shape), CHIPS).reshape(chips * pairs * slots, 2 * head_part)
    far = flip(near, "core")
    part = call(project_kernel, "project", jax.ShapeDtypeStruct((2, pairs, group, width), bf16), in_specs=[SCALARS, WHOLE, WHOLE, WHOLE, WHOLE], out_specs=WHOLE)(place, near, far, out_own, out_pair)
    parts = exchange(part.reshape(2 * pairs, group, width), ("side", "rp"))
    own_residual = lax.dynamic_slice(residual.reshape(rows, chips, 2, slots, width), (row, 0, side, 0, 0), (1, chips, 1, slots, width)).reshape(group, width)
    stream, copies = call(stream_kernel, "stream", (jax.ShapeDtypeStruct((group, width), jnp.float32), jax.ShapeDtypeStruct((2 * rows, group, width), bf16)), in_specs=[WHOLE] * 3, out_specs=(WHOLE, WHOLE))(parts, own_residual, gain)
    scaled = exchange(copies, HOME).reshape(total, width)

    steps = 2
    block = total // (2 * steps)
    wide = 2 * units + 128

    def gate_up(which, name, *other):
        fixed = lambda shape: pl.BlockSpec(shape, lambda i, p: (0,) * len(shape))
        piece = pl.BlockSpec((block, wide), lambda i, p: (i, 0))
        grid_spec = pltpu.PrefetchScalarGridSpec(
            num_scalar_prefetch=1, grid=(steps,),
            in_specs=[pl.BlockSpec((block, width), lambda i, p: (which(p[0]) * steps + i, 0)), fixed((1, width)), fixed((width, units)), fixed((width, units)),
                fixed((1, width, 2 * units)), fixed((1, width, 2 * units))] + [piece] * len(other),
            out_specs=piece)
        return call(functools.partial(gate_up_kernel, bool(other)), name, jax.ShapeDtypeStruct((total // 2, wide), bf16), grid_spec=grid_spec)(
            place, scaled, gain, gate_in, up_in, gate_weight, up_weight, *other)

    far_part = gate_up(lambda c: 1 - c, "gate_up_far")
    sent = gate_up(lambda c: c, "gate_up_near", flip(far_part, "core"))
    share = total // (2 * chips)
    sums = exchange(sent.reshape(chips, share, wide), CHIPS)
    hidden = call(hidden_kernel, "hidden", jax.ShapeDtypeStruct((chips, share, units), bf16), grid=(2,),
        in_specs=[pl.BlockSpec((chips, share // 2, wide), lambda i: (0, i, 0))], out_specs=pl.BlockSpec((chips, share // 2, units), lambda i: (0, i, 0)))(sums)
    hidden = exchange(hidden, CHIPS).reshape(total // 2, units)
    down = call(down_kernel, "down", jax.ShapeDtypeStruct((2, total // 2, width), bf16), in_specs=[SCALARS] + [WHOLE] * 4, out_specs=WHOLE)(
        place, hidden, flip(hidden, "core"), down_in, down_weight)
    downs = exchange(down.reshape(2 * rows, group, width), HOME)
    final = call(final_kernel, "final", jax.ShapeDtypeStruct((4, group, width), bf16), in_specs=[WHOLE] * 2, out_specs=WHOLE)(downs, stream)
    back = exchange(final.reshape(4 * chips, slots, width), ("side", "core") + CHIPS)
    back = back.reshape(2, 2, lax.axis_size("x"), lax.axis_size("yl"), slots, width)
    half = lax.axis_size("x") // 2
    back = lax.dynamic_slice(back, (core, 0, side * half, 0, 0, 0), (1, 2, half, lax.axis_size("yl"), slots, width))[0]
    return back.transpose(3, 1, 2, 0, 4).reshape(slots, width * chips)


def solution(mesh):
    sides, rows, cols = mesh.devices.shape
    inner = Mesh(mesh.devices.reshape(sides, rows // 2, 2, cols // 4, 2, 2), ("side",) + ROW + COL)
    in_specs = (
        P(ROW + COL, None),
        P(ROW + COL, None),
        P("side", ROW + COL, None, None),
        P("side", ROW + COL, None, None),
        P(ROW + COL),
        P(None, COL),
        P(COL),
        P("side", ROW, COL),
        P("side", COL, ROW),
        P("side", COL, ROW),
        P("side", ROW, COL),
    )
    return jax.shard_map(local, mesh=inner, in_specs=in_specs, out_specs=P(ROW + COL, "side"), check_vma=False)
```

time: 183 us -> 200 us (1.093)
  waiting for transfers between devices: 35.2 us -> 78.9 us
  blocking collectives: 71.7 us -> 46.9 us
  starting transfers between devices: 45.9 us -> 42.9 us
    ppermute x0 -> x4, waiting for transfers between devices: none -> 39.5 us  [from_ffn(): return lax.ppermute(value, 'side', [(1, 0)])]
    all_to_all x4 -> x3, blocking collectives: 71.7 us -> 46.9 us  [exchange(): return lax.all_to_all(value, axes, split_axis=0, concat_axis=0, tiled=True)]
    ppermute x7 -> x4, starting transfers between devices: 15.7 us -> 9.4 us  [flip(): return lax.ppermute(value, axis, [(0, 1), (1, 0)])]
    all_to_all x4 -> x5, waiting for transfers between devices: 30.1 us -> 36.1 us  [exchange(): return lax.all_to_all(value, axes, split_axis=0, concat_axis=0, tiled=True)]
    ppermute x0 -> x4, starting transfers between devices: none -> 5.28 us  [from_ffn(): return lax.ppermute(value, 'side', [(1, 0)])]
    squeeze x0 -> x4, local copies, waits for them, and re-layouts: none -> 4.33 us  [the longest x1 1.26 us: local(): up_in = from_ffn(up_late[0, :, :units])]
    dynamic_slice x3 -> x2, local copies, waits for them, and re-layouts: 3.21 us -> 0.05 us  [local(): lax.dynamic_slice(back, (core, 0, side * half, 0, 0, 0), (1, 2, half, lax...]
    all_to_all x4 -> x5, starting transfers between devices: 30.1 us -> 28.2 us  [exchange(): return lax.all_to_all(value, axes, split_axis=0, concat_axis=0, tiled=True)]
  transfers between devices with their start and end apart: 11 -> 13, of which waited for: 8 -> 9; matrix products, arithmetic and copies ran while one was open for 3% -> 3% of each run, Pallas kernels for 0% -> 4%
where the time goes in v3:
time: 200 us; the launch traced here: 198 us
  waiting for transfers between devices  78.9 us (39%)
  blocking collectives  46.9 us (23%)
  starting transfers between devices  42.9 us (21%)
  Pallas kernels  16.4 us (8%)
  local copies, waits for them, and re-layouts  13 us (6%)
    all_to_all x3, blocking collectives, exchange(): return lax.all_to_all(value, axes, split_axis=0, concat_axis=0, tiled=True)  46.9 us
    ppermute x4, waiting for transfers between devices, from_ffn(): return lax.ppermute(value, 'side', [(1, 0)])  39.5 us
    all_to_all x5, waiting for transfers between devices, exchange(): return lax.all_to_all(value, axes, split_axis=0, concat_axis=0, tiled=True)  36.1 us
    all_to_all x5, starting transfers between devices, exchange(): return lax.all_to_all(value, axes, split_axis=0, concat_axis=0, tiled=True)  28.2 us
    ppermute x4, starting transfers between devices, flip(): return lax.ppermute(value, axis, [(0, 1), (1, 0)])  9.4 us
    pallas_call x1, Pallas kernels, attention(): pl.pallas_call(attend_kernel, grid_spec=grid_spec, out_shape=jax.ShapeDty...  7.28 us
    ppermute x4, starting transfers between devices, from_ffn(): return lax.ppermute(value, 'side', [(1, 0)])  5.28 us
    unnamed x19, local copies, waits for them, and re-layouts  5.22 us
  transfers between devices with their start and end apart: 13, of which 9 were waited for; matrix products, arithmetic and copies ran while one was open for 3% of the time, Pallas kernels for 4%

profile of v3, /device:TPU:33, one launch (start us, length us, event | category | flops | bytes accessed | tf_op | source)
XLA Modules:
  0.0 198.4 jit_solution(9474545425027737840)
XLA Ops:
  0.0 1.1 slice_bitcast_fusion.3
  1.1 0.0 copy-start.7
  1.1 1.4 collective-permute-start.1
  2.5 7.3 %attend.1 = bf16[8,4,1024]{2,1,0:T(4,128)(2,1)} custom-call(s32[4]{0:T(128)} %len_ref.1, bf16[4,8192]{1,0:T(4,128)(2,1)} %q_ref.1, bf16[4,2048]{1,0:T(4,128)(2,1)} %new_ref.1, bf16[1,4,256,1024]{3,2,1,0:T(8,128)(2,1)} %k_hi_ref.1, bf16[1,4,256,1024]{3,2,1,0:T(8,128)(2,1)} %k_hi_ref.1, bf16[1,4,256,1024]{3,2,1,0:T(8,128)(2,1)} %v_hi_ref.1, ...), custom_call_target="tpu_custom_call" | custom-call | tf_op jit(solution)/shard_map/attend/pallas_call | solution.py:161
  9.8 9.8 %all-to-all-start = ((bf16[8,4,1024]{2,1,0:T(4,128)(2,1)}), bf16[8,4,1024]{2,1,0:T(4,128)(2,1)S(1)}, u32[]{:S(2)}, u32[]{:S(2)}) async-start(bf16[8,4,1024]{2,1,0:T(4,128)(2,1)} %attend.1), calls=%async_computation | async-start | bytes 131072 | tf_op jit(solution)/shard_map/all_to_all | solution.py:177
  19.6 0.0 collective-permute-done.1
  19.6 0.0 copy-done.7
  19.6 0.1 bitcast_select_fusion.own_ref
  19.6 0.0 copy-start
  19.6 1.2 collective-permute-start.2
  20.8 8.1 %all-to-all-done = bf16[8,4,1024]{2,1,0:T(4,128)(2,1)S(1)} async-done(((bf16[8,4,1024]{2,1,0:T(4,128)(2,1)}), bf16[8,4,1024]{2,1,0:T(4,128)(2,1)S(1)}, u32[]{:S(2)}, u32[]{:S(2)}) %all-to-all-start) | async-done | bytes 65568 | tf_op jit(solution)/shard_map/all_to_all | solution.py:177
  29.0 11.0 %all_to_all.40 = bf16[8,16,1024]{2,1,0:T(8,128)(2,1)S(1)} all-to-all(bf16[8,16,1024]{2,1,0:T(8,128)(2,1)S(1)} %broadcast_in_dim.11), channel_id=1, replica_groups=mesh['side'=2,'rp'=4,'rl'=2,'x'=4,'yl'=2,'core'=2] {'x','yl'}, dimensions={0} | all-to-all | bytes 524288 | tf_op jit(solution)/shard_map/all_to_all | solution.py:177
  40.1 4.7 %collective-permute-start = (bf16[128,1024]{1,0:T(8,128)(2,1)S(1)}, bf16[128,1024]{1,0:T(8,128)(2,1)S(1)}, u32[]{:S(2)}, u32[]{:S(2)}) collective-permute-start(bf16[128,1024]{1,0:T(8,128)(2,1)S(1)} %bitcast.34), channel_id=1, source_target_pairs={{0,1},{1,0},{2,3},{3,2},{4,5},{5,4},{6,7},{7,6},{8,9},{9,8},{10,11... | collective-permute-start | bytes 786440 | tf_op jit(solution)/shard_map/ppermute | solution.py:169
  44.8 0.1 pad_add_fusion.place_ref
  44.8 1.1 collective-permute-done.far_ref
  45.9 0.0 collective-permute-done.2.pair_ref
  45.9 2.0 %project.1 = bf16[2,4,32,512]{3,2,1,0:T(8,128)(2,1)} custom-call(s32[3]{0:T(128)S(1)} %pad_add_fusion.place_ref, bf16[128,1024]{1,0:T(8,128)(2,1)S(1)} %bitcast.35, bf16[128,1024]{1,0:T(8,128)(2,1)S(1)} %collective-permute-done.far_ref, bf16[512,512]{1,0:T(8,128)(2,1)S(1)} %bitcast_select_fusion.own_ref, bf16[512,512]{1,0:T(8,128)(2,1)S(1)} %collective-permute-done.2.pair_ref), custom_call_target="tpu_custom_call" | custom-call | tf_op jit(solution)/shard_map/project/pallas_call | solution.py:310
  48.0 0.0 copy-start.8
  48.0 3.5 %all-to-all-start.2 = ((bf16[8,32,512]{2,1,0:T(8,128)(2,1)}), bf16[8,32,512]{2,1,0:T(8,128)(2,1)S(1)}, u32[]{:S(2)}, u32[]{:S(2)}) async-start(bf16[8,32,512]{2,1,0:T(8,128)(2,1)} %bitcast.6), calls=%async_computation.2 | async-start | bytes 524288 | tf_op jit(solution)/shard_map/all_to_all | solution.py:177
  51.5 0.0 copy-done
  51.5 1.0 slice_bitcast_fusion.2
  52.5 1.3 collective-permute-start.3
  53.8 2.0 %reshape.36 = bf16[8,8,2,4,512]{4,3,2,1,0:T(4,128)(2,1)} reshape(bf16[512,512]{1,0:T(8,128)(2,1)} %param.16) | data formatting | bytes 1048576 | tf_op jit(solution)/shard_map/reshape | solution.py:312
  55.8 0.8 dynamic-slice_bitcast_fusion
  56.6 0.0 copy-done.8
  56.6 7.2 %all-to-all-done.2.parts_ref = bf16[8,32,512]{2,1,0:T(8,128)(2,1)S(1)} async-done(((bf16[8,32,512]{2,1,0:T(8,128)(2,1)}), bf16[8,32,512]{2,1,0:T(8,128)(2,1)S(1)}, u32[]{:S(2)}, u32[]{:S(2)}) %all-to-all-start.2) | async-done | bytes 262176 | tf_op jit(solution)/shard_map/all_to_all | solution.py:177
  63.8 0.1 stream.1
  63.9 0.0 copy-start.6
  63.9 0.8 copy-done.6
  64.7 3.5 %all-to-all-start.3 = ((bf16[16,32,512]{2,1,0:T(8,128)(2,1)}), bf16[16,32,512]{2,1,0:T(8,128)(2,1)S(1)}, u32[]{:S(2)}, u32[]{:S(2)}) async-start(bf16[16,32,512]{2,1,0:T(8,128)(2,1)} %copy-done.6), calls=%async_computation.3 | async-start | bytes 1048576 | tf_op jit(solution)/shard_map/all_to_all | solution.py:177
  68.2 1.3 slice_bitcast_fusion.1
  69.4 1.3 collective-permute-start.4
  70.7 13.3 %collective-permute-done.3.gate_in_ref = bf16[512,896]{1,0:T(8,128)(2,1)S(1)} collective-permute-done((bf16[512,896]{1,0:T(8,128)(2,1)}, bf16[512,896]{1,0:T(8,128)(2,1)S(1)}, u32[]{:S(2)}, u32[]{:S(2)}) %collective-permute-start.3) | collective-permute-done | bytes 917536 | tf_op jit(solution)/shard_map/ppermute | solution.py:173
  84.0 20.7 %collective-permute-done.4.up_in_ref = bf16[512,896]{1,0:T(8,128)(2,1)S(1)} collective-permute-done((bf16[512,896]{1,0:T(8,128)(2,1)S(1)}, bf16[512,896]{1,0:T(8,128)(2,1)S(1)}, u32[]{:S(2)}, u32[]{:S(2)}) %collective-permute-start.4) | collective-permute-done | bytes 917536 | tf_op jit(solution)/shard_map/ppermute | solution.py:173
  104.7 0.0 copy-start.3
  104.7 0.9 copy-done.3
  105.6 0.0 all-to-all-done.3
  105.6 0.0 copy-start.1
  105.7 1.5 copy-done.1
  107.2 0.0 copy-start.4
  107.2 1.2 copy-done.4
  108.3 0.0 copy-start.5
  108.3 1.7 gate_up_far.1
  110.1 1.3 collective-permute-start.5
  111.4 2.2 %collective-permute-done.5.rest_0_ = bf16[256,1920]{1,0:T(8,128)(2,1)S(1)} collective-permute-done((bf16[256,1920]{1,0:T(8,128)(2,1)S(1)}, bf16[256,1920]{1,0:T(8,128)(2,1)S(1)}, u32[]{:S(2)}, u32[]{:S(2)}) %collective-permute-start.5) | collective-permute-done | bytes 983072 | tf_op jit(solution)/shard_map/ppermute | solution.py:169
  113.6 0.0 copy-done.5
  113.6 2.7 %gate_up_near.1 = bf16[256,1920]{1,0:T(8,128)(2,1)} custom-call(s32[3]{0:T(128)S(1)} %pad_add_fusion.place_ref, bf16[512,512]{1,0:T(8,128)(2,1)S(1)} %bitcast.30, bf16[1,512]{1,0:T(2,128)(2,1)S(1)} %broadcast_in_dim.12.gain_ref, bf16[512,896]{1,0:T(8,128)(2,1)S(1)} %collective-permute-done.3.gate_in_ref, bf16[512,896]{1,0:T(8,128)(2,1)S(1)} %copy-done.5, ...), custom_call_target="tpu_custom_call" | custom-call | tf_op jit(solution)/shard_map/gate_up_near/pallas_call | solution.py:328
  116.3 3.7 %all-to-all-start.4 = ((bf16[8,32,1920]{2,1,0:T(8,128)(2,1)}), bf16[8,32,1920]{2,1,0:T(8,128)(2,1)S(1)}, u32[]{:S(2)}, u32[]{:S(2)}) async-start(bf16[8,32,1920]{2,1,0:T(8,128)(2,1)} %bitcast.10), calls=%async_computation.4 | async-start | bytes 1966080 | tf_op jit(solution)/shard_map/all_to_all | solution.py:177
  120.0 0.0 copy-done.2
  120.0 1.0 slice_bitcast_fusion
  121.0 1.3 collective-permute-start.7
  122.3 13.1 %all-to-all-done.4.parts_ref = bf16[8,32,1920]{2,1,0:T(8,128)(2,1)S(1)} async-done(((bf16[8,32,1920]{2,1,0:T(8,128)(2,1)}), bf16[8,32,1920]{2,1,0:T(8,128)(2,1)S(1)}, u32[]{:S(2)}, u32[]{:S(2)}) %all-to-all-start.4) | async-done | bytes 983072 | tf_op jit(solution)/shard_map/all_to_all | solution.py:177
  135.4 0.6 hidden.1
  136.0 10.3 %all_to_all.41 = bf16[8,32,896]{2,1,0:T(8,128)(2,1)S(1)} all-to-all(bf16[8,32,896]{2,1,0:T(8,128)(2,1)S(1)} %hidden.1), channel_id=1, replica_groups=mesh['side'=2,'rp'=4,'rl'=2,'x'=4,'yl'=2,'core'=2] {'x','yl'}, dimensions={0} | all-to-all | bytes 917504 | tf_op jit(solution)/shard_map/all_to_all | solution.py:177
  146.2 2.2 %collective-permute-start.6 = (bf16[256,896]{1,0:T(8,128)(2,1)S(1)}, bf16[256,896]{1,0:T(8,128)(2,1)S(1)}, u32[]{:S(2)}, u32[]{:S(2)}) collective-permute-start(bf16[256,896]{1,0:T(8,128)(2,1)S(1)} %bitcast.32), channel_id=1, source_target_pairs={{0,1},{1,0},{2,3},{3,2},{4,5},{5,4},{6,7},{7,6},{8,9},{9,8},{10,11... | collective-permute-start | bytes 1376264 | tf_op jit(solution)/shard_map/ppermute | solution.py:169
  148.5 5.6 %collective-permute-done.7.weight_in_ref = bf16[896,512]{1,0:T(8,128)(2,1)} collective-permute-done((bf16[896,512]{1,0:T(8,128)(2,1)}, bf16[896,512]{1,0:T(8,128)(2,1)}, u32[]{:S(2)}, u32[]{:S(2)}) %collective-permute-start.7) | collective-permute-done | bytes 917536 | tf_op jit(solution)/shard_map/ppermute | solution.py:173
  154.0 0.0 collective-permute-done.6.theirs_ref
  154.0 1.9 down.1
  156.0 25.6 %all_to_all.42.parts_ref = bf16[16,32,512]{2,1,0:T(8,128)(2,1)S(1)} all-to-all(bf16[16,32,512]{2,1,0:T(8,128)(2,1)S(1)} %bitcast.31), channel_id=1, replica_groups=mesh['side'=2,'rp'=4,'rl'=2,'x'=4,'yl'=2,'core'=2] {'side','rl','rp'}, dimensions={0} | all-to-all | bytes 1048576 | tf_op jit(solution)/shard_map/all_to_all | solution.py:177
  181.5 0.1 final.1
  181.6 0.7 reshape.42
  182.3 7.7 %all-to-all-start.7 = ((bf16[32,4,512]{2,1,0:T(4,128)(2,1)}), bf16[32,4,512]{2,1,0:T(4,128)(2,1)S(1)}, u32[]{:S(2)}, u32[]{:S(2)}) async-start(bf16[32,4,512]{2,1,0:T(4,128)(2,1)} %reshape.42), calls=%async_computation.7 | async-start | bytes 262144 | tf_op jit(solution)/shard_map/all_to_all | solution.py:177
  190.1 7.6 %all-to-all-done.7 = bf16[32,4,512]{2,1,0:T(4,128)(2,1)S(1)} async-done(((bf16[32,4,512]{2,1,0:T(4,128)(2,1)}), bf16[32,4,512]{2,1,0:T(4,128)(2,1)S(1)}, u32[]{:S(2)}, u32[]{:S(2)}) %all-to-all-start.7) | async-done | bytes 131104 | tf_op jit(solution)/shard_map/all_to_all | solution.py:177
  197.7 0.6 reshape.44
  (8 shorter events, 0.1 us)
Async XLA Ops:
  1.1 18.5 %copy-start.7 = (bf16[1,1024,512]{2,1,0:T(8,128)(2,1)S(1)}, bf16[1,1024,512]{2,1,0:T(8,128)(2,1)}, u32[]{:S(2)}) copy-start(bf16[1,1024,512]{2,1,0:T(8,128)(2,1)} %param.18) | copy-start | bytes 3145732
  1.1 18.5 %collective-permute-start.1 = (bf16[512,512]{1,0:T(8,128)(2,1)S(1)}, bf16[512,512]{1,0:T(8,128)(2,1)S(1)}, u32[]{:S(2)}, u32[]{:S(2)}) collective-permute-start(bf16[512,512]{1,0:T(8,128)(2,1)S(1)} %slice_bitcast_fusion.3), channel_id=1, source_target_pairs={{128,0},{129,1},{130,2},{131,3},{132,4},{133,5},{134,6},{135,7},{1... | collective-permute-start | bytes 1572872 | tf_op jit(solution)/shard_map/ppermute | solution.py:173
  9.8 19.2 %all-to-all-start = ((bf16[8,4,1024]{2,1,0:T(4,128)(2,1)}), bf16[8,4,1024]{2,1,0:T(4,128)(2,1)S(1)}, u32[]{:S(2)}, u32[]{:S(2)}) async-start(bf16[8,4,1024]{2,1,0:T(4,128)(2,1)} %attend.1), calls=%async_computation | async-start | bytes 131072 | tf_op jit(solution)/shard_map/all_to_all | solution.py:177
  19.6 31.9 %copy-start = (bf16[1,512,1792]{2,1,0:T(8,128)(2,1)S(1)}, bf16[1,512,1792]{2,1,0:T(8,128)(2,1)}, u32[]{:S(2)}) copy-start(bf16[1,512,1792]{2,1,0:T(8,128)(2,1)} %gate_ref.3) | copy-start | bytes 5505028
  19.6 26.3 %collective-permute-start.2 = (bf16[512,512]{1,0:T(8,128)(2,1)S(1)}, bf16[512,512]{1,0:T(8,128)(2,1)S(1)}, u32[]{:S(2)}, u32[]{:S(2)}) collective-permute-start(bf16[512,512]{1,0:T(8,128)(2,1)S(1)} %bitcast_select_fusion.own_ref), channel_id=1, source_target_pairs={{0,16},{16,0},{1,17},{17,1},{2,18},{18,2},{3,19},{19,3},{4,20},{20... | collective-permute-start | bytes 1572872 | tf_op jit(solution)/shard_map/ppermute | solution.py:169
  40.1 5.8 %collective-permute-start = (bf16[128,1024]{1,0:T(8,128)(2,1)S(1)}, bf16[128,1024]{1,0:T(8,128)(2,1)S(1)}, u32[]{:S(2)}, u32[]{:S(2)}) collective-permute-start(bf16[128,1024]{1,0:T(8,128)(2,1)S(1)} %bitcast.34), channel_id=1, source_target_pairs={{0,1},{1,0},{2,3},{3,2},{4,5},{5,4},{6,7},{7,6},{8,9},{9,8},{10,11... | collective-permute-start | bytes 786440 | tf_op jit(solution)/shard_map/ppermute | solution.py:169
  48.0 8.7 %copy-start.8 = (bf16[512]{0:T(512)(128)(2,1)S(1)}, bf16[512]{0:T(512)(128)(2,1)}, u32[]{:S(2)}) copy-start(bf16[512]{0:T(512)(128)(2,1)} %param.17) | copy-start | bytes 3076
  48.0 15.8 %all-to-all-start.2 = ((bf16[8,32,512]{2,1,0:T(8,128)(2,1)}), bf16[8,32,512]{2,1,0:T(8,128)(2,1)S(1)}, u32[]{:S(2)}, u32[]{:S(2)}) async-start(bf16[8,32,512]{2,1,0:T(8,128)(2,1)} %bitcast.6), calls=%async_computation.2 | async-start | bytes 524288 | tf_op jit(solution)/shard_map/all_to_all | solution.py:177
  52.5 31.5 %collective-permute-start.3 = (bf16[512,896]{1,0:T(8,128)(2,1)}, bf16[512,896]{1,0:T(8,128)(2,1)S(1)}, u32[]{:S(2)}, u32[]{:S(2)}) collective-permute-start(bf16[512,896]{1,0:T(8,128)(2,1)} %slice_bitcast_fusion.2), channel_id=1, source_target_pairs={{128,0},{129,1},{130,2},{131,3},{132,4},{133,5},{134,6},{135,7},{1... | collective-permute-start | bytes 2752520 | tf_op jit(solution)/shard_map/ppermute | solution.py:173
  63.9 0.8 copy-start.6
  64.7 41.0 %all-to-all-start.3 = ((bf16[16,32,512]{2,1,0:T(8,128)(2,1)}), bf16[16,32,512]{2,1,0:T(8,128)(2,1)S(1)}, u32[]{:S(2)}, u32[]{:S(2)}) async-start(bf16[16,32,512]{2,1,0:T(8,128)(2,1)} %copy-done.6), calls=%async_computation.3 | async-start | bytes 1048576 | tf_op jit(solution)/shard_map/all_to_all | solution.py:177
  69.4 35.3 %collective-permute-start.4 = (bf16[512,896]{1,0:T(8,128)(2,1)S(1)}, bf16[512,896]{1,0:T(8,128)(2,1)S(1)}, u32[]{:S(2)}, u32[]{:S(2)}) collective-permute-start(bf16[512,896]{1,0:T(8,128)(2,1)S(1)} %slice_bitcast_fusion.1), channel_id=1, source_target_pairs={{128,0},{129,1},{130,2},{131,3},{132,4},{133,5},{134,6},{135,7},{1... | collective-permute-start | bytes 2752520 | tf_op jit(solution)/shard_map/ppermute | solution.py:173
  104.7 0.9 copy-start.3
  105.6 1.5 copy-start.1
  107.2 1.2 copy-start.4
  108.3 5.2 %copy-start.5 = (bf16[512,896]{1,0:T(8,128)(2,1)S(1)}, bf16[512,896]{1,0:T(8,128)(2,1)}, u32[]{:S(2)}) copy-start(bf16[512,896]{1,0:T(8,128)(2,1)} %copy-done.3) | copy-start | bytes 2752516
  110.1 3.5 %collective-permute-start.5 = (bf16[256,1920]{1,0:T(8,128)(2,1)S(1)}, bf16[256,1920]{1,0:T(8,128)(2,1)S(1)}, u32[]{:S(2)}, u32[]{:S(2)}) collective-permute-start(bf16[256,1920]{1,0:T(8,128)(2,1)S(1)} %gate_up_far.1), channel_id=1, source_target_pairs={{0,1},{1,0},{2,3},{3,2},{4,5},{5,4},{6,7},{7,6},{8,9},{9,8},{10,11... | collective-permute-start | bytes 2949128 | tf_op jit(solution)/shard_map/ppermute | solution.py:169
  116.3 3.7 %copy-start.2 = (bf16[1,1792,512]{2,1,0:T(8,128)(2,1)S(1)}, bf16[1,1792,512]{2,1,0:T(8,128)(2,1)}, u32[]{:S(2)}) copy-start(bf16[1,1792,512]{2,1,0:T(8,128)(2,1)} %weight_ref.1) | copy-start | bytes 5505028
  116.3 19.1 %all-to-all-start.4 = ((bf16[8,32,1920]{2,1,0:T(8,128)(2,1)}), bf16[8,32,1920]{2,1,0:T(8,128)(2,1)S(1)}, u32[]{:S(2)}, u32[]{:S(2)}) async-start(bf16[8,32,1920]{2,1,0:T(8,128)(2,1)} %bitcast.10), calls=%async_computation.4 | async-start | bytes 1966080 | tf_op jit(solution)/shard_map/all_to_all | solution.py:177
  121.0 33.0 %collective-permute-start.7 = (bf16[896,512]{1,0:T(8,128)(2,1)}, bf16[896,512]{1,0:T(8,128)(2,1)}, u32[]{:S(2)}, u32[]{:S(2)}) collective-permute-start(bf16[896,512]{1,0:T(8,128)(2,1)} %slice_bitcast_fusion), channel_id=1, source_target_pairs={{128,0},{129,1},{130,2},{131,3},{132,4},{133,5},{134,6},{135,7},{1... | collective-permute-start | bytes 2752520 | tf_op jit(solution)/shard_map/ppermute | solution.py:173
  146.2 7.8 %collective-permute-start.6 = (bf16[256,896]{1,0:T(8,128)(2,1)S(1)}, bf16[256,896]{1,0:T(8,128)(2,1)S(1)}, u32[]{:S(2)}, u32[]{:S(2)}) collective-permute-start(bf16[256,896]{1,0:T(8,128)(2,1)S(1)} %bitcast.32), channel_id=1, source_target_pairs={{0,1},{1,0},{2,3},{3,2},{4,5},{5,4},{6,7},{7,6},{8,9},{9,8},{10,11... | collective-permute-start | bytes 1376264 | tf_op jit(solution)/shard_map/ppermute | solution.py:169
  182.3 15.4 %all-to-all-start.7 = ((bf16[32,4,512]{2,1,0:T(4,128)(2,1)}), bf16[32,4,512]{2,1,0:T(4,128)(2,1)S(1)}, u32[]{:S(2)}, u32[]{:S(2)}) async-start(bf16[32,4,512]{2,1,0:T(4,128)(2,1)} %reshape.42), calls=%async_computation.7 | async-start | bytes 262144 | tf_op jit(solution)/shard_map/all_to_all | solution.py:177

commit v4 on v3

--- a/solution.py
+++ b/solution.py
@@ -23,6 +23,7 @@
 ROW = ("rp", "rl")
 HOME = ("side", "rl", "rp")
 WHOLE = pl.BlockSpec(memory_space=pltpu.VMEM)
+HELD = pl.BlockSpec(memory_space=pl.ANY)
 SCALARS = pl.BlockSpec(memory_space=pltpu.SMEM)
 
 
@@ -128,13 +129,13 @@
     for h in range(H):
         block, q_at = h // heads, h % heads
         side, low, home = block % sides, (block // sides) % 2, block // (2 * sides)
-        at = (low * heads + q_at) * HD
-        out_all[slot, side * pairs + home:side * pairs + home + 1, at:at + HD] = out[h:h + 1]
+        at = (side * pairs + home) * 2 + low
+        out_all[slot, at:at + 1, q_at * HD:(q_at + 1) * HD] = out[h:h + 1]
 
     @pl.when(slot == slots - 1)
     def _():
         for d in range(o_ref.shape[0]):
-            o_ref[d] = jnp.concatenate([out_all[j, d:d + 1] for j in range(slots)], axis=0).astype(jnp.bfloat16)
+            o_ref[d] = jnp.concatenate([out_all[j, 2 * d:2 * d + 2] for j in range(slots)], axis=0).astype(jnp.bfloat16)
 
 
 def attention(queries, new_entries, cache_keys, cache_values, lengths, pairs):
@@ -150,17 +151,17 @@
         return (0, at, 1, 0)
 
     high = pl.BlockSpec((1, 1, half, width), last_long)
-    heads = H * HD // (2 * pairs)
+    heads = H * HD // (4 * pairs)
     grid_spec = pltpu.PrefetchScalarGridSpec(
         num_scalar_prefetch=1, grid=(slots,),
         in_specs=[pl.BlockSpec((slots, H * HD), lambda s, n: (0, 0)), pl.BlockSpec((slots, 2 * width), lambda s, n: (0, 0)), low, high, low, high],
-        out_specs=pl.BlockSpec((2 * pairs, slots, heads), lambda s, n: (0, 0, 0)),
+        out_specs=pl.BlockSpec((2 * pairs, 2 * slots, heads), lambda s, n: (0, 0, 0)),
         scratch_shapes=[
             pltpu.VMEM((slots, H, HD), jnp.float32), pltpu.VMEM((slots, 2 * KVH, HD), jnp.float32),
-            pltpu.VMEM((H, 2 * half), jnp.float32), pltpu.VMEM((H, HD), jnp.float32), pltpu.VMEM((slots, 2 * pairs, heads), jnp.float32)])
+            pltpu.VMEM((H, 2 * half), jnp.float32), pltpu.VMEM((H, HD), jnp.float32), pltpu.VMEM((slots, 4 * pairs, heads), jnp.float32)])
     return pl.pallas_call(
         attend_kernel, grid_spec=grid_spec,
-        out_shape=jax.ShapeDtypeStruct((2 * pairs, slots, heads), jnp.bfloat16),
+        out_shape=jax.ShapeDtypeStruct((2 * pairs, 2 * slots, heads), jnp.bfloat16),
         compiler_params=pltpu.CompilerParams(vmem_limit_bytes=60 << 20), name="attend",
     )(lengths, queries, new_entries, cache_keys, cache_keys, cache_values, cache_values)
 
@@ -185,24 +186,22 @@
     return pl.pallas_call(kernel, out_shape=out_shape, name=name, compiler_params=pltpu.CompilerParams(vmem_limit_bytes=24 << 20), **options)
 
 
-def project_kernel(place_ref, near_ref, far_ref, own_ref, pair_ref, o_ref):
+def project_kernel(place_ref, near_ref, far_ref, own_ref, pair_ref, held_ref, o_ref):
     core, low = place_ref[0], place_ref[1]
-    rows, heads = near_ref.shape[0], own_ref.shape[0]
-    homes = o_ref.shape[1]
-    chips = rows // (homes * 4)
-    to = lax.broadcasted_iota(jnp.int32, (rows, rows), 0)
-    source = lax.broadcasted_iota(jnp.int32, (rows, rows), 1)
-    wanted = ((to // 4) % chips) * (homes * 4) + (to // (chips * 4)) * 4 + to % 4
-    order = (source == wanted).astype(jnp.bfloat16)
+    homes, group = o_ref.shape[1], o_ref.shape[2]
+    rows = homes * group
+    to = lax.broadcasted_iota(jnp.int32, (rows, 2 * rows), 0)
+    source = lax.broadcasted_iota(jnp.int32, (rows, 2 * rows), 1)
+    pick_own = (source == 2 * to + low).astype(jnp.bfloat16)
+    pick_pair = (source == 2 * to + 1 - low).astype(jnp.bfloat16)
     for left_ref, place in ((near_ref, core), (far_ref, 1 - core)):
-        part = matmul(left_ref[:, pl.ds(pl.multiple_of(low * heads, heads), heads)], own_ref[...])
-        part = part + matmul(left_ref[:, pl.ds(pl.multiple_of((1 - low) * heads, heads), heads)], pair_ref[...])
-        moved = matmul(order, part.astype(jnp.bfloat16)).astype(jnp.bfloat16)
+        part = matmul(matmul(pick_own, left_ref[...]).astype(jnp.bfloat16), own_ref[...])
+        part = part + matmul(matmul(pick_pair, left_ref[...]).astype(jnp.bfloat16), pair_ref[...])
         for home in range(homes):
-            o_ref[place, home] = moved[home * chips * 4:(home + 1) * chips * 4]
-
-
-def stream_kernel(parts_ref, residual_ref, gain_ref, stream_ref, copies_ref):
+            o_ref[place, home] = part[home * group:(home + 1) * group].astype(jnp.bfloat16)
+
+
+def stream_kernel(parts_ref, residual_ref, gain_ref, held_ref, stream_ref, copies_ref):
     stream = residual_ref[...].astype(jnp.float32)
     for i in range(parts_ref.shape[0]):
         stream = stream + parts_ref[i].astype(jnp.float32)
@@ -213,7 +212,7 @@
 
 
 def gate_up_kernel(merge, place_ref, x_ref, gain_ref, gate_in_ref, up_in_ref, gate_ref, up_ref, *rest):
-    other_ref, o_ref = rest if merge else (None, rest[0])
+    other_ref, o_ref = rest[0], rest[1]
     side = place_ref[2]
     units = gate_in_ref.shape[1]
     x = x_ref[...]
@@ -244,7 +243,7 @@
     o_ref[:, 2 * units:] = jnp.where(lane == 0, high, jnp.where(lane == 1, squares - high, 0.0)).astype(jnp.bfloat16)
 
 
-def hidden_kernel(parts_ref, copies_ref):
+def hidden_kernel(parts_ref, held_ref, copies_ref):
     units = copies_ref.shape[2]
     sums = parts_ref[0].astype(jnp.float32)
     for i in range(1, parts_ref.shape[0]):
@@ -258,30 +257,37 @@
         copies_ref[i] = hidden
 
 
-def down_kernel(place_ref, mine_ref, theirs_ref, weight_in_ref, weight_ref, o_ref):
+def down_kernel(place_ref, mine_ref, theirs_ref, first_ref, rest_ref, weight_ref, o_ref):
     core, side = place_ref[0], place_ref[2]
-    units = weight_in_ref.shape[0]
-
-    def fill(weight):
-        o_ref[core] = matmul(mine_ref[...], weight).astype(jnp.bfloat16)
-        o_ref[1 - core] = matmul(theirs_ref[...], weight).astype(jnp.bfloat16)
+    cut = first_ref.shape[0]
+    units = cut + rest_ref.shape[0]
+
+    def fill(first, rest):
+        for left_ref, place in ((mine_ref, core), (theirs_ref, 1 - core)):
+            part = (matmul(left_ref[:, :cut], first) + matmul(left_ref[:, cut:], rest)).astype(jnp.bfloat16)
+            group = o_ref.shape[2]
+            for row in range(o_ref.shape[0]):
+                o_ref[row, place] = part[row * group:(row + 1) * group]
 
     @pl.when(side == 0)
     def _():
-        fill(weight_in_ref[...])
+        fill(first_ref[...], rest_ref[...])
 
     @pl.when(side != 0)
     def _():
-        fill(weight_ref[0, units:, :])
-
-
-def final_kernel(parts_ref, stream_ref, copies_ref):
+        fill(weight_ref[0, units:units + cut, :], weight_ref[0, units + cut:, :])
+
+
+def final_kernel(place_ref, parts_ref, stream_ref, copies_ref):
+    core_half = stream_ref.shape[0]
     total = parts_ref[0].astype(jnp.float32)
     for i in range(1, parts_ref.shape[0]):
         total = total + parts_ref[i].astype(jnp.float32)
-    final = (stream_ref[...] + total).astype(jnp.bfloat16)
-    for i in range(copies_ref.shape[0]):
-        copies_ref[i] = final
+    for half in range(2):
+        rows = slice(half * core_half, (half + 1) * core_half)
+        final = total[rows] + jnp.where(place_ref[2] == half, stream_ref[...], 0.0)
+        for i in range(copies_ref.shape[0]):
+            copies_ref[i, rows] = final.astype(jnp.bfloat16)
 
 
 def local(queries, new_entries, cache_keys, cache_values, lengths, residual, norm_gain, out_weight, gate_weight, up_weight, down_weight):
@@ -303,46 +309,50 @@
     by_pair, gate_late, up_late, down_late = lax.optimization_barrier((by_pair, gate_weight, up_weight, down_weight))
     gate_in = from_ffn(gate_late[0, :, :units])
     up_in = from_ffn(up_late[0, :, :units])
-    down_in = from_ffn(down_late[0, :units])
-    mine = exchange(by_pair, ("side", "rp"))[:pairs].reshape(pairs * slots, 2 * head_part)
-    near = exchange(jnp.broadcast_to(mine[None], (chips,) + mine.shape), CHIPS).reshape(chips * pairs * slots, 2 * head_part)
+    cut = units // 2 // 256 * 256 + 256
+    down_first = from_ffn(down_late[0, :cut])
+    down_rest = from_ffn(down_late[0, cut:units])
+    arrived = lax.ppermute(by_pair[pairs:], "side", [(0, 1)])
+    mine = jnp.where(side == 0, by_pair[:pairs], arrived)
+    near = exchange(jnp.broadcast_to(mine[:, None], (pairs, chips) + mine.shape[1:]).reshape((pairs * chips,) + mine.shape[1:]), ("rp",) + CHIPS).reshape(pairs * chips * 2 * slots, head_part)
     far = flip(near, "core")
-    part = call(project_kernel, "project", jax.ShapeDtypeStruct((2, pairs, group, width), bf16), in_specs=[SCALARS, WHOLE, WHOLE, WHOLE, WHOLE], out_specs=WHOLE)(place, near, far, out_own, out_pair)
+    part = call(project_kernel, "project", jax.ShapeDtypeStruct((2, pairs, group, width), bf16), in_specs=[SCALARS, WHOLE, WHOLE, WHOLE, WHOLE, HELD], out_specs=WHOLE)(place, near, far, out_own, out_pair, gate_in)
     parts = exchange(part.reshape(2 * pairs, group, width), ("side", "rp"))
     own_residual = lax.dynamic_slice(residual.reshape(rows, chips, 2, slots, width), (row, 0, side, 0, 0), (1, chips, 1, slots, width)).reshape(group, width)
-    stream, copies = call(stream_kernel, "stream", (jax.ShapeDtypeStruct((group, width), jnp.float32), jax.ShapeDtypeStruct((2 * rows, group, width), bf16)), in_specs=[WHOLE] * 3, out_specs=(WHOLE, WHOLE))(parts, own_residual, gain)
+    stream, copies = call(stream_kernel, "stream", (jax.ShapeDtypeStruct((group, width), jnp.float32), jax.ShapeDtypeStruct((2 * rows, group, width), bf16)), in_specs=[WHOLE] * 3 + [HELD], out_specs=(WHOLE, WHOLE))(parts, own_residual, gain, up_in)
     scaled = exchange(copies, HOME).reshape(total, width)
 
     steps = 2
     block = total // (2 * steps)
     wide = 2 * units + 128
 
-    def gate_up(which, name, *other):
+    def gate_up(which, name, extra, other):
         fixed = lambda shape: pl.BlockSpec(shape, lambda i, p: (0,) * len(shape))
         piece = pl.BlockSpec((block, wide), lambda i, p: (i, 0))
         grid_spec = pltpu.PrefetchScalarGridSpec(
             num_scalar_prefetch=1, grid=(steps,),
             in_specs=[pl.BlockSpec((block, width), lambda i, p: (which(p[0]) * steps + i, 0)), fixed((1, width)), fixed((width, units)), fixed((width, units)),
-                fixed((1, width, 2 * units)), fixed((1, width, 2 * units))] + [piece] * len(other),
+                fixed((1, width, 2 * units)), fixed((1, width, 2 * units))] + [piece if other else HELD],
             out_specs=piece)
-        return call(functools.partial(gate_up_kernel, bool(other)), name, jax.ShapeDtypeStruct((total // 2, wide), bf16), grid_spec=grid_spec)(
-            place, scaled, gain, gate_in, up_in, gate_weight, up_weight, *other)
-
-    far_part = gate_up(lambda c: 1 - c, "gate_up_far")
-    sent = gate_up(lambda c: c, "gate_up_near", flip(far_part, "core"))
+        return call(functools.partial(gate_up_kernel, other), name, jax.ShapeDtypeStruct((total // 2, wide), bf16), grid_spec=grid_spec)(
+            place, scaled, gain, gate_in, up_in, gate_weight, up_weight, extra)
+
+    far_part = gate_up(lambda c: 1 - c, "gate_up_far", down_first, False)
+    sent = gate_up(lambda c: c, "gate_up_near", flip(far_part, "core"), True)
     share = total // (2 * chips)
     sums = exchange(sent.reshape(chips, share, wide), CHIPS)
     hidden = call(hidden_kernel, "hidden", jax.ShapeDtypeStruct((chips, share, units), bf16), grid=(2,),
-        in_specs=[pl.BlockSpec((chips, share // 2, wide), lambda i: (0, i, 0))], out_specs=pl.BlockSpec((chips, share // 2, units), lambda i: (0, i, 0)))(sums)
+        in_specs=[pl.BlockSpec((chips, share // 2, wide), lambda i: (0, i, 0)), HELD], out_specs=pl.BlockSpec((chips, share // 2, units), lambda i: (0, i, 0)))(sums, down_rest)
     hidden = exchange(hidden, CHIPS).reshape(total // 2, units)
-    down = call(down_kernel, "down", jax.ShapeDtypeStruct((2, total // 2, width), bf16), in_specs=[SCALARS] + [WHOLE] * 4, out_specs=WHOLE)(
-        place, hidden, flip(hidden, "core"), down_in, down_weight)
-    downs = exchange(down.reshape(2 * rows, group, width), HOME)
-    final = call(final_kernel, "final", jax.ShapeDtypeStruct((4, group, width), bf16), in_specs=[WHOLE] * 2, out_specs=WHOLE)(downs, stream)
+    down = call(down_kernel, "down", jax.ShapeDtypeStruct((rows, 2, group, width), bf16), in_specs=[SCALARS] + [WHOLE] * 5, out_specs=WHOLE)(
+        place, hidden, flip(hidden, "core"), down_first, down_rest, down_weight)
+    downs = exchange(down.reshape(rows, 2 * group, width), ("rl", "rp"))
+    final = call(final_kernel, "final", jax.ShapeDtypeStruct((2, 2 * group, width), bf16), in_specs=[SCALARS] + [WHOLE] * 2, out_specs=WHOLE)(place, downs, stream)
     back = exchange(final.reshape(4 * chips, slots, width), ("side", "core") + CHIPS)
     back = back.reshape(2, 2, lax.axis_size("x"), lax.axis_size("yl"), slots, width)
     half = lax.axis_size("x") // 2
-    back = lax.dynamic_slice(back, (core, 0, side * half, 0, 0, 0), (1, 2, half, lax.axis_size("yl"), slots, width))[0]
+    back = lax.dynamic_slice_in_dim(back, side * half, half, 2).astype(jnp.float32)
+    back = (back[0] + back[1]).astype(bf16)
     return back.transpose(3, 1, 2, 0, 4).reshape(slots, width * chips)
 
 

time: 200 us -> 194 us (0.970)
  starting transfers between devices: 42.9 us -> 57.9 us
  waiting for transfers between devices: 78.9 us -> 64.1 us
  blocking collectives: 46.9 us -> 33.3 us
  local copies, waits for them, and re-layouts: 13 us -> 19.2 us
    all_to_all x5, waiting for transfers between devices: 36.1 us -> 21.2 us  [exchange(): return lax.all_to_all(value, axes, split_axis=0, concat_axis=0, tiled=True)]
    all_to_all x3 -> x2, blocking collectives: 46.9 us -> 33.3 us  [exchange(): return lax.all_to_all(value, axes, split_axis=0, concat_axis=0, tiled=True)]
    all_to_all x5, starting transfers between devices: 28.2 us -> 35.4 us  [exchange(): return lax.all_to_all(value, axes, split_axis=0, concat_axis=0, tiled=True)]
    ppermute x0 -> x1, starting transfers between devices: none -> 6.27 us  [local(): arrived = lax.ppermute(by_pair[pairs:], 'side', [(0, 1)])]
    ppermute x4, waiting for transfers between devices: 3.28 us -> 6.88 us  [flip(): return lax.ppermute(value, axis, [(0, 1), (1, 0)])]
    ppermute x4 -> x5, waiting for transfers between devices: 39.5 us -> 36 us  [from_ffn(): return lax.ppermute(value, 'side', [(1, 0)])]
    unnamed x19 -> x23, local copies, waits for them, and re-layouts: 5.22 us -> 7.93 us
    ppermute x4 -> x5, starting transfers between devices: 5.28 us -> 6.57 us  [from_ffn(): return lax.ppermute(value, 'side', [(1, 0)])]
  transfers between devices with their start and end apart: 13 -> 15, of which waited for: 9 -> 9; matrix products, arithmetic and copies ran while one was open for 3% -> 6% of each run, Pallas kernels for 4% -> 4%
where the time goes in v4:
time: 194 us; the launch traced here: 193 us
  waiting for transfers between devices  64.1 us (33%)
  starting transfers between devices  57.9 us (30%)
  blocking collectives  33.3 us (17%)
  local copies, waits for them, and re-layouts  19.2 us (10%)
  Pallas kernels  16.7 us (9%)
    ppermute x5, waiting for transfers between devices, from_ffn(): return lax.ppermute(value, 'side', [(1, 0)])  36 us
    all_to_all x5, starting transfers between devices, exchange(): return lax.all_to_all(value, axes, split_axis=0, concat_axis=0, tiled=True)  35.4 us
    all_to_all x2, blocking collectives, exchange(): return lax.all_to_all(value, axes, split_axis=0, concat_axis=0, tiled=True)  33.3 us
    all_to_all x5, waiting for transfers between devices, exchange(): return lax.all_to_all(value, axes, split_axis=0, concat_axis=0, tiled=True)  21.2 us
    ppermute x4, starting transfers between devices, flip(): return lax.ppermute(value, axis, [(0, 1), (1, 0)])  9.69 us
    unnamed x23, local copies, waits for them, and re-layouts  7.93 us
    ppermute x4, waiting for transfers between devices, flip(): return lax.ppermute(value, axis, [(0, 1), (1, 0)])  6.88 us
    ppermute x5, starting transfers between devices, from_ffn(): return lax.ppermute(value, 'side', [(1, 0)])  6.57 us
  transfers between devices with their start and end apart: 15, of which 9 were waited for; matrix products, arithmetic and copies ran while one was open for 6% of the time, Pallas kernels for 4%

profile of v4, /device:TPU:33, one launch (start us, length us, event | category | flops | bytes accessed | tf_op | source)
XLA Modules:
  0.0 193.1 jit_solution(14271917032487224258)
XLA Ops:
  0.0 1.1 slice_bitcast_fusion.3
  1.1 0.0 copy-start
  1.1 1.4 collective-permute-start.2
  2.5 6.3 %attend.1 = bf16[8,8,512]{2,1,0:T(8,128)(2,1)} custom-call(s32[4]{0:T(128)} %len_ref.1, bf16[4,8192]{1,0:T(4,128)(2,1)} %q_ref.1, bf16[4,2048]{1,0:T(4,128)(2,1)} %new_ref.1, bf16[1,4,256,1024]{3,2,1,0:T(8,128)(2,1)} %k_hi_ref.1, bf16[1,4,256,1024]{3,2,1,0:T(8,128)(2,1)} %k_hi_ref.1, bf16[1,4,256,1024]{3,2,1,0:T(8,128)(2,1)} %v_hi_ref.1, ...), custom_call_target="tpu_custom_call" | custom-call | tf_op jit(solution)/shard_map/attend/pallas_call | solution.py:162
  8.8 0.8 slice.31
  9.7 6.3 %collective-permute-start = (bf16[4,8,512]{2,1,0:T(8,128)(2,1)S(1)}, bf16[4,8,512]{2,1,0:T(8,128)(2,1)S(1)}, u32[]{:S(2)}, u32[]{:S(2)}) collective-permute-start(bf16[4,8,512]{2,1,0:T(8,128)(2,1)S(1)} %slice.31), channel_id=1, source_target_pairs={{0,128},{1,129},{2,130},{3,131},{4,132},{5,133},{6,134},{7,135},{8... | collective-permute-start | bytes 98312 | tf_op jit(solution)/shard_map/ppermute | solution.py:315
  16.0 0.0 copy-done
  16.0 1.0 slice_bitcast_fusion.1
  17.0 1.3 collective-permute-start.4
  18.3 0.0 collective-permute-done
  18.3 0.7 broadcast_in_dim.4
  19.0 11.1 %all-to-all-start = ((bf16[32,8,512]{2,1,0:T(8,128)(2,1)}), bf16[32,8,512]{2,1,0:T(8,128)(2,1)S(1)}, u32[]{:S(2)}, u32[]{:S(2)}) async-start(bf16[32,8,512]{2,1,0:T(8,128)(2,1)} %bitcast.3), calls=%async_computation | async-start | bytes 524288 | tf_op jit(solution)/shard_map/all_to_all | solution.py:178
  30.2 0.0 collective-permute-done.2
  30.2 1.3 bitcast_select_fusion.own_ref
  31.5 1.2 collective-permute-start.3
  32.7 2.2 %slice_bitcast_fusion = bf16[512,896]{1,0:T(8,128)(2,1)} fusion(bf16[1,512,1792]{2,1,0:T(8,128)(2,1)} %up_ref.3), kind=kLoop, calls=%fused_computation | loop fusion | bytes 1835008 | tf_op jit(solution)/shard_map/squeeze | solution.py:311
  34.9 1.3 collective-permute-start.5
  36.2 4.2 %all-to-all-done = bf16[32,8,512]{2,1,0:T(8,128)(2,1)S(1)} async-done(((bf16[32,8,512]{2,1,0:T(8,128)(2,1)}), bf16[32,8,512]{2,1,0:T(8,128)(2,1)S(1)}, u32[]{:S(2)}, u32[]{:S(2)}) %all-to-all-start) | async-done | bytes 262176 | tf_op jit(solution)/shard_map/all_to_all | solution.py:178
  40.4 4.7 %collective-permute-start.1 = (bf16[256,512]{1,0:T(8,128)(2,1)S(1)}, bf16[256,512]{1,0:T(8,128)(2,1)}, u32[]{:S(2)}, u32[]{:S(2)}) collective-permute-start(bf16[256,512]{1,0:T(8,128)(2,1)S(1)} %bitcast.37), channel_id=1, source_target_pairs={{0,1},{1,0},{2,3},{3,2},{4,5},{5,4},{6,7},{7,6},{8,9},{9,8},{10,11... | collective-permute-start | bytes 786440 | tf_op jit(solution)/shard_map/ppermute | solution.py:170
  45.1 0.1 pad_add_fusion.place_ref
  45.2 1.2 collective-permute-done.1.far_ref
  46.4 0.0 collective-permute-done.4.held_ref.gate_in_ref
  46.4 2.0 %collective-permute-done.3.pair_ref = bf16[512,512]{1,0:T(8,128)(2,1)} collective-permute-done((bf16[512,512]{1,0:T(8,128)(2,1)S(1)}, bf16[512,512]{1,0:T(8,128)(2,1)}, u32[]{:S(2)}, u32[]{:S(2)}) %collective-permute-start.3) | collective-permute-done | bytes 524320 | tf_op jit(solution)/shard_map/ppermute | solution.py:170
  48.4 1.9 project.1
  50.3 0.7 copy-done.7
  51.0 10.7 %all-to-all-start.1 = ((bf16[8,32,512]{2,1,0:T(8,128)(2,1)}), bf16[8,32,512]{2,1,0:T(8,128)(2,1)S(1)}, u32[]{:S(2)}, u32[]{:S(2)}) async-start(bf16[8,32,512]{2,1,0:T(8,128)(2,1)} %bitcast.39), calls=%async_computation.1 | async-start | bytes 524288 | tf_op jit(solution)/shard_map/all_to_all | solution.py:178
  61.7 1.2 reshape.42
  62.8 0.6 dynamic-slice_bitcast_fusion
  63.5 0.8 reshape.43.residual_ref
  64.3 0.0 collective-permute-done.5.held_ref.up_in_ref
  64.3 9.3 %all-to-all-done.1.parts_ref = bf16[8,32,512]{2,1,0:T(8,128)(2,1)S(1)} async-done(((bf16[8,32,512]{2,1,0:T(8,128)(2,1)}), bf16[8,32,512]{2,1,0:T(8,128)(2,1)S(1)}, u32[]{:S(2)}, u32[]{:S(2)}) %all-to-all-start.1) | async-done | bytes 262176 | tf_op jit(solution)/shard_map/all_to_all | solution.py:178
  73.5 0.1 stream.1
  73.6 0.8 copy-done.8
  74.4 4.0 %all-to-all-start.2 = ((bf16[16,32,512]{2,1,0:T(8,128)(2,1)}), bf16[16,32,512]{2,1,0:T(8,128)(2,1)S(1)}, u32[]{:S(2)}, u32[]{:S(2)}) async-start(bf16[16,32,512]{2,1,0:T(8,128)(2,1)} %copy-done.8), calls=%async_computation.2 | async-start | bytes 1048576 | tf_op jit(solution)/shard_map/all_to_all | solution.py:178
  78.4 1.1 slice_bitcast_fusion.2
  79.5 1.3 collective-permute-start.6
  80.8 19.2 %collective-permute-done.6.rest_0_.first_ref = bf16[512,512]{1,0:T(8,128)(2,1)S(1)} collective-permute-done((bf16[512,512]{1,0:T(8,128)(2,1)S(1)}, bf16[512,512]{1,0:T(8,128)(2,1)S(1)}, u32[]{:S(2)}, u32[]{:S(2)}) %collective-permute-start.6) | collective-permute-done | bytes 524320 | tf_op jit(solution)/shard_map/ppermute | solution.py:174
  100.0 0.8 copy-done.4
  100.8 0.0 all-to-all-done.2
  100.8 1.5 copy-done.1
  102.3 1.0 copy-done.5
  103.3 2.9 %gate_up_far.1 = bf16[256,1920]{1,0:T(8,128)(2,1)S(1)} custom-call(s32[3]{0:T(128)S(1)} %pad_add_fusion.place_ref, bf16[512,512]{1,0:T(8,128)(2,1)S(1)} %bitcast.31, bf16[1,512]{1,0:T(2,128)(2,1)S(1)} %broadcast_in_dim.10.gain_ref, bf16[512,896]{1,0:T(8,128)(2,1)S(1)} %collective-permute-done.4.held_ref.gate_in_ref, ...), custom_call_target="tpu_custom_call" | custom-call | tf_op jit(solution)/shard_map/gate_up_far/pallas_call | solution.py:337
  106.2 1.8 collective-permute-start.7
  108.0 2.2 %collective-permute-done.7.rest_0_ = bf16[256,1920]{1,0:T(8,128)(2,1)S(1)} collective-permute-done((bf16[256,1920]{1,0:T(8,128)(2,1)S(1)}, bf16[256,1920]{1,0:T(8,128)(2,1)S(1)}, u32[]{:S(2)}, u32[]{:S(2)}) %collective-permute-start.7) | collective-permute-done | bytes 983072 | tf_op jit(solution)/shard_map/ppermute | solution.py:170
  110.2 3.1 %gate_up_near.1 = bf16[256,1920]{1,0:T(8,128)(2,1)S(1)} custom-call(s32[3]{0:T(128)S(1)} %pad_add_fusion.place_ref, bf16[512,512]{1,0:T(8,128)(2,1)S(1)} %bitcast.32, bf16[1,512]{1,0:T(2,128)(2,1)S(1)} %broadcast_in_dim.10.gain_ref, bf16[512,896]{1,0:T(8,128)(2,1)S(1)} %collective-permute-done.4.held_ref.gate_in_ref, ...), custom_call_target="tpu_custom_call" | custom-call | tf_op jit(solution)/shard_map/gate_up_near/pallas_call | solution.py:337
  113.3 1.0 copy-done.3
  114.3 3.6 %all-to-all-start.3 = ((bf16[8,32,1920]{2,1,0:T(8,128)(2,1)}), bf16[8,32,1920]{2,1,0:T(8,128)(2,1)S(1)}, u32[]{:S(2)}, u32[]{:S(2)}) async-start(bf16[8,32,1920]{2,1,0:T(8,128)(2,1)} %bitcast.33), calls=%async_computation.3 | async-start | bytes 1966080 | tf_op jit(solution)/shard_map/all_to_all | solution.py:178
  117.9 1.1 slice_bitcast_fusion.4
  118.9 1.3 collective-permute-start.8
  120.2 16.9 %collective-permute-done.8.held_ref.rest_ref = bf16[384,512]{1,0:T(8,128)(2,1)S(1)} collective-permute-done((bf16[384,512]{1,0:T(8,128)(2,1)S(1)}, bf16[384,512]{1,0:T(8,128)(2,1)S(1)}, u32[]{:S(2)}, u32[]{:S(2)}) %collective-permute-start.8) | collective-permute-done | bytes 393248 | tf_op jit(solution)/shard_map/ppermute | solution.py:174
  137.1 0.0 all-to-all-done.3.parts_ref
  137.1 0.6 hidden.1
  137.7 13.1 %all_to_all.35 = bf16[8,32,896]{2,1,0:T(8,128)(2,1)S(1)} all-to-all(bf16[8,32,896]{2,1,0:T(8,128)(2,1)S(1)} %hidden.1), channel_id=1, replica_groups=mesh['side'=2,'rp'=4,'rl'=2,'x'=4,'yl'=2,'core'=2] {'x','yl'}, dimensions={0} | all-to-all | bytes 917504 | tf_op jit(solution)/shard_map/all_to_all | solution.py:178
  150.8 2.0 %collective-permute-start.9 = (bf16[256,896]{1,0:T(8,128)(2,1)S(1)}, bf16[256,896]{1,0:T(8,128)(2,1)S(1)}, u32[]{:S(2)}, u32[]{:S(2)}) collective-permute-start(bf16[256,896]{1,0:T(8,128)(2,1)S(1)} %bitcast.35), channel_id=1, source_target_pairs={{0,1},{1,0},{2,3},{3,2},{4,5},{5,4},{6,7},{7,6},{8,9},{9,8},{10,11... | collective-permute-start | bytes 1376264 | tf_op jit(solution)/shard_map/ppermute | solution.py:170
  152.8 1.4 collective-permute-done.9.theirs_ref
  154.2 1.5 copy-done.2
  155.7 1.2 down.1
  157.0 20.2 %all_to_all.36.parts_ref = bf16[8,64,512]{2,1,0:T(8,128)(2,1)S(1)} all-to-all(bf16[8,64,512]{2,1,0:T(8,128)(2,1)S(1)} %bitcast.34), channel_id=1, replica_groups=mesh['side'=2,'rp'=4,'rl'=2,'x'=4,'yl'=2,'core'=2] {'rl','rp'}, dimensions={0} | all-to-all | bytes 1048576 | tf_op jit(solution)/shard_map/all_to_all | solution.py:178
  177.2 0.6 final.1
  177.8 0.7 reshape.48
  178.5 6.0 %all-to-all-start.6 = ((bf16[32,4,512]{2,1,0:T(4,128)(2,1)}), bf16[32,4,512]{2,1,0:T(4,128)(2,1)S(1)}, u32[]{:S(2)}, u32[]{:S(2)}) async-start(bf16[32,4,512]{2,1,0:T(4,128)(2,1)} %reshape.48), calls=%async_computation.6 | async-start | bytes 262144 | tf_op jit(solution)/shard_map/all_to_all | solution.py:178
  184.6 7.7 %all-to-all-done.6 = bf16[32,4,512]{2,1,0:T(4,128)(2,1)S(1)} async-done(((bf16[32,4,512]{2,1,0:T(4,128)(2,1)}), bf16[32,4,512]{2,1,0:T(4,128)(2,1)S(1)}, u32[]{:S(2)}, u32[]{:S(2)}) %all-to-all-start.6) | async-done | bytes 131104 | tf_op jit(solution)/shard_map/all_to_all | solution.py:178
  192.3 0.1 copy_convert_fusion
  192.4 0.6 reshape.50
  (17 shorter events, 0.1 us)
Async XLA Ops:
  1.1 14.9 %copy-start = (bf16[1,512,1792]{2,1,0:T(8,128)(2,1)S(1)}, bf16[1,512,1792]{2,1,0:T(8,128)(2,1)}, u32[]{:S(2)}) copy-start(bf16[1,512,1792]{2,1,0:T(8,128)(2,1)} %gate_ref.3) | copy-start | bytes 5505028
  1.1 29.1 %collective-permute-start.2 = (bf16[512,512]{1,0:T(8,128)(2,1)S(1)}, bf16[512,512]{1,0:T(8,128)(2,1)}, u32[]{:S(2)}, u32[]{:S(2)}) collective-permute-start(bf16[512,512]{1,0:T(8,128)(2,1)S(1)} %slice_bitcast_fusion.3), channel_id=1, source_target_pairs={{128,0},{129,1},{130,2},{131,3},{132,4},{133,5},{134,6},{135,7},{1... | collective-permute-start | bytes 1572872 | tf_op jit(solution)/shard_map/ppermute | solution.py:174
  8.8 9.4 %copy-start.9 = (bf16[8,8,512]{2,1,0:T(8,128)(2,1)S(1)}, bf16[8,8,512]{2,1,0:T(8,128)(2,1)}, u32[]{:S(2)}) copy-start(bf16[8,8,512]{2,1,0:T(8,128)(2,1)} %attend.1) | copy-start | bytes 196612
  9.7 8.6 %collective-permute-start = (bf16[4,8,512]{2,1,0:T(8,128)(2,1)S(1)}, bf16[4,8,512]{2,1,0:T(8,128)(2,1)S(1)}, u32[]{:S(2)}, u32[]{:S(2)}) collective-permute-start(bf16[4,8,512]{2,1,0:T(8,128)(2,1)S(1)} %slice.31), channel_id=1, source_target_pairs={{0,128},{1,129},{2,130},{3,131},{4,132},{5,133},{6,134},{7,135},{8... | collective-permute-start | bytes 98312 | tf_op jit(solution)/shard_map/ppermute | solution.py:315
  17.0 29.4 %collective-permute-start.4 = (bf16[512,896]{1,0:T(8,128)(2,1)}, bf16[512,896]{1,0:T(8,128)(2,1)S(1)}, u32[]{:S(2)}, u32[]{:S(2)}) collective-permute-start(bf16[512,896]{1,0:T(8,128)(2,1)} %slice_bitcast_fusion.1), channel_id=1, source_target_pairs={{128,0},{129,1},{130,2},{131,3},{132,4},{133,5},{134,6},{135,7},{1... | collective-permute-start | bytes 2752520 | tf_op jit(solution)/shard_map/ppermute | solution.py:174
  19.0 21.4 %all-to-all-start = ((bf16[32,8,512]{2,1,0:T(8,128)(2,1)}), bf16[32,8,512]{2,1,0:T(8,128)(2,1)S(1)}, u32[]{:S(2)}, u32[]{:S(2)}) async-start(bf16[32,8,512]{2,1,0:T(8,128)(2,1)} %bitcast.3), calls=%async_computation | async-start | bytes 524288 | tf_op jit(solution)/shard_map/all_to_all | solution.py:178
  31.5 16.9 %collective-permute-start.3 = (bf16[512,512]{1,0:T(8,128)(2,1)S(1)}, bf16[512,512]{1,0:T(8,128)(2,1)}, u32[]{:S(2)}, u32[]{:S(2)}) collective-permute-start(bf16[512,512]{1,0:T(8,128)(2,1)S(1)} %bitcast_select_fusion.own_ref), channel_id=1, source_target_pairs={{0,16},{16,0},{1,17},{17,1},{2,18},{18,2},{3,19},{19,3},{4,20},{20... | collective-permute-start | bytes 1572872 | tf_op jit(solution)/shard_map/ppermute | solution.py:170
  34.9 29.4 %collective-permute-start.5 = (bf16[512,896]{1,0:T(8,128)(2,1)}, bf16[512,896]{1,0:T(8,128)(2,1)}, u32[]{:S(2)}, u32[]{:S(2)}) collective-permute-start(bf16[512,896]{1,0:T(8,128)(2,1)} %slice_bitcast_fusion), channel_id=1, source_target_pairs={{128,0},{129,1},{130,2},{131,3},{132,4},{133,5},{134,6},{135,7},{1... | collective-permute-start | bytes 2752520 | tf_op jit(solution)/shard_map/ppermute | solution.py:174
  40.4 6.0 %collective-permute-start.1 = (bf16[256,512]{1,0:T(8,128)(2,1)S(1)}, bf16[256,512]{1,0:T(8,128)(2,1)}, u32[]{:S(2)}, u32[]{:S(2)}) collective-permute-start(bf16[256,512]{1,0:T(8,128)(2,1)S(1)} %bitcast.37), channel_id=1, source_target_pairs={{0,1},{1,0},{2,3},{3,2},{4,5},{5,4},{6,7},{7,6},{8,9},{9,8},{10,11... | collective-permute-start | bytes 786440 | tf_op jit(solution)/shard_map/ppermute | solution.py:170
  45.2 19.1 %copy-start.10 = (bf16[512]{0:T(512)(128)(2,1)S(1)}, bf16[512]{0:T(512)(128)(2,1)}, u32[]{:S(2)}) copy-start(bf16[512]{0:T(512)(128)(2,1)} %param.17) | copy-start | bytes 3076
  50.3 0.7 copy-start.7
  51.0 22.5 %all-to-all-start.1 = ((bf16[8,32,512]{2,1,0:T(8,128)(2,1)}), bf16[8,32,512]{2,1,0:T(8,128)(2,1)S(1)}, u32[]{:S(2)}, u32[]{:S(2)}) async-start(bf16[8,32,512]{2,1,0:T(8,128)(2,1)} %bitcast.39), calls=%async_computation.1 | async-start | bytes 524288 | tf_op jit(solution)/shard_map/all_to_all | solution.py:178
  73.6 0.8 copy-start.8
  74.4 26.3 %all-to-all-start.2 = ((bf16[16,32,512]{2,1,0:T(8,128)(2,1)}), bf16[16,32,512]{2,1,0:T(8,128)(2,1)S(1)}, u32[]{:S(2)}, u32[]{:S(2)}) async-start(bf16[16,32,512]{2,1,0:T(8,128)(2,1)} %copy-done.8), calls=%async_computation.2 | async-start | bytes 1048576 | tf_op jit(solution)/shard_map/all_to_all | solution.py:178
  79.5 20.5 %collective-permute-start.6 = (bf16[512,512]{1,0:T(8,128)(2,1)S(1)}, bf16[512,512]{1,0:T(8,128)(2,1)S(1)}, u32[]{:S(2)}, u32[]{:S(2)}) collective-permute-start(bf16[512,512]{1,0:T(8,128)(2,1)S(1)} %slice_bitcast_fusion.2), channel_id=1, source_target_pairs={{128,0},{129,1},{130,2},{131,3},{132,4},{133,5},{134,6},{135,7},{1... | collective-permute-start | bytes 1572872 | tf_op jit(solution)/shard_map/ppermute | solution.py:174
  100.0 0.8 copy-start.4
  100.8 1.5 copy-start.1
  102.3 1.0 copy-start.5
  106.2 4.0 %collective-permute-start.7 = (bf16[256,1920]{1,0:T(8,128)(2,1)S(1)}, bf16[256,1920]{1,0:T(8,128)(2,1)S(1)}, u32[]{:S(2)}, u32[]{:S(2)}) collective-permute-start(bf16[256,1920]{1,0:T(8,128)(2,1)S(1)} %gate_up_far.1), channel_id=1, source_target_pairs={{0,1},{1,0},{2,3},{3,2},{4,5},{5,4},{6,7},{7,6},{8,9},{9,8},{10,11... | collective-permute-start | bytes 2949128 | tf_op jit(solution)/shard_map/ppermute | solution.py:170
  113.3 1.0 copy-start.3
  114.3 22.8 %all-to-all-start.3 = ((bf16[8,32,1920]{2,1,0:T(8,128)(2,1)}), bf16[8,32,1920]{2,1,0:T(8,128)(2,1)S(1)}, u32[]{:S(2)}, u32[]{:S(2)}) async-start(bf16[8,32,1920]{2,1,0:T(8,128)(2,1)} %bitcast.33), calls=%async_computation.3 | async-start | bytes 1966080 | tf_op jit(solution)/shard_map/all_to_all | solution.py:178
  117.8 36.4 %copy-start.6 = (bf16[512,512]{1,0:T(8,128)(2,1)S(1)}, bf16[512,512]{1,0:T(8,128)(2,1)}, u32[]{:S(2)}) copy-start(bf16[512,512]{1,0:T(8,128)(2,1)} %copy-done.4) | copy-start | bytes 1572868
  118.9 18.2 %collective-permute-start.8 = (bf16[384,512]{1,0:T(8,128)(2,1)S(1)}, bf16[384,512]{1,0:T(8,128)(2,1)S(1)}, u32[]{:S(2)}, u32[]{:S(2)}) collective-permute-start(bf16[384,512]{1,0:T(8,128)(2,1)S(1)} %slice_bitcast_fusion.4), channel_id=1, source_target_pairs={{128,0},{129,1},{130,2},{131,3},{132,4},{133,5},{134,6},{135,7},{1... | collective-permute-start | bytes 1179656 | tf_op jit(solution)/shard_map/ppermute | solution.py:174
  150.8 3.5 %collective-permute-start.9 = (bf16[256,896]{1,0:T(8,128)(2,1)S(1)}, bf16[256,896]{1,0:T(8,128)(2,1)S(1)}, u32[]{:S(2)}, u32[]{:S(2)}) collective-permute-start(bf16[256,896]{1,0:T(8,128)(2,1)S(1)} %bitcast.35), channel_id=1, source_target_pairs={{0,1},{1,0},{2,3},{3,2},{4,5},{5,4},{6,7},{7,6},{8,9},{9,8},{10,11... | collective-permute-start | bytes 1376264 | tf_op jit(solution)/shard_map/ppermute | solution.py:170
  154.2 1.5 copy-start.2
  178.5 13.7 %all-to-all-start.6 = ((bf16[32,4,512]{2,1,0:T(4,128)(2,1)}), bf16[32,4,512]{2,1,0:T(4,128)(2,1)S(1)}, u32[]{:S(2)}, u32[]{:S(2)}) async-start(bf16[32,4,512]{2,1,0:T(4,128)(2,1)} %reshape.48), calls=%async_computation.6 | async-start | bytes 262144 | tf_op jit(solution)/shard_map/all_to_all | solution.py:178

commit v5 on v3

v5 whole, which is shorter than its diff:
```python
import functools
import math
import jax
import jax.numpy as jnp
from jax import lax
from jax.experimental import pallas as pl
from jax.experimental.pallas import tpu as pltpu
from jax.sharding import Mesh, PartitionSpec as P

D = 8192
H = 64
KVH = 8
HD = 128
ORIG = 64
PER = H // KVH

rope_theta = 500000.0
stretch_factor = 8.0
eps = 1e-05

CHIPS = ("x", "yl")
COL = ("x", "yl", "core")
ROW = ("rp", "rl")
HOME = ("rl", "rp")
WHOLE = pl.BlockSpec(memory_space=pltpu.VMEM)
HELD = pl.BlockSpec(memory_space=pl.ANY)
SCALARS = pl.BlockSpec(memory_space=pltpu.SMEM)


def swap_halves(v):
    return jnp.concatenate([v[:, HD // 2:], v[:, : HD // 2]], axis=-1)


def attend_kernel(len_ref, place_ref, q_ref, new_ref, k_lo_ref, k_hi_ref, v_lo_ref, v_hi_ref, *rest):
    o_refs, (q_all, new_all, s_all, acc, out_all) = rest[:-5], rest[-5:]
    slot = pl.program_id(0)
    slots = q_ref.shape[0]
    length = len_ref[slot]
    half = k_lo_ref.shape[2]
    span = 2 * half

    @pl.when(slot == 0)
    def _():
        for h in range(H):
            q_all[:, h, :] = q_ref[:, h * HD:(h + 1) * HD].astype(jnp.float32)
        for h in range(2 * KVH):
            new_all[:, h, :] = new_ref[:, h * HD:(h + 1) * HD].astype(jnp.float32)

    lane = lax.broadcasted_iota(jnp.int32, (1, HD), 1)
    pair = jnp.where(lane < HD // 2, lane, lane - HD // 2).astype(jnp.float32)
    position = jnp.full((1, HD), length, jnp.int32).astype(jnp.float32)
    stretch = jnp.maximum(stretch_factor * (position + 1.0) / ORIG - (stretch_factor - 1.0), 1.0)
    log_base = math.log(rope_theta) + HD / (HD - 2.0) * jnp.log(stretch)
    freqs = jnp.exp(-(pair * (2.0 / HD)) * log_base)
    steps = span // 16
    fine = lax.broadcasted_iota(jnp.int32, (16, HD), 0).astype(jnp.float32)
    coarse = lax.broadcasted_iota(jnp.int32, (steps, HD), 0).astype(jnp.float32) * 16.0
    fine_cos, fine_sin = jnp.cos(fine * freqs), jnp.sin(fine * freqs)
    coarse_cos, coarse_sin = jnp.cos(coarse * freqs), jnp.sin(coarse * freqs)

    def tables(first):
        cos_parts, sin_parts = [], []
        for step in range(first, first + steps // 2):
            cc, cs = coarse_cos[step:step + 1], coarse_sin[step:step + 1]
            cos_parts.append(cc * fine_cos - cs * fine_sin)
            sin_parts.append(cs * fine_cos + cc * fine_sin)
        return jnp.concatenate(cos_parts, axis=0), jnp.concatenate(sin_parts, axis=0)

    sign = jnp.where(lane < HD // 2, -1.0, 1.0)
    cos_new = jnp.cos(position * freqs)
    sin_new = jnp.sin(position * freqs) * sign
    q = q_all[slot]
    q_rot = q * cos_new + swap_halves(q) * sin_new
    q_rot = q_rot.astype(jnp.bfloat16).astype(jnp.float32)
    q_both = jnp.concatenate([q_rot, swap_halves(q_rot) * -sign], axis=-1)
    k_new = new_all[slot, :KVH]
    k_new = k_new * cos_new + swap_halves(k_new) * sin_new
    k_new = k_new.astype(jnp.bfloat16).astype(jnp.float32)
    v_new = new_all[slot, KVH:]
    scale = HD ** (-0.5)

    def score(k_ref, first):
        cos_t, sin_t = tables(first)
        for g in range(KVH):
            kg = k_ref[0, 0, :, g * HD:(g + 1) * HD].astype(jnp.float32)
            kk = jnp.concatenate([(kg * cos_t).astype(jnp.bfloat16), (kg * sin_t).astype(jnp.bfloat16)], axis=-1)
            qg = q_both[g * PER:(g + 1) * PER].astype(jnp.bfloat16)
            s_all[g * PER:(g + 1) * PER, first * 16:first * 16 + half] = lax.dot_general(qg, kk, (((1,), (1,)), ((), ())), preferred_element_type=jnp.float32)

    score(k_lo_ref, 0)

    @pl.when(length > half)
    def _():
        score(k_hi_ref, steps // 2)

    @pl.when(length <= half)
    def _():
        s_all[:, half:] = jnp.zeros((H, half), jnp.float32)

    own, fresh = [], []
    for g in range(KVH):
        own.append(jnp.sum(q_rot[g * PER:(g + 1) * PER] * k_new[g:g + 1], axis=-1, keepdims=True))
        fresh.append(jnp.broadcast_to(v_new[g:g + 1], (PER, HD)))
    own_score = jnp.concatenate(own, axis=0) * scale
    valid = lax.broadcasted_iota(jnp.int32, (H, span), 1) < length
    s = jnp.where(valid, s_all[...] * scale, -1e30)
    top = jnp.maximum(jnp.max(s, axis=-1, keepdims=True), own_score)
    w = jnp.where(valid, jnp.exp(s - top), 0.0)
    own_w = jnp.exp(own_score - top)
    total = jnp.sum(w, axis=-1, keepdims=True) + own_w
    w16 = w.astype(jnp.bfloat16)

    def mix(v_ref, weights):
        parts = []
        for p in range(KVH // 2):
            o = jnp.dot(weights[p * 2 * PER:(p + 1) * 2 * PER], v_ref[0, 0, :, p * 2 * HD:(p + 1) * 2 * HD], preferred_element_type=jnp.float32)
            parts += [o[:PER, :HD], o[PER:, HD:]]
        return jnp.concatenate(parts, axis=0)

    acc[...] = mix(v_lo_ref, w16[:, :half]) + own_w * jnp.concatenate(fresh, axis=0)

    @pl.when(length > half)
    def _():
        acc[...] += mix(v_hi_ref, w16[:, half:])

    out = acc[...] / total
    pairs = len(o_refs)
    per_row = H // (2 * pairs)
    for h in range(H):
        at, q_at = h // per_row, h % per_row
        out_all[at // 2, slot, at % 2:at % 2 + 1, q_at * HD:(q_at + 1) * HD] = out[h:h + 1]

    @pl.when(slot == slots - 1)
    def _():
        for k in range(pairs):
            home = lax.rem(place_ref[2] + k, pairs)
            o_refs[k][...] = jnp.concatenate([out_all[home, j] for j in range(slots)], axis=0).astype(jnp.bfloat16)


def attention(place, queries, new_entries, cache_keys, cache_values, lengths, pairs):
    slots = queries.shape[0]
    half = cache_keys.shape[2] // 2
    width = KVH * HD
    low = pl.BlockSpec((1, 1, half, width), lambda s, n, p: (0, s, 0, 0))

    def last_long(s, n, p):
        at = 0
        for j in range(1, slots):
            at = jnp.where((s >= j) & (n[j] > half), j, at)
        return (0, at, 1, 0)

    high = pl.BlockSpec((1, 1, half, width), last_long)
    heads = H * HD // (2 * pairs)
    grid_spec = pltpu.PrefetchScalarGridSpec(
        num_scalar_prefetch=2, grid=(slots,),
        in_specs=[pl.BlockSpec((slots, H * HD), lambda s, n, p: (0, 0)), pl.BlockSpec((slots, 2 * width), lambda s, n, p: (0, 0)), low, high, low, high],
        out_specs=[pl.BlockSpec((2 * slots, heads), lambda s, n, p: (0, 0))] * pairs,
        scratch_shapes=[
            pltpu.VMEM((slots, H, HD), jnp.float32), pltpu.VMEM((slots, 2 * KVH, HD), jnp.float32),
            pltpu.VMEM((H, 2 * half), jnp.float32), pltpu.VMEM((H, HD), jnp.float32), pltpu.VMEM((pairs, slots, 2, heads), jnp.float32)])
    return pl.pallas_call(
        attend_kernel, grid_spec=grid_spec,
        out_shape=[jax.ShapeDtypeStruct((2 * slots, heads), jnp.bfloat16)] * pairs,
        compiler_params=pltpu.CompilerParams(vmem_limit_bytes=60 << 20), name="attend",
    )(lengths, place, queries, new_entries, cache_keys, cache_keys, cache_values, cache_values)


def flip(value, axis):
    return lax.ppermute(value, axis, [(0, 1), (1, 0)])


def turn(value, steps):
    count = lax.axis_size("rp")
    return lax.ppermute(value, "rp", [(i, (i + steps) % count) for i in range(count)])


def to_ffn(value, steps):
    count = lax.axis_size("rp")
    return lax.ppermute(value, ("side", "rp"), [(i, count + (i + steps) % count) for i in range(count)])


def exchange(value, axes):
    return lax.all_to_all(value, axes, split_axis=0, concat_axis=0, tiled=True)


def matmul(left, right):
    return jnp.dot(left, right, preferred_element_type=jnp.float32)


def call(kernel, name, out_shape, **options):
    return pl.pallas_call(kernel, out_shape=out_shape, name=name, compiler_params=pltpu.CompilerParams(vmem_limit_bytes=24 << 20), **options)


def fan_kernel(*refs):
    blocks, o_ref = refs[:-2], refs[-1]
    rows = blocks[0].shape[0]
    for i in range(o_ref.shape[0]):
        for k, block in enumerate(blocks):
            o_ref[i, k * rows:(k + 1) * rows] = block[...]


def project_kernel(place_ref, near_ref, far_ref, own_ref, pair_a_ref, pair_b_ref, held_ref, *o_refs):
    core, low = place_ref[0], place_ref[1]
    pairs, group = len(o_refs), o_refs[0].shape[1]
    slots = near_ref.shape[0] // (2 * pairs * (group // 4))
    rows = pairs * group
    to = lax.broadcasted_iota(jnp.int32, (rows, 2 * rows), 0)
    source = lax.broadcasted_iota(jnp.int32, (rows, 2 * rows), 1)
    block = (pairs - to // group) % pairs
    first = ((to % group) // slots) * (2 * slots * pairs) + block * (2 * slots) + (to % slots) * 2
    pick_own = (source == first + low).astype(jnp.bfloat16)
    pick_pair = (source == first + 1 - low).astype(jnp.bfloat16)
    cut = pair_a_ref.shape[0]
    for left_ref, place in ((near_ref, core), (far_ref, 1 - core)):
        part = matmul(matmul(pick_own, left_ref[...]).astype(jnp.bfloat16), own_ref[0])
        theirs = matmul(pick_pair, left_ref[...]).astype(jnp.bfloat16)
        part = part + matmul(theirs[:, :cut], pair_a_ref[...]) + matmul(theirs[:, cut:], pair_b_ref[...])
        for k in range(pairs):
            o_refs[k][place] = part[k * group:(k + 1) * group].astype(jnp.bfloat16)


def stream_kernel(*refs):
    parts, (residual_ref, gain_ref, held_ref, stream_ref, copies_ref) = refs[:-5], refs[-5:]
    stream = residual_ref[...].astype(jnp.float32)
    for part_ref in parts:
        stream = stream + part_ref[...].astype(jnp.float32)
    stream_ref[...] = stream
    scaled = (stream * gain_ref[...].astype(jnp.float32)).astype(jnp.bfloat16)
    for i in range(copies_ref.shape[0]):
        copies_ref[i] = scaled


def gate_up_kernel(mine_ref, theirs_ref, gain_ref, gain_theirs_ref, gate_ref, gate_theirs_ref, up_ref, up_theirs_ref, o_ref):
    half = gate_ref.shape[1]
    mine, theirs = mine_ref[...], theirs_ref[...]
    o_ref[:, :half] = (matmul(mine, gate_ref[...]) + matmul(theirs, gate_theirs_ref[...])).astype(jnp.bfloat16)
    o_ref[:, half:2 * half] = (matmul(mine, up_ref[...]) + matmul(theirs, up_theirs_ref[...])).astype(jnp.bfloat16)
    one = mine.astype(jnp.float32) * (1.0 / gain_ref[...].astype(jnp.float32))
    two = theirs.astype(jnp.float32) * (1.0 / gain_theirs_ref[...].astype(jnp.float32))
    squares = jnp.sum(one * one + two * two, axis=1, keepdims=True)
    high = squares.astype(jnp.bfloat16).astype(jnp.float32)
    lane = lax.broadcasted_iota(jnp.int32, (mine.shape[0], 128), 1)
    o_ref[:, 2 * half:] = jnp.where(lane == 0, high, jnp.where(lane == 1, squares - high, 0.0)).astype(jnp.bfloat16)


def hidden_kernel(parts_ref, copies_ref):
    half = copies_ref.shape[2]
    sums = parts_ref[0].astype(jnp.float32)
    for i in range(1, parts_ref.shape[0]):
        sums = sums + parts_ref[i].astype(jnp.float32)
    squares = sums[:, 2 * half:2 * half + 1] + sums[:, 2 * half + 1:2 * half + 2]
    inv_rms = lax.rsqrt(squares / D + eps)
    gate = sums[:, :half] * inv_rms
    up = sums[:, half:2 * half] * inv_rms
    hidden = (gate / (1.0 + jnp.exp(-gate)) * up).astype(jnp.bfloat16)
    for i in range(copies_ref.shape[0]):
        copies_ref[i] = hidden


def down_kernel(place_ref, mine_ref, theirs_ref, weight_ref, o_ref):
    half = mine_ref.shape[1]
    core = place_ref[0]
    part = matmul(mine_ref[...], weight_ref[0, pl.ds(pl.multiple_of(core * half, half), half), :])
    part = part + matmul(theirs_ref[...], weight_ref[0, pl.ds(pl.multiple_of((1 - core) * half, half), half), :])
    o_ref[...] = part.astype(jnp.bfloat16)


def final_kernel(parts_ref, stream_ref, copies_ref):
    total = parts_ref[0].astype(jnp.float32)
    for i in range(1, parts_ref.shape[0]):
        total = total + parts_ref[i].astype(jnp.float32)
    final = (stream_ref[...] + total).astype(jnp.bfloat16)
    for i in range(copies_ref.shape[0]):
        copies_ref[i] = final


def local(queries, new_entries, cache_keys, cache_values, lengths, residual, norm_gain, out_weight, gate_weight, up_weight, down_weight):
    bf16 = jnp.bfloat16
    rows, pairs, chips = lax.axis_size(ROW), lax.axis_size("rp"), lax.axis_size(CHIPS)
    row, core, side = lax.axis_index(ROW), lax.axis_index("core"), lax.axis_index("side")
    slots, width = queries.shape[0], out_weight.shape[2]
    heads = out_weight.shape[1]
    half = gate_weight.shape[2] // 2
    group = chips * 2 * slots
    total = rows * group
    place = jnp.stack([core, lax.axis_index("rl"), lax.axis_index("rp")]).astype(jnp.int32)

    pair_a = flip(out_weight[0, :heads // 2], "rl")
    pair_b = flip(out_weight[0, heads // 2:], "rl")
    gain = norm_gain[None, :]
    gain_theirs = flip(gain, "core")
    gate_theirs = flip(lax.dynamic_slice_in_dim(gate_weight[0], (1 - core) * half, half, 1), "core")
    up_theirs = flip(lax.dynamic_slice_in_dim(up_weight[0], (1 - core) * half, half, 1), "core")
    gate_mine = lax.dynamic_slice_in_dim(gate_weight[0], core * half, half, 1)
    up_mine = lax.dynamic_slice_in_dim(up_weight[0], core * half, half, 1)

    blocks = attention(place, queries, new_entries, cache_keys, cache_values, lengths, pairs)
    blocks = [to_ffn(block, k) for k, block in enumerate(blocks)]
    fanned = call(fan_kernel, "fan", jax.ShapeDtypeStruct((chips, pairs * 2 * slots, heads), bf16), in_specs=[WHOLE] * pairs + [HELD], out_specs=WHOLE)(*blocks, pair_a)
    near = exchange(fanned, CHIPS).reshape(chips * pairs * 2 * slots, heads)
    far = flip(near, "core")
    own, *parts = call(project_kernel, "project", [jax.ShapeDtypeStruct((2, group // 2, width), bf16)] * pairs, in_specs=[SCALARS] + [WHOLE] * 5 + [HELD], out_specs=[WHOLE] * pairs)(
        place, near, far, out_weight, pair_a, pair_b, gain_theirs)
    parts = [own] + [turn(part, k + 1) for k, part in enumerate(parts)]
    parts = [part.reshape(group, width) for part in parts]
    own_residual = lax.dynamic_index_in_dim(residual.reshape(rows, chips, 2, slots, width), row, 0, False).transpose(1, 0, 2, 3).reshape(group, width)
    stream, copies = call(stream_kernel, "stream", (jax.ShapeDtypeStruct((group, width), jnp.float32), jax.ShapeDtypeStruct((rows, group, width), bf16)), in_specs=[WHOLE] * (pairs + 2) + [HELD], out_specs=(WHOLE, WHOLE))(
        *parts, own_residual, gain, gain_theirs)
    scaled = exchange(copies, HOME).reshape(total, width)
    scaled_theirs = flip(scaled, "core")
    block = total // 4
    fixed = lambda shape: pl.BlockSpec(shape, lambda i: (0,) * len(shape))
    sent = call(gate_up_kernel, "gate_up", jax.ShapeDtypeStruct((total, 2 * half + 128), bf16), grid=(4,),
        in_specs=[pl.BlockSpec((block, width), lambda i: (i, 0))] * 2 + [fixed((1, width))] * 2 + [fixed((width, half))] * 4,
        out_specs=pl.BlockSpec((block, 2 * half + 128), lambda i: (i, 0)))(scaled, scaled_theirs, gain, gain_theirs, gate_mine, gate_theirs, up_mine, up_theirs)
    sums = exchange(sent.reshape(chips, group, 2 * half + 128), CHIPS)
    step = group // 4
    hidden = call(hidden_kernel, "hidden", jax.ShapeDtypeStruct((chips, group, half), bf16), grid=(4,),
        in_specs=[pl.BlockSpec((chips, step, 2 * half + 128), lambda i: (0, i, 0))], out_specs=pl.BlockSpec((chips, step, half), lambda i: (0, i, 0)))(sums)
    hidden = exchange(hidden, CHIPS).reshape(total, half)
    down = call(down_kernel, "down", jax.ShapeDtypeStruct((total, width), bf16), in_specs=[SCALARS] + [WHOLE] * 3, out_specs=WHOLE)(place, hidden, flip(hidden, "core"), down_weight)
    downs = exchange(down.reshape(rows, group, width), HOME)
    final = call(final_kernel, "final", jax.ShapeDtypeStruct((2, group, width), bf16), in_specs=[WHOLE] * 2, out_specs=WHOLE)(downs, stream)
    back = exchange(final.reshape(4 * chips, slots, width), ("side", "core") + CHIPS)
    back = back.reshape(2, 2, lax.axis_size("x"), lax.axis_size("yl"), slots, width)[1]
    part = lax.axis_size("x") // 2
    back = lax.dynamic_slice_in_dim(back, side * part, part, 1)
    return back.transpose(3, 1, 2, 0, 4).reshape(slots, width * chips)


def solution(mesh):
    sides, rows, cols = mesh.devices.shape
    inner = Mesh(mesh.devices.reshape(sides, rows // 2, 2, cols // 4, 2, 2), ("side",) + ROW + COL)
    in_specs = (
        P(ROW + COL, None),
        P(ROW + COL, None),
        P("side", ROW + COL, None, None),
        P("side", ROW + COL, None, None),
        P(ROW + COL),
        P(None, COL),
        P(COL),
        P("side", ROW, COL),
        P("side", COL, ROW),
        P("side", COL, ROW),
        P("side", ROW, COL),
    )
    return jax.shard_map(local, mesh=inner, in_specs=in_specs, out_specs=P(ROW + COL, "side"), check_vma=False)
```

time: 200 us -> 173 us (0.86)
  waiting for transfers between devices: 78.9 us -> 27.5 us
  starting transfers between devices: 42.9 us -> 56 us
  blocking collectives: 46.9 us -> 59.7 us
  local copies, waits for them, and re-layouts: 13 us -> 10.2 us
    ppermute x4 -> x7, waiting for transfers between devices: 39.5 us -> 4.26 us  [the longest x3 3.23 us: turn(): lax.ppermute(value, 'rp', [(i, (i + steps) % count) for i in range(count)])]
    all_to_all x5 -> x3, waiting for transfers between devices: 36.1 us -> 19.6 us  [exchange(): return lax.all_to_all(value, axes, split_axis=0, concat_axis=0, tiled=True)]
    ppermute x4 -> x7, starting transfers between devices: 5.28 us -> 20.2 us  [the longest x4 14.9 us: to_ffn(): lax.ppermute(value, ('side', 'rp'), [(i, count + (i + steps) % count) for...]
    all_to_all x3, blocking collectives: 46.9 us -> 59.7 us  [exchange(): return lax.all_to_all(value, axes, split_axis=0, concat_axis=0, tiled=True)]
    all_to_all x5 -> x3, starting transfers between devices: 28.2 us -> 20.6 us  [exchange(): return lax.all_to_all(value, axes, split_axis=0, concat_axis=0, tiled=True)]
    ppermute x4 -> x8, starting transfers between devices: 9.4 us -> 15.2 us  [flip(): return lax.ppermute(value, axis, [(0, 1), (1, 0)])]
    unnamed x19 -> x11, local copies, waits for them, and re-layouts: 5.22 us -> 0.06 us
    dynamic_slice x2 -> x3, local copies, waits for them, and re-layouts: 0.05 us -> 3.87 us  [the longest x1 2.67 us: local(): lax.dynamic_slice_in_dim(gate_weight[0], (1 - core) * half, half, 1)]
  transfers between devices with their start and end apart: 13 -> 18, of which waited for: 9 -> 7; matrix products, arithmetic and copies ran while one was open for 3% -> 4% of each run, Pallas kernels for 4% -> 4%
where the time goes in v5:
time: 173 us; the launch traced here: 171 us
  blocking collectives  59.7 us (35%)
  starting transfers between devices  56 us (32%)
  waiting for transfers between devices  27.5 us (16%)
  Pallas kernels  17.2 us (10%)
  local copies, waits for them, and re-layouts  10.2 us (6%)
    all_to_all x3, blocking collectives, exchange(): return lax.all_to_all(value, axes, split_axis=0, concat_axis=0, tiled=True)  59.7 us
    all_to_all x3, starting transfers between devices, exchange(): return lax.all_to_all(value, axes, split_axis=0, concat_axis=0, tiled=True)  20.6 us
    all_to_all x3, waiting for transfers between devices, exchange(): return lax.all_to_all(value, axes, split_axis=0, concat_axis=0, tiled=True)  19.6 us
    ppermute x8, starting transfers between devices, flip(): return lax.ppermute(value, axis, [(0, 1), (1, 0)])  15.2 us
    ppermute x4, starting transfers between devices, to_ffn(): lax.ppermute(value, ('side', 'rp'), [(i, count + (i + steps) % count) for...  14.9 us
    pallas_call x1, Pallas kernels, attention(): pl.pallas_call(attend_kernel, grid_spec=grid_spec, out_shape=[jax.ShapeDt...  6.76 us
    ppermute x3, starting transfers between devices, turn(): lax.ppermute(value, 'rp', [(i, (i + steps) % count) for i in range(count)])  5.32 us
    pallas_call x1, Pallas kernels, local(): call(gate_up_kernel, 'gate_up', jax.ShapeDtypeStruct((total, 2 * half + 1...  4.09 us
  transfers between devices with their start and end apart: 18, of which 7 were waited for; matrix products, arithmetic and copies ran while one was open for 4% of the time, Pallas kernels for 4%

profile of v5, /device:TPU:33, one launch (start us, length us, event | category | flops | bytes accessed | tf_op | source)
XLA Modules:
  0.0 171.4 jit_solution(10597328049294618316)
XLA Ops:
  0.0 2.1 %slice_bitcast_fusion = (bf16[512,512]{1,0:T(8,128)(2,1)}, bf16[512,512]{1,0:T(8,128)(2,1)S(1)}) fusion(bf16[1,1024,512]{2,1,0:T(8,128)(2,1)} %own_ref.1), kind=kLoop, calls=%fused_computation.4 | loop fusion | bytes 2097152 | tf_op jit(solution)/shard_map/squeeze | solution.py:289
  2.1 0.0 collective-permute-start.4
  2.1 0.7 pad_add_fusion.place_ref
  2.7 6.8 %attend.1 = (bf16[8,1024]{1,0:T(8,128)(2,1)}, bf16[8,1024]{1,0:T(8,128)(2,1)}, bf16[8,1024]{1,0:T(8,128)(2,1)}, bf16[8,1024]{1,0:T(8,128)(2,1)}) custom-call(s32[4]{0:T(128)} %len_ref.1, s32[3]{0:T(128)} %pad_add_fusion.place_ref, bf16[4,8192]{1,0:T(4,128)(2,1)} %q_ref.1, bf16[4,2048]{1,0:T(4,128)(2,1)} %new_ref.1, bf16[1,4,256,1024]{3,2,1,0:T(8,128)(2,1)} %k_hi_ref.1, ...), custom_call_target="tpu_custom_call" | custom-call | tf_op jit(solution)/shard_map/attend/pallas_call | solution.py:161
  9.5 0.0 copy-start.4
  9.5 0.0 copy-start
  9.5 0.0 copy-start.2
  9.5 5.0 %collective-permute-start = (bf16[8,1024]{1,0:T(8,128)(2,1)}, bf16[8,1024]{1,0:T(8,128)(2,1)S(1)}, u32[]{:S(2)}, u32[]{:S(2)}) collective-permute-start(bf16[8,1024]{1,0:T(8,128)(2,1)} %get-tuple-element.15), channel_id=1, source_target_pairs={{0,128},{32,160},{64,192},{96,224},{1,129},{33,161},{65,193},{97,2... | collective-permute-start | bytes 49160 | tf_op jit(solution)/shard_map/ppermute | solution.py:179
  14.5 4.0 %collective-permute-start.1 = (bf16[8,1024]{1,0:T(8,128)(2,1)}, bf16[8,1024]{1,0:T(8,128)(2,1)S(1)}, u32[]{:S(2)}, u32[]{:S(2)}) collective-permute-start(bf16[8,1024]{1,0:T(8,128)(2,1)} %get-tuple-element.16), channel_id=1, source_target_pairs={{0,160},{32,192},{64,224},{96,128},{1,161},{33,193},{65,225},{97,1... | collective-permute-start | bytes 49160 | tf_op jit(solution)/shard_map/ppermute | solution.py:179
  18.5 4.6 %collective-permute-start.2 = (bf16[8,1024]{1,0:T(8,128)(2,1)}, bf16[8,1024]{1,0:T(8,128)(2,1)S(1)}, u32[]{:S(2)}, u32[]{:S(2)}) collective-permute-start(bf16[8,1024]{1,0:T(8,128)(2,1)} %get-tuple-element.17), channel_id=1, source_target_pairs={{0,192},{32,224},{64,128},{96,160},{1,193},{33,225},{65,129},{97,1... | collective-permute-start | bytes 49160 | tf_op jit(solution)/shard_map/ppermute | solution.py:179
  23.1 1.3 collective-permute-start.3
  24.4 0.0 collective-permute-done.refs_0_
  24.4 0.0 collective-permute-done.1.refs_1_
  24.5 0.0 collective-permute-done.2.refs_2_
  24.5 1.0 collective-permute-done.3.refs_3_
  25.5 0.0 collective-permute-done.4.refs_4_.pair_a_ref
  25.5 0.9 fan.1
  26.4 4.1 %all-to-all-start = ((bf16[8,32,1024]{2,1,0:T(8,128)(2,1)}), bf16[8,32,1024]{2,1,0:T(8,128)(2,1)S(1)}, u32[]{:S(2)}, u32[]{:S(2)}) async-start(bf16[8,32,1024]{2,1,0:T(8,128)(2,1)} %fan.1), calls=%async_computation | async-start | bytes 1048576 | tf_op jit(solution)/shard_map/all_to_all | solution.py:183
  30.5 1.2 collective-permute-start.6
  31.6 6.0 %all-to-all-done = bf16[8,32,1024]{2,1,0:T(8,128)(2,1)S(1)} async-done(((bf16[8,32,1024]{2,1,0:T(8,128)(2,1)}), bf16[8,32,1024]{2,1,0:T(8,128)(2,1)S(1)}, u32[]{:S(2)}, u32[]{:S(2)}) %all-to-all-start) | async-done | bytes 524320 | tf_op jit(solution)/shard_map/all_to_all | solution.py:183
  37.6 3.5 %collective-permute-start.5 = (bf16[256,1024]{1,0:T(8,128)(2,1)S(1)}, bf16[256,1024]{1,0:T(8,128)(2,1)S(1)}, u32[]{:S(2)}, u32[]{:S(2)}) collective-permute-start(bf16[256,1024]{1,0:T(8,128)(2,1)S(1)} %bitcast.38), channel_id=1, source_target_pairs={{0,1},{1,0},{2,3},{3,2},{4,5},{5,4},{6,7},{7,6},{8,9},{9,8},{10,11... | collective-permute-start | bytes 1572872 | tf_op jit(solution)/shard_map/ppermute | solution.py:169
  41.1 0.0 copy-done.4
  41.2 0.1 collective-permute-start.7
  41.2 2.0 %reshape.51 = bf16[8,8,2,4,512]{4,3,2,1,0:T(4,128)(2,1)} reshape(bf16[512,512]{1,0:T(8,128)(2,1)} %param.16) | data formatting | bytes 1048576 | tf_op jit(solution)/shard_map/reshape | solution.py:306
  43.2 0.0 collective-permute-done.7.held_ref.refs_6_.gain_theirs_ref
  43.2 0.0 collective-permute-done.6.pair_b_ref
  43.2 0.0 collective-permute-done.5.far_ref
  43.2 0.0 copy-done
  43.3 0.0 copy-done.2
  43.3 1.7 project.1
  45.0 1.7 %collective-permute-start.8 = (bf16[2,32,512]{2,1,0:T(8,128)(2,1)S(1)}, bf16[2,32,512]{2,1,0:T(8,128)(2,1)S(1)}, u32[]{:S(2)}, u32[]{:S(2)}) collective-permute-start(bf16[2,32,512]{2,1,0:T(8,128)(2,1)S(1)} %get-tuple-element.20), channel_id=1, source_target_pairs={{0,32},{32,64},{64,96},{96,0},{1,33},{33,65},{65,97},{97,1},{2,34}... | collective-permute-start | bytes 196616 | tf_op jit(solution)/shard_map/ppermute | solution.py:174
  46.7 0.8 collective-permute-start.9
  47.5 2.7 %collective-permute-start.10 = (bf16[2,32,512]{2,1,0:T(8,128)(2,1)S(1)}, bf16[2,32,512]{2,1,0:T(8,128)(2,1)S(1)}, u32[]{:S(2)}, u32[]{:S(2)}) collective-permute-start(bf16[2,32,512]{2,1,0:T(8,128)(2,1)S(1)} %get-tuple-element.22), channel_id=1, source_target_pairs={{0,96},{32,0},{64,32},{96,64},{1,97},{33,1},{65,33},{97,65},{2,98}... | collective-permute-start | bytes 196616 | tf_op jit(solution)/shard_map/ppermute | solution.py:174
  50.3 0.9 copy_bitcast_fusion
  51.2 0.0 collective-permute-done.8
  51.2 3.2 %collective-permute-done.9 = bf16[2,32,512]{2,1,0:T(8,128)(2,1)S(1)} collective-permute-done((bf16[2,32,512]{2,1,0:T(8,128)(2,1)S(1)}, bf16[2,32,512]{2,1,0:T(8,128)(2,1)S(1)}, u32[]{:S(2)}, u32[]{:S(2)}) %collective-permute-start.9) | collective-permute-done | bytes 65568 | tf_op jit(solution)/shard_map/ppermute | solution.py:174
  54.4 0.0 collective-permute-done.10
  54.4 0.8 stream.1
  55.3 5.8 %all-to-all-start.1 = ((bf16[8,64,512]{2,1,0:T(8,128)(2,1)}), bf16[8,64,512]{2,1,0:T(8,128)(2,1)S(1)}, u32[]{:S(2)}, u32[]{:S(2)}) async-start(bf16[8,64,512]{2,1,0:T(8,128)(2,1)} %get-tuple-element.23), calls=%async_computation.1 | async-start | bytes 1048576 | tf_op jit(solution)/shard_map/all_to_all | solution.py:183
  61.1 0.0 copy-start.3
  61.1 2.7 %dynamic-slice_bitcast_fusion.2 = (bf16[512,896]{1,0:T(8,128)(2,1)}, bf16[512,896]{1,0:T(8,128)(2,1)S(1)}) fusion(bf16[1,512,1792]{2,1,0:T(8,128)(2,1)} %param.19, s32[]{:T(128)S(6)} %select_n.17, s32[]{:T(128)S(6)} %select_n.16), kind=kLoop, calls=%fused_computation.2 | loop fusion | bytes 3670024 | tf_op jit(solution)/shard_map/dynamic_slice | solution.py:292
  63.8 3.1 %collective-permute-start.12 = (bf16[512,896]{1,0:T(8,128)(2,1)}, bf16[512,896]{1,0:T(8,128)(2,1)S(1)}, u32[]{:S(2)}, u32[]{:S(2)}) collective-permute-start(bf16[512,896]{1,0:T(8,128)(2,1)} %get-tuple-element.27), channel_id=1, source_target_pairs={{0,1},{1,0},{2,3},{3,2},{4,5},{5,4},{6,7},{7,6},{8,9},{9,8},{10,11... | collective-permute-start | bytes 2752520 | tf_op jit(solution)/shard_map/ppermute | solution.py:169
  66.8 0.0 copy-done.3
  66.8 1.2 dynamic-slice_bitcast_fusion
  68.0 0.0 collective-permute-start.13
  68.0 6.0 %all-to-all-done.1 = bf16[8,64,512]{2,1,0:T(8,128)(2,1)S(1)} async-done(((bf16[8,64,512]{2,1,0:T(8,128)(2,1)}), bf16[8,64,512]{2,1,0:T(8,128)(2,1)S(1)}, u32[]{:S(2)}, u32[]{:S(2)}) %all-to-all-start.1) | async-done | bytes 524320 | tf_op jit(solution)/shard_map/all_to_all | solution.py:183
  74.0 4.4 %collective-permute-start.11 = (bf16[512,512]{1,0:T(8,128)(2,1)S(1)}, bf16[512,512]{1,0:T(8,128)(2,1)S(1)}, u32[]{:S(2)}, u32[]{:S(2)}) collective-permute-start(bf16[512,512]{1,0:T(8,128)(2,1)S(1)} %bitcast.35), channel_id=1, source_target_pairs={{0,1},{1,0},{2,3},{3,2},{4,5},{5,4},{6,7},{7,6},{8,9},{9,8},{10,11... | collective-permute-start | bytes 1572872 | tf_op jit(solution)/shard_map/ppermute | solution.py:169
  78.4 0.0 collective-permute-done.12.gate_theirs_ref
  78.4 0.0 collective-permute-done.13.up_theirs_ref
  78.4 1.5 collective-permute-done.11.theirs_ref
  79.9 4.1 %gate_up.1 = bf16[512,1920]{1,0:T(8,128)(2,1)S(1)} custom-call(bf16[512,512]{1,0:T(8,128)(2,1)S(1)} %bitcast.36, bf16[512,512]{1,0:T(8,128)(2,1)S(1)} %collective-permute-done.11.theirs_ref, bf16[1,512]{1,0:T(2,128)(2,1)S(1)} %broadcast_in_dim.3.refs_5_.gain_ref, bf16[1,512]{1,0:T(2,128)(2,1)S(1)} %collective-permute-done.7.held_ref.refs_6_.gain_theirs_ref, ...), custom_call_target="tpu_custom_call" | custom-call | tf_op jit(solution)/shard_map/gate_up/pallas_call | solution.py:313
  84.0 27.0 %all_to_all.30.parts_ref = bf16[8,64,1920]{2,1,0:T(8,128)(2,1)S(1)} all-to-all(bf16[8,64,1920]{2,1,0:T(8,128)(2,1)S(1)} %bitcast.32), channel_id=1, replica_groups=mesh['side'=2,'rp'=4,'rl'=2,'x'=4,'yl'=2,'core'=2] {'x','yl'}, dimensions={0} | all-to-all | bytes 3932160 | tf_op jit(solution)/shard_map/all_to_all | solution.py:183
  111.0 1.1 hidden.1
  112.1 14.9 %all_to_all.31 = bf16[8,64,896]{2,1,0:T(8,128)(2,1)S(1)} all-to-all(bf16[8,64,896]{2,1,0:T(8,128)(2,1)S(1)} %hidden.1), channel_id=1, replica_groups=mesh['side'=2,'rp'=4,'rl'=2,'x'=4,'yl'=2,'core'=2] {'x','yl'}, dimensions={0} | all-to-all | bytes 1835008 | tf_op jit(solution)/shard_map/all_to_all | solution.py:183
  127.0 2.9 %collective-permute-start.14 = (bf16[512,896]{1,0:T(8,128)(2,1)S(1)}, bf16[512,896]{1,0:T(8,128)(2,1)S(1)}, u32[]{:S(2)}, u32[]{:S(2)}) collective-permute-start(bf16[512,896]{1,0:T(8,128)(2,1)S(1)} %bitcast.33), channel_id=1, source_target_pairs={{0,1},{1,0},{2,3},{3,2},{4,5},{5,4},{6,7},{7,6},{8,9},{9,8},{10,11... | collective-permute-start | bytes 2752520 | tf_op jit(solution)/shard_map/ppermute | solution.py:169
  130.0 2.1 %collective-permute-done.14.theirs_ref = bf16[512,896]{1,0:T(8,128)(2,1)S(1)} collective-permute-done((bf16[512,896]{1,0:T(8,128)(2,1)S(1)}, bf16[512,896]{1,0:T(8,128)(2,1)S(1)}, u32[]{:S(2)}, u32[]{:S(2)}) %collective-permute-start.14) | collective-permute-done | bytes 917536 | tf_op jit(solution)/shard_map/ppermute | solution.py:169
  132.1 0.0 copy-done.1
  132.1 1.8 %down.1 = bf16[512,512]{1,0:T(8,128)(2,1)S(1)} custom-call(s32[3]{0:T(128)S(1)} %copy-done.2, bf16[512,896]{1,0:T(8,128)(2,1)S(1)} %bitcast.34, bf16[512,896]{1,0:T(8,128)(2,1)S(1)} %collective-permute-done.14.theirs_ref, bf16[1,1792,512]{2,1,0:T(8,128)(2,1)S(1)} %copy-done.1), custom_call_target="tpu_custom_call" | custom-call | tf_op jit(solution)/shard_map/down/pallas_call | solution.py:321
  133.9 17.7 %all_to_all.32.parts_ref = bf16[8,64,512]{2,1,0:T(8,128)(2,1)S(1)} all-to-all(bf16[8,64,512]{2,1,0:T(8,128)(2,1)S(1)} %bitcast.37), channel_id=1, replica_groups=mesh['side'=2,'rp'=4,'rl'=2,'x'=4,'yl'=2,'core'=2] {'rl','rp'}, dimensions={0} | all-to-all | bytes 1048576 | tf_op jit(solution)/shard_map/all_to_all | solution.py:183
  151.6 0.1 final.1
  151.7 0.7 reshape.57
  152.3 10.7 %all-to-all-start.5 = ((bf16[32,4,512]{2,1,0:T(4,128)(2,1)}), bf16[32,4,512]{2,1,0:T(4,128)(2,1)S(1)}, u32[]{:S(2)}, u32[]{:S(2)}) async-start(bf16[32,4,512]{2,1,0:T(4,128)(2,1)} %reshape.57), calls=%async_computation.5 | async-start | bytes 262144 | tf_op jit(solution)/shard_map/all_to_all | solution.py:183
  163.0 7.6 %all-to-all-done.5 = bf16[32,4,512]{2,1,0:T(4,128)(2,1)S(1)} async-done(((bf16[32,4,512]{2,1,0:T(4,128)(2,1)}), bf16[32,4,512]{2,1,0:T(4,128)(2,1)S(1)}, u32[]{:S(2)}, u32[]{:S(2)}) %all-to-all-start.5) | async-done | bytes 131104 | tf_op jit(solution)/shard_map/all_to_all | solution.py:183
  170.8 0.6 reshape.58
  (6 shorter events, 0.1 us)
Async XLA Ops:
  2.1 23.4 %collective-permute-start.4 = (bf16[512,512]{1,0:T(8,128)(2,1)S(1)}, bf16[512,512]{1,0:T(8,128)(2,1)S(1)}, u32[]{:S(2)}, u32[]{:S(2)}) collective-permute-start(bf16[512,512]{1,0:T(8,128)(2,1)S(1)} %get-tuple-element.30), channel_id=1, source_target_pairs={{0,16},{16,0},{1,17},{17,1},{2,18},{18,2},{3,19},{19,3},{4,20},{20... | collective-permute-start | bytes 1572872 | tf_op jit(solution)/shard_map/ppermute | solution.py:169
  9.5 31.6 %copy-start.4 = (bf16[512]{0:T(512)(128)(2,1)S(1)}, bf16[512]{0:T(512)(128)(2,1)}, u32[]{:S(2)}) copy-start(bf16[512]{0:T(512)(128)(2,1)} %param.17) | copy-start | bytes 3076
  9.5 33.7 %copy-start = (bf16[1,1024,512]{2,1,0:T(8,128)(2,1)S(1)}, bf16[1,1024,512]{2,1,0:T(8,128)(2,1)}, u32[]{:S(2)}) copy-start(bf16[1,1024,512]{2,1,0:T(8,128)(2,1)} %own_ref.1) | copy-start | bytes 3145732
  9.5 33.7 %copy-start.2 = (s32[3]{0:T(128)S(1)}, s32[3]{0:T(128)}, u32[]{:S(2)}) copy-start(s32[3]{0:T(128)} %pad_add_fusion.place_ref) | copy-start | bytes 40
  9.5 14.9 %collective-permute-start = (bf16[8,1024]{1,0:T(8,128)(2,1)}, bf16[8,1024]{1,0:T(8,128)(2,1)S(1)}, u32[]{:S(2)}, u32[]{:S(2)}) collective-permute-start(bf16[8,1024]{1,0:T(8,128)(2,1)} %get-tuple-element.15), channel_id=1, source_target_pairs={{0,128},{32,160},{64,192},{96,224},{1,129},{33,161},{65,193},{97,2... | collective-permute-start | bytes 49160 | tf_op jit(solution)/shard_map/ppermute | solution.py:179
  14.5 10.0 %collective-permute-start.1 = (bf16[8,1024]{1,0:T(8,128)(2,1)}, bf16[8,1024]{1,0:T(8,128)(2,1)S(1)}, u32[]{:S(2)}, u32[]{:S(2)}) collective-permute-start(bf16[8,1024]{1,0:T(8,128)(2,1)} %get-tuple-element.16), channel_id=1, source_target_pairs={{0,160},{32,192},{64,224},{96,128},{1,161},{33,193},{65,225},{97,1... | collective-permute-start | bytes 49160 | tf_op jit(solution)/shard_map/ppermute | solution.py:179
  18.5 6.0 %collective-permute-start.2 = (bf16[8,1024]{1,0:T(8,128)(2,1)}, bf16[8,1024]{1,0:T(8,128)(2,1)S(1)}, u32[]{:S(2)}, u32[]{:S(2)}) collective-permute-start(bf16[8,1024]{1,0:T(8,128)(2,1)} %get-tuple-element.17), channel_id=1, source_target_pairs={{0,192},{32,224},{64,128},{96,160},{1,193},{33,225},{65,129},{97,1... | collective-permute-start | bytes 49160 | tf_op jit(solution)/shard_map/ppermute | solution.py:179
  23.1 2.4 %collective-permute-start.3 = (bf16[8,1024]{1,0:T(8,128)(2,1)}, bf16[8,1024]{1,0:T(8,128)(2,1)S(1)}, u32[]{:S(2)}, u32[]{:S(2)}) collective-permute-start(bf16[8,1024]{1,0:T(8,128)(2,1)} %get-tuple-element.18), channel_id=1, source_target_pairs={{0,224},{32,128},{64,160},{96,192},{1,225},{33,129},{65,161},{97,1... | collective-permute-start | bytes 49160 | tf_op jit(solution)/shard_map/ppermute | solution.py:179
  26.4 11.3 %all-to-all-start = ((bf16[8,32,1024]{2,1,0:T(8,128)(2,1)}), bf16[8,32,1024]{2,1,0:T(8,128)(2,1)S(1)}, u32[]{:S(2)}, u32[]{:S(2)}) async-start(bf16[8,32,1024]{2,1,0:T(8,128)(2,1)} %fan.1), calls=%async_computation | async-start | bytes 1048576 | tf_op jit(solution)/shard_map/all_to_all | solution.py:183
  30.5 12.8 %collective-permute-start.6 = (bf16[512,512]{1,0:T(8,128)(2,1)}, bf16[512,512]{1,0:T(8,128)(2,1)S(1)}, u32[]{:S(2)}, u32[]{:S(2)}) collective-permute-start(bf16[512,512]{1,0:T(8,128)(2,1)} %get-tuple-element.29), channel_id=1, source_target_pairs={{0,16},{16,0},{1,17},{17,1},{2,18},{18,2},{3,19},{19,3},{4,20},{20... | collective-permute-start | bytes 1572872 | tf_op jit(solution)/shard_map/ppermute | solution.py:169
  37.6 5.6 %collective-permute-start.5 = (bf16[256,1024]{1,0:T(8,128)(2,1)S(1)}, bf16[256,1024]{1,0:T(8,128)(2,1)S(1)}, u32[]{:S(2)}, u32[]{:S(2)}) collective-permute-start(bf16[256,1024]{1,0:T(8,128)(2,1)S(1)} %bitcast.38), channel_id=1, source_target_pairs={{0,1},{1,0},{2,3},{3,2},{4,5},{5,4},{6,7},{7,6},{8,9},{9,8},{10,11... | collective-permute-start | bytes 1572872 | tf_op jit(solution)/shard_map/ppermute | solution.py:169
  41.2 2.1 %collective-permute-start.7 = (bf16[1,512]{1,0:T(2,128)(2,1)S(1)}, bf16[1,512]{1,0:T(2,128)(2,1)S(1)}, u32[]{:S(2)}, u32[]{:S(2)}) collective-permute-start(bf16[1,512]{1,0:T(2,128)(2,1)S(1)} %broadcast_in_dim.3.refs_5_.gain_ref), channel_id=1, source_target_pairs={{0,1},{1,0},{2,3},{3,2},{4,5},{5,4},{6,7},{7,6},{8,9},{9,8},{10,11... | collective-permute-start | bytes 3080 | tf_op jit(solution)/shard_map/ppermute | solution.py:169
  45.0 6.2 %collective-permute-start.8 = (bf16[2,32,512]{2,1,0:T(8,128)(2,1)S(1)}, bf16[2,32,512]{2,1,0:T(8,128)(2,1)S(1)}, u32[]{:S(2)}, u32[]{:S(2)}) collective-permute-start(bf16[2,32,512]{2,1,0:T(8,128)(2,1)S(1)} %get-tuple-element.20), channel_id=1, source_target_pairs={{0,32},{32,64},{64,96},{96,0},{1,33},{33,65},{65,97},{97,1},{2,34}... | collective-permute-start | bytes 196616 | tf_op jit(solution)/shard_map/ppermute | solution.py:174
  46.7 7.7 %collective-permute-start.9 = (bf16[2,32,512]{2,1,0:T(8,128)(2,1)S(1)}, bf16[2,32,512]{2,1,0:T(8,128)(2,1)S(1)}, u32[]{:S(2)}, u32[]{:S(2)}) collective-permute-start(bf16[2,32,512]{2,1,0:T(8,128)(2,1)S(1)} %get-tuple-element.21), channel_id=1, source_target_pairs={{0,64},{32,96},{64,0},{96,32},{1,65},{33,97},{65,1},{97,33},{2,66}... | collective-permute-start | bytes 196616 | tf_op jit(solution)/shard_map/ppermute | solution.py:174
  47.5 6.9 %collective-permute-start.10 = (bf16[2,32,512]{2,1,0:T(8,128)(2,1)S(1)}, bf16[2,32,512]{2,1,0:T(8,128)(2,1)S(1)}, u32[]{:S(2)}, u32[]{:S(2)}) collective-permute-start(bf16[2,32,512]{2,1,0:T(8,128)(2,1)S(1)} %get-tuple-element.22), channel_id=1, source_target_pairs={{0,96},{32,0},{64,32},{96,64},{1,97},{33,1},{65,33},{97,65},{2,98}... | collective-permute-start | bytes 196616 | tf_op jit(solution)/shard_map/ppermute | solution.py:174
  55.3 18.7 %all-to-all-start.1 = ((bf16[8,64,512]{2,1,0:T(8,128)(2,1)}), bf16[8,64,512]{2,1,0:T(8,128)(2,1)S(1)}, u32[]{:S(2)}, u32[]{:S(2)}) async-start(bf16[8,64,512]{2,1,0:T(8,128)(2,1)} %get-tuple-element.23), calls=%async_computation.1 | async-start | bytes 1048576 | tf_op jit(solution)/shard_map/all_to_all | solution.py:183
  61.1 5.8 %copy-start.3 = (bf16[1,512,1792]{2,1,0:T(8,128)(2,1)S(1)}, bf16[1,512,1792]{2,1,0:T(8,128)(2,1)}, u32[]{:S(2)}) copy-start(bf16[1,512,1792]{2,1,0:T(8,128)(2,1)} %param.20) | copy-start | bytes 5505028
  63.8 14.6 %collective-permute-start.12 = (bf16[512,896]{1,0:T(8,128)(2,1)}, bf16[512,896]{1,0:T(8,128)(2,1)S(1)}, u32[]{:S(2)}, u32[]{:S(2)}) collective-permute-start(bf16[512,896]{1,0:T(8,128)(2,1)} %get-tuple-element.27), channel_id=1, source_target_pairs={{0,1},{1,0},{2,3},{3,2},{4,5},{5,4},{6,7},{7,6},{8,9},{9,8},{10,11... | collective-permute-start | bytes 2752520 | tf_op jit(solution)/shard_map/ppermute | solution.py:169
  68.0 10.3 %collective-permute-start.13 = (bf16[512,896]{1,0:T(8,128)(2,1)}, bf16[512,896]{1,0:T(8,128)(2,1)}, u32[]{:S(2)}, u32[]{:S(2)}) collective-permute-start(bf16[512,896]{1,0:T(8,128)(2,1)} %get-tuple-element.25), channel_id=1, source_target_pairs={{0,1},{1,0},{2,3},{3,2},{4,5},{5,4},{6,7},{7,6},{8,9},{9,8},{10,11... | collective-permute-start | bytes 2752520 | tf_op jit(solution)/shard_map/ppermute | solution.py:169
  74.0 5.9 %collective-permute-start.11 = (bf16[512,512]{1,0:T(8,128)(2,1)S(1)}, bf16[512,512]{1,0:T(8,128)(2,1)S(1)}, u32[]{:S(2)}, u32[]{:S(2)}) collective-permute-start(bf16[512,512]{1,0:T(8,128)(2,1)S(1)} %bitcast.35), channel_id=1, source_target_pairs={{0,1},{1,0},{2,3},{3,2},{4,5},{5,4},{6,7},{7,6},{8,9},{9,8},{10,11... | collective-permute-start | bytes 1572872 | tf_op jit(solution)/shard_map/ppermute | solution.py:169
  111.0 21.0 %copy-start.1 = (bf16[1,1792,512]{2,1,0:T(8,128)(2,1)S(1)}, bf16[1,1792,512]{2,1,0:T(8,128)(2,1)}, u32[]{:S(2)}) copy-start(bf16[1,1792,512]{2,1,0:T(8,128)(2,1)} %weight_ref.1) | copy-start | bytes 5505028
  127.0 5.0 %collective-permute-start.14 = (bf16[512,896]{1,0:T(8,128)(2,1)S(1)}, bf16[512,896]{1,0:T(8,128)(2,1)S(1)}, u32[]{:S(2)}, u32[]{:S(2)}) collective-permute-start(bf16[512,896]{1,0:T(8,128)(2,1)S(1)} %bitcast.33), channel_id=1, source_target_pairs={{0,1},{1,0},{2,3},{3,2},{4,5},{5,4},{6,7},{7,6},{8,9},{9,8},{10,11... | collective-permute-start | bytes 2752520 | tf_op jit(solution)/shard_map/ppermute | solution.py:169
  152.3 18.3 %all-to-all-start.5 = ((bf16[32,4,512]{2,1,0:T(4,128)(2,1)}), bf16[32,4,512]{2,1,0:T(4,128)(2,1)S(1)}, u32[]{:S(2)}, u32[]{:S(2)}) async-start(bf16[32,4,512]{2,1,0:T(4,128)(2,1)} %reshape.57), calls=%async_computation.5 | async-start | bytes 262144 | tf_op jit(solution)/shard_map/all_to_all | solution.py:183

commit v6 on v5

v6 whole, which is shorter than its diff:
```python
import functools
import math
import jax
import jax.numpy as jnp
from jax import lax
from jax.experimental import pallas as pl
from jax.experimental.pallas import tpu as pltpu
from jax.sharding import Mesh, PartitionSpec as P

D = 8192
H = 64
KVH = 8
HD = 128
ORIG = 64
PER = H // KVH

rope_theta = 500000.0
stretch_factor = 8.0
eps = 1e-05

CHIPS = ("x", "yl")
COL = ("x", "yl", "core")
ROW = ("rp", "rl")
HOME = ("rl", "rp")
WHOLE = pl.BlockSpec(memory_space=pltpu.VMEM)
HELD = pl.BlockSpec(memory_space=pl.ANY)
SCALARS = pl.BlockSpec(memory_space=pltpu.SMEM)


def swap_halves(v):
    return jnp.concatenate([v[:, HD // 2:], v[:, : HD // 2]], axis=-1)


def attend_kernel(len_ref, q_ref, new_ref, k_lo_ref, k_hi_ref, v_lo_ref, v_hi_ref, *rest):
    o_refs, (q_all, new_all, s_all, acc, out_all, fine_all, coarse_all, at_all) = rest[:-8], rest[-8:]
    slot = pl.program_id(0)
    slots = q_ref.shape[0]
    length = len_ref[slot]
    half = k_lo_ref.shape[2]
    span = 2 * half

    @pl.when(slot == 0)
    def _():
        for h in range(H):
            q_all[:, h, :] = q_ref[:, h * HD:(h + 1) * HD].astype(jnp.float32)
        for h in range(2 * KVH):
            new_all[:, h, :] = new_ref[:, h * HD:(h + 1) * HD].astype(jnp.float32)

    steps = span // 16
    lane = lax.broadcasted_iota(jnp.int32, (1, HD), 1)
    sign = jnp.where(lane < HD // 2, -1.0, 1.0)

    @pl.when(slot == 0)
    def _():
        pair = jnp.where(lane < HD // 2, lane, lane - HD // 2).astype(jnp.float32)
        positions = jnp.concatenate([jnp.full((8, HD), len_ref[j], jnp.int32) for j in range(slots)], axis=0).astype(jnp.float32)
        stretch = jnp.maximum(stretch_factor * (positions + 1.0) / ORIG - (stretch_factor - 1.0), 1.0)
        log_base = math.log(rope_theta) + HD / (HD - 2.0) * jnp.log(stretch)
        freqs = jnp.exp(-(pair * (2.0 / HD)) * log_base)
        low = lax.broadcasted_iota(jnp.int32, (16, HD), 0).astype(jnp.float32)
        high = lax.broadcasted_iota(jnp.int32, (steps, HD), 0).astype(jnp.float32) * 16.0
        each = [freqs[8 * j:8 * j + 1] for j in range(slots)]
        angles = jnp.concatenate([low * f for f in each] + [high * f for f in each] + [positions * freqs], axis=0)
        cosine, sine = jnp.cos(angles), jnp.sin(angles)
        for j in range(slots):
            fine_all[j, 0] = cosine[16 * j:16 * j + 16]
            fine_all[j, 1] = sine[16 * j:16 * j + 16]
            at = 16 * slots + steps * j
            coarse_all[j, 0] = cosine[at:at + steps]
            coarse_all[j, 1] = sine[at:at + steps]
            at = (16 + steps) * slots + 8 * j
            at_all[j, 0] = cosine[at:at + 8]
            at_all[j, 1] = sine[at:at + 8]

    fine_cos, fine_sin = fine_all[slot, 0], fine_all[slot, 1]
    coarse_cos, coarse_sin = coarse_all[slot, 0], coarse_all[slot, 1]

    def tables(first):
        cos_parts, sin_parts = [], []
        for step in range(first, first + steps // 2):
            cc, cs = coarse_cos[step:step + 1], coarse_sin[step:step + 1]
            cos_parts.append(cc * fine_cos - cs * fine_sin)
            sin_parts.append(cs * fine_cos + cc * fine_sin)
        return jnp.concatenate(cos_parts, axis=0), jnp.concatenate(sin_parts, axis=0)

    cos_new = at_all[slot, 0, :1]
    sin_new = at_all[slot, 1, :1] * sign
    q = q_all[slot]
    q_rot = q * cos_new + swap_halves(q) * sin_new
    q_rot = q_rot.astype(jnp.bfloat16).astype(jnp.float32)
    q_both = jnp.concatenate([q_rot, swap_halves(q_rot) * -sign], axis=-1)
    k_new = new_all[slot, :KVH]
    k_new = k_new * cos_new + swap_halves(k_new) * sin_new
    k_new = k_new.astype(jnp.bfloat16).astype(jnp.float32)
    v_new = new_all[slot, KVH:]
    scale = HD ** (-0.5)

    def score(k_ref, first):
        cos_t, sin_t = tables(first)
        for g in range(KVH):
            kg = k_ref[0, 0, :, g * HD:(g + 1) * HD].astype(jnp.float32)
            kk = jnp.concatenate([(kg * cos_t).astype(jnp.bfloat16), (kg * sin_t).astype(jnp.bfloat16)], axis=-1)
            qg = q_both[g * PER:(g + 1) * PER].astype(jnp.bfloat16)
            s_all[g * PER:(g + 1) * PER, first * 16:first * 16 + half] = lax.dot_general(qg, kk, (((1,), (1,)), ((), ())), preferred_element_type=jnp.float32)

    score(k_lo_ref, 0)

    @pl.when(length > half)
    def _():
        score(k_hi_ref, steps // 2)

    @pl.when(length <= half)
    def _():
        s_all[:, half:] = jnp.zeros((H, half), jnp.float32)

    own, fresh = [], []
    for g in range(KVH):
        own.append(jnp.sum(q_rot[g * PER:(g + 1) * PER] * k_new[g:g + 1], axis=-1, keepdims=True))
        fresh.append(jnp.broadcast_to(v_new[g:g + 1], (PER, HD)))
    own_score = jnp.concatenate(own, axis=0) * scale
    valid = lax.broadcasted_iota(jnp.int32, (H, span), 1) < length
    s = jnp.where(valid, s_all[...] * scale, -1e30)
    top = jnp.maximum(jnp.max(s, axis=-1, keepdims=True), own_score)
    w = jnp.where(valid, jnp.exp(s - top), 0.0)
    own_w = jnp.exp(own_score - top)
    total = jnp.sum(w, axis=-1, keepdims=True) + own_w
    w16 = w.astype(jnp.bfloat16)

    def mix(v_ref, weights):
        parts = []
        for p in range(KVH // 2):
            o = jnp.dot(weights[p * 2 * PER:(p + 1) * 2 * PER], v_ref[0, 0, :, p * 2 * HD:(p + 1) * 2 * HD], preferred_element_type=jnp.float32)
            parts += [o[:PER, :HD], o[PER:, HD:]]
        return jnp.concatenate(parts, axis=0)

    acc[...] = mix(v_lo_ref, w16[:, :half]) + own_w * jnp.concatenate(fresh, axis=0)

    @pl.when(length > half)
    def _():
        acc[...] += mix(v_hi_ref, w16[:, half:])

    out = acc[...] / total
    pairs = len(o_refs)
    per_row = H // (2 * pairs)
    for h in range(H):
        at, q_at = h // per_row, h % per_row
        out_all[at // 2, slot, at % 2:at % 2 + 1, q_at * HD:(q_at + 1) * HD] = out[h:h + 1]

    @pl.when(slot == slots - 1)
    def _():
        for k in range(pairs):
            home = lax.rem(lax.axis_index("rp") + k, pairs)
            o_refs[k][...] = jnp.concatenate([out_all[home, j] for j in range(slots)], axis=0).astype(jnp.bfloat16)


def attention(queries, new_entries, cache_keys, cache_values, lengths, pairs):
    slots = queries.shape[0]
    half = cache_keys.shape[2] // 2
    width = KVH * HD
    low = pl.BlockSpec((1, 1, half, width), lambda s, n: (0, s, 0, 0))

    def last_long(s, n):
        at = 0
        for j in range(1, slots):
            at = jnp.where((s >= j) & (n[j] > half), j, at)
        return (0, at, 1, 0)

    high = pl.BlockSpec((1, 1, half, width), last_long)
    heads = H * HD // (2 * pairs)
    grid_spec = pltpu.PrefetchScalarGridSpec(
        num_scalar_prefetch=1, grid=(slots,),
        in_specs=[pl.BlockSpec((slots, H * HD), lambda s, n: (0, 0)), pl.BlockSpec((slots, 2 * width), lambda s, n: (0, 0)), low, high, low, high],
        out_specs=[pl.BlockSpec((2 * slots, heads), lambda s, n: (0, 0))] * pairs,
        scratch_shapes=[
            pltpu.VMEM((slots, H, HD), jnp.float32), pltpu.VMEM((slots, 2 * KVH, HD), jnp.float32),
            pltpu.VMEM((H, 2 * half), jnp.float32), pltpu.VMEM((H, HD), jnp.float32), pltpu.VMEM((pairs, slots, 2, heads), jnp.float32),
            pltpu.VMEM((slots, 2, 16, HD), jnp.float32), pltpu.VMEM((slots, 2, 2 * half // 16, HD), jnp.float32), pltpu.VMEM((slots, 2, 8, HD), jnp.float32)])
    return pl.pallas_call(
        attend_kernel, grid_spec=grid_spec,
        out_shape=[jax.ShapeDtypeStruct((2 * slots, heads), jnp.bfloat16)] * pairs,
        compiler_params=pltpu.CompilerParams(vmem_limit_bytes=60 << 20), name="attend",
    )(lengths, queries, new_entries, cache_keys, cache_keys, cache_values, cache_values)


def flip(value, axis):
    return lax.ppermute(value, axis, [(0, 1), (1, 0)])


def turn(value, steps):
    count = lax.axis_size("rp")
    return lax.ppermute(value, "rp", [(i, (i + steps) % count) for i in range(count)])


def to_ffn(value, steps):
    count = lax.axis_size("rp")
    return lax.ppermute(value, ("side", "rp"), [(i, count + (i + steps) % count) for i in range(count)])


def exchange(value, axes):
    return lax.all_to_all(value, axes, split_axis=0, concat_axis=0, tiled=True)


def matmul(left, right):
    return jnp.dot(left, right, preferred_element_type=jnp.float32)


def call(kernel, name, out_shape, **options):
    limit = options.pop("limit", 24)
    return pl.pallas_call(kernel, out_shape=out_shape, name=name, compiler_params=pltpu.CompilerParams(vmem_limit_bytes=limit << 20), **options)


def fan_kernel(*refs):
    blocks, o_ref = refs[:-2], refs[-1]
    rows = blocks[0].shape[0]
    for i in range(o_ref.shape[0]):
        for k, block in enumerate(blocks):
            o_ref[i, k * rows:(k + 1) * rows] = block[...]


def project_kernel(near_ref, far_ref, own_ref, pair_ref, *o_refs):
    core, low = lax.axis_index("core"), lax.axis_index("rl")
    pairs, group = len(o_refs), o_refs[0].shape[1]
    slots = near_ref.shape[0] // (2 * pairs * (group // 4))
    rows = pairs * group
    to = lax.broadcasted_iota(jnp.int32, (rows, 2 * rows), 0)
    source = lax.broadcasted_iota(jnp.int32, (rows, 2 * rows), 1)
    block = (pairs - to // group) % pairs
    first = ((to % group) // slots) * (2 * slots * pairs) + block * (2 * slots) + (to % slots) * 2
    pick_own = (source == first + low).astype(jnp.bfloat16)
    pick_pair = (source == first + 1 - low).astype(jnp.bfloat16)
    for left_ref, place in ((near_ref, core), (far_ref, 1 - core)):
        part = matmul(matmul(pick_own, left_ref[...]).astype(jnp.bfloat16), own_ref[0])
        part = part + matmul(matmul(pick_pair, left_ref[...]).astype(jnp.bfloat16), pair_ref[0])
        for k in range(pairs):
            o_refs[k][place] = part[k * group:(k + 1) * group].astype(jnp.bfloat16)


def stream_kernel(*refs):
    parts, (residual_ref, gain_ref, stream_ref, copies_ref) = refs[:-4], refs[-4:]
    group = stream_ref.shape[0]
    chips = group // 8
    row = lax.axis_index("rp") * 2 + lax.axis_index("rl")
    to = lax.broadcasted_iota(jnp.int32, (group, group), 0)
    source = lax.broadcasted_iota(jnp.int32, (group, group), 1)
    order = (source == (to // 4 % chips) * 8 + (to // (4 * chips)) * 4 + to % 4).astype(jnp.bfloat16)
    stream = matmul(order, residual_ref[pl.ds(pl.multiple_of(row * group, group), group), :])
    for part_ref in parts:
        stream = stream + part_ref[...].astype(jnp.float32)
    stream_ref[...] = stream
    scaled = (stream * gain_ref[...].astype(jnp.float32)).astype(jnp.bfloat16)
    for i in range(copies_ref.shape[0]):
        copies_ref[i] = scaled


def gate_up_kernel(mine_ref, theirs_ref, gate_ref, gate_theirs_ref, up_ref, up_theirs_ref, o_ref):
    both = jnp.concatenate([gate_ref[...], up_ref[...]], axis=1)
    both_theirs = jnp.concatenate([gate_theirs_ref[...], up_theirs_ref[...]], axis=1)
    o_ref[...] = (matmul(mine_ref[...], both) + matmul(theirs_ref[...], both_theirs)).astype(jnp.bfloat16)


def squares_kernel(mine_ref, theirs_ref, gain_ref, gain_theirs_ref, o_ref):
    one = mine_ref[...].astype(jnp.float32) * (1.0 / gain_ref[...].astype(jnp.float32))
    two = theirs_ref[...].astype(jnp.float32) * (1.0 / gain_theirs_ref[...].astype(jnp.float32))
    squares = jnp.sum(one * one + two * two, axis=1, keepdims=True)
    at = lax.broadcasted_iota(jnp.int32, (128, 128), 0) == lax.broadcasted_iota(jnp.int32, (128, 128), 1)
    for i in range(o_ref.shape[0]):
        o_ref[i:i + 1] = jnp.sum(jnp.where(at, squares[i * 128:(i + 1) * 128], 0.0), axis=0, keepdims=True)


def hidden_kernel(parts_ref, squares_ref, copies_ref):
    group = parts_ref.shape[1]
    chip = lax.axis_index("x") * 2 + lax.axis_index("yl")
    sums = parts_ref[0].astype(jnp.float32)
    for i in range(1, parts_ref.shape[0]):
        sums = sums + parts_ref[i].astype(jnp.float32)
    to = lax.broadcasted_iota(jnp.int32, (group, 128), 0) + lax.rem(chip, 128 // group) * group
    lane = lax.broadcasted_iota(jnp.int32, (group, 128), 1)
    line = lax.broadcasted_iota(jnp.int32, squares_ref.shape, 0) == chip // (128 // group)
    wanted = jnp.sum(jnp.where(line, squares_ref[...], 0.0), axis=0, keepdims=True)
    squares = jnp.sum(jnp.where(to == lane, wanted, 0.0), axis=1, keepdims=True)
    inv_rms = lax.rsqrt(squares / D + eps)
    for i in range(copies_ref.shape[2] // 128):
        gate = sums[:, i * 256:i * 256 + 128] * inv_rms
        up = sums[:, i * 256 + 128:i * 256 + 256] * inv_rms
        hidden = (gate / (1.0 + jnp.exp(-gate)) * up).astype(jnp.bfloat16)
        for j in range(copies_ref.shape[0]):
            copies_ref[j, :, i * 128:(i + 1) * 128] = hidden


def down_kernel(mine_ref, theirs_ref, weight_ref, o_ref):
    half = mine_ref.shape[1]
    core = lax.axis_index("core")
    part = matmul(mine_ref[...], weight_ref[0, pl.ds(pl.multiple_of(core * half, half), half), :])
    part = part + matmul(theirs_ref[...], weight_ref[0, pl.ds(pl.multiple_of((1 - core) * half, half), half), :])
    o_ref[...] = part.astype(jnp.bfloat16)


def final_kernel(parts_ref, stream_ref, copies_ref):
    total = parts_ref[0].astype(jnp.float32)
    for i in range(1, parts_ref.shape[0]):
        total = total + parts_ref[i].astype(jnp.float32)
    final = stream_ref[...] + total
    count, slots = copies_ref.shape[0] // 2, copies_ref.shape[1]
    for i in range(count):
        block = final[i * slots:(i + 1) * slots].astype(jnp.bfloat16)
        copies_ref[i] = block
        copies_ref[count + i] = block


def output_kernel(back_ref, o_ref):
    width = back_ref.shape[2]
    chips = back_ref.shape[0] // 4
    half = chips // 2
    side = lax.axis_index("side")
    for chip in range(half):
        for core in range(2):
            at = (2 * chip + core) * width
            o_ref[:, at:at + width] = back_ref[(2 + core) * chips + side * half + chip]


def local(queries, new_entries, cache_keys, cache_values, lengths, residual, norm_gain, out_weight, gate_weight, up_weight, down_weight):
    bf16 = jnp.bfloat16
    rows, pairs, chips = lax.axis_size(ROW), lax.axis_size("rp"), lax.axis_size(CHIPS)
    core = lax.axis_index("core")
    slots, width = queries.shape[0], out_weight.shape[2]
    heads = out_weight.shape[1]
    half = gate_weight.shape[2] // 2
    group = chips * 2 * slots
    total = rows * group
    pair = flip(out_weight, "rl")
    gain = norm_gain[None, :]
    gain_theirs = flip(gain, "core")
    gate_theirs = flip(lax.dynamic_slice_in_dim(gate_weight[0], (1 - core) * half, half, 1), "core")
    up_theirs = flip(lax.dynamic_slice_in_dim(up_weight[0], (1 - core) * half, half, 1), "core")

    gate_mine = lax.dynamic_slice_in_dim(gate_weight[0], core * half, half, 1)
    up_mine = lax.dynamic_slice_in_dim(up_weight[0], core * half, half, 1)
    blocks = attention(queries, new_entries, cache_keys, cache_values, lengths, pairs)
    blocks = [to_ffn(block, k) for k, block in enumerate(blocks)]
    fanned = call(fan_kernel, "fan", jax.ShapeDtypeStruct((chips, pairs * 2 * slots, heads), bf16), in_specs=[WHOLE] * pairs + [HELD], out_specs=WHOLE)(*blocks, pair)
    near = exchange(fanned, CHIPS).reshape(chips * pairs * 2 * slots, heads)
    far = flip(near, "core")
    own, *parts = call(project_kernel, "project", [jax.ShapeDtypeStruct((2, group // 2, width), bf16)] * pairs, in_specs=[WHOLE] * 4, out_specs=[WHOLE] * pairs)(near, far, out_weight, pair)
    parts = [own] + [turn(part, k + 1) for k, part in enumerate(parts)]
    parts = [part.reshape(group, width) for part in parts]
    stream, copies = call(stream_kernel, "stream", (jax.ShapeDtypeStruct((group, width), jnp.float32), jax.ShapeDtypeStruct((rows, group, width), bf16)), in_specs=[WHOLE] * (pairs + 2), out_specs=(WHOLE, WHOLE))(
        *parts, residual, gain)
    scaled = exchange(copies, HOME).reshape(total, width)
    scaled_theirs = flip(scaled, "core")
    steps = half // 128
    fixed = pl.BlockSpec((total, width), lambda i: (0, 0))
    piece = pl.BlockSpec((width, 128), lambda i: (0, i))
    grid_spec = pltpu.PrefetchScalarGridSpec(num_scalar_prefetch=0, grid=(steps,), in_specs=[fixed, fixed] + [piece] * 4, out_specs=pl.BlockSpec((total, 256), lambda i: (0, i)))
    sent = call(gate_up_kernel, "gate_up", pltpu.HBM((total, 2 * half), bf16), grid_spec=grid_spec)(scaled, scaled_theirs, gate_mine, gate_theirs, up_mine, up_theirs)
    squares = call(squares_kernel, "squares", jax.ShapeDtypeStruct((total // 128, 128), jnp.float32), in_specs=[WHOLE] * 4, out_specs=WHOLE)(scaled, scaled_theirs, gain, gain_theirs)
    squares = squares + flip(squares, "yl")
    for distance in (1, 2):
        squares = squares + lax.ppermute(squares, "x", [(i, i ^ distance) for i in range(lax.axis_size("x"))])
    sums = exchange(sent.reshape(chips, group, 2 * half), CHIPS)
    hidden = call(hidden_kernel, "hidden", jax.ShapeDtypeStruct((chips, group, half), bf16), in_specs=[WHOLE] * 2, out_specs=WHOLE)(sums, squares)
    hidden = exchange(hidden, CHIPS).reshape(total, half)
    down = call(down_kernel, "down", jax.ShapeDtypeStruct((total, width), bf16), in_specs=[WHOLE] * 3, out_specs=WHOLE)(hidden, flip(hidden, "core"), down_weight)
    downs = exchange(down.reshape(rows, group, width), HOME)
    final = call(final_kernel, "final", jax.ShapeDtypeStruct((4 * chips, slots, width), bf16), in_specs=[WHOLE] * 2, out_specs=WHOLE)(downs, stream)
    back = exchange(final, ("side", "core") + CHIPS)
    return call(output_kernel, "output", jax.ShapeDtypeStruct((slots, width * chips), bf16), in_specs=[WHOLE], out_specs=WHOLE)(back)


def solution(mesh):
    sides, rows, cols = mesh.devices.shape
    inner = Mesh(mesh.devices.reshape(sides, rows // 2, 2, cols // 4, 2, 2), ("side",) + ROW + COL)
    in_specs = (
        P(ROW + COL, None),
        P(ROW + COL, None),
        P("side", ROW + COL, None, None),
        P("side", ROW + COL, None, None),
        P(ROW + COL),
        P(None, COL),
        P(COL),
        P("side", ROW, COL),
        P("side", COL, ROW),
        P("side", COL, ROW),
        P("side", ROW, COL),
    )
    return jax.shard_map(local, mesh=inner, in_specs=in_specs, out_specs=P(ROW + COL, "side"), check_vma=False)
```

time: 173 us -> 183 us (1.058)
  waiting for transfers between devices: 27.5 us -> 42 us
  local copies, waits for them, and re-layouts: 10.2 us -> 2.39 us
  blocking collectives: 59.7 us -> 63.8 us
    ppermute x8, waiting for transfers between devices: 3.65 us -> 19 us  [flip(): return lax.ppermute(value, axis, [(0, 1), (1, 0)])]
    all_to_all x3 -> x2, starting transfers between devices: 20.6 us -> 9.91 us  [exchange(): return lax.all_to_all(value, axes, split_axis=0, concat_axis=0, tiled=True)]
    all_to_all x3 -> x2, waiting for transfers between devices: 19.6 us -> 8.87 us  [exchange(): return lax.all_to_all(value, axes, split_axis=0, concat_axis=0, tiled=True)]
    ppermute x0 -> x2, waiting for transfers between devices: none -> 9.42 us  [local(): lax.ppermute(squares, 'x', [(i, i ^ distance) for i in range(lax.axis_siz...]
    ppermute x3, starting transfers between devices: 5.32 us -> 9.78 us  [turn(): lax.ppermute(value, 'rp', [(i, (i + steps) % count) for i in range(count)])]
    ppermute x0 -> x2, starting transfers between devices: none -> 4.27 us  [local(): lax.ppermute(squares, 'x', [(i, i ^ distance) for i in range(lax.axis_siz...]
    all_to_all x3 -> x4, blocking collectives: 59.7 us -> 63.8 us  [exchange(): return lax.all_to_all(value, axes, split_axis=0, concat_axis=0, tiled=True)]
    pallas_call x2 -> x4, Pallas kernels: 4.17 us -> 7.88 us  [the longest x1 6.83 us: local(): call(gate_up_kernel, 'gate_up', pltpu.HBM((total, 2 * half), bf16), grid_...]
  transfers between devices with their start and end apart: 18 -> 19, of which waited for: 7 -> 12; matrix products, arithmetic and copies ran while one was open for 4% -> 1% of each run, Pallas kernels for 4% -> 4%
where the time goes in v6:
time: 183 us; the launch traced here: 182 us
  blocking collectives  63.8 us (35%)
  starting transfers between devices  54.9 us (30%)
  waiting for transfers between devices  42 us (23%)
  Pallas kernels  18.8 us (10%)
  local copies, waits for them, and re-layouts  2.39 us (1%)
    all_to_all x4, blocking collectives, exchange(): return lax.all_to_all(value, axes, split_axis=0, concat_axis=0, tiled=True)  63.8 us
    ppermute x8, waiting for transfers between devices, flip(): return lax.ppermute(value, axis, [(0, 1), (1, 0)])  19 us
    ppermute x8, starting transfers between devices, flip(): return lax.ppermute(value, axis, [(0, 1), (1, 0)])  15.7 us
    ppermute x4, starting transfers between devices, to_ffn(): lax.ppermute(value, ('side', 'rp'), [(i, count + (i + steps) % count) for...  15.3 us
    all_to_all x2, starting transfers between devices, exchange(): return lax.all_to_all(value, axes, split_axis=0, concat_axis=0, tiled=True)  9.91 us
    ppermute x3, starting transfers between devices, turn(): lax.ppermute(value, 'rp', [(i, (i + steps) % count) for i in range(count)])  9.78 us
    ppermute x2, waiting for transfers between devices, local(): lax.ppermute(squares, 'x', [(i, i ^ distance) for i in range(lax.axis_siz...  9.42 us
    all_to_all x2, waiting for transfers between devices, exchange(): return lax.all_to_all(value, axes, split_axis=0, concat_axis=0, tiled=True)  8.87 us
  transfers between devices with their start and end apart: 19, of which 12 were waited for; matrix products, arithmetic and copies ran while one was open for 1% of the time, Pallas kernels for 4%

profile of v6, /device:TPU:33, one launch (start us, length us, event | category | flops | bytes accessed | tf_op | source)
XLA Modules:
  0.0 181.9 jit_solution(3498382230957519188)
XLA Ops:
  0.0 0.0 collective-permute-start.4
  0.0 7.0 %attend.1 = (bf16[8,1024]{1,0:T(8,128)(2,1)}, bf16[8,1024]{1,0:T(8,128)(2,1)}, bf16[8,1024]{1,0:T(8,128)(2,1)}, bf16[8,1024]{1,0:T(8,128)(2,1)}) custom-call(s32[4]{0:T(128)} %len_ref.1, bf16[4,8192]{1,0:T(4,128)(2,1)} %q_ref.1, bf16[4,2048]{1,0:T(4,128)(2,1)} %new_ref.1, bf16[1,4,256,1024]{3,2,1,0:T(8,128)(2,1)} %k_hi_ref.1, ...), custom_call_target="tpu_custom_call" | custom-call | tf_op jit(solution)/shard_map/attend/pallas_call | solution.py:178
  7.0 0.0 copy-start.1
  7.0 5.0 %collective-permute-start = (bf16[8,1024]{1,0:T(8,128)(2,1)}, bf16[8,1024]{1,0:T(8,128)(2,1)S(1)}, u32[]{:S(2)}, u32[]{:S(2)}) collective-permute-start(bf16[8,1024]{1,0:T(8,128)(2,1)} %get-tuple-element.15), channel_id=1, source_target_pairs={{0,128},{32,160},{64,192},{96,224},{1,129},{33,161},{65,193},{97,2... | collective-permute-start | bytes 49160 | tf_op jit(solution)/shard_map/ppermute | solution.py:196
  11.9 4.1 %collective-permute-start.1 = (bf16[8,1024]{1,0:T(8,128)(2,1)}, bf16[8,1024]{1,0:T(8,128)(2,1)S(1)}, u32[]{:S(2)}, u32[]{:S(2)}) collective-permute-start(bf16[8,1024]{1,0:T(8,128)(2,1)} %get-tuple-element.16), channel_id=1, source_target_pairs={{0,160},{32,192},{64,224},{96,128},{1,161},{33,193},{65,225},{97,1... | collective-permute-start | bytes 49160 | tf_op jit(solution)/shard_map/ppermute | solution.py:196
  16.0 4.9 %collective-permute-start.2 = (bf16[8,1024]{1,0:T(8,128)(2,1)}, bf16[8,1024]{1,0:T(8,128)(2,1)S(1)}, u32[]{:S(2)}, u32[]{:S(2)}) collective-permute-start(bf16[8,1024]{1,0:T(8,128)(2,1)} %get-tuple-element.17), channel_id=1, source_target_pairs={{0,192},{32,224},{64,128},{96,160},{1,193},{33,225},{65,129},{97,1... | collective-permute-start | bytes 49160 | tf_op jit(solution)/shard_map/ppermute | solution.py:196
  21.0 1.3 collective-permute-start.3
  22.3 0.0 collective-permute-done.refs_0_
  22.3 0.0 collective-permute-done.1.refs_1_
  22.3 0.0 collective-permute-done.2.refs_2_
  22.3 1.1 collective-permute-done.3.refs_3_
  23.4 1.2 collective-permute-done.4.refs_4_.pair_ref
  24.6 12.2 %all_to_all.30 = bf16[8,32,1024]{2,1,0:T(8,128)(2,1)S(1)} all-to-all(bf16[8,32,1024]{2,1,0:T(8,128)(2,1)S(1)} %fan.1), channel_id=1, replica_groups=mesh['side'=2,'rp'=4,'rl'=2,'x'=4,'yl'=2,'core'=2] {'x','yl'}, dimensions={0} | all-to-all | bytes 1048576 | tf_op jit(solution)/shard_map/all_to_all | solution.py:200
  36.8 0.0 copy-start.5
  36.8 0.0 copy-start.2
  36.8 0.0 copy-start.3
  36.9 3.5 %collective-permute-start.5 = (bf16[256,1024]{1,0:T(8,128)(2,1)S(1)}, bf16[256,1024]{1,0:T(8,128)(2,1)S(1)}, u32[]{:S(2)}, u32[]{:S(2)}) collective-permute-start(bf16[256,1024]{1,0:T(8,128)(2,1)S(1)} %bitcast.22), channel_id=1, source_target_pairs={{0,1},{1,0},{2,3},{3,2},{4,5},{5,4},{6,7},{7,6},{8,9},{9,8},{10,11... | collective-permute-start | bytes 1572872 | tf_op jit(solution)/shard_map/ppermute | solution.py:186
  40.3 1.5 collective-permute-done.5.far_ref
  41.9 0.0 copy-done.1
  41.9 1.2 project.1
  43.0 3.4 %collective-permute-start.6 = (bf16[2,32,512]{2,1,0:T(8,128)(2,1)S(1)}, bf16[2,32,512]{2,1,0:T(8,128)(2,1)S(1)}, u32[]{:S(2)}, u32[]{:S(2)}) collective-permute-start(bf16[2,32,512]{2,1,0:T(8,128)(2,1)S(1)} %get-tuple-element.20), channel_id=1, source_target_pairs={{0,32},{32,64},{64,96},{96,0},{1,33},{33,65},{65,97},{97,1},{2,34}... | collective-permute-start | bytes 196616 | tf_op jit(solution)/shard_map/ppermute | solution.py:191
  46.4 4.0 %collective-permute-start.7 = (bf16[2,32,512]{2,1,0:T(8,128)(2,1)S(1)}, bf16[2,32,512]{2,1,0:T(8,128)(2,1)S(1)}, u32[]{:S(2)}, u32[]{:S(2)}) collective-permute-start(bf16[2,32,512]{2,1,0:T(8,128)(2,1)S(1)} %get-tuple-element.21), channel_id=1, source_target_pairs={{0,64},{32,96},{64,0},{96,32},{1,65},{33,97},{65,1},{97,33},{2,66}... | collective-permute-start | bytes 196616 | tf_op jit(solution)/shard_map/ppermute | solution.py:191
  50.4 2.4 %collective-permute-start.8 = (bf16[2,32,512]{2,1,0:T(8,128)(2,1)S(1)}, bf16[2,32,512]{2,1,0:T(8,128)(2,1)S(1)}, u32[]{:S(2)}, u32[]{:S(2)}) collective-permute-start(bf16[2,32,512]{2,1,0:T(8,128)(2,1)S(1)} %get-tuple-element.22), channel_id=1, source_target_pairs={{0,96},{32,0},{64,32},{96,64},{1,97},{33,1},{65,33},{97,65},{2,98}... | collective-permute-start | bytes 196616 | tf_op jit(solution)/shard_map/ppermute | solution.py:191
  52.8 0.0 copy-done.5
  52.8 0.0 collective-permute-done.6
  52.8 0.7 collective-permute-done.7
  53.5 3.0 %collective-permute-done.8 = bf16[2,32,512]{2,1,0:T(8,128)(2,1)S(1)} collective-permute-done((bf16[2,32,512]{2,1,0:T(8,128)(2,1)S(1)}, bf16[2,32,512]{2,1,0:T(8,128)(2,1)S(1)}, u32[]{:S(2)}, u32[]{:S(2)}) %collective-permute-start.8) | collective-permute-done | bytes 65568 | tf_op jit(solution)/shard_map/ppermute | solution.py:191
  56.5 0.0 copy-done.2
  56.5 1.0 stream.1
  57.5 6.3 %all-to-all-start.1 = ((bf16[8,64,512]{2,1,0:T(8,128)(2,1)}), bf16[8,64,512]{2,1,0:T(8,128)(2,1)S(1)}, u32[]{:S(2)}, u32[]{:S(2)}) async-start(bf16[8,64,512]{2,1,0:T(8,128)(2,1)} %get-tuple-element.23), calls=%async_computation.1 | async-start | bytes 1048576 | tf_op jit(solution)/shard_map/all_to_all | solution.py:200
  63.8 0.0 copy-done.3
  63.8 0.0 copy-start.4
  63.8 1.2 dynamic-slice_bitcast_fusion.2
  65.0 1.9 %collective-permute-start.10 = (bf16[512,896]{1,0:T(8,128)(2,1)}, bf16[512,896]{1,0:T(8,128)(2,1)}, u32[]{:S(2)}, u32[]{:S(2)}) collective-permute-start(bf16[512,896]{1,0:T(8,128)(2,1)} %get-tuple-element.27), channel_id=1, source_target_pairs={{0,1},{1,0},{2,3},{3,2},{4,5},{5,4},{6,7},{7,6},{8,9},{9,8},{10,11... | collective-permute-start | bytes 2752520 | tf_op jit(solution)/shard_map/ppermute | solution.py:186
  66.8 0.0 copy-done.4
  66.8 1.2 dynamic-slice_bitcast_fusion
  68.0 0.6 collective-permute-start.11
  68.7 8.9 %all-to-all-done.1 = bf16[8,64,512]{2,1,0:T(8,128)(2,1)S(1)} async-done(((bf16[8,64,512]{2,1,0:T(8,128)(2,1)}), bf16[8,64,512]{2,1,0:T(8,128)(2,1)S(1)}, u32[]{:S(2)}, u32[]{:S(2)}) %all-to-all-start.1) | async-done | bytes 524320 | tf_op jit(solution)/shard_map/all_to_all | solution.py:200
  77.5 3.5 %collective-permute-start.9 = (bf16[512,512]{1,0:T(8,128)(2,1)S(1)}, bf16[512,512]{1,0:T(8,128)(2,1)S(1)}, u32[]{:S(2)}, u32[]{:S(2)}) collective-permute-start(bf16[512,512]{1,0:T(8,128)(2,1)S(1)} %bitcast.17), channel_id=1, source_target_pairs={{0,1},{1,0},{2,3},{3,2},{4,5},{5,4},{6,7},{7,6},{8,9},{9,8},{10,11... | collective-permute-start | bytes 1572872 | tf_op jit(solution)/shard_map/ppermute | solution.py:186
  81.1 0.0 collective-permute-done.10.gate_theirs_ref
  81.1 0.0 collective-permute-done.11.up_theirs_ref
  81.1 1.5 collective-permute-done.9.theirs_ref
  82.6 6.8 %gate_up.1 = bf16[512,1792]{1,0:T(8,128)(2,1)} custom-call(bf16[512,512]{1,0:T(8,128)(2,1)S(1)} %bitcast.18, bf16[512,512]{1,0:T(8,128)(2,1)S(1)} %collective-permute-done.9.theirs_ref, bf16[512,896]{1,0:T(8,128)(2,1)S(1)} %get-tuple-element.28.gate_ref, bf16[512,896]{1,0:T(8,128)(2,1)} %collective-permute-done.10.gate_theirs_ref, ...), custom_call_target="tpu_custom_call" | custom-call | tf_op jit(solution)/shard_map/gate_up/pallas_call | solution.py:354
  89.4 3.6 %all-to-all-start.2 = ((bf16[8,64,1792]{2,1,0:T(8,128)(2,1)}), bf16[8,64,1792]{2,1,0:T(8,128)(2,1)S(1)}, u32[]{:S(2)}, u32[]{:S(2)}) async-start(bf16[8,64,1792]{2,1,0:T(8,128)(2,1)} %bitcast.29), calls=%async_computation.2 | async-start | bytes 3670016 | tf_op jit(solution)/shard_map/all_to_all | solution.py:200
  93.0 0.5 collective-permute-start.12
  93.5 0.8 collective-permute-done.12.gain_theirs_ref
  94.3 0.3 squares.1
  94.7 1.6 collective-permute-start.13
  96.3 11.8 %collective-permute-done.13 = f32[4,128]{1,0:T(4,128)S(1)} collective-permute-done((f32[4,128]{1,0:T(4,128)S(1)}, f32[4,128]{1,0:T(4,128)S(1)}, u32[]{:S(2)}, u32[]{:S(2)}) %collective-permute-start.13) | collective-permute-done | bytes 2080 | tf_op jit(solution)/shard_map/ppermute | solution.py:186
  108.1 1.7 collective-permute-start.14
  109.8 8.0 %collective-permute-done.14 = f32[4,128]{1,0:T(4,128)S(1)} collective-permute-done((f32[4,128]{1,0:T(4,128)S(1)}, f32[4,128]{1,0:T(4,128)S(1)}, u32[]{:S(2)}, u32[]{:S(2)}) %collective-permute-start.14) | collective-permute-done | bytes 2080 | tf_op jit(solution)/shard_map/ppermute | solution.py:358
  117.8 2.5 %collective-permute-start.15 = (f32[4,128]{1,0:T(4,128)S(1)}, f32[4,128]{1,0:T(4,128)S(1)}, u32[]{:S(2)}, u32[]{:S(2)}) collective-permute-start(f32[4,128]{1,0:T(4,128)S(1)} %add.20), channel_id=1, source_target_pairs={{0,8},{4,12},{8,0},{12,4},{1,9},{5,13},{9,1},{13,5},{2,10},{6,14},... | collective-permute-start | bytes 6152 | tf_op jit(solution)/shard_map/ppermute | solution.py:358
  120.4 1.4 collective-permute-done.15
  121.8 0.0 all-to-all-done.2.parts_ref
  121.8 0.5 hidden.1
  122.3 15.6 %all_to_all.31 = bf16[8,64,896]{2,1,0:T(8,128)(2,1)S(1)} all-to-all(bf16[8,64,896]{2,1,0:T(8,128)(2,1)S(1)} %hidden.1), channel_id=1, replica_groups=mesh['side'=2,'rp'=4,'rl'=2,'x'=4,'yl'=2,'core'=2] {'x','yl'}, dimensions={0} | all-to-all | bytes 1835008 | tf_op jit(solution)/shard_map/all_to_all | solution.py:200
  137.9 4.0 %collective-permute-start.16 = (bf16[512,896]{1,0:T(8,128)(2,1)S(1)}, bf16[512,896]{1,0:T(8,128)(2,1)S(1)}, u32[]{:S(2)}, u32[]{:S(2)}) collective-permute-start(bf16[512,896]{1,0:T(8,128)(2,1)S(1)} %bitcast.20), channel_id=1, source_target_pairs={{0,1},{1,0},{2,3},{3,2},{4,5},{5,4},{6,7},{7,6},{8,9},{9,8},{10,11... | collective-permute-start | bytes 2752520 | tf_op jit(solution)/shard_map/ppermute | solution.py:186
  141.9 2.1 %collective-permute-done.16.theirs_ref = bf16[512,896]{1,0:T(8,128)(2,1)S(1)} collective-permute-done((bf16[512,896]{1,0:T(8,128)(2,1)S(1)}, bf16[512,896]{1,0:T(8,128)(2,1)S(1)}, u32[]{:S(2)}, u32[]{:S(2)}) %collective-permute-start.16) | collective-permute-done | bytes 917536 | tf_op jit(solution)/shard_map/ppermute | solution.py:186
  144.0 0.0 copy-done
  144.0 1.2 down.1
  145.3 17.4 %all_to_all.32.parts_ref = bf16[8,64,512]{2,1,0:T(8,128)(2,1)S(1)} all-to-all(bf16[8,64,512]{2,1,0:T(8,128)(2,1)S(1)} %bitcast.24), channel_id=1, replica_groups=mesh['side'=2,'rp'=4,'rl'=2,'x'=4,'yl'=2,'core'=2] {'rl','rp'}, dimensions={0} | all-to-all | bytes 1048576 | tf_op jit(solution)/shard_map/all_to_all | solution.py:200
  162.7 0.1 final.1
  162.8 18.5 %all_to_all.33.back_ref = bf16[32,4,512]{2,1,0:T(4,128)(2,1)S(1)} all-to-all(bf16[32,4,512]{2,1,0:T(4,128)(2,1)S(1)} %final.1), channel_id=1, replica_groups=mesh['side'=2,'rp'=4,'rl'=2,'x'=4,'yl'=2,'core'=2] {'side','core','x','yl'}, dimensions={0} | all-to-all | bytes 262144 | tf_op jit(solution)/shard_map/all_to_all | solution.py:200
  181.3 0.6 output.1
  (6 shorter events, 0.0 us)
Async XLA Ops:
  0.0 24.6 %collective-permute-start.4 = (bf16[1,1024,512]{2,1,0:T(8,128)(2,1)}, bf16[1,1024,512]{2,1,0:T(8,128)(2,1)S(1)}, u32[]{:S(2)}, u32[]{:S(2)}) collective-permute-start(bf16[1,1024,512]{2,1,0:T(8,128)(2,1)} %own_ref.1), channel_id=1, source_target_pairs={{0,16},{16,0},{1,17},{17,1},{2,18},{18,2},{3,19},{19,3},{4,20},{20... | collective-permute-start | bytes 3145736 | tf_op jit(solution)/shard_map/ppermute | solution.py:186
  7.0 34.9 %copy-start.1 = (bf16[1,1024,512]{2,1,0:T(8,128)(2,1)S(1)}, bf16[1,1024,512]{2,1,0:T(8,128)(2,1)}, u32[]{:S(2)}) copy-start(bf16[1,1024,512]{2,1,0:T(8,128)(2,1)} %own_ref.1) | copy-start | bytes 3145732
  7.0 15.3 %collective-permute-start = (bf16[8,1024]{1,0:T(8,128)(2,1)}, bf16[8,1024]{1,0:T(8,128)(2,1)S(1)}, u32[]{:S(2)}, u32[]{:S(2)}) collective-permute-start(bf16[8,1024]{1,0:T(8,128)(2,1)} %get-tuple-element.15), channel_id=1, source_target_pairs={{0,128},{32,160},{64,192},{96,224},{1,129},{33,161},{65,193},{97,2... | collective-permute-start | bytes 49160 | tf_op jit(solution)/shard_map/ppermute | solution.py:196
  11.9 10.4 %collective-permute-start.1 = (bf16[8,1024]{1,0:T(8,128)(2,1)}, bf16[8,1024]{1,0:T(8,128)(2,1)S(1)}, u32[]{:S(2)}, u32[]{:S(2)}) collective-permute-start(bf16[8,1024]{1,0:T(8,128)(2,1)} %get-tuple-element.16), channel_id=1, source_target_pairs={{0,160},{32,192},{64,224},{96,128},{1,161},{33,193},{65,225},{97,1... | collective-permute-start | bytes 49160 | tf_op jit(solution)/shard_map/ppermute | solution.py:196
  16.0 6.3 %collective-permute-start.2 = (bf16[8,1024]{1,0:T(8,128)(2,1)}, bf16[8,1024]{1,0:T(8,128)(2,1)S(1)}, u32[]{:S(2)}, u32[]{:S(2)}) collective-permute-start(bf16[8,1024]{1,0:T(8,128)(2,1)} %get-tuple-element.17), channel_id=1, source_target_pairs={{0,192},{32,224},{64,128},{96,160},{1,193},{33,225},{65,129},{97,1... | collective-permute-start | bytes 49160 | tf_op jit(solution)/shard_map/ppermute | solution.py:196
  21.0 2.4 %collective-permute-start.3 = (bf16[8,1024]{1,0:T(8,128)(2,1)}, bf16[8,1024]{1,0:T(8,128)(2,1)S(1)}, u32[]{:S(2)}, u32[]{:S(2)}) collective-permute-start(bf16[8,1024]{1,0:T(8,128)(2,1)} %get-tuple-element.18), channel_id=1, source_target_pairs={{0,224},{32,128},{64,160},{96,192},{1,225},{33,129},{65,161},{97,1... | collective-permute-start | bytes 49160 | tf_op jit(solution)/shard_map/ppermute | solution.py:196
  36.8 16.0 %copy-start.5 = (bf16[512]{0:T(512)(128)(2,1)S(1)}, bf16[512]{0:T(512)(128)(2,1)}, u32[]{:S(2)}) copy-start(bf16[512]{0:T(512)(128)(2,1)} %param.17) | copy-start | bytes 3076
  36.8 19.6 %copy-start.2 = (bf16[512,512]{1,0:T(8,128)(2,1)S(1)}, bf16[512,512]{1,0:T(8,128)(2,1)}, u32[]{:S(2)}) copy-start(bf16[512,512]{1,0:T(8,128)(2,1)} %refs_4_.1) | copy-start | bytes 1572868
  36.8 26.9 %copy-start.3 = (bf16[1,512,1792]{2,1,0:T(8,128)(2,1)S(1)}, bf16[1,512,1792]{2,1,0:T(8,128)(2,1)}, u32[]{:S(2)}) copy-start(bf16[1,512,1792]{2,1,0:T(8,128)(2,1)} %param.19) | copy-start | bytes 5505028
  36.9 5.0 %collective-permute-start.5 = (bf16[256,1024]{1,0:T(8,128)(2,1)S(1)}, bf16[256,1024]{1,0:T(8,128)(2,1)S(1)}, u32[]{:S(2)}, u32[]{:S(2)}) collective-permute-start(bf16[256,1024]{1,0:T(8,128)(2,1)S(1)} %bitcast.22), channel_id=1, source_target_pairs={{0,1},{1,0},{2,3},{3,2},{4,5},{5,4},{6,7},{7,6},{8,9},{9,8},{10,11... | collective-permute-start | bytes 1572872 | tf_op jit(solution)/shard_map/ppermute | solution.py:186
  43.0 9.8 %collective-permute-start.6 = (bf16[2,32,512]{2,1,0:T(8,128)(2,1)S(1)}, bf16[2,32,512]{2,1,0:T(8,128)(2,1)S(1)}, u32[]{:S(2)}, u32[]{:S(2)}) collective-permute-start(bf16[2,32,512]{2,1,0:T(8,128)(2,1)S(1)} %get-tuple-element.20), channel_id=1, source_target_pairs={{0,32},{32,64},{64,96},{96,0},{1,33},{33,65},{65,97},{97,1},{2,34}... | collective-permute-start | bytes 196616 | tf_op jit(solution)/shard_map/ppermute | solution.py:191
  46.4 7.1 %collective-permute-start.7 = (bf16[2,32,512]{2,1,0:T(8,128)(2,1)S(1)}, bf16[2,32,512]{2,1,0:T(8,128)(2,1)S(1)}, u32[]{:S(2)}, u32[]{:S(2)}) collective-permute-start(bf16[2,32,512]{2,1,0:T(8,128)(2,1)S(1)} %get-tuple-element.21), channel_id=1, source_target_pairs={{0,64},{32,96},{64,0},{96,32},{1,65},{33,97},{65,1},{97,33},{2,66}... | collective-permute-start | bytes 196616 | tf_op jit(solution)/shard_map/ppermute | solution.py:191
  50.4 6.0 %collective-permute-start.8 = (bf16[2,32,512]{2,1,0:T(8,128)(2,1)S(1)}, bf16[2,32,512]{2,1,0:T(8,128)(2,1)S(1)}, u32[]{:S(2)}, u32[]{:S(2)}) collective-permute-start(bf16[2,32,512]{2,1,0:T(8,128)(2,1)S(1)} %get-tuple-element.22), channel_id=1, source_target_pairs={{0,96},{32,0},{64,32},{96,64},{1,97},{33,1},{65,33},{97,65},{2,98}... | collective-permute-start | bytes 196616 | tf_op jit(solution)/shard_map/ppermute | solution.py:191
  57.5 20.0 %all-to-all-start.1 = ((bf16[8,64,512]{2,1,0:T(8,128)(2,1)}), bf16[8,64,512]{2,1,0:T(8,128)(2,1)S(1)}, u32[]{:S(2)}, u32[]{:S(2)}) async-start(bf16[8,64,512]{2,1,0:T(8,128)(2,1)} %get-tuple-element.23), calls=%async_computation.1 | async-start | bytes 1048576 | tf_op jit(solution)/shard_map/all_to_all | solution.py:200
  63.8 3.1 %copy-start.4 = (bf16[1,512,1792]{2,1,0:T(8,128)(2,1)S(1)}, bf16[1,512,1792]{2,1,0:T(8,128)(2,1)}, u32[]{:S(2)}) copy-start(bf16[1,512,1792]{2,1,0:T(8,128)(2,1)} %param.20) | copy-start | bytes 5505028
  65.0 16.1 %collective-permute-start.10 = (bf16[512,896]{1,0:T(8,128)(2,1)}, bf16[512,896]{1,0:T(8,128)(2,1)}, u32[]{:S(2)}, u32[]{:S(2)}) collective-permute-start(bf16[512,896]{1,0:T(8,128)(2,1)} %get-tuple-element.27), channel_id=1, source_target_pairs={{0,1},{1,0},{2,3},{3,2},{4,5},{5,4},{6,7},{7,6},{8,9},{9,8},{10,11... | collective-permute-start | bytes 2752520 | tf_op jit(solution)/shard_map/ppermute | solution.py:186
  68.0 13.0 %collective-permute-start.11 = (bf16[512,896]{1,0:T(8,128)(2,1)}, bf16[512,896]{1,0:T(8,128)(2,1)}, u32[]{:S(2)}, u32[]{:S(2)}) collective-permute-start(bf16[512,896]{1,0:T(8,128)(2,1)} %get-tuple-element.25), channel_id=1, source_target_pairs={{0,1},{1,0},{2,3},{3,2},{4,5},{5,4},{6,7},{7,6},{8,9},{9,8},{10,11... | collective-permute-start | bytes 2752520 | tf_op jit(solution)/shard_map/ppermute | solution.py:186
  77.5 5.1 %collective-permute-start.9 = (bf16[512,512]{1,0:T(8,128)(2,1)S(1)}, bf16[512,512]{1,0:T(8,128)(2,1)S(1)}, u32[]{:S(2)}, u32[]{:S(2)}) collective-permute-start(bf16[512,512]{1,0:T(8,128)(2,1)S(1)} %bitcast.17), channel_id=1, source_target_pairs={{0,1},{1,0},{2,3},{3,2},{4,5},{5,4},{6,7},{7,6},{8,9},{9,8},{10,11... | collective-permute-start | bytes 1572872 | tf_op jit(solution)/shard_map/ppermute | solution.py:186
  89.4 32.4 %all-to-all-start.2 = ((bf16[8,64,1792]{2,1,0:T(8,128)(2,1)}), bf16[8,64,1792]{2,1,0:T(8,128)(2,1)S(1)}, u32[]{:S(2)}, u32[]{:S(2)}) async-start(bf16[8,64,1792]{2,1,0:T(8,128)(2,1)} %bitcast.29), calls=%async_computation.2 | async-start | bytes 3670016 | tf_op jit(solution)/shard_map/all_to_all | solution.py:200
  93.0 1.3 collective-permute-start.12
  94.7 13.4 %collective-permute-start.13 = (f32[4,128]{1,0:T(4,128)S(1)}, f32[4,128]{1,0:T(4,128)S(1)}, u32[]{:S(2)}, u32[]{:S(2)}) collective-permute-start(f32[4,128]{1,0:T(4,128)S(1)} %squares.1), channel_id=1, source_target_pairs={{0,2},{2,0},{1,3},{3,1},{4,6},{6,4},{5,7},{7,5},{8,10},{10,8},{9,1... | collective-permute-start | bytes 6152 | tf_op jit(solution)/shard_map/ppermute | solution.py:186
  108.1 9.7 %collective-permute-start.14 = (f32[4,128]{1,0:T(4,128)S(1)}, f32[4,128]{1,0:T(4,128)S(1)}, u32[]{:S(2)}, u32[]{:S(2)}) collective-permute-start(f32[4,128]{1,0:T(4,128)S(1)} %add.19), channel_id=1, source_target_pairs={{0,4},{4,0},{8,12},{12,8},{1,5},{5,1},{9,13},{13,9},{2,6},{6,2},{1... | collective-permute-start | bytes 6152 | tf_op jit(solution)/shard_map/ppermute | solution.py:358
  117.8 3.9 %collective-permute-start.15 = (f32[4,128]{1,0:T(4,128)S(1)}, f32[4,128]{1,0:T(4,128)S(1)}, u32[]{:S(2)}, u32[]{:S(2)}) collective-permute-start(f32[4,128]{1,0:T(4,128)S(1)} %add.20), channel_id=1, source_target_pairs={{0,8},{4,12},{8,0},{12,4},{1,9},{5,13},{9,1},{13,5},{2,10},{6,14},... | collective-permute-start | bytes 6152 | tf_op jit(solution)/shard_map/ppermute | solution.py:358
  121.8 22.3 %copy-start = (bf16[1,1792,512]{2,1,0:T(8,128)(2,1)S(1)}, bf16[1,1792,512]{2,1,0:T(8,128)(2,1)}, u32[]{:S(2)}) copy-start(bf16[1,1792,512]{2,1,0:T(8,128)(2,1)} %weight_ref.1) | copy-start | bytes 5505028
  137.9 6.1 %collective-permute-start.16 = (bf16[512,896]{1,0:T(8,128)(2,1)S(1)}, bf16[512,896]{1,0:T(8,128)(2,1)S(1)}, u32[]{:S(2)}, u32[]{:S(2)}) collective-permute-start(bf16[512,896]{1,0:T(8,128)(2,1)S(1)} %bitcast.20), channel_id=1, source_target_pairs={{0,1},{1,0},{2,3},{3,2},{4,5},{5,4},{6,7},{7,6},{8,9},{9,8},{10,11... | collective-permute-start | bytes 2752520 | tf_op jit(solution)/shard_map/ppermute | solution.py:186

commit v7 on v6

--- a/solution.py
+++ b/solution.py
@@ -217,11 +217,12 @@
             o_ref[i, k * rows:(k + 1) * rows] = block[...]
 
 
-def project_kernel(near_ref, far_ref, own_ref, pair_ref, *o_refs):
+def project_kernel(near_ref, far_ref, own_ref, pair_a_ref, pair_b_ref, held_ref, *o_refs):
     core, low = lax.axis_index("core"), lax.axis_index("rl")
     pairs, group = len(o_refs), o_refs[0].shape[1]
     slots = near_ref.shape[0] // (2 * pairs * (group // 4))
     rows = pairs * group
+    cut = pair_a_ref.shape[0]
     to = lax.broadcasted_iota(jnp.int32, (rows, 2 * rows), 0)
     source = lax.broadcasted_iota(jnp.int32, (rows, 2 * rows), 1)
     block = (pairs - to // group) % pairs
@@ -230,7 +231,8 @@
     pick_pair = (source == first + 1 - low).astype(jnp.bfloat16)
     for left_ref, place in ((near_ref, core), (far_ref, 1 - core)):
         part = matmul(matmul(pick_own, left_ref[...]).astype(jnp.bfloat16), own_ref[0])
-        part = part + matmul(matmul(pick_pair, left_ref[...]).astype(jnp.bfloat16), pair_ref[0])
+        theirs = matmul(pick_pair, left_ref[...]).astype(jnp.bfloat16)
+        part = part + matmul(theirs[:, :cut], pair_a_ref[...]) + matmul(theirs[:, cut:], pair_b_ref[...])
         for k in range(pairs):
             o_refs[k][place] = part[k * group:(k + 1) * group].astype(jnp.bfloat16)
 
@@ -252,39 +254,31 @@
         copies_ref[i] = scaled
 
 
-def gate_up_kernel(mine_ref, theirs_ref, gate_ref, gate_theirs_ref, up_ref, up_theirs_ref, o_ref):
-    both = jnp.concatenate([gate_ref[...], up_ref[...]], axis=1)
-    both_theirs = jnp.concatenate([gate_theirs_ref[...], up_theirs_ref[...]], axis=1)
-    o_ref[...] = (matmul(mine_ref[...], both) + matmul(theirs_ref[...], both_theirs)).astype(jnp.bfloat16)
-
-
-def squares_kernel(mine_ref, theirs_ref, gain_ref, gain_theirs_ref, o_ref):
-    one = mine_ref[...].astype(jnp.float32) * (1.0 / gain_ref[...].astype(jnp.float32))
-    two = theirs_ref[...].astype(jnp.float32) * (1.0 / gain_theirs_ref[...].astype(jnp.float32))
+def gate_up_kernel(mine_ref, theirs_ref, gain_ref, gain_theirs_ref, gate_ref, gate_theirs_ref, up_ref, up_theirs_ref, o_ref):
+    half = gate_ref.shape[1]
+    mine, theirs = mine_ref[...], theirs_ref[...]
+    o_ref[:, :half] = (matmul(mine, gate_ref[...]) + matmul(theirs, gate_theirs_ref[...])).astype(jnp.bfloat16)
+    o_ref[:, half:2 * half] = (matmul(mine, up_ref[...]) + matmul(theirs, up_theirs_ref[...])).astype(jnp.bfloat16)
+    one = mine.astype(jnp.float32) * (1.0 / gain_ref[...].astype(jnp.float32))
+    two = theirs.astype(jnp.float32) * (1.0 / gain_theirs_ref[...].astype(jnp.float32))
     squares = jnp.sum(one * one + two * two, axis=1, keepdims=True)
-    at = lax.broadcasted_iota(jnp.int32, (128, 128), 0) == lax.broadcasted_iota(jnp.int32, (128, 128), 1)
-    for i in range(o_ref.shape[0]):
-        o_ref[i:i + 1] = jnp.sum(jnp.where(at, squares[i * 128:(i + 1) * 128], 0.0), axis=0, keepdims=True)
-
-
-def hidden_kernel(parts_ref, squares_ref, copies_ref):
-    group = parts_ref.shape[1]
-    chip = lax.axis_index("x") * 2 + lax.axis_index("yl")
+    high = squares.astype(jnp.bfloat16).astype(jnp.float32)
+    lane = lax.broadcasted_iota(jnp.int32, (mine.shape[0], 128), 1)
+    o_ref[:, 2 * half:] = jnp.where(lane == 0, high, jnp.where(lane == 1, squares - high, 0.0)).astype(jnp.bfloat16)
+
+
+def hidden_kernel(parts_ref, copies_ref):
+    half = copies_ref.shape[2]
     sums = parts_ref[0].astype(jnp.float32)
     for i in range(1, parts_ref.shape[0]):
         sums = sums + parts_ref[i].astype(jnp.float32)
-    to = lax.broadcasted_iota(jnp.int32, (group, 128), 0) + lax.rem(chip, 128 // group) * group
-    lane = lax.broadcasted_iota(jnp.int32, (group, 128), 1)
-    line = lax.broadcasted_iota(jnp.int32, squares_ref.shape, 0) == chip // (128 // group)
-    wanted = jnp.sum(jnp.where(line, squares_ref[...], 0.0), axis=0, keepdims=True)
-    squares = jnp.sum(jnp.where(to == lane, wanted, 0.0), axis=1, keepdims=True)
+    squares = sums[:, 2 * half:2 * half + 1] + sums[:, 2 * half + 1:2 * half + 2]
     inv_rms = lax.rsqrt(squares / D + eps)
-    for i in range(copies_ref.shape[2] // 128):
-        gate = sums[:, i * 256:i * 256 + 128] * inv_rms
-        up = sums[:, i * 256 + 128:i * 256 + 256] * inv_rms
-        hidden = (gate / (1.0 + jnp.exp(-gate)) * up).astype(jnp.bfloat16)
-        for j in range(copies_ref.shape[0]):
-            copies_ref[j, :, i * 128:(i + 1) * 128] = hidden
+    gate = sums[:, :half] * inv_rms
+    up = sums[:, half:2 * half] * inv_rms
+    hidden = (gate / (1.0 + jnp.exp(-gate)) * up).astype(jnp.bfloat16)
+    for i in range(copies_ref.shape[0]):
+        copies_ref[i] = hidden
 
 
 def down_kernel(mine_ref, theirs_ref, weight_ref, o_ref):
@@ -327,7 +321,9 @@
     half = gate_weight.shape[2] // 2
     group = chips * 2 * slots
     total = rows * group
-    pair = flip(out_weight, "rl")
+    cut = heads // 8 * 3
+    pair_a = flip(out_weight[0, :cut], "rl")
+    pair_b = flip(out_weight[0, cut:], "rl")
     gain = norm_gain[None, :]
     gain_theirs = flip(gain, "core")
     gate_theirs = flip(lax.dynamic_slice_in_dim(gate_weight[0], (1 - core) * half, half, 1), "core")
@@ -337,27 +333,20 @@
     up_mine = lax.dynamic_slice_in_dim(up_weight[0], core * half, half, 1)
     blocks = attention(queries, new_entries, cache_keys, cache_values, lengths, pairs)
     blocks = [to_ffn(block, k) for k, block in enumerate(blocks)]
-    fanned = call(fan_kernel, "fan", jax.ShapeDtypeStruct((chips, pairs * 2 * slots, heads), bf16), in_specs=[WHOLE] * pairs + [HELD], out_specs=WHOLE)(*blocks, pair)
+    fanned = call(fan_kernel, "fan", jax.ShapeDtypeStruct((chips, pairs * 2 * slots, heads), bf16), in_specs=[WHOLE] * pairs + [HELD], out_specs=WHOLE)(*blocks, pair_a)
     near = exchange(fanned, CHIPS).reshape(chips * pairs * 2 * slots, heads)
     far = flip(near, "core")
-    own, *parts = call(project_kernel, "project", [jax.ShapeDtypeStruct((2, group // 2, width), bf16)] * pairs, in_specs=[WHOLE] * 4, out_specs=[WHOLE] * pairs)(near, far, out_weight, pair)
+    own, *parts = call(project_kernel, "project", [jax.ShapeDtypeStruct((2, group // 2, width), bf16)] * pairs, in_specs=[WHOLE] * 5 + [HELD], out_specs=[WHOLE] * pairs)(near, far, out_weight, pair_a, pair_b, gain_theirs)
     parts = [own] + [turn(part, k + 1) for k, part in enumerate(parts)]
     parts = [part.reshape(group, width) for part in parts]
     stream, copies = call(stream_kernel, "stream", (jax.ShapeDtypeStruct((group, width), jnp.float32), jax.ShapeDtypeStruct((rows, group, width), bf16)), in_specs=[WHOLE] * (pairs + 2), out_specs=(WHOLE, WHOLE))(
         *parts, residual, gain)
     scaled = exchange(copies, HOME).reshape(total, width)
     scaled_theirs = flip(scaled, "core")
-    steps = half // 128
-    fixed = pl.BlockSpec((total, width), lambda i: (0, 0))
-    piece = pl.BlockSpec((width, 128), lambda i: (0, i))
-    grid_spec = pltpu.PrefetchScalarGridSpec(num_scalar_prefetch=0, grid=(steps,), in_specs=[fixed, fixed] + [piece] * 4, out_specs=pl.BlockSpec((total, 256), lambda i: (0, i)))
-    sent = call(gate_up_kernel, "gate_up", pltpu.HBM((total, 2 * half), bf16), grid_spec=grid_spec)(scaled, scaled_theirs, gate_mine, gate_theirs, up_mine, up_theirs)
-    squares = call(squares_kernel, "squares", jax.ShapeDtypeStruct((total // 128, 128), jnp.float32), in_specs=[WHOLE] * 4, out_specs=WHOLE)(scaled, scaled_theirs, gain, gain_theirs)
-    squares = squares + flip(squares, "yl")
-    for distance in (1, 2):
-        squares = squares + lax.ppermute(squares, "x", [(i, i ^ distance) for i in range(lax.axis_size("x"))])
-    sums = exchange(sent.reshape(chips, group, 2 * half), CHIPS)
-    hidden = call(hidden_kernel, "hidden", jax.ShapeDtypeStruct((chips, group, half), bf16), in_specs=[WHOLE] * 2, out_specs=WHOLE)(sums, squares)
+    sent = call(gate_up_kernel, "gate_up", jax.ShapeDtypeStruct((total, 2 * half + 128), bf16), in_specs=[WHOLE] * 8, out_specs=WHOLE)(
+        scaled, scaled_theirs, gain, gain_theirs, gate_mine, gate_theirs, up_mine, up_theirs)
+    sums = exchange(sent.reshape(chips, group, 2 * half + 128), CHIPS)
+    hidden = call(hidden_kernel, "hidden", jax.ShapeDtypeStruct((chips, group, half), bf16), in_specs=[WHOLE], out_specs=WHOLE)(sums)
     hidden = exchange(hidden, CHIPS).reshape(total, half)
     down = call(down_kernel, "down", jax.ShapeDtypeStruct((total, width), bf16), in_specs=[WHOLE] * 3, out_specs=WHOLE)(hidden, flip(hidden, "core"), down_weight)
     downs = exchange(down.reshape(rows, group, width), HOME)

time: 183 us -> 172 us (0.940)
  waiting for transfers between devices: 42 us -> 21.2 us
  blocking collectives: 63.8 us -> 81.1 us
  starting transfers between devices: 54.9 us -> 46.8 us
  local copies, waits for them, and re-layouts: 2.39 us -> 5.81 us
  Pallas kernels: 18.8 us -> 16.2 us
    all_to_all x4, blocking collectives: 63.8 us -> 81.1 us  [exchange(): return lax.all_to_all(value, axes, split_axis=0, concat_axis=0, tiled=True)]
    ppermute x8, waiting for transfers between devices: 19 us -> 8.75 us  [flip(): return lax.ppermute(value, axis, [(0, 1), (1, 0)])]
    ppermute x2 -> x0, waiting for transfers between devices: 9.42 us -> none  [local(): lax.ppermute(squares, 'x', [(i, i ^ distance) for i in range(lax.axis_siz...]
    ppermute x3, starting transfers between devices: 9.78 us -> 4.74 us  [turn(): lax.ppermute(value, 'rp', [(i, (i + steps) % count) for i in range(count)])]
    ppermute x2 -> x0, starting transfers between devices: 4.27 us -> none  [local(): lax.ppermute(squares, 'x', [(i, i ^ distance) for i in range(lax.axis_siz...]
    pallas_call x2 -> x1, Pallas kernels: 7.18 us -> 3.64 us  [local(): call(gate_up_kernel, 'gate_up', jax.ShapeDtypeStruct((total, 2 * half + 1...]
    ppermute x8, starting transfers between devices: 15.7 us -> 18.1 us  [flip(): return lax.ppermute(value, axis, [(0, 1), (1, 0)])]
    squeeze x0 -> x2, local copies, waits for them, and re-layouts: none -> 1.91 us  [the longest x1 1.02 us: local(): pair_a = flip(out_weight[0, :cut], 'rl')]
  transfers between devices with their start and end apart: 19 -> 17, of which waited for: 12 -> 9; matrix products, arithmetic and copies ran while one was open for 1% -> 3% of each run, Pallas kernels for 4% -> 4%
where the time goes in v7:
time: 172 us; the launch traced here: 171 us
  blocking collectives  81.1 us (47%)
  starting transfers between devices  46.8 us (27%)
  waiting for transfers between devices  21.2 us (12%)
  Pallas kernels  16.2 us (9%)
  local copies, waits for them, and re-layouts  5.81 us (3%)
    all_to_all x4, blocking collectives, exchange(): return lax.all_to_all(value, axes, split_axis=0, concat_axis=0, tiled=True)  81.1 us
    ppermute x8, starting transfers between devices, flip(): return lax.ppermute(value, axis, [(0, 1), (1, 0)])  18.1 us
    ppermute x4, starting transfers between devices, to_ffn(): lax.ppermute(value, ('side', 'rp'), [(i, count + (i + steps) % count) for...  14.9 us
    all_to_all x2, starting transfers between devices, exchange(): return lax.all_to_all(value, axes, split_axis=0, concat_axis=0, tiled=True)  9.16 us
    ppermute x8, waiting for transfers between devices, flip(): return lax.ppermute(value, axis, [(0, 1), (1, 0)])  8.75 us
    pallas_call x1, Pallas kernels, attention(): pl.pallas_call(attend_kernel, grid_spec=grid_spec, out_shape=[jax.ShapeDt...  6.97 us
    all_to_all x2, waiting for transfers between devices, exchange(): return lax.all_to_all(value, axes, split_axis=0, concat_axis=0, tiled=True)  6.96 us
    ppermute x3, starting transfers between devices, turn(): lax.ppermute(value, 'rp', [(i, (i + steps) % count) for i in range(count)])  4.74 us
  transfers between devices with their start and end apart: 17, of which 9 were waited for; matrix products, arithmetic and copies ran while one was open for 3% of the time, Pallas kernels for 4%

profile of v7, /device:TPU:33, one launch (start us, length us, event | category | flops | bytes accessed | tf_op | source)
XLA Modules:
  0.0 171.2 jit_solution(16338453037970168322)
XLA Ops:
  0.0 1.0 slice_bitcast_fusion.1
  1.0 0.1 collective-permute-start.4
  1.1 7.0 %attend.1 = (bf16[8,1024]{1,0:T(8,128)(2,1)}, bf16[8,1024]{1,0:T(8,128)(2,1)}, bf16[8,1024]{1,0:T(8,128)(2,1)}, bf16[8,1024]{1,0:T(8,128)(2,1)}) custom-call(s32[4]{0:T(128)} %len_ref.1, bf16[4,8192]{1,0:T(4,128)(2,1)} %q_ref.1, bf16[4,2048]{1,0:T(4,128)(2,1)} %new_ref.1, bf16[1,4,256,1024]{3,2,1,0:T(8,128)(2,1)} %k_hi_ref.1, ...), custom_call_target="tpu_custom_call" | custom-call | tf_op jit(solution)/shard_map/attend/pallas_call | solution.py:178
  8.1 0.0 copy-start
  8.1 0.0 copy-start.4
  8.1 5.0 %collective-permute-start = (bf16[8,1024]{1,0:T(8,128)(2,1)}, bf16[8,1024]{1,0:T(8,128)(2,1)S(1)}, u32[]{:S(2)}, u32[]{:S(2)}) collective-permute-start(bf16[8,1024]{1,0:T(8,128)(2,1)} %get-tuple-element.15), channel_id=1, source_target_pairs={{0,128},{32,160},{64,192},{96,224},{1,129},{33,161},{65,193},{97,2... | collective-permute-start | bytes 49160 | tf_op jit(solution)/shard_map/ppermute | solution.py:196
  13.1 4.1 %collective-permute-start.1 = (bf16[8,1024]{1,0:T(8,128)(2,1)}, bf16[8,1024]{1,0:T(8,128)(2,1)S(1)}, u32[]{:S(2)}, u32[]{:S(2)}) collective-permute-start(bf16[8,1024]{1,0:T(8,128)(2,1)} %get-tuple-element.16), channel_id=1, source_target_pairs={{0,160},{32,192},{64,224},{96,128},{1,161},{33,193},{65,225},{97,1... | collective-permute-start | bytes 49160 | tf_op jit(solution)/shard_map/ppermute | solution.py:196
  17.2 4.5 %collective-permute-start.2 = (bf16[8,1024]{1,0:T(8,128)(2,1)}, bf16[8,1024]{1,0:T(8,128)(2,1)S(1)}, u32[]{:S(2)}, u32[]{:S(2)}) collective-permute-start(bf16[8,1024]{1,0:T(8,128)(2,1)} %get-tuple-element.17), channel_id=1, source_target_pairs={{0,192},{32,224},{64,128},{96,160},{1,193},{33,225},{65,129},{97,1... | collective-permute-start | bytes 49160 | tf_op jit(solution)/shard_map/ppermute | solution.py:196
  21.7 1.3 collective-permute-start.3
  23.0 0.0 collective-permute-done.refs_0_
  23.0 0.0 collective-permute-done.1.refs_1_
  23.0 0.0 collective-permute-done.2.refs_2_
  23.0 1.0 collective-permute-done.3.refs_3_
  24.1 0.0 collective-permute-done.4.refs_4_.pair_a_ref
  24.1 0.8 fan.1
  24.9 4.9 %all-to-all-start = ((bf16[8,32,1024]{2,1,0:T(8,128)(2,1)}), bf16[8,32,1024]{2,1,0:T(8,128)(2,1)S(1)}, u32[]{:S(2)}, u32[]{:S(2)}) async-start(bf16[8,32,1024]{2,1,0:T(8,128)(2,1)} %fan.1), calls=%async_computation | async-start | bytes 1048576 | tf_op jit(solution)/shard_map/all_to_all | solution.py:200
  29.8 0.0 copy-done
  29.8 0.9 slice_bitcast_fusion
  30.7 0.0 copy-start.2
  30.7 0.5 collective-permute-start.6
  31.2 6.4 %all-to-all-done = bf16[8,32,1024]{2,1,0:T(8,128)(2,1)S(1)} async-done(((bf16[8,32,1024]{2,1,0:T(8,128)(2,1)}), bf16[8,32,1024]{2,1,0:T(8,128)(2,1)S(1)}, u32[]{:S(2)}, u32[]{:S(2)}) %all-to-all-start) | async-done | bytes 524320 | tf_op jit(solution)/shard_map/all_to_all | solution.py:200
  37.6 2.6 %collective-permute-start.5 = (bf16[256,1024]{1,0:T(8,128)(2,1)S(1)}, bf16[256,1024]{1,0:T(8,128)(2,1)S(1)}, u32[]{:S(2)}, u32[]{:S(2)}) collective-permute-start(bf16[256,1024]{1,0:T(8,128)(2,1)S(1)} %bitcast.26), channel_id=1, source_target_pairs={{0,1},{1,0},{2,3},{3,2},{4,5},{5,4},{6,7},{7,6},{8,9},{9,8},{10,11... | collective-permute-start | bytes 1572872 | tf_op jit(solution)/shard_map/ppermute | solution.py:186
  40.3 0.0 copy-done.4
  40.3 0.1 collective-permute-start.7
  40.4 1.4 collective-permute-done.7.held_ref.gain_theirs_ref
  41.8 3.7 %collective-permute-done.6.pair_b_ref = bf16[640,512]{1,0:T(8,128)(2,1)S(1)} collective-permute-done((bf16[640,512]{1,0:T(8,128)(2,1)}, bf16[640,512]{1,0:T(8,128)(2,1)S(1)}, u32[]{:S(2)}, u32[]{:S(2)}) %collective-permute-start.6) | collective-permute-done | bytes 655392 | tf_op jit(solution)/shard_map/ppermute | solution.py:186
  45.5 0.0 collective-permute-done.5.far_ref
  45.5 1.2 project.1
  46.7 1.2 collective-permute-start.8
  47.9 1.3 collective-permute-start.9
  49.2 2.3 %collective-permute-start.10 = (bf16[2,32,512]{2,1,0:T(8,128)(2,1)S(1)}, bf16[2,32,512]{2,1,0:T(8,128)(2,1)S(1)}, u32[]{:S(2)}, u32[]{:S(2)}) collective-permute-start(bf16[2,32,512]{2,1,0:T(8,128)(2,1)S(1)} %get-tuple-element.22), channel_id=1, source_target_pairs={{0,96},{32,0},{64,32},{96,64},{1,97},{33,1},{65,33},{97,65},{2,98}... | collective-permute-start | bytes 196616 | tf_op jit(solution)/shard_map/ppermute | solution.py:191
  51.5 2.0 %collective-permute-done.8 = bf16[2,32,512]{2,1,0:T(8,128)(2,1)S(1)} collective-permute-done((bf16[2,32,512]{2,1,0:T(8,128)(2,1)S(1)}, bf16[2,32,512]{2,1,0:T(8,128)(2,1)S(1)}, u32[]{:S(2)}, u32[]{:S(2)}) %collective-permute-start.8) | collective-permute-done | bytes 65568 | tf_op jit(solution)/shard_map/ppermute | solution.py:191
  53.5 2.4 %collective-permute-done.9 = bf16[2,32,512]{2,1,0:T(8,128)(2,1)S(1)} collective-permute-done((bf16[2,32,512]{2,1,0:T(8,128)(2,1)S(1)}, bf16[2,32,512]{2,1,0:T(8,128)(2,1)S(1)}, u32[]{:S(2)}, u32[]{:S(2)}) %collective-permute-start.9) | collective-permute-done | bytes 65568 | tf_op jit(solution)/shard_map/ppermute | solution.py:191
  55.9 0.0 collective-permute-done.10
  55.9 0.0 copy-done.2
  55.9 1.0 stream.1
  56.9 4.2 %all-to-all-start.1 = ((bf16[8,64,512]{2,1,0:T(8,128)(2,1)}), bf16[8,64,512]{2,1,0:T(8,128)(2,1)S(1)}, u32[]{:S(2)}, u32[]{:S(2)}) async-start(bf16[8,64,512]{2,1,0:T(8,128)(2,1)} %get-tuple-element.23), calls=%async_computation.1 | async-start | bytes 1048576 | tf_op jit(solution)/shard_map/all_to_all | solution.py:200
  61.1 0.0 copy-start.3
  61.1 2.7 %dynamic-slice_bitcast_fusion.2 = (bf16[512,896]{1,0:T(8,128)(2,1)}, bf16[512,896]{1,0:T(8,128)(2,1)S(1)}) fusion(bf16[1,512,1792]{2,1,0:T(8,128)(2,1)} %param.19, s32[]{:T(128)S(6)} %select_n.9, s32[]{:T(128)S(6)} %select_n.8), kind=kLoop, calls=%fused_computation.2 | loop fusion | bytes 3670024 | tf_op jit(solution)/shard_map/dynamic_slice | solution.py:329
  63.8 5.2 %collective-permute-start.12 = (bf16[512,896]{1,0:T(8,128)(2,1)}, bf16[512,896]{1,0:T(8,128)(2,1)S(1)}, u32[]{:S(2)}, u32[]{:S(2)}) collective-permute-start(bf16[512,896]{1,0:T(8,128)(2,1)} %get-tuple-element.27), channel_id=1, source_target_pairs={{0,1},{1,0},{2,3},{3,2},{4,5},{5,4},{6,7},{7,6},{8,9},{9,8},{10,11... | collective-permute-start | bytes 2752520 | tf_op jit(solution)/shard_map/ppermute | solution.py:186
  69.0 0.0 copy-done.3
  69.0 1.2 dynamic-slice_bitcast_fusion
  70.1 0.0 collective-permute-start.13
  70.2 0.5 all-to-all-done.1
  70.7 6.5 %collective-permute-start.11 = (bf16[512,512]{1,0:T(8,128)(2,1)S(1)}, bf16[512,512]{1,0:T(8,128)(2,1)S(1)}, u32[]{:S(2)}, u32[]{:S(2)}) collective-permute-start(bf16[512,512]{1,0:T(8,128)(2,1)S(1)} %bitcast.24), channel_id=1, source_target_pairs={{0,1},{1,0},{2,3},{3,2},{4,5},{5,4},{6,7},{7,6},{8,9},{9,8},{10,11... | collective-permute-start | bytes 1572872 | tf_op jit(solution)/shard_map/ppermute | solution.py:186
  77.2 0.0 collective-permute-done.12.gate_theirs_ref
  77.2 0.0 collective-permute-done.13.up_theirs_ref
  77.2 1.5 collective-permute-done.11.theirs_ref
  78.8 3.6 %gate_up.1 = bf16[512,1920]{1,0:T(8,128)(2,1)S(1)} custom-call(bf16[512,512]{1,0:T(8,128)(2,1)S(1)} %bitcast.25, bf16[512,512]{1,0:T(8,128)(2,1)S(1)} %collective-permute-done.11.theirs_ref, bf16[1,512]{1,0:T(2,128)(2,1)S(1)} %broadcast_in_dim.3.refs_5_.gain_ref, bf16[1,512]{1,0:T(2,128)(2,1)S(1)} %collective-permute-done.7.held_ref.gain_theirs_ref, ...), custom_call_target="tpu_custom_call" | custom-call | tf_op jit(solution)/shard_map/gate_up/pallas_call | solution.py:346
  82.4 29.1 %all_to_all.30.parts_ref = bf16[8,64,1920]{2,1,0:T(8,128)(2,1)S(1)} all-to-all(bf16[8,64,1920]{2,1,0:T(8,128)(2,1)S(1)} %bitcast.21), channel_id=1, replica_groups=mesh['side'=2,'rp'=4,'rl'=2,'x'=4,'yl'=2,'core'=2] {'x','yl'}, dimensions={0} | all-to-all | bytes 3932160 | tf_op jit(solution)/shard_map/all_to_all | solution.py:200
  111.5 0.0 copy-start.1
  111.5 0.5 hidden.1
  112.1 14.8 %all_to_all.31 = bf16[8,64,896]{2,1,0:T(8,128)(2,1)S(1)} all-to-all(bf16[8,64,896]{2,1,0:T(8,128)(2,1)S(1)} %hidden.1), channel_id=1, replica_groups=mesh['side'=2,'rp'=4,'rl'=2,'x'=4,'yl'=2,'core'=2] {'x','yl'}, dimensions={0} | all-to-all | bytes 1835008 | tf_op jit(solution)/shard_map/all_to_all | solution.py:200
  126.9 3.1 %collective-permute-start.14 = (bf16[512,896]{1,0:T(8,128)(2,1)S(1)}, bf16[512,896]{1,0:T(8,128)(2,1)S(1)}, u32[]{:S(2)}, u32[]{:S(2)}) collective-permute-start(bf16[512,896]{1,0:T(8,128)(2,1)S(1)} %bitcast.22), channel_id=1, source_target_pairs={{0,1},{1,0},{2,3},{3,2},{4,5},{5,4},{6,7},{7,6},{8,9},{9,8},{10,11... | collective-permute-start | bytes 2752520 | tf_op jit(solution)/shard_map/ppermute | solution.py:186
  129.9 2.1 %collective-permute-done.14.theirs_ref = bf16[512,896]{1,0:T(8,128)(2,1)S(1)} collective-permute-done((bf16[512,896]{1,0:T(8,128)(2,1)S(1)}, bf16[512,896]{1,0:T(8,128)(2,1)S(1)}, u32[]{:S(2)}, u32[]{:S(2)}) %collective-permute-start.14) | collective-permute-done | bytes 917536 | tf_op jit(solution)/shard_map/ppermute | solution.py:186
  132.0 0.0 copy-done.1
  132.0 1.2 down.1
  133.3 18.7 %all_to_all.32.parts_ref = bf16[8,64,512]{2,1,0:T(8,128)(2,1)S(1)} all-to-all(bf16[8,64,512]{2,1,0:T(8,128)(2,1)S(1)} %bitcast.28), channel_id=1, replica_groups=mesh['side'=2,'rp'=4,'rl'=2,'x'=4,'yl'=2,'core'=2] {'rl','rp'}, dimensions={0} | all-to-all | bytes 1048576 | tf_op jit(solution)/shard_map/all_to_all | solution.py:200
  152.0 0.1 final.1
  152.1 18.5 %all_to_all.33.back_ref = bf16[32,4,512]{2,1,0:T(4,128)(2,1)S(1)} all-to-all(bf16[32,4,512]{2,1,0:T(4,128)(2,1)S(1)} %final.1), channel_id=1, replica_groups=mesh['side'=2,'rp'=4,'rl'=2,'x'=4,'yl'=2,'core'=2] {'side','core','x','yl'}, dimensions={0} | all-to-all | bytes 262144 | tf_op jit(solution)/shard_map/all_to_all | solution.py:200
  170.6 0.6 output.1
  (1 shorter events, 0.0 us)
Async XLA Ops:
  1.0 23.0 %collective-permute-start.4 = (bf16[384,512]{1,0:T(8,128)(2,1)S(1)}, bf16[384,512]{1,0:T(8,128)(2,1)S(1)}, u32[]{:S(2)}, u32[]{:S(2)}) collective-permute-start(bf16[384,512]{1,0:T(8,128)(2,1)S(1)} %slice_bitcast_fusion.1), channel_id=1, source_target_pairs={{0,16},{16,0},{1,17},{17,1},{2,18},{18,2},{3,19},{19,3},{4,20},{20... | collective-permute-start | bytes 1179656 | tf_op jit(solution)/shard_map/ppermute | solution.py:186
  8.1 21.7 %copy-start = (bf16[1,1024,512]{2,1,0:T(8,128)(2,1)S(1)}, bf16[1,1024,512]{2,1,0:T(8,128)(2,1)}, u32[]{:S(2)}) copy-start(bf16[1,1024,512]{2,1,0:T(8,128)(2,1)} %own_ref.1) | copy-start | bytes 3145732
  8.1 32.2 %copy-start.4 = (bf16[512]{0:T(512)(128)(2,1)S(1)}, bf16[512]{0:T(512)(128)(2,1)}, u32[]{:S(2)}) copy-start(bf16[512]{0:T(512)(128)(2,1)} %param.17) | copy-start | bytes 3076
  8.1 14.9 %collective-permute-start = (bf16[8,1024]{1,0:T(8,128)(2,1)}, bf16[8,1024]{1,0:T(8,128)(2,1)S(1)}, u32[]{:S(2)}, u32[]{:S(2)}) collective-permute-start(bf16[8,1024]{1,0:T(8,128)(2,1)} %get-tuple-element.15), channel_id=1, source_target_pairs={{0,128},{32,160},{64,192},{96,224},{1,129},{33,161},{65,193},{97,2... | collective-permute-start | bytes 49160 | tf_op jit(solution)/shard_map/ppermute | solution.py:196
  13.1 9.9 %collective-permute-start.1 = (bf16[8,1024]{1,0:T(8,128)(2,1)}, bf16[8,1024]{1,0:T(8,128)(2,1)S(1)}, u32[]{:S(2)}, u32[]{:S(2)}) collective-permute-start(bf16[8,1024]{1,0:T(8,128)(2,1)} %get-tuple-element.16), channel_id=1, source_target_pairs={{0,160},{32,192},{64,224},{96,128},{1,161},{33,193},{65,225},{97,1... | collective-permute-start | bytes 49160 | tf_op jit(solution)/shard_map/ppermute | solution.py:196
  17.2 5.8 %collective-permute-start.2 = (bf16[8,1024]{1,0:T(8,128)(2,1)}, bf16[8,1024]{1,0:T(8,128)(2,1)S(1)}, u32[]{:S(2)}, u32[]{:S(2)}) collective-permute-start(bf16[8,1024]{1,0:T(8,128)(2,1)} %get-tuple-element.17), channel_id=1, source_target_pairs={{0,192},{32,224},{64,128},{96,160},{1,193},{33,225},{65,129},{97,1... | collective-permute-start | bytes 49160 | tf_op jit(solution)/shard_map/ppermute | solution.py:196
  21.7 2.4 %collective-permute-start.3 = (bf16[8,1024]{1,0:T(8,128)(2,1)}, bf16[8,1024]{1,0:T(8,128)(2,1)S(1)}, u32[]{:S(2)}, u32[]{:S(2)}) collective-permute-start(bf16[8,1024]{1,0:T(8,128)(2,1)} %get-tuple-element.18), channel_id=1, source_target_pairs={{0,224},{32,128},{64,160},{96,192},{1,225},{33,129},{65,161},{97,1... | collective-permute-start | bytes 49160 | tf_op jit(solution)/shard_map/ppermute | solution.py:196
  24.9 12.7 %all-to-all-start = ((bf16[8,32,1024]{2,1,0:T(8,128)(2,1)}), bf16[8,32,1024]{2,1,0:T(8,128)(2,1)S(1)}, u32[]{:S(2)}, u32[]{:S(2)}) async-start(bf16[8,32,1024]{2,1,0:T(8,128)(2,1)} %fan.1), calls=%async_computation | async-start | bytes 1048576 | tf_op jit(solution)/shard_map/all_to_all | solution.py:200
  30.7 25.2 %copy-start.2 = (bf16[512,512]{1,0:T(8,128)(2,1)S(1)}, bf16[512,512]{1,0:T(8,128)(2,1)}, u32[]{:S(2)}) copy-start(bf16[512,512]{1,0:T(8,128)(2,1)} %refs_4_.1) | copy-start | bytes 1572868
  30.7 14.7 %collective-permute-start.6 = (bf16[640,512]{1,0:T(8,128)(2,1)}, bf16[640,512]{1,0:T(8,128)(2,1)S(1)}, u32[]{:S(2)}, u32[]{:S(2)}) collective-permute-start(bf16[640,512]{1,0:T(8,128)(2,1)} %slice_bitcast_fusion), channel_id=1, source_target_pairs={{0,16},{16,0},{1,17},{17,1},{2,18},{18,2},{3,19},{19,3},{4,20},{20... | collective-permute-start | bytes 1966088 | tf_op jit(solution)/shard_map/ppermute | solution.py:186
  37.6 7.8 %collective-permute-start.5 = (bf16[256,1024]{1,0:T(8,128)(2,1)S(1)}, bf16[256,1024]{1,0:T(8,128)(2,1)S(1)}, u32[]{:S(2)}, u32[]{:S(2)}) collective-permute-start(bf16[256,1024]{1,0:T(8,128)(2,1)S(1)} %bitcast.26), channel_id=1, source_target_pairs={{0,1},{1,0},{2,3},{3,2},{4,5},{5,4},{6,7},{7,6},{8,9},{9,8},{10,11... | collective-permute-start | bytes 1572872 | tf_op jit(solution)/shard_map/ppermute | solution.py:186
  40.3 1.5 collective-permute-start.7
  46.7 6.8 %collective-permute-start.8 = (bf16[2,32,512]{2,1,0:T(8,128)(2,1)S(1)}, bf16[2,32,512]{2,1,0:T(8,128)(2,1)S(1)}, u32[]{:S(2)}, u32[]{:S(2)}) collective-permute-start(bf16[2,32,512]{2,1,0:T(8,128)(2,1)S(1)} %get-tuple-element.20), channel_id=1, source_target_pairs={{0,32},{32,64},{64,96},{96,0},{1,33},{33,65},{65,97},{97,1},{2,34}... | collective-permute-start | bytes 196616 | tf_op jit(solution)/shard_map/ppermute | solution.py:191
  47.9 8.0 %collective-permute-start.9 = (bf16[2,32,512]{2,1,0:T(8,128)(2,1)S(1)}, bf16[2,32,512]{2,1,0:T(8,128)(2,1)S(1)}, u32[]{:S(2)}, u32[]{:S(2)}) collective-permute-start(bf16[2,32,512]{2,1,0:T(8,128)(2,1)S(1)} %get-tuple-element.21), channel_id=1, source_target_pairs={{0,64},{32,96},{64,0},{96,32},{1,65},{33,97},{65,1},{97,33},{2,66}... | collective-permute-start | bytes 196616 | tf_op jit(solution)/shard_map/ppermute | solution.py:191
  49.2 6.7 %collective-permute-start.10 = (bf16[2,32,512]{2,1,0:T(8,128)(2,1)S(1)}, bf16[2,32,512]{2,1,0:T(8,128)(2,1)S(1)}, u32[]{:S(2)}, u32[]{:S(2)}) collective-permute-start(bf16[2,32,512]{2,1,0:T(8,128)(2,1)S(1)} %get-tuple-element.22), channel_id=1, source_target_pairs={{0,96},{32,0},{64,32},{96,64},{1,97},{33,1},{65,33},{97,65},{2,98}... | collective-permute-start | bytes 196616 | tf_op jit(solution)/shard_map/ppermute | solution.py:191
  56.9 13.8 %all-to-all-start.1 = ((bf16[8,64,512]{2,1,0:T(8,128)(2,1)}), bf16[8,64,512]{2,1,0:T(8,128)(2,1)S(1)}, u32[]{:S(2)}, u32[]{:S(2)}) async-start(bf16[8,64,512]{2,1,0:T(8,128)(2,1)} %get-tuple-element.23), calls=%async_computation.1 | async-start | bytes 1048576 | tf_op jit(solution)/shard_map/all_to_all | solution.py:200
  61.1 7.9 %copy-start.3 = (bf16[1,512,1792]{2,1,0:T(8,128)(2,1)S(1)}, bf16[1,512,1792]{2,1,0:T(8,128)(2,1)}, u32[]{:S(2)}) copy-start(bf16[1,512,1792]{2,1,0:T(8,128)(2,1)} %param.20) | copy-start | bytes 5505028
  63.8 13.4 %collective-permute-start.12 = (bf16[512,896]{1,0:T(8,128)(2,1)}, bf16[512,896]{1,0:T(8,128)(2,1)S(1)}, u32[]{:S(2)}, u32[]{:S(2)}) collective-permute-start(bf16[512,896]{1,0:T(8,128)(2,1)} %get-tuple-element.27), channel_id=1, source_target_pairs={{0,1},{1,0},{2,3},{3,2},{4,5},{5,4},{6,7},{7,6},{8,9},{9,8},{10,11... | collective-permute-start | bytes 2752520 | tf_op jit(solution)/shard_map/ppermute | solution.py:186
  70.1 7.1 %collective-permute-start.13 = (bf16[512,896]{1,0:T(8,128)(2,1)}, bf16[512,896]{1,0:T(8,128)(2,1)}, u32[]{:S(2)}, u32[]{:S(2)}) collective-permute-start(bf16[512,896]{1,0:T(8,128)(2,1)} %get-tuple-element.25), channel_id=1, source_target_pairs={{0,1},{1,0},{2,3},{3,2},{4,5},{5,4},{6,7},{7,6},{8,9},{9,8},{10,11... | collective-permute-start | bytes 2752520 | tf_op jit(solution)/shard_map/ppermute | solution.py:186
  70.7 8.1 %collective-permute-start.11 = (bf16[512,512]{1,0:T(8,128)(2,1)S(1)}, bf16[512,512]{1,0:T(8,128)(2,1)S(1)}, u32[]{:S(2)}, u32[]{:S(2)}) collective-permute-start(bf16[512,512]{1,0:T(8,128)(2,1)S(1)} %bitcast.24), channel_id=1, source_target_pairs={{0,1},{1,0},{2,3},{3,2},{4,5},{5,4},{6,7},{7,6},{8,9},{9,8},{10,11... | collective-permute-start | bytes 1572872 | tf_op jit(solution)/shard_map/ppermute | solution.py:186
  111.5 20.5 %copy-start.1 = (bf16[1,1792,512]{2,1,0:T(8,128)(2,1)S(1)}, bf16[1,1792,512]{2,1,0:T(8,128)(2,1)}, u32[]{:S(2)}) copy-start(bf16[1,1792,512]{2,1,0:T(8,128)(2,1)} %weight_ref.1) | copy-start | bytes 5505028
  126.9 5.2 %collective-permute-start.14 = (bf16[512,896]{1,0:T(8,128)(2,1)S(1)}, bf16[512,896]{1,0:T(8,128)(2,1)S(1)}, u32[]{:S(2)}, u32[]{:S(2)}) collective-permute-start(bf16[512,896]{1,0:T(8,128)(2,1)S(1)} %bitcast.22), channel_id=1, source_target_pairs={{0,1},{1,0},{2,3},{3,2},{4,5},{5,4},{6,7},{7,6},{8,9},{9,8},{10,11... | collective-permute-start | bytes 2752520 | tf_op jit(solution)/shard_map/ppermute | solution.py:186

commit v8 on v7

--- a/solution.py
+++ b/solution.py
@@ -210,19 +210,18 @@
 
 
 def fan_kernel(*refs):
-    blocks, o_ref = refs[:-2], refs[-1]
+    blocks, o_ref = refs[:-3], refs[-1]
     rows = blocks[0].shape[0]
     for i in range(o_ref.shape[0]):
         for k, block in enumerate(blocks):
             o_ref[i, k * rows:(k + 1) * rows] = block[...]
 
 
-def project_kernel(near_ref, far_ref, own_ref, pair_a_ref, pair_b_ref, held_ref, *o_refs):
+def project_kernel(near_ref, far_ref, own_ref, pair_ref, *o_refs):
     core, low = lax.axis_index("core"), lax.axis_index("rl")
     pairs, group = len(o_refs), o_refs[0].shape[1]
     slots = near_ref.shape[0] // (2 * pairs * (group // 4))
     rows = pairs * group
-    cut = pair_a_ref.shape[0]
     to = lax.broadcasted_iota(jnp.int32, (rows, 2 * rows), 0)
     source = lax.broadcasted_iota(jnp.int32, (rows, 2 * rows), 1)
     block = (pairs - to // group) % pairs
@@ -231,8 +230,7 @@
     pick_pair = (source == first + 1 - low).astype(jnp.bfloat16)
     for left_ref, place in ((near_ref, core), (far_ref, 1 - core)):
         part = matmul(matmul(pick_own, left_ref[...]).astype(jnp.bfloat16), own_ref[0])
-        theirs = matmul(pick_pair, left_ref[...]).astype(jnp.bfloat16)
-        part = part + matmul(theirs[:, :cut], pair_a_ref[...]) + matmul(theirs[:, cut:], pair_b_ref[...])
+        part = part + matmul(matmul(pick_pair, left_ref[...]).astype(jnp.bfloat16), pair_ref[0])
         for k in range(pairs):
             o_refs[k][place] = part[k * group:(k + 1) * group].astype(jnp.bfloat16)
 
@@ -321,9 +319,7 @@
     half = gate_weight.shape[2] // 2
     group = chips * 2 * slots
     total = rows * group
-    cut = heads // 8 * 3
-    pair_a = flip(out_weight[0, :cut], "rl")
-    pair_b = flip(out_weight[0, cut:], "rl")
+    pair = flip(out_weight, "rl")
     gain = norm_gain[None, :]
     gain_theirs = flip(gain, "core")
     gate_theirs = flip(lax.dynamic_slice_in_dim(gate_weight[0], (1 - core) * half, half, 1), "core")
@@ -333,10 +329,10 @@
     up_mine = lax.dynamic_slice_in_dim(up_weight[0], core * half, half, 1)
     blocks = attention(queries, new_entries, cache_keys, cache_values, lengths, pairs)
     blocks = [to_ffn(block, k) for k, block in enumerate(blocks)]
-    fanned = call(fan_kernel, "fan", jax.ShapeDtypeStruct((chips, pairs * 2 * slots, heads), bf16), in_specs=[WHOLE] * pairs + [HELD], out_specs=WHOLE)(*blocks, pair_a)
+    fanned = call(fan_kernel, "fan", jax.ShapeDtypeStruct((chips, pairs * 2 * slots, heads), bf16), in_specs=[WHOLE] * pairs + [HELD, HELD], out_specs=WHOLE)(*blocks, pair, gain_theirs)
     near = exchange(fanned, CHIPS).reshape(chips * pairs * 2 * slots, heads)
     far = flip(near, "core")
-    own, *parts = call(project_kernel, "project", [jax.ShapeDtypeStruct((2, group // 2, width), bf16)] * pairs, in_specs=[WHOLE] * 5 + [HELD], out_specs=[WHOLE] * pairs)(near, far, out_weight, pair_a, pair_b, gain_theirs)
+    own, *parts = call(project_kernel, "project", [jax.ShapeDtypeStruct((2, group // 2, width), bf16)] * pairs, in_specs=[WHOLE] * 4, out_specs=[WHOLE] * pairs)(near, far, out_weight, pair)
     parts = [own] + [turn(part, k + 1) for k, part in enumerate(parts)]
     parts = [part.reshape(group, width) for part in parts]
     stream, copies = call(stream_kernel, "stream", (jax.ShapeDtypeStruct((group, width), jnp.float32), jax.ShapeDtypeStruct((rows, group, width), bf16)), in_specs=[WHOLE] * (pairs + 2), out_specs=(WHOLE, WHOLE))(

time: 172 us -> 172 us (level)
  blocking collectives: 81.1 us -> 89.7 us
  local copies, waits for them, and re-layouts: 5.81 us -> 3.11 us
  waiting for transfers between devices: 21.2 us -> 18.6 us
  starting transfers between devices: 46.8 us -> 44.9 us
    all_to_all x4 -> x5, blocking collectives: 81.1 us -> 89.7 us  [exchange(): return lax.all_to_all(value, axes, split_axis=0, concat_axis=0, tiled=True)]
    ppermute x3, starting transfers between devices: 4.74 us -> 9.77 us  [turn(): lax.ppermute(value, 'rp', [(i, (i + steps) % count) for i in range(count)])]
    ppermute x8 -> x7, waiting for transfers between devices: 8.75 us -> 5.18 us  [flip(): return lax.ppermute(value, axis, [(0, 1), (1, 0)])]
    all_to_all x2 -> x1, starting transfers between devices: 9.16 us -> 6.22 us  [exchange(): return lax.all_to_all(value, axes, split_axis=0, concat_axis=0, tiled=True)]
    ppermute x8 -> x7, starting transfers between devices: 18.1 us -> 15.2 us  [flip(): return lax.ppermute(value, axis, [(0, 1), (1, 0)])]
    squeeze x2 -> x0, local copies, waits for them, and re-layouts: 1.91 us -> none  [the longest x1 1.02 us: local(): pair_a = flip(out_weight[0, :cut], 'rl')]
    all_to_all x2 -> x1, waiting for transfers between devices: 6.96 us -> 8.73 us  [exchange(): return lax.all_to_all(value, axes, split_axis=0, concat_axis=0, tiled=True)]
  transfers between devices with their start and end apart: 17 -> 15, of which waited for: 9 -> 7; matrix products, arithmetic and copies ran while one was open for 3% -> 2% of each run, Pallas kernels for 4% -> 4%
where the time goes in v8:
time: 172 us
  blocking collectives  89.7 us (52%)
  starting transfers between devices  44.9 us (26%)
  waiting for transfers between devices  18.6 us (11%)
  Pallas kernels  15.3 us (9%)
  local copies, waits for them, and re-layouts  3.11 us (2%)
    all_to_all x5, blocking collectives, exchange(): return lax.all_to_all(value, axes, split_axis=0, concat_axis=0, tiled=True)  89.7 us
    ppermute x7, starting transfers between devices, flip(): return lax.ppermute(value, axis, [(0, 1), (1, 0)])  15.2 us
    ppermute x4, starting transfers between devices, to_ffn(): lax.ppermute(value, ('side', 'rp'), [(i, count + (i + steps) % count) for...  13.7 us
    ppermute x3, starting transfers between devices, turn(): lax.ppermute(value, 'rp', [(i, (i + steps) % count) for i in range(count)])  9.77 us
    all_to_all x1, waiting for transfers between devices, exchange(): return lax.all_to_all(value, axes, split_axis=0, concat_axis=0, tiled=True)  8.73 us
    pallas_call x1, Pallas kernels, attention(): pl.pallas_call(attend_kernel, grid_spec=grid_spec, out_shape=[jax.ShapeDt...  6.95 us
    all_to_all x1, starting transfers between devices, exchange(): return lax.all_to_all(value, axes, split_axis=0, concat_axis=0, tiled=True)  6.22 us
    ppermute x7, waiting for transfers between devices, flip(): return lax.ppermute(value, axis, [(0, 1), (1, 0)])  5.18 us
  transfers between devices with their start and end apart: 15, of which 7 were waited for; matrix products, arithmetic and copies ran while one was open for 2% of the time, Pallas kernels for 4%

profile of v8, /device:TPU:33, one launch (start us, length us, event | category | flops | bytes accessed | tf_op | source)
XLA Modules:
  0.0 171.7 jit_solution(11922911411683029047)
XLA Ops:
  0.0 0.0 collective-permute-start.4
  0.0 0.7 broadcast_in_dim.3.refs_5_.gain_ref
  0.7 2.5 %collective-permute-start.5 = (bf16[1,512]{1,0:T(2,128)(2,1)S(1)}, bf16[1,512]{1,0:T(2,128)(2,1)S(1)}, u32[]{:S(2)}, u32[]{:S(2)}) collective-permute-start(bf16[1,512]{1,0:T(2,128)(2,1)S(1)} %broadcast_in_dim.3.refs_5_.gain_ref), channel_id=1, source_target_pairs={{0,1},{1,0},{2,3},{3,2},{4,5},{5,4},{6,7},{7,6},{8,9},{9,8},{10,11... | collective-permute-start | bytes 3080 | tf_op jit(solution)/shard_map/ppermute | solution.py:186
  3.2 7.0 %attend.1 = (bf16[8,1024]{1,0:T(8,128)(2,1)}, bf16[8,1024]{1,0:T(8,128)(2,1)}, bf16[8,1024]{1,0:T(8,128)(2,1)}, bf16[8,1024]{1,0:T(8,128)(2,1)}) custom-call(s32[4]{0:T(128)} %len_ref.1, bf16[4,8192]{1,0:T(4,128)(2,1)} %q_ref.1, bf16[4,2048]{1,0:T(4,128)(2,1)} %new_ref.1, bf16[1,4,256,1024]{3,2,1,0:T(8,128)(2,1)} %k_hi_ref.1, ...), custom_call_target="tpu_custom_call" | custom-call | tf_op jit(solution)/shard_map/attend/pallas_call | solution.py:178
  10.2 0.0 copy-start.1
  10.2 3.2 %collective-permute-start = (bf16[8,1024]{1,0:T(8,128)(2,1)}, bf16[8,1024]{1,0:T(8,128)(2,1)S(1)}, u32[]{:S(2)}, u32[]{:S(2)}) collective-permute-start(bf16[8,1024]{1,0:T(8,128)(2,1)} %get-tuple-element.15), channel_id=1, source_target_pairs={{0,128},{32,160},{64,192},{96,224},{1,129},{33,161},{65,193},{97,2... | collective-permute-start | bytes 49160 | tf_op jit(solution)/shard_map/ppermute | solution.py:196
  13.4 3.6 %collective-permute-start.1 = (bf16[8,1024]{1,0:T(8,128)(2,1)}, bf16[8,1024]{1,0:T(8,128)(2,1)S(1)}, u32[]{:S(2)}, u32[]{:S(2)}) collective-permute-start(bf16[8,1024]{1,0:T(8,128)(2,1)} %get-tuple-element.16), channel_id=1, source_target_pairs={{0,160},{32,192},{64,224},{96,128},{1,161},{33,193},{65,225},{97,1... | collective-permute-start | bytes 49160 | tf_op jit(solution)/shard_map/ppermute | solution.py:196
  17.0 5.6 %collective-permute-start.2 = (bf16[8,1024]{1,0:T(8,128)(2,1)}, bf16[8,1024]{1,0:T(8,128)(2,1)S(1)}, u32[]{:S(2)}, u32[]{:S(2)}) collective-permute-start(bf16[8,1024]{1,0:T(8,128)(2,1)} %get-tuple-element.17), channel_id=1, source_target_pairs={{0,192},{32,224},{64,128},{96,160},{1,193},{33,225},{65,129},{97,1... | collective-permute-start | bytes 49160 | tf_op jit(solution)/shard_map/ppermute | solution.py:196
  22.6 0.0 collective-permute-done.5.refs_5_.gain_theirs_ref
  22.6 1.3 collective-permute-start.3
  23.9 0.0 collective-permute-done.refs_0_
  23.9 0.0 collective-permute-done.1.refs_1_
  23.9 0.0 collective-permute-done.2.refs_2_
  24.0 1.0 collective-permute-done.3.refs_3_
  25.0 0.0 collective-permute-done.4.refs_4_.pair_ref
  25.0 11.8 %all_to_all.30 = bf16[8,32,1024]{2,1,0:T(8,128)(2,1)S(1)} all-to-all(bf16[8,32,1024]{2,1,0:T(8,128)(2,1)S(1)} %fan.1), channel_id=1, replica_groups=mesh['side'=2,'rp'=4,'rl'=2,'x'=4,'yl'=2,'core'=2] {'x','yl'}, dimensions={0} | all-to-all | bytes 1048576 | tf_op jit(solution)/shard_map/all_to_all | solution.py:200
  36.8 0.0 copy-start.2
  36.8 0.0 copy-start.3
  36.8 3.5 %collective-permute-start.6 = (bf16[256,1024]{1,0:T(8,128)(2,1)S(1)}, bf16[256,1024]{1,0:T(8,128)(2,1)S(1)}, u32[]{:S(2)}, u32[]{:S(2)}) collective-permute-start(bf16[256,1024]{1,0:T(8,128)(2,1)S(1)} %bitcast.22), channel_id=1, source_target_pairs={{0,1},{1,0},{2,3},{3,2},{4,5},{5,4},{6,7},{7,6},{8,9},{9,8},{10,11... | collective-permute-start | bytes 1572872 | tf_op jit(solution)/shard_map/ppermute | solution.py:186
  40.3 1.5 collective-permute-done.6.far_ref
  41.9 0.0 copy-done.1
  41.9 1.2 project.1
  43.0 3.4 %collective-permute-start.7 = (bf16[2,32,512]{2,1,0:T(8,128)(2,1)S(1)}, bf16[2,32,512]{2,1,0:T(8,128)(2,1)S(1)}, u32[]{:S(2)}, u32[]{:S(2)}) collective-permute-start(bf16[2,32,512]{2,1,0:T(8,128)(2,1)S(1)} %get-tuple-element.20), channel_id=1, source_target_pairs={{0,32},{32,64},{64,96},{96,0},{1,33},{33,65},{65,97},{97,1},{2,34}... | collective-permute-start | bytes 196616 | tf_op jit(solution)/shard_map/ppermute | solution.py:191
  46.4 4.0 %collective-permute-start.8 = (bf16[2,32,512]{2,1,0:T(8,128)(2,1)S(1)}, bf16[2,32,512]{2,1,0:T(8,128)(2,1)S(1)}, u32[]{:S(2)}, u32[]{:S(2)}) collective-permute-start(bf16[2,32,512]{2,1,0:T(8,128)(2,1)S(1)} %get-tuple-element.21), channel_id=1, source_target_pairs={{0,64},{32,96},{64,0},{96,32},{1,65},{33,97},{65,1},{97,33},{2,66}... | collective-permute-start | bytes 196616 | tf_op jit(solution)/shard_map/ppermute | solution.py:191
  50.4 2.4 %collective-permute-start.9 = (bf16[2,32,512]{2,1,0:T(8,128)(2,1)S(1)}, bf16[2,32,512]{2,1,0:T(8,128)(2,1)S(1)}, u32[]{:S(2)}, u32[]{:S(2)}) collective-permute-start(bf16[2,32,512]{2,1,0:T(8,128)(2,1)S(1)} %get-tuple-element.22), channel_id=1, source_target_pairs={{0,96},{32,0},{64,32},{96,64},{1,97},{33,1},{65,33},{97,65},{2,98}... | collective-permute-start | bytes 196616 | tf_op jit(solution)/shard_map/ppermute | solution.py:191
  52.8 0.0 collective-permute-done.7
  52.8 0.7 collective-permute-done.8
  53.5 3.0 %collective-permute-done.9 = bf16[2,32,512]{2,1,0:T(8,128)(2,1)S(1)} collective-permute-done((bf16[2,32,512]{2,1,0:T(8,128)(2,1)S(1)}, bf16[2,32,512]{2,1,0:T(8,128)(2,1)S(1)}, u32[]{:S(2)}, u32[]{:S(2)}) %collective-permute-start.9) | collective-permute-done | bytes 65568 | tf_op jit(solution)/shard_map/ppermute | solution.py:191
  56.5 0.0 copy-done.2
  56.5 1.0 stream.1
  57.5 6.2 %all-to-all-start.1 = ((bf16[8,64,512]{2,1,0:T(8,128)(2,1)}), bf16[8,64,512]{2,1,0:T(8,128)(2,1)S(1)}, u32[]{:S(2)}, u32[]{:S(2)}) async-start(bf16[8,64,512]{2,1,0:T(8,128)(2,1)} %get-tuple-element.23), calls=%async_computation.1 | async-start | bytes 1048576 | tf_op jit(solution)/shard_map/all_to_all | solution.py:200
  63.7 0.0 copy-done.3
  63.7 0.0 copy-start.4
  63.7 1.2 dynamic-slice_bitcast_fusion.2
  64.9 1.9 %collective-permute-start.11 = (bf16[512,896]{1,0:T(8,128)(2,1)}, bf16[512,896]{1,0:T(8,128)(2,1)S(1)}, u32[]{:S(2)}, u32[]{:S(2)}) collective-permute-start(bf16[512,896]{1,0:T(8,128)(2,1)} %get-tuple-element.27), channel_id=1, source_target_pairs={{0,1},{1,0},{2,3},{3,2},{4,5},{5,4},{6,7},{7,6},{8,9},{9,8},{10,11... | collective-permute-start | bytes 2752520 | tf_op jit(solution)/shard_map/ppermute | solution.py:186
  66.8 0.0 copy-done.4
  66.8 1.2 dynamic-slice_bitcast_fusion
  68.1 0.6 collective-permute-start.12
  68.7 8.7 %all-to-all-done.1 = bf16[8,64,512]{2,1,0:T(8,128)(2,1)S(1)} async-done(((bf16[8,64,512]{2,1,0:T(8,128)(2,1)}), bf16[8,64,512]{2,1,0:T(8,128)(2,1)S(1)}, u32[]{:S(2)}, u32[]{:S(2)}) %all-to-all-start.1) | async-done | bytes 524320 | tf_op jit(solution)/shard_map/all_to_all | solution.py:200
  77.4 3.6 %collective-permute-start.10 = (bf16[512,512]{1,0:T(8,128)(2,1)S(1)}, bf16[512,512]{1,0:T(8,128)(2,1)S(1)}, u32[]{:S(2)}, u32[]{:S(2)}) collective-permute-start(bf16[512,512]{1,0:T(8,128)(2,1)S(1)} %bitcast.20), channel_id=1, source_target_pairs={{0,1},{1,0},{2,3},{3,2},{4,5},{5,4},{6,7},{7,6},{8,9},{9,8},{10,11... | collective-permute-start | bytes 1572872 | tf_op jit(solution)/shard_map/ppermute | solution.py:186
  81.0 0.0 collective-permute-done.11.gate_theirs_ref
  81.0 0.0 collective-permute-done.12.up_theirs_ref
  81.0 1.5 collective-permute-done.10.theirs_ref
  82.5 3.6 %gate_up.1 = bf16[512,1920]{1,0:T(8,128)(2,1)S(1)} custom-call(bf16[512,512]{1,0:T(8,128)(2,1)S(1)} %bitcast.21, bf16[512,512]{1,0:T(8,128)(2,1)S(1)} %collective-permute-done.10.theirs_ref, bf16[1,512]{1,0:T(2,128)(2,1)S(1)} %broadcast_in_dim.3.refs_5_.gain_ref, bf16[1,512]{1,0:T(2,128)(2,1)S(1)} %collective-permute-done.5.refs_5_.gain_theirs_ref, ...), custom_call_target="tpu_custom_call" | custom-call | tf_op jit(solution)/shard_map/gate_up/pallas_call | solution.py:342
  86.2 27.2 %all_to_all.31.parts_ref = bf16[8,64,1920]{2,1,0:T(8,128)(2,1)S(1)} all-to-all(bf16[8,64,1920]{2,1,0:T(8,128)(2,1)S(1)} %bitcast.17), channel_id=1, replica_groups=mesh['side'=2,'rp'=4,'rl'=2,'x'=4,'yl'=2,'core'=2] {'x','yl'}, dimensions={0} | all-to-all | bytes 3932160 | tf_op jit(solution)/shard_map/all_to_all | solution.py:200
  113.4 0.0 copy-start
  113.4 0.5 hidden.1
  113.9 14.8 %all_to_all.32 = bf16[8,64,896]{2,1,0:T(8,128)(2,1)S(1)} all-to-all(bf16[8,64,896]{2,1,0:T(8,128)(2,1)S(1)} %hidden.1), channel_id=1, replica_groups=mesh['side'=2,'rp'=4,'rl'=2,'x'=4,'yl'=2,'core'=2] {'x','yl'}, dimensions={0} | all-to-all | bytes 1835008 | tf_op jit(solution)/shard_map/all_to_all | solution.py:200
  128.7 3.1 %collective-permute-start.13 = (bf16[512,896]{1,0:T(8,128)(2,1)S(1)}, bf16[512,896]{1,0:T(8,128)(2,1)S(1)}, u32[]{:S(2)}, u32[]{:S(2)}) collective-permute-start(bf16[512,896]{1,0:T(8,128)(2,1)S(1)} %bitcast.18), channel_id=1, source_target_pairs={{0,1},{1,0},{2,3},{3,2},{4,5},{5,4},{6,7},{7,6},{8,9},{9,8},{10,11... | collective-permute-start | bytes 2752520 | tf_op jit(solution)/shard_map/ppermute | solution.py:186
  131.8 2.1 %collective-permute-done.13.theirs_ref = bf16[512,896]{1,0:T(8,128)(2,1)S(1)} collective-permute-done((bf16[512,896]{1,0:T(8,128)(2,1)S(1)}, bf16[512,896]{1,0:T(8,128)(2,1)S(1)}, u32[]{:S(2)}, u32[]{:S(2)}) %collective-permute-start.13) | collective-permute-done | bytes 917536 | tf_op jit(solution)/shard_map/ppermute | solution.py:186
  133.9 0.0 copy-done
  133.9 1.2 down.1
  135.1 17.3 %all_to_all.33.parts_ref = bf16[8,64,512]{2,1,0:T(8,128)(2,1)S(1)} all-to-all(bf16[8,64,512]{2,1,0:T(8,128)(2,1)S(1)} %bitcast.24), channel_id=1, replica_groups=mesh['side'=2,'rp'=4,'rl'=2,'x'=4,'yl'=2,'core'=2] {'rl','rp'}, dimensions={0} | all-to-all | bytes 1048576 | tf_op jit(solution)/shard_map/all_to_all | solution.py:200
  152.5 0.1 final.1
  152.5 18.6 %all_to_all.34.back_ref = bf16[32,4,512]{2,1,0:T(4,128)(2,1)S(1)} all-to-all(bf16[32,4,512]{2,1,0:T(4,128)(2,1)S(1)} %final.1), channel_id=1, replica_groups=mesh['side'=2,'rp'=4,'rl'=2,'x'=4,'yl'=2,'core'=2] {'side','core','x','yl'}, dimensions={0} | all-to-all | bytes 262144 | tf_op jit(solution)/shard_map/all_to_all | solution.py:200
  171.1 0.6 output.1
  (1 shorter events, 0.0 us)
Async XLA Ops:
  0.0 25.0 %collective-permute-start.4 = (bf16[1,1024,512]{2,1,0:T(8,128)(2,1)}, bf16[1,1024,512]{2,1,0:T(8,128)(2,1)S(1)}, u32[]{:S(2)}, u32[]{:S(2)}) collective-permute-start(bf16[1,1024,512]{2,1,0:T(8,128)(2,1)} %own_ref.1), channel_id=1, source_target_pairs={{0,16},{16,0},{1,17},{17,1},{2,18},{18,2},{3,19},{19,3},{4,20},{20... | collective-permute-start | bytes 3145736 | tf_op jit(solution)/shard_map/ppermute | solution.py:186
  0.7 21.9 %collective-permute-start.5 = (bf16[1,512]{1,0:T(2,128)(2,1)S(1)}, bf16[1,512]{1,0:T(2,128)(2,1)S(1)}, u32[]{:S(2)}, u32[]{:S(2)}) collective-permute-start(bf16[1,512]{1,0:T(2,128)(2,1)S(1)} %broadcast_in_dim.3.refs_5_.gain_ref), channel_id=1, source_target_pairs={{0,1},{1,0},{2,3},{3,2},{4,5},{5,4},{6,7},{7,6},{8,9},{9,8},{10,11... | collective-permute-start | bytes 3080 | tf_op jit(solution)/shard_map/ppermute | solution.py:186
  10.2 31.7 %copy-start.1 = (bf16[1,1024,512]{2,1,0:T(8,128)(2,1)S(1)}, bf16[1,1024,512]{2,1,0:T(8,128)(2,1)}, u32[]{:S(2)}) copy-start(bf16[1,1024,512]{2,1,0:T(8,128)(2,1)} %own_ref.1) | copy-start | bytes 3145732
  10.2 13.8 %collective-permute-start = (bf16[8,1024]{1,0:T(8,128)(2,1)}, bf16[8,1024]{1,0:T(8,128)(2,1)S(1)}, u32[]{:S(2)}, u32[]{:S(2)}) collective-permute-start(bf16[8,1024]{1,0:T(8,128)(2,1)} %get-tuple-element.15), channel_id=1, source_target_pairs={{0,128},{32,160},{64,192},{96,224},{1,129},{33,161},{65,193},{97,2... | collective-permute-start | bytes 49160 | tf_op jit(solution)/shard_map/ppermute | solution.py:196
  13.4 10.5 %collective-permute-start.1 = (bf16[8,1024]{1,0:T(8,128)(2,1)}, bf16[8,1024]{1,0:T(8,128)(2,1)S(1)}, u32[]{:S(2)}, u32[]{:S(2)}) collective-permute-start(bf16[8,1024]{1,0:T(8,128)(2,1)} %get-tuple-element.16), channel_id=1, source_target_pairs={{0,160},{32,192},{64,224},{96,128},{1,161},{33,193},{65,225},{97,1... | collective-permute-start | bytes 49160 | tf_op jit(solution)/shard_map/ppermute | solution.py:196
  17.0 6.9 %collective-permute-start.2 = (bf16[8,1024]{1,0:T(8,128)(2,1)}, bf16[8,1024]{1,0:T(8,128)(2,1)S(1)}, u32[]{:S(2)}, u32[]{:S(2)}) collective-permute-start(bf16[8,1024]{1,0:T(8,128)(2,1)} %get-tuple-element.17), channel_id=1, source_target_pairs={{0,192},{32,224},{64,128},{96,160},{1,193},{33,225},{65,129},{97,1... | collective-permute-start | bytes 49160 | tf_op jit(solution)/shard_map/ppermute | solution.py:196
  22.6 2.4 %collective-permute-start.3 = (bf16[8,1024]{1,0:T(8,128)(2,1)}, bf16[8,1024]{1,0:T(8,128)(2,1)S(1)}, u32[]{:S(2)}, u32[]{:S(2)}) collective-permute-start(bf16[8,1024]{1,0:T(8,128)(2,1)} %get-tuple-element.18), channel_id=1, source_target_pairs={{0,224},{32,128},{64,160},{96,192},{1,225},{33,129},{65,161},{97,1... | collective-permute-start | bytes 49160 | tf_op jit(solution)/shard_map/ppermute | solution.py:196
  36.8 19.7 %copy-start.2 = (bf16[512,512]{1,0:T(8,128)(2,1)S(1)}, bf16[512,512]{1,0:T(8,128)(2,1)}, u32[]{:S(2)}) copy-start(bf16[512,512]{1,0:T(8,128)(2,1)} %refs_4_.1) | copy-start | bytes 1572868
  36.8 26.9 %copy-start.3 = (bf16[1,512,1792]{2,1,0:T(8,128)(2,1)S(1)}, bf16[1,512,1792]{2,1,0:T(8,128)(2,1)}, u32[]{:S(2)}) copy-start(bf16[1,512,1792]{2,1,0:T(8,128)(2,1)} %param.19) | copy-start | bytes 5505028
  36.8 5.0 %collective-permute-start.6 = (bf16[256,1024]{1,0:T(8,128)(2,1)S(1)}, bf16[256,1024]{1,0:T(8,128)(2,1)S(1)}, u32[]{:S(2)}, u32[]{:S(2)}) collective-permute-start(bf16[256,1024]{1,0:T(8,128)(2,1)S(1)} %bitcast.22), channel_id=1, source_target_pairs={{0,1},{1,0},{2,3},{3,2},{4,5},{5,4},{6,7},{7,6},{8,9},{9,8},{10,11... | collective-permute-start | bytes 1572872 | tf_op jit(solution)/shard_map/ppermute | solution.py:186
  43.0 9.8 %collective-permute-start.7 = (bf16[2,32,512]{2,1,0:T(8,128)(2,1)S(1)}, bf16[2,32,512]{2,1,0:T(8,128)(2,1)S(1)}, u32[]{:S(2)}, u32[]{:S(2)}) collective-permute-start(bf16[2,32,512]{2,1,0:T(8,128)(2,1)S(1)} %get-tuple-element.20), channel_id=1, source_target_pairs={{0,32},{32,64},{64,96},{96,0},{1,33},{33,65},{65,97},{97,1},{2,34}... | collective-permute-start | bytes 196616 | tf_op jit(solution)/shard_map/ppermute | solution.py:191
  46.4 7.1 %collective-permute-start.8 = (bf16[2,32,512]{2,1,0:T(8,128)(2,1)S(1)}, bf16[2,32,512]{2,1,0:T(8,128)(2,1)S(1)}, u32[]{:S(2)}, u32[]{:S(2)}) collective-permute-start(bf16[2,32,512]{2,1,0:T(8,128)(2,1)S(1)} %get-tuple-element.21), channel_id=1, source_target_pairs={{0,64},{32,96},{64,0},{96,32},{1,65},{33,97},{65,1},{97,33},{2,66}... | collective-permute-start | bytes 196616 | tf_op jit(solution)/shard_map/ppermute | solution.py:191
  50.4 6.1 %collective-permute-start.9 = (bf16[2,32,512]{2,1,0:T(8,128)(2,1)S(1)}, bf16[2,32,512]{2,1,0:T(8,128)(2,1)S(1)}, u32[]{:S(2)}, u32[]{:S(2)}) collective-permute-start(bf16[2,32,512]{2,1,0:T(8,128)(2,1)S(1)} %get-tuple-element.22), channel_id=1, source_target_pairs={{0,96},{32,0},{64,32},{96,64},{1,97},{33,1},{65,33},{97,65},{2,98}... | collective-permute-start | bytes 196616 | tf_op jit(solution)/shard_map/ppermute | solution.py:191
  57.5 19.9 %all-to-all-start.1 = ((bf16[8,64,512]{2,1,0:T(8,128)(2,1)}), bf16[8,64,512]{2,1,0:T(8,128)(2,1)S(1)}, u32[]{:S(2)}, u32[]{:S(2)}) async-start(bf16[8,64,512]{2,1,0:T(8,128)(2,1)} %get-tuple-element.23), calls=%async_computation.1 | async-start | bytes 1048576 | tf_op jit(solution)/shard_map/all_to_all | solution.py:200
  63.7 3.1 %copy-start.4 = (bf16[1,512,1792]{2,1,0:T(8,128)(2,1)S(1)}, bf16[1,512,1792]{2,1,0:T(8,128)(2,1)}, u32[]{:S(2)}) copy-start(bf16[1,512,1792]{2,1,0:T(8,128)(2,1)} %param.20) | copy-start | bytes 5505028
  64.9 16.1 %collective-permute-start.11 = (bf16[512,896]{1,0:T(8,128)(2,1)}, bf16[512,896]{1,0:T(8,128)(2,1)S(1)}, u32[]{:S(2)}, u32[]{:S(2)}) collective-permute-start(bf16[512,896]{1,0:T(8,128)(2,1)} %get-tuple-element.27), channel_id=1, source_target_pairs={{0,1},{1,0},{2,3},{3,2},{4,5},{5,4},{6,7},{7,6},{8,9},{9,8},{10,11... | collective-permute-start | bytes 2752520 | tf_op jit(solution)/shard_map/ppermute | solution.py:186
  68.1 12.9 %collective-permute-start.12 = (bf16[512,896]{1,0:T(8,128)(2,1)}, bf16[512,896]{1,0:T(8,128)(2,1)}, u32[]{:S(2)}, u32[]{:S(2)}) collective-permute-start(bf16[512,896]{1,0:T(8,128)(2,1)} %get-tuple-element.25), channel_id=1, source_target_pairs={{0,1},{1,0},{2,3},{3,2},{4,5},{5,4},{6,7},{7,6},{8,9},{9,8},{10,11... | collective-permute-start | bytes 2752520 | tf_op jit(solution)/shard_map/ppermute | solution.py:186
  77.4 5.1 %collective-permute-start.10 = (bf16[512,512]{1,0:T(8,128)(2,1)S(1)}, bf16[512,512]{1,0:T(8,128)(2,1)S(1)}, u32[]{:S(2)}, u32[]{:S(2)}) collective-permute-start(bf16[512,512]{1,0:T(8,128)(2,1)S(1)} %bitcast.20), channel_id=1, source_target_pairs={{0,1},{1,0},{2,3},{3,2},{4,5},{5,4},{6,7},{7,6},{8,9},{9,8},{10,11... | collective-permute-start | bytes 1572872 | tf_op jit(solution)/shard_map/ppermute | solution.py:186
  113.4 20.5 %copy-start = (bf16[1,1792,512]{2,1,0:T(8,128)(2,1)S(1)}, bf16[1,1792,512]{2,1,0:T(8,128)(2,1)}, u32[]{:S(2)}) copy-start(bf16[1,1792,512]{2,1,0:T(8,128)(2,1)} %weight_ref.1) | copy-start | bytes 5505028
  128.7 5.2 %collective-permute-start.13 = (bf16[512,896]{1,0:T(8,128)(2,1)S(1)}, bf16[512,896]{1,0:T(8,128)(2,1)S(1)}, u32[]{:S(2)}, u32[]{:S(2)}) collective-permute-start(bf16[512,896]{1,0:T(8,128)(2,1)S(1)} %bitcast.18), channel_id=1, source_target_pairs={{0,1},{1,0},{2,3},{3,2},{4,5},{5,4},{6,7},{7,6},{8,9},{9,8},{10,11... | collective-permute-start | bytes 2752520 | tf_op jit(solution)/shard_map/ppermute | solution.py:186

commit v9 on v7

--- a/solution.py
+++ b/solution.py
@@ -210,14 +210,14 @@
 
 
 def fan_kernel(*refs):
-    blocks, o_ref = refs[:-2], refs[-1]
+    blocks, o_ref = refs[:-3], refs[-1]
     rows = blocks[0].shape[0]
     for i in range(o_ref.shape[0]):
         for k, block in enumerate(blocks):
             o_ref[i, k * rows:(k + 1) * rows] = block[...]
 
 
-def project_kernel(near_ref, far_ref, own_ref, pair_a_ref, pair_b_ref, held_ref, *o_refs):
+def project_kernel(near_ref, far_ref, own_ref, pair_a_ref, pair_b_ref, *o_refs):
     core, low = lax.axis_index("core"), lax.axis_index("rl")
     pairs, group = len(o_refs), o_refs[0].shape[1]
     slots = near_ref.shape[0] // (2 * pairs * (group // 4))
@@ -254,17 +254,23 @@
         copies_ref[i] = scaled
 
 
-def gate_up_kernel(mine_ref, theirs_ref, gain_ref, gain_theirs_ref, gate_ref, gate_theirs_ref, up_ref, up_theirs_ref, o_ref):
+def gate_up_kernel(x_ref, gain_ref, gate_ref, up_ref, *rest):
+    other_ref, o_ref = rest if len(rest) == 2 else (None, rest[0])
     half = gate_ref.shape[1]
-    mine, theirs = mine_ref[...], theirs_ref[...]
-    o_ref[:, :half] = (matmul(mine, gate_ref[...]) + matmul(theirs, gate_theirs_ref[...])).astype(jnp.bfloat16)
-    o_ref[:, half:2 * half] = (matmul(mine, up_ref[...]) + matmul(theirs, up_theirs_ref[...])).astype(jnp.bfloat16)
-    one = mine.astype(jnp.float32) * (1.0 / gain_ref[...].astype(jnp.float32))
-    two = theirs.astype(jnp.float32) * (1.0 / gain_theirs_ref[...].astype(jnp.float32))
-    squares = jnp.sum(one * one + two * two, axis=1, keepdims=True)
-    high = squares.astype(jnp.bfloat16).astype(jnp.float32)
-    lane = lax.broadcasted_iota(jnp.int32, (mine.shape[0], 128), 1)
-    o_ref[:, 2 * half:] = jnp.where(lane == 0, high, jnp.where(lane == 1, squares - high, 0.0)).astype(jnp.bfloat16)
+    x = x_ref[...]
+    one = x.astype(jnp.float32) * (1.0 / gain_ref[...].astype(jnp.float32))
+    squares = jnp.sum(one * one, axis=1, keepdims=True)
+    gate, up = matmul(x, gate_ref[...]), matmul(x, up_ref[...])
+    lane = lax.broadcasted_iota(jnp.int32, (x.shape[0], 128), 1)
+    if other_ref is not None:
+        gate = gate + other_ref[:, :half]
+        up = up + other_ref[:, half:2 * half]
+        squares = squares + other_ref[:, 2 * half:]
+        high = squares.astype(jnp.bfloat16).astype(jnp.float32)
+        squares = jnp.where(lane == 0, high, jnp.where(lane == 1, squares - high, 0.0))
+    o_ref[:, :half] = gate.astype(o_ref.dtype)
+    o_ref[:, half:2 * half] = up.astype(o_ref.dtype)
+    o_ref[:, 2 * half:] = jnp.broadcast_to(squares, lane.shape).astype(o_ref.dtype)
 
 
 def hidden_kernel(parts_ref, copies_ref):
@@ -281,12 +287,15 @@
         copies_ref[i] = hidden
 
 
-def down_kernel(mine_ref, theirs_ref, weight_ref, o_ref):
-    half = mine_ref.shape[1]
+def down_kernel(x_ref, weight_ref, *rest):
+    other_ref, o_ref = rest if len(rest) == 2 else (None, rest[0])
+    half = x_ref.shape[1]
     core = lax.axis_index("core")
-    part = matmul(mine_ref[...], weight_ref[0, pl.ds(pl.multiple_of(core * half, half), half), :])
-    part = part + matmul(theirs_ref[...], weight_ref[0, pl.ds(pl.multiple_of((1 - core) * half, half), half), :])
-    o_ref[...] = part.astype(jnp.bfloat16)
+    at = core if other_ref is None else 1 - core
+    part = matmul(x_ref[...], weight_ref[0, pl.ds(pl.multiple_of(at * half, half), half), :])
+    if other_ref is not None:
+        part = part + other_ref[...]
+    o_ref[...] = part.astype(o_ref.dtype)
 
 
 def final_kernel(parts_ref, stream_ref, copies_ref):
@@ -321,11 +330,11 @@
     half = gate_weight.shape[2] // 2
     group = chips * 2 * slots
     total = rows * group
-    cut = heads // 8 * 3
+    cut = heads // 16 * 7
     pair_a = flip(out_weight[0, :cut], "rl")
     pair_b = flip(out_weight[0, cut:], "rl")
     gain = norm_gain[None, :]
-    gain_theirs = flip(gain, "core")
+    gain_theirs = flip(norm_gain, "core")
     gate_theirs = flip(lax.dynamic_slice_in_dim(gate_weight[0], (1 - core) * half, half, 1), "core")
     up_theirs = flip(lax.dynamic_slice_in_dim(up_weight[0], (1 - core) * half, half, 1), "core")
 
@@ -333,22 +342,26 @@
     up_mine = lax.dynamic_slice_in_dim(up_weight[0], core * half, half, 1)
     blocks = attention(queries, new_entries, cache_keys, cache_values, lengths, pairs)
     blocks = [to_ffn(block, k) for k, block in enumerate(blocks)]
-    fanned = call(fan_kernel, "fan", jax.ShapeDtypeStruct((chips, pairs * 2 * slots, heads), bf16), in_specs=[WHOLE] * pairs + [HELD], out_specs=WHOLE)(*blocks, pair_a)
+    fanned = call(fan_kernel, "fan", jax.ShapeDtypeStruct((chips, pairs * 2 * slots, heads), bf16), in_specs=[WHOLE] * pairs + [HELD, HELD], out_specs=WHOLE)(*blocks, pair_a, gain_theirs)
     near = exchange(fanned, CHIPS).reshape(chips * pairs * 2 * slots, heads)
     far = flip(near, "core")
-    own, *parts = call(project_kernel, "project", [jax.ShapeDtypeStruct((2, group // 2, width), bf16)] * pairs, in_specs=[WHOLE] * 5 + [HELD], out_specs=[WHOLE] * pairs)(near, far, out_weight, pair_a, pair_b, gain_theirs)
+    own, *parts = call(project_kernel, "project", [jax.ShapeDtypeStruct((2, group // 2, width), bf16)] * pairs, in_specs=[WHOLE] * 5, out_specs=[WHOLE] * pairs)(near, far, out_weight, pair_a, pair_b)
     parts = [own] + [turn(part, k + 1) for k, part in enumerate(parts)]
     parts = [part.reshape(group, width) for part in parts]
     stream, copies = call(stream_kernel, "stream", (jax.ShapeDtypeStruct((group, width), jnp.float32), jax.ShapeDtypeStruct((rows, group, width), bf16)), in_specs=[WHOLE] * (pairs + 2), out_specs=(WHOLE, WHOLE))(
         *parts, residual, gain)
     scaled = exchange(copies, HOME).reshape(total, width)
     scaled_theirs = flip(scaled, "core")
-    sent = call(gate_up_kernel, "gate_up", jax.ShapeDtypeStruct((total, 2 * half + 128), bf16), in_specs=[WHOLE] * 8, out_specs=WHOLE)(
-        scaled, scaled_theirs, gain, gain_theirs, gate_mine, gate_theirs, up_mine, up_theirs)
+    wide = 2 * half + 128
+    own = call(gate_up_kernel, "gate_up_own", jax.ShapeDtypeStruct((total, wide), jnp.float32), in_specs=[WHOLE] * 4, out_specs=WHOLE)(scaled, gain, gate_mine, up_mine)
+    sent = call(gate_up_kernel, "gate_up", jax.ShapeDtypeStruct((total, wide), bf16), in_specs=[WHOLE] * 5, out_specs=WHOLE)(
+        scaled_theirs, gain_theirs[None, :], gate_theirs, up_theirs, own)
     sums = exchange(sent.reshape(chips, group, 2 * half + 128), CHIPS)
     hidden = call(hidden_kernel, "hidden", jax.ShapeDtypeStruct((chips, group, half), bf16), in_specs=[WHOLE], out_specs=WHOLE)(sums)
     hidden = exchange(hidden, CHIPS).reshape(total, half)
-    down = call(down_kernel, "down", jax.ShapeDtypeStruct((total, width), bf16), in_specs=[WHOLE] * 3, out_specs=WHOLE)(hidden, flip(hidden, "core"), down_weight)
+    hidden_theirs = flip(hidden, "core")
+    own = call(down_kernel, "down_own", jax.ShapeDtypeStruct((total, width), jnp.float32), in_specs=[WHOLE] * 2, out_specs=WHOLE)(hidden, down_weight)
+    down = call(down_kernel, "down", jax.ShapeDtypeStruct((total, width), bf16), in_specs=[WHOLE] * 3, out_specs=WHOLE)(hidden_theirs, down_weight, own)
     downs = exchange(down.reshape(rows, group, width), HOME)
     final = call(final_kernel, "final", jax.ShapeDtypeStruct((4 * chips, slots, width), bf16), in_specs=[WHOLE] * 2, out_specs=WHOLE)(downs, stream)
     back = exchange(final, ("side", "core") + CHIPS)

time: 172 us -> 171 us (level)
  blocking collectives: 81.1 us -> 78.4 us
  waiting for transfers between devices: 21.2 us -> 23.5 us
    all_to_all x2, waiting for transfers between devices: 6.96 us -> 12.1 us  [exchange(): return lax.all_to_all(value, axes, split_axis=0, concat_axis=0, tiled=True)]
    ppermute x8, starting transfers between devices: 18.1 us -> 15.3 us  [flip(): return lax.ppermute(value, axis, [(0, 1), (1, 0)])]
    all_to_all x4, blocking collectives: 81.1 us -> 78.4 us  [exchange(): return lax.all_to_all(value, axes, split_axis=0, concat_axis=0, tiled=True)]
    ppermute x8, waiting for transfers between devices: 8.75 us -> 6.14 us  [flip(): return lax.ppermute(value, axis, [(0, 1), (1, 0)])]
    pallas_call x1 -> x3, Pallas kernels: 3.64 us -> 4.43 us  [the longest x1 2.47 us: local(): call(gate_up_kernel, 'gate_up', jax.ShapeDtypeStruct((total, wide), bf16)...]
  transfers between devices with their start and end apart: 17 -> 17, of which waited for: 9 -> 7; matrix products, arithmetic and copies ran while one was open for 3% -> 4% of each run, Pallas kernels for 4% -> 5%
where the time goes in v9:
time: 171 us
  blocking collectives  78.4 us (46%)
  starting transfers between devices  45.6 us (27%)
  waiting for transfers between devices  23.5 us (14%)
  Pallas kernels  16 us (9%)
  local copies, waits for them, and re-layouts  7.06 us (4%)
    all_to_all x4, blocking collectives, exchange(): return lax.all_to_all(value, axes, split_axis=0, concat_axis=0, tiled=True)  78.4 us
    ppermute x8, starting transfers between devices, flip(): return lax.ppermute(value, axis, [(0, 1), (1, 0)])  15.3 us
    ppermute x4, starting transfers between devices, to_ffn(): lax.ppermute(value, ('side', 'rp'), [(i, count + (i + steps) % count) for...  14.1 us
    all_to_all x2, waiting for transfers between devices, exchange(): return lax.all_to_all(value, axes, split_axis=0, concat_axis=0, tiled=True)  12.1 us
    all_to_all x2, starting transfers between devices, exchange(): return lax.all_to_all(value, axes, split_axis=0, concat_axis=0, tiled=True)  10.7 us
    pallas_call x1, Pallas kernels, attention(): pl.pallas_call(attend_kernel, grid_spec=grid_spec, out_shape=[jax.ShapeDt...  6.56 us
    ppermute x8, waiting for transfers between devices, flip(): return lax.ppermute(value, axis, [(0, 1), (1, 0)])  6.14 us
    ppermute x3, starting transfers between devices, turn(): lax.ppermute(value, 'rp', [(i, (i + steps) % count) for i in range(count)])  5.53 us
  transfers between devices with their start and end apart: 17, of which 7 were waited for; matrix products, arithmetic and copies ran while one was open for 4% of the time, Pallas kernels for 5%

profile of v9, /device:TPU:33, one launch (start us, length us, event | category | flops | bytes accessed | tf_op | source)
XLA Modules:
  0.0 170.8 jit_solution(9238020904610433185)
XLA Ops:
  0.0 1.0 slice_bitcast_fusion.1
  1.1 0.1 collective-permute-start.4
  1.2 2.5 %collective-permute-start.5 = (bf16[512]{0:T(512)(128)(2,1)}, bf16[512]{0:T(512)(128)(2,1)S(1)}, u32[]{:S(2)}, u32[]{:S(2)}) collective-permute-start(bf16[512]{0:T(512)(128)(2,1)} %param.17), channel_id=1, source_target_pairs={{0,1},{1,0},{2,3},{3,2},{4,5},{5,4},{6,7},{7,6},{8,9},{9,8},{10,11... | collective-permute-start | bytes 3080 | tf_op jit(solution)/shard_map/ppermute | solution.py:186
  3.7 6.6 %attend.1 = (bf16[8,1024]{1,0:T(8,128)(2,1)}, bf16[8,1024]{1,0:T(8,128)(2,1)}, bf16[8,1024]{1,0:T(8,128)(2,1)}, bf16[8,1024]{1,0:T(8,128)(2,1)}) custom-call(s32[4]{0:T(128)} %len_ref.1, bf16[4,8192]{1,0:T(4,128)(2,1)} %q_ref.1, bf16[4,2048]{1,0:T(4,128)(2,1)} %new_ref.1, bf16[1,4,256,1024]{3,2,1,0:T(8,128)(2,1)} %k_hi_ref.1, ...), custom_call_target="tpu_custom_call" | custom-call | tf_op jit(solution)/shard_map/attend/pallas_call | solution.py:178
  10.2 0.0 copy-start.1
  10.2 3.2 %collective-permute-start = (bf16[8,1024]{1,0:T(8,128)(2,1)}, bf16[8,1024]{1,0:T(8,128)(2,1)S(1)}, u32[]{:S(2)}, u32[]{:S(2)}) collective-permute-start(bf16[8,1024]{1,0:T(8,128)(2,1)} %get-tuple-element.15), channel_id=1, source_target_pairs={{0,128},{32,160},{64,192},{96,224},{1,129},{33,161},{65,193},{97,2... | collective-permute-start | bytes 49160 | tf_op jit(solution)/shard_map/ppermute | solution.py:196
  13.5 4.4 %collective-permute-start.1 = (bf16[8,1024]{1,0:T(8,128)(2,1)}, bf16[8,1024]{1,0:T(8,128)(2,1)S(1)}, u32[]{:S(2)}, u32[]{:S(2)}) collective-permute-start(bf16[8,1024]{1,0:T(8,128)(2,1)} %get-tuple-element.16), channel_id=1, source_target_pairs={{0,160},{32,192},{64,224},{96,128},{1,161},{33,193},{65,225},{97,1... | collective-permute-start | bytes 49160 | tf_op jit(solution)/shard_map/ppermute | solution.py:196
  17.9 5.2 %collective-permute-start.2 = (bf16[8,1024]{1,0:T(8,128)(2,1)}, bf16[8,1024]{1,0:T(8,128)(2,1)S(1)}, u32[]{:S(2)}, u32[]{:S(2)}) collective-permute-start(bf16[8,1024]{1,0:T(8,128)(2,1)} %get-tuple-element.17), channel_id=1, source_target_pairs={{0,192},{32,224},{64,128},{96,160},{1,193},{33,225},{65,129},{97,1... | collective-permute-start | bytes 49160 | tf_op jit(solution)/shard_map/ppermute | solution.py:196
  23.1 0.0 collective-permute-done.5.refs_5_
  23.1 1.3 collective-permute-start.3
  24.4 0.0 collective-permute-done.refs_0_
  24.4 0.0 collective-permute-done.1.refs_1_
  24.4 0.0 collective-permute-done.2.refs_2_
  24.4 1.0 collective-permute-done.3.refs_3_
  25.4 0.0 collective-permute-done.4.refs_4_.pair_a_ref
  25.4 0.9 fan.1
  26.3 4.0 %all-to-all-start = ((bf16[8,32,1024]{2,1,0:T(8,128)(2,1)}), bf16[8,32,1024]{2,1,0:T(8,128)(2,1)S(1)}, u32[]{:S(2)}, u32[]{:S(2)}) async-start(bf16[8,32,1024]{2,1,0:T(8,128)(2,1)} %fan.1), calls=%async_computation | async-start | bytes 1048576 | tf_op jit(solution)/shard_map/all_to_all | solution.py:200
  30.3 0.0 copy-done.1
  30.3 0.0 copy-start.3
  30.3 0.0 copy-start.2
  30.3 0.9 slice_bitcast_fusion
  31.2 1.4 collective-permute-start.7
  32.7 5.5 %all-to-all-done = bf16[8,32,1024]{2,1,0:T(8,128)(2,1)S(1)} async-done(((bf16[8,32,1024]{2,1,0:T(8,128)(2,1)}), bf16[8,32,1024]{2,1,0:T(8,128)(2,1)S(1)}, u32[]{:S(2)}, u32[]{:S(2)}) %all-to-all-start) | async-done | bytes 524320 | tf_op jit(solution)/shard_map/all_to_all | solution.py:200
  38.2 2.6 %collective-permute-start.6 = (bf16[256,1024]{1,0:T(8,128)(2,1)S(1)}, bf16[256,1024]{1,0:T(8,128)(2,1)S(1)}, u32[]{:S(2)}, u32[]{:S(2)}) collective-permute-start(bf16[256,1024]{1,0:T(8,128)(2,1)S(1)} %bitcast.27), channel_id=1, source_target_pairs={{0,1},{1,0},{2,3},{3,2},{4,5},{5,4},{6,7},{7,6},{8,9},{9,8},{10,11... | collective-permute-start | bytes 1572872 | tf_op jit(solution)/shard_map/ppermute | solution.py:186
  40.7 4.5 %collective-permute-done.7.pair_b_ref = bf16[576,512]{1,0:T(8,128)(2,1)S(1)} collective-permute-done((bf16[576,512]{1,0:T(8,128)(2,1)}, bf16[576,512]{1,0:T(8,128)(2,1)S(1)}, u32[]{:S(2)}, u32[]{:S(2)}) %collective-permute-start.7) | collective-permute-done | bytes 589856 | tf_op jit(solution)/shard_map/ppermute | solution.py:186
  45.2 0.0 collective-permute-done.6.far_ref
  45.2 1.2 project.1
  46.5 1.9 %collective-permute-start.8 = (bf16[2,32,512]{2,1,0:T(8,128)(2,1)S(1)}, bf16[2,32,512]{2,1,0:T(8,128)(2,1)S(1)}, u32[]{:S(2)}, u32[]{:S(2)}) collective-permute-start(bf16[2,32,512]{2,1,0:T(8,128)(2,1)S(1)} %get-tuple-element.20), channel_id=1, source_target_pairs={{0,32},{32,64},{64,96},{96,0},{1,33},{33,65},{65,97},{97,1},{2,34}... | collective-permute-start | bytes 196616 | tf_op jit(solution)/shard_map/ppermute | solution.py:191
  48.4 0.1 collective-permute-start.9
  48.5 3.5 %collective-permute-start.10 = (bf16[2,32,512]{2,1,0:T(8,128)(2,1)S(1)}, bf16[2,32,512]{2,1,0:T(8,128)(2,1)S(1)}, u32[]{:S(2)}, u32[]{:S(2)}) collective-permute-start(bf16[2,32,512]{2,1,0:T(8,128)(2,1)S(1)} %get-tuple-element.22), channel_id=1, source_target_pairs={{0,96},{32,0},{64,32},{96,64},{1,97},{33,1},{65,33},{97,65},{2,98}... | collective-permute-start | bytes 196616 | tf_op jit(solution)/shard_map/ppermute | solution.py:191
  52.0 0.0 copy-done.3
  52.0 0.0 collective-permute-done.8
  52.0 4.2 %collective-permute-done.9 = bf16[2,32,512]{2,1,0:T(8,128)(2,1)S(1)} collective-permute-done((bf16[2,32,512]{2,1,0:T(8,128)(2,1)S(1)}, bf16[2,32,512]{2,1,0:T(8,128)(2,1)S(1)}, u32[]{:S(2)}, u32[]{:S(2)}) %collective-permute-start.9) | collective-permute-done | bytes 65568 | tf_op jit(solution)/shard_map/ppermute | solution.py:191
  56.3 0.0 collective-permute-done.10
  56.3 0.0 copy-done.2
  56.3 1.0 stream.1
  57.2 6.7 %all-to-all-start.1 = ((bf16[8,64,512]{2,1,0:T(8,128)(2,1)}), bf16[8,64,512]{2,1,0:T(8,128)(2,1)S(1)}, u32[]{:S(2)}, u32[]{:S(2)}) async-start(bf16[8,64,512]{2,1,0:T(8,128)(2,1)} %get-tuple-element.23), calls=%async_computation.1 | async-start | bytes 1048576 | tf_op jit(solution)/shard_map/all_to_all | solution.py:200
  63.9 2.5 %dynamic-slice_bitcast_fusion.1 = (bf16[512,896]{1,0:T(8,128)(2,1)S(1)}, bf16[512,896]{1,0:T(8,128)(2,1)}) fusion(bf16[1,512,1792]{2,1,0:T(8,128)(2,1)} %param.19, s32[]{:T(128)S(6)} %select_n.9, s32[]{:T(128)S(6)} %select_n.8), kind=kLoop, calls=%fused_computation.1 | loop fusion | bytes 3670024 | tf_op jit(solution)/shard_map/dynamic_slice | solution.py:341
  66.5 2.1 %collective-permute-start.12 = (bf16[512,896]{1,0:T(8,128)(2,1)}, bf16[512,896]{1,0:T(8,128)(2,1)S(1)}, u32[]{:S(2)}, u32[]{:S(2)}) collective-permute-start(bf16[512,896]{1,0:T(8,128)(2,1)} %get-tuple-element.28), channel_id=1, source_target_pairs={{0,1},{1,0},{2,3},{3,2},{4,5},{5,4},{6,7},{7,6},{8,9},{9,8},{10,11... | collective-permute-start | bytes 2752520 | tf_op jit(solution)/shard_map/ppermute | solution.py:186
  68.6 2.5 %dynamic-slice_bitcast_fusion = (bf16[512,896]{1,0:T(8,128)(2,1)S(1)}, bf16[512,896]{1,0:T(8,128)(2,1)}) fusion(bf16[1,512,1792]{2,1,0:T(8,128)(2,1)} %param.20, s32[]{:T(128)S(6)} %select_n.9, s32[]{:T(128)S(6)} %select_n.8), kind=kLoop, calls=%fused_computation | loop fusion | bytes 3670024 | tf_op jit(solution)/shard_map/dynamic_slice | solution.py:342
  71.1 0.0 collective-permute-start.13
  71.1 6.5 %all-to-all-done.1 = bf16[8,64,512]{2,1,0:T(8,128)(2,1)S(1)} async-done(((bf16[8,64,512]{2,1,0:T(8,128)(2,1)}), bf16[8,64,512]{2,1,0:T(8,128)(2,1)S(1)}, u32[]{:S(2)}, u32[]{:S(2)}) %all-to-all-start.1) | async-done | bytes 524320 | tf_op jit(solution)/shard_map/all_to_all | solution.py:200
  77.7 3.6 %collective-permute-start.11 = (bf16[512,512]{1,0:T(8,128)(2,1)S(1)}, bf16[512,512]{1,0:T(8,128)(2,1)S(1)}, u32[]{:S(2)}, u32[]{:S(2)}) collective-permute-start(bf16[512,512]{1,0:T(8,128)(2,1)S(1)} %bitcast.24), channel_id=1, source_target_pairs={{0,1},{1,0},{2,3},{3,2},{4,5},{5,4},{6,7},{7,6},{8,9},{9,8},{10,11... | collective-permute-start | bytes 1572872 | tf_op jit(solution)/shard_map/ppermute | solution.py:186
  81.2 1.3 gate_up_own.1.rest_0_
  82.5 0.0 collective-permute-done.12.gate_ref
  82.5 0.0 collective-permute-done.13.up_ref
  82.5 0.3 collective-permute-done.11.x_ref
  82.8 2.5 %gate_up.1 = bf16[512,1920]{1,0:T(8,128)(2,1)S(1)} custom-call(bf16[512,512]{1,0:T(8,128)(2,1)S(1)} %collective-permute-done.11.x_ref, bf16[1,512]{1,0:T(2,128)(2,1)S(1)} %broadcast_in_dim.7.gain_ref, bf16[512,896]{1,0:T(8,128)(2,1)S(1)} %collective-permute-done.12.gate_ref, bf16[512,896]{1,0:T(8,128)(2,1)} %collective-permute-done.13.up_ref, ...), custom_call_target="tpu_custom_call" | custom-call | tf_op jit(solution)/shard_map/gate_up/pallas_call | solution.py:357
  85.2 28.6 %all_to_all.30.parts_ref = bf16[8,64,1920]{2,1,0:T(8,128)(2,1)S(1)} all-to-all(bf16[8,64,1920]{2,1,0:T(8,128)(2,1)S(1)} %bitcast.21), channel_id=1, replica_groups=mesh['side'=2,'rp'=4,'rl'=2,'x'=4,'yl'=2,'core'=2] {'x','yl'}, dimensions={0} | all-to-all | bytes 3932160 | tf_op jit(solution)/shard_map/all_to_all | solution.py:200
  113.9 0.0 copy-start
  113.9 0.6 hidden.1
  114.4 14.8 %all_to_all.31 = bf16[8,64,896]{2,1,0:T(8,128)(2,1)S(1)} all-to-all(bf16[8,64,896]{2,1,0:T(8,128)(2,1)S(1)} %hidden.1), channel_id=1, replica_groups=mesh['side'=2,'rp'=4,'rl'=2,'x'=4,'yl'=2,'core'=2] {'x','yl'}, dimensions={0} | all-to-all | bytes 1835008 | tf_op jit(solution)/shard_map/all_to_all | solution.py:200
  129.2 3.1 %collective-permute-start.14 = (bf16[512,896]{1,0:T(8,128)(2,1)S(1)}, bf16[512,896]{1,0:T(8,128)(2,1)S(1)}, u32[]{:S(2)}, u32[]{:S(2)}) collective-permute-start(bf16[512,896]{1,0:T(8,128)(2,1)S(1)} %bitcast.22), channel_id=1, source_target_pairs={{0,1},{1,0},{2,3},{3,2},{4,5},{5,4},{6,7},{7,6},{8,9},{9,8},{10,11... | collective-permute-start | bytes 2752520 | tf_op jit(solution)/shard_map/ppermute | solution.py:186
  132.3 0.0 copy-done
  132.3 0.7 down_own.1.rest_0_
  133.0 1.4 collective-permute-done.14.x_ref
  134.4 0.7 down.1
  135.1 17.4 %all_to_all.32.parts_ref = bf16[8,64,512]{2,1,0:T(8,128)(2,1)S(1)} all-to-all(bf16[8,64,512]{2,1,0:T(8,128)(2,1)S(1)} %bitcast.26), channel_id=1, replica_groups=mesh['side'=2,'rp'=4,'rl'=2,'x'=4,'yl'=2,'core'=2] {'rl','rp'}, dimensions={0} | all-to-all | bytes 1048576 | tf_op jit(solution)/shard_map/all_to_all | solution.py:200
  152.5 0.1 final.1
  152.6 17.6 %all_to_all.33.back_ref = bf16[32,4,512]{2,1,0:T(4,128)(2,1)S(1)} all-to-all(bf16[32,4,512]{2,1,0:T(4,128)(2,1)S(1)} %final.1), channel_id=1, replica_groups=mesh['side'=2,'rp'=4,'rl'=2,'x'=4,'yl'=2,'core'=2] {'side','core','x','yl'}, dimensions={0} | all-to-all | bytes 262144 | tf_op jit(solution)/shard_map/all_to_all | solution.py:200
  170.2 0.6 output.1
  (2 shorter events, 0.0 us)
Async XLA Ops:
  1.1 24.4 %collective-permute-start.4 = (bf16[448,512]{1,0:T(8,128)(2,1)S(1)}, bf16[448,512]{1,0:T(8,128)(2,1)S(1)}, u32[]{:S(2)}, u32[]{:S(2)}) collective-permute-start(bf16[448,512]{1,0:T(8,128)(2,1)S(1)} %slice_bitcast_fusion.1), channel_id=1, source_target_pairs={{0,16},{16,0},{1,17},{17,1},{2,18},{18,2},{3,19},{19,3},{4,20},{20... | collective-permute-start | bytes 1376264 | tf_op jit(solution)/shard_map/ppermute | solution.py:186
  1.2 21.9 %collective-permute-start.5 = (bf16[512]{0:T(512)(128)(2,1)}, bf16[512]{0:T(512)(128)(2,1)S(1)}, u32[]{:S(2)}, u32[]{:S(2)}) collective-permute-start(bf16[512]{0:T(512)(128)(2,1)} %param.17), channel_id=1, source_target_pairs={{0,1},{1,0},{2,3},{3,2},{4,5},{5,4},{6,7},{7,6},{8,9},{9,8},{10,11... | collective-permute-start | bytes 3080 | tf_op jit(solution)/shard_map/ppermute | solution.py:186
  10.2 20.1 %copy-start.1 = (bf16[1,1024,512]{2,1,0:T(8,128)(2,1)S(1)}, bf16[1,1024,512]{2,1,0:T(8,128)(2,1)}, u32[]{:S(2)}) copy-start(bf16[1,1024,512]{2,1,0:T(8,128)(2,1)} %own_ref.1) | copy-start | bytes 3145732
  10.2 14.2 %collective-permute-start = (bf16[8,1024]{1,0:T(8,128)(2,1)}, bf16[8,1024]{1,0:T(8,128)(2,1)S(1)}, u32[]{:S(2)}, u32[]{:S(2)}) collective-permute-start(bf16[8,1024]{1,0:T(8,128)(2,1)} %get-tuple-element.15), channel_id=1, source_target_pairs={{0,128},{32,160},{64,192},{96,224},{1,129},{33,161},{65,193},{97,2... | collective-permute-start | bytes 49160 | tf_op jit(solution)/shard_map/ppermute | solution.py:196
  13.5 10.9 %collective-permute-start.1 = (bf16[8,1024]{1,0:T(8,128)(2,1)}, bf16[8,1024]{1,0:T(8,128)(2,1)S(1)}, u32[]{:S(2)}, u32[]{:S(2)}) collective-permute-start(bf16[8,1024]{1,0:T(8,128)(2,1)} %get-tuple-element.16), channel_id=1, source_target_pairs={{0,160},{32,192},{64,224},{96,128},{1,161},{33,193},{65,225},{97,1... | collective-permute-start | bytes 49160 | tf_op jit(solution)/shard_map/ppermute | solution.py:196
  17.9 6.6 %collective-permute-start.2 = (bf16[8,1024]{1,0:T(8,128)(2,1)}, bf16[8,1024]{1,0:T(8,128)(2,1)S(1)}, u32[]{:S(2)}, u32[]{:S(2)}) collective-permute-start(bf16[8,1024]{1,0:T(8,128)(2,1)} %get-tuple-element.17), channel_id=1, source_target_pairs={{0,192},{32,224},{64,128},{96,160},{1,193},{33,225},{65,129},{97,1... | collective-permute-start | bytes 49160 | tf_op jit(solution)/shard_map/ppermute | solution.py:196
  23.1 2.4 %collective-permute-start.3 = (bf16[8,1024]{1,0:T(8,128)(2,1)}, bf16[8,1024]{1,0:T(8,128)(2,1)S(1)}, u32[]{:S(2)}, u32[]{:S(2)}) collective-permute-start(bf16[8,1024]{1,0:T(8,128)(2,1)} %get-tuple-element.18), channel_id=1, source_target_pairs={{0,224},{32,128},{64,160},{96,192},{1,225},{33,129},{65,161},{97,1... | collective-permute-start | bytes 49160 | tf_op jit(solution)/shard_map/ppermute | solution.py:196
  26.3 11.9 %all-to-all-start = ((bf16[8,32,1024]{2,1,0:T(8,128)(2,1)}), bf16[8,32,1024]{2,1,0:T(8,128)(2,1)S(1)}, u32[]{:S(2)}, u32[]{:S(2)}) async-start(bf16[8,32,1024]{2,1,0:T(8,128)(2,1)} %fan.1), calls=%async_computation | async-start | bytes 1048576 | tf_op jit(solution)/shard_map/all_to_all | solution.py:200
  30.3 21.7 %copy-start.3 = (bf16[512]{0:T(512)(128)(2,1)S(1)}, bf16[512]{0:T(512)(128)(2,1)}, u32[]{:S(2)}) copy-start(bf16[512]{0:T(512)(128)(2,1)} %param.17) | copy-start | bytes 3076
  30.3 25.9 %copy-start.2 = (bf16[512,512]{1,0:T(8,128)(2,1)S(1)}, bf16[512,512]{1,0:T(8,128)(2,1)}, u32[]{:S(2)}) copy-start(bf16[512,512]{1,0:T(8,128)(2,1)} %refs_4_.1) | copy-start | bytes 1572868
  31.2 14.0 %collective-permute-start.7 = (bf16[576,512]{1,0:T(8,128)(2,1)}, bf16[576,512]{1,0:T(8,128)(2,1)S(1)}, u32[]{:S(2)}, u32[]{:S(2)}) collective-permute-start(bf16[576,512]{1,0:T(8,128)(2,1)} %slice_bitcast_fusion), channel_id=1, source_target_pairs={{0,16},{16,0},{1,17},{17,1},{2,18},{18,2},{3,19},{19,3},{4,20},{20... | collective-permute-start | bytes 1769480 | tf_op jit(solution)/shard_map/ppermute | solution.py:186
  38.2 7.0 %collective-permute-start.6 = (bf16[256,1024]{1,0:T(8,128)(2,1)S(1)}, bf16[256,1024]{1,0:T(8,128)(2,1)S(1)}, u32[]{:S(2)}, u32[]{:S(2)}) collective-permute-start(bf16[256,1024]{1,0:T(8,128)(2,1)S(1)} %bitcast.27), channel_id=1, source_target_pairs={{0,1},{1,0},{2,3},{3,2},{4,5},{5,4},{6,7},{7,6},{8,9},{9,8},{10,11... | collective-permute-start | bytes 1572872 | tf_op jit(solution)/shard_map/ppermute | solution.py:186
  46.5 5.5 %collective-permute-start.8 = (bf16[2,32,512]{2,1,0:T(8,128)(2,1)S(1)}, bf16[2,32,512]{2,1,0:T(8,128)(2,1)S(1)}, u32[]{:S(2)}, u32[]{:S(2)}) collective-permute-start(bf16[2,32,512]{2,1,0:T(8,128)(2,1)S(1)} %get-tuple-element.20), channel_id=1, source_target_pairs={{0,32},{32,64},{64,96},{96,0},{1,33},{33,65},{65,97},{97,1},{2,34}... | collective-permute-start | bytes 196616 | tf_op jit(solution)/shard_map/ppermute | solution.py:191
  48.4 7.8 %collective-permute-start.9 = (bf16[2,32,512]{2,1,0:T(8,128)(2,1)S(1)}, bf16[2,32,512]{2,1,0:T(8,128)(2,1)S(1)}, u32[]{:S(2)}, u32[]{:S(2)}) collective-permute-start(bf16[2,32,512]{2,1,0:T(8,128)(2,1)S(1)} %get-tuple-element.21), channel_id=1, source_target_pairs={{0,64},{32,96},{64,0},{96,32},{1,65},{33,97},{65,1},{97,33},{2,66}... | collective-permute-start | bytes 196616 | tf_op jit(solution)/shard_map/ppermute | solution.py:191
  48.5 7.7 %collective-permute-start.10 = (bf16[2,32,512]{2,1,0:T(8,128)(2,1)S(1)}, bf16[2,32,512]{2,1,0:T(8,128)(2,1)S(1)}, u32[]{:S(2)}, u32[]{:S(2)}) collective-permute-start(bf16[2,32,512]{2,1,0:T(8,128)(2,1)S(1)} %get-tuple-element.22), channel_id=1, source_target_pairs={{0,96},{32,0},{64,32},{96,64},{1,97},{33,1},{65,33},{97,65},{2,98}... | collective-permute-start | bytes 196616 | tf_op jit(solution)/shard_map/ppermute | solution.py:191
  57.2 20.4 %all-to-all-start.1 = ((bf16[8,64,512]{2,1,0:T(8,128)(2,1)}), bf16[8,64,512]{2,1,0:T(8,128)(2,1)S(1)}, u32[]{:S(2)}, u32[]{:S(2)}) async-start(bf16[8,64,512]{2,1,0:T(8,128)(2,1)} %get-tuple-element.23), calls=%async_computation.1 | async-start | bytes 1048576 | tf_op jit(solution)/shard_map/all_to_all | solution.py:200
  66.5 16.0 %collective-permute-start.12 = (bf16[512,896]{1,0:T(8,128)(2,1)}, bf16[512,896]{1,0:T(8,128)(2,1)S(1)}, u32[]{:S(2)}, u32[]{:S(2)}) collective-permute-start(bf16[512,896]{1,0:T(8,128)(2,1)} %get-tuple-element.28), channel_id=1, source_target_pairs={{0,1},{1,0},{2,3},{3,2},{4,5},{5,4},{6,7},{7,6},{8,9},{9,8},{10,11... | collective-permute-start | bytes 2752520 | tf_op jit(solution)/shard_map/ppermute | solution.py:186
  71.1 11.4 %collective-permute-start.13 = (bf16[512,896]{1,0:T(8,128)(2,1)}, bf16[512,896]{1,0:T(8,128)(2,1)}, u32[]{:S(2)}, u32[]{:S(2)}) collective-permute-start(bf16[512,896]{1,0:T(8,128)(2,1)} %get-tuple-element.26), channel_id=1, source_target_pairs={{0,1},{1,0},{2,3},{3,2},{4,5},{5,4},{6,7},{7,6},{8,9},{9,8},{10,11... | collective-permute-start | bytes 2752520 | tf_op jit(solution)/shard_map/ppermute | solution.py:186
  77.7 5.1 %collective-permute-start.11 = (bf16[512,512]{1,0:T(8,128)(2,1)S(1)}, bf16[512,512]{1,0:T(8,128)(2,1)S(1)}, u32[]{:S(2)}, u32[]{:S(2)}) collective-permute-start(bf16[512,512]{1,0:T(8,128)(2,1)S(1)} %bitcast.24), channel_id=1, source_target_pairs={{0,1},{1,0},{2,3},{3,2},{4,5},{5,4},{6,7},{7,6},{8,9},{9,8},{10,11... | collective-permute-start | bytes 1572872 | tf_op jit(solution)/shard_map/ppermute | solution.py:186
  113.9 18.4 %copy-start = (bf16[1,1792,512]{2,1,0:T(8,128)(2,1)S(1)}, bf16[1,1792,512]{2,1,0:T(8,128)(2,1)}, u32[]{:S(2)}) copy-start(bf16[1,1792,512]{2,1,0:T(8,128)(2,1)} %weight_ref.3) | copy-start | bytes 5505028
  129.2 5.2 %collective-permute-start.14 = (bf16[512,896]{1,0:T(8,128)(2,1)S(1)}, bf16[512,896]{1,0:T(8,128)(2,1)S(1)}, u32[]{:S(2)}, u32[]{:S(2)}) collective-permute-start(bf16[512,896]{1,0:T(8,128)(2,1)S(1)} %bitcast.22), channel_id=1, source_target_pairs={{0,1},{1,0},{2,3},{3,2},{4,5},{5,4},{6,7},{7,6},{8,9},{9,8},{10,11... | collective-permute-start | bytes 2752520 | tf_op jit(solution)/shard_map/ppermute | solution.py:186

commit v10 on v9

--- a/solution.py
+++ b/solution.py
@@ -330,7 +330,7 @@
     half = gate_weight.shape[2] // 2
     group = chips * 2 * slots
     total = rows * group
-    cut = heads // 16 * 7
+    cut = heads // 16 * 11
     pair_a = flip(out_weight[0, :cut], "rl")
     pair_b = flip(out_weight[0, cut:], "rl")
     gain = norm_gain[None, :]

time: 171 us -> 175 us (1.023)
  blocking collectives: 78.4 us -> 90.2 us
  starting transfers between devices: 45.6 us -> 37.7 us
    all_to_all x4 -> x5, blocking collectives: 78.4 us -> 90.2 us  [exchange(): return lax.all_to_all(value, axes, split_axis=0, concat_axis=0, tiled=True)]
    ppermute x8, waiting for transfers between devices: 6.14 us -> 9.99 us  [flip(): return lax.ppermute(value, axis, [(0, 1), (1, 0)])]
    all_to_all x2 -> x1, starting transfers between devices: 10.7 us -> 7.33 us  [exchange(): return lax.all_to_all(value, axes, split_axis=0, concat_axis=0, tiled=True)]
    ppermute x8, starting transfers between devices: 15.3 us -> 12.1 us  [flip(): return lax.ppermute(value, axis, [(0, 1), (1, 0)])]
    all_to_all x2 -> x1, waiting for transfers between devices: 12.1 us -> 8.96 us  [exchange(): return lax.all_to_all(value, axes, split_axis=0, concat_axis=0, tiled=True)]
  transfers between devices with their start and end apart: 17 -> 16, of which waited for: 7 -> 7; matrix products, arithmetic and copies ran while one was open for 4% -> 3% of each run, Pallas kernels for 5% -> 5%
where the time goes in v10:
time: 175 us; the launch traced here: 174 us
  blocking collectives  90.2 us (52%)
  starting transfers between devices  37.7 us (22%)
  waiting for transfers between devices  24.3 us (14%)
  Pallas kernels  15.6 us (9%)
  local copies, waits for them, and re-layouts  6.32 us (4%)
    all_to_all x5, blocking collectives, exchange(): return lax.all_to_all(value, axes, split_axis=0, concat_axis=0, tiled=True)  90.2 us
    ppermute x4, starting transfers between devices, to_ffn(): lax.ppermute(value, ('side', 'rp'), [(i, count + (i + steps) % count) for...  13.3 us
    ppermute x8, starting transfers between devices, flip(): return lax.ppermute(value, axis, [(0, 1), (1, 0)])  12.1 us
    ppermute x8, waiting for transfers between devices, flip(): return lax.ppermute(value, axis, [(0, 1), (1, 0)])  9.99 us
    all_to_all x1, waiting for transfers between devices, exchange(): return lax.all_to_all(value, axes, split_axis=0, concat_axis=0, tiled=True)  8.96 us
    all_to_all x1, starting transfers between devices, exchange(): return lax.all_to_all(value, axes, split_axis=0, concat_axis=0, tiled=True)  7.33 us
    pallas_call x1, Pallas kernels, attention(): pl.pallas_call(attend_kernel, grid_spec=grid_spec, out_shape=[jax.ShapeDt...  6.95 us
    ppermute x3, starting transfers between devices, turn(): lax.ppermute(value, 'rp', [(i, (i + steps) % count) for i in range(count)])  4.95 us
  transfers between devices with their start and end apart: 16, of which 7 were waited for; matrix products, arithmetic and copies ran while one was open for 3% of the time, Pallas kernels for 5%

profile of v10, /device:TPU:33, one launch (start us, length us, event | category | flops | bytes accessed | tf_op | source)
XLA Modules:
  0.0 174.3 jit_solution(16251630224225279062)
XLA Ops:
  0.0 1.2 slice_bitcast_fusion
  1.2 0.1 collective-permute-start.4
  1.3 2.5 %collective-permute-start.5 = (bf16[512]{0:T(512)(128)(2,1)}, bf16[512]{0:T(512)(128)(2,1)S(1)}, u32[]{:S(2)}, u32[]{:S(2)}) collective-permute-start(bf16[512]{0:T(512)(128)(2,1)} %param.17), channel_id=1, source_target_pairs={{0,1},{1,0},{2,3},{3,2},{4,5},{5,4},{6,7},{7,6},{8,9},{9,8},{10,11... | collective-permute-start | bytes 3080 | tf_op jit(solution)/shard_map/ppermute | solution.py:186
  3.8 7.0 %attend.1 = (bf16[8,1024]{1,0:T(8,128)(2,1)}, bf16[8,1024]{1,0:T(8,128)(2,1)}, bf16[8,1024]{1,0:T(8,128)(2,1)}, bf16[8,1024]{1,0:T(8,128)(2,1)}) custom-call(s32[4]{0:T(128)} %len_ref.1, bf16[4,8192]{1,0:T(4,128)(2,1)} %q_ref.1, bf16[4,2048]{1,0:T(4,128)(2,1)} %new_ref.1, bf16[1,4,256,1024]{3,2,1,0:T(8,128)(2,1)} %k_hi_ref.1, ...), custom_call_target="tpu_custom_call" | custom-call | tf_op jit(solution)/shard_map/attend/pallas_call | solution.py:178
  10.7 0.0 copy-start.1
  10.7 3.2 %collective-permute-start = (bf16[8,1024]{1,0:T(8,128)(2,1)}, bf16[8,1024]{1,0:T(8,128)(2,1)S(1)}, u32[]{:S(2)}, u32[]{:S(2)}) collective-permute-start(bf16[8,1024]{1,0:T(8,128)(2,1)} %get-tuple-element.15), channel_id=1, source_target_pairs={{0,128},{32,160},{64,192},{96,224},{1,129},{33,161},{65,193},{97,2... | collective-permute-start | bytes 49160 | tf_op jit(solution)/shard_map/ppermute | solution.py:196
  14.0 4.1 %collective-permute-start.1 = (bf16[8,1024]{1,0:T(8,128)(2,1)}, bf16[8,1024]{1,0:T(8,128)(2,1)S(1)}, u32[]{:S(2)}, u32[]{:S(2)}) collective-permute-start(bf16[8,1024]{1,0:T(8,128)(2,1)} %get-tuple-element.16), channel_id=1, source_target_pairs={{0,160},{32,192},{64,224},{96,128},{1,161},{33,193},{65,225},{97,1... | collective-permute-start | bytes 49160 | tf_op jit(solution)/shard_map/ppermute | solution.py:196
  18.1 4.7 %collective-permute-start.2 = (bf16[8,1024]{1,0:T(8,128)(2,1)}, bf16[8,1024]{1,0:T(8,128)(2,1)S(1)}, u32[]{:S(2)}, u32[]{:S(2)}) collective-permute-start(bf16[8,1024]{1,0:T(8,128)(2,1)} %get-tuple-element.17), channel_id=1, source_target_pairs={{0,192},{32,224},{64,128},{96,160},{1,193},{33,225},{65,129},{97,1... | collective-permute-start | bytes 49160 | tf_op jit(solution)/shard_map/ppermute | solution.py:196
  22.8 0.0 collective-permute-done.5.refs_5_
  22.8 1.3 collective-permute-start.3
  24.1 0.0 collective-permute-done.refs_0_
  24.1 0.0 collective-permute-done.1.refs_1_
  24.1 0.0 collective-permute-done.2.refs_2_
  24.1 1.0 collective-permute-done.3.refs_3_
  25.2 0.0 collective-permute-done.4.refs_4_.pair_a_ref
  25.2 12.9 %all_to_all.30 = bf16[8,32,1024]{2,1,0:T(8,128)(2,1)S(1)} all-to-all(bf16[8,32,1024]{2,1,0:T(8,128)(2,1)S(1)} %fan.1), channel_id=1, replica_groups=mesh['side'=2,'rp'=4,'rl'=2,'x'=4,'yl'=2,'core'=2] {'x','yl'}, dimensions={0} | all-to-all | bytes 1048576 | tf_op jit(solution)/shard_map/all_to_all | solution.py:200
  38.1 0.0 copy-start.3
  38.1 0.0 copy-start.2
  38.1 2.1 %collective-permute-start.6 = (bf16[256,1024]{1,0:T(8,128)(2,1)S(1)}, bf16[256,1024]{1,0:T(8,128)(2,1)S(1)}, u32[]{:S(2)}, u32[]{:S(2)}) collective-permute-start(bf16[256,1024]{1,0:T(8,128)(2,1)S(1)} %bitcast.27), channel_id=1, source_target_pairs={{0,1},{1,0},{2,3},{3,2},{4,5},{5,4},{6,7},{7,6},{8,9},{9,8},{10,11... | collective-permute-start | bytes 1572872 | tf_op jit(solution)/shard_map/ppermute | solution.py:186
  40.2 0.0 copy-done.1
  40.3 1.1 collective-permute-start.7
  41.3 8.3 %collective-permute-done.7.pair_b_ref = bf16[320,512]{1,0:T(8,128)(2,1)S(1)} collective-permute-done((bf16[320,512]{1,0:T(8,128)(2,1)S(1)}, bf16[320,512]{1,0:T(8,128)(2,1)S(1)}, u32[]{:S(2)}, u32[]{:S(2)}) %collective-permute-start.7) | collective-permute-done | bytes 327712 | tf_op jit(solution)/shard_map/ppermute | solution.py:186
  49.7 0.0 collective-permute-done.6.far_ref
  49.7 1.2 project.1
  50.9 1.4 collective-permute-start.8
  52.3 0.9 collective-permute-start.9
  53.2 2.7 %collective-permute-start.10 = (bf16[2,32,512]{2,1,0:T(8,128)(2,1)S(1)}, bf16[2,32,512]{2,1,0:T(8,128)(2,1)S(1)}, u32[]{:S(2)}, u32[]{:S(2)}) collective-permute-start(bf16[2,32,512]{2,1,0:T(8,128)(2,1)S(1)} %get-tuple-element.22), channel_id=1, source_target_pairs={{0,96},{32,0},{64,32},{96,64},{1,97},{33,1},{65,33},{97,65},{2,98}... | collective-permute-start | bytes 196616 | tf_op jit(solution)/shard_map/ppermute | solution.py:191
  55.9 0.0 copy-done.3
  55.9 0.4 collective-permute-done.8
  56.3 3.9 %collective-permute-done.9 = bf16[2,32,512]{2,1,0:T(8,128)(2,1)S(1)} collective-permute-done((bf16[2,32,512]{2,1,0:T(8,128)(2,1)S(1)}, bf16[2,32,512]{2,1,0:T(8,128)(2,1)S(1)}, u32[]{:S(2)}, u32[]{:S(2)}) %collective-permute-start.9) | collective-permute-done | bytes 65568 | tf_op jit(solution)/shard_map/ppermute | solution.py:191
  60.2 0.0 collective-permute-done.10
  60.2 0.0 copy-done.2
  60.2 1.0 stream.1
  61.2 7.3 %all-to-all-start.1 = ((bf16[8,64,512]{2,1,0:T(8,128)(2,1)}), bf16[8,64,512]{2,1,0:T(8,128)(2,1)S(1)}, u32[]{:S(2)}, u32[]{:S(2)}) async-start(bf16[8,64,512]{2,1,0:T(8,128)(2,1)} %get-tuple-element.23), calls=%async_computation.1 | async-start | bytes 1048576 | tf_op jit(solution)/shard_map/all_to_all | solution.py:200
  68.5 2.5 %dynamic-slice_bitcast_fusion.1 = (bf16[512,896]{1,0:T(8,128)(2,1)S(1)}, bf16[512,896]{1,0:T(8,128)(2,1)}) fusion(bf16[1,512,1792]{2,1,0:T(8,128)(2,1)} %param.19, s32[]{:T(128)S(6)} %select_n.9, s32[]{:T(128)S(6)} %select_n.8), kind=kLoop, calls=%fused_computation.1 | loop fusion | bytes 3670024 | tf_op jit(solution)/shard_map/dynamic_slice | solution.py:341
  71.1 1.1 collective-permute-start.12
  72.2 2.6 %dynamic-slice_bitcast_fusion = (bf16[512,896]{1,0:T(8,128)(2,1)S(1)}, bf16[512,896]{1,0:T(8,128)(2,1)}) fusion(bf16[1,512,1792]{2,1,0:T(8,128)(2,1)} %param.20, s32[]{:T(128)S(6)} %select_n.9, s32[]{:T(128)S(6)} %select_n.8), kind=kLoop, calls=%fused_computation | loop fusion | bytes 3670024 | tf_op jit(solution)/shard_map/dynamic_slice | solution.py:342
  74.7 0.0 collective-permute-start.13
  74.7 9.0 %all-to-all-done.1 = bf16[8,64,512]{2,1,0:T(8,128)(2,1)S(1)} async-done(((bf16[8,64,512]{2,1,0:T(8,128)(2,1)}), bf16[8,64,512]{2,1,0:T(8,128)(2,1)S(1)}, u32[]{:S(2)}, u32[]{:S(2)}) %all-to-all-start.1) | async-done | bytes 524320 | tf_op jit(solution)/shard_map/all_to_all | solution.py:200
  83.7 2.1 %collective-permute-start.11 = (bf16[512,512]{1,0:T(8,128)(2,1)S(1)}, bf16[512,512]{1,0:T(8,128)(2,1)S(1)}, u32[]{:S(2)}, u32[]{:S(2)}) collective-permute-start(bf16[512,512]{1,0:T(8,128)(2,1)S(1)} %bitcast.24), channel_id=1, source_target_pairs={{0,1},{1,0},{2,3},{3,2},{4,5},{5,4},{6,7},{7,6},{8,9},{9,8},{10,11... | collective-permute-start | bytes 1572872 | tf_op jit(solution)/shard_map/ppermute | solution.py:186
  85.8 1.3 gate_up_own.1.rest_0_
  87.0 0.0 collective-permute-done.12.gate_ref
  87.0 0.0 collective-permute-done.13.up_ref
  87.0 0.3 collective-permute-done.11.x_ref
  87.3 2.5 %gate_up.1 = bf16[512,1920]{1,0:T(8,128)(2,1)S(1)} custom-call(bf16[512,512]{1,0:T(8,128)(2,1)S(1)} %collective-permute-done.11.x_ref, bf16[1,512]{1,0:T(2,128)(2,1)S(1)} %broadcast_in_dim.7.gain_ref, bf16[512,896]{1,0:T(8,128)(2,1)S(1)} %collective-permute-done.12.gate_ref, bf16[512,896]{1,0:T(8,128)(2,1)} %collective-permute-done.13.up_ref, ...), custom_call_target="tpu_custom_call" | custom-call | tf_op jit(solution)/shard_map/gate_up/pallas_call | solution.py:357
  89.8 27.1 %all_to_all.31.parts_ref = bf16[8,64,1920]{2,1,0:T(8,128)(2,1)S(1)} all-to-all(bf16[8,64,1920]{2,1,0:T(8,128)(2,1)S(1)} %bitcast.21), channel_id=1, replica_groups=mesh['side'=2,'rp'=4,'rl'=2,'x'=4,'yl'=2,'core'=2] {'x','yl'}, dimensions={0} | all-to-all | bytes 3932160 | tf_op jit(solution)/shard_map/all_to_all | solution.py:200
  116.8 0.0 copy-start
  116.8 0.5 hidden.1
  117.4 14.8 %all_to_all.32 = bf16[8,64,896]{2,1,0:T(8,128)(2,1)S(1)} all-to-all(bf16[8,64,896]{2,1,0:T(8,128)(2,1)S(1)} %hidden.1), channel_id=1, replica_groups=mesh['side'=2,'rp'=4,'rl'=2,'x'=4,'yl'=2,'core'=2] {'x','yl'}, dimensions={0} | all-to-all | bytes 1835008 | tf_op jit(solution)/shard_map/all_to_all | solution.py:200
  132.2 3.1 %collective-permute-start.14 = (bf16[512,896]{1,0:T(8,128)(2,1)S(1)}, bf16[512,896]{1,0:T(8,128)(2,1)S(1)}, u32[]{:S(2)}, u32[]{:S(2)}) collective-permute-start(bf16[512,896]{1,0:T(8,128)(2,1)S(1)} %bitcast.22), channel_id=1, source_target_pairs={{0,1},{1,0},{2,3},{3,2},{4,5},{5,4},{6,7},{7,6},{8,9},{9,8},{10,11... | collective-permute-start | bytes 2752520 | tf_op jit(solution)/shard_map/ppermute | solution.py:186
  135.2 0.0 copy-done
  135.2 0.7 down_own.1.rest_0_
  136.0 1.4 collective-permute-done.14.x_ref
  137.3 0.7 down.1
  138.1 17.4 %all_to_all.33.parts_ref = bf16[8,64,512]{2,1,0:T(8,128)(2,1)S(1)} all-to-all(bf16[8,64,512]{2,1,0:T(8,128)(2,1)S(1)} %bitcast.26), channel_id=1, replica_groups=mesh['side'=2,'rp'=4,'rl'=2,'x'=4,'yl'=2,'core'=2] {'rl','rp'}, dimensions={0} | all-to-all | bytes 1048576 | tf_op jit(solution)/shard_map/all_to_all | solution.py:200
  155.4 0.1 final.1
  155.5 18.2 %all_to_all.34.back_ref = bf16[32,4,512]{2,1,0:T(4,128)(2,1)S(1)} all-to-all(bf16[32,4,512]{2,1,0:T(4,128)(2,1)S(1)} %final.1), channel_id=1, replica_groups=mesh['side'=2,'rp'=4,'rl'=2,'x'=4,'yl'=2,'core'=2] {'side','core','x','yl'}, dimensions={0} | all-to-all | bytes 262144 | tf_op jit(solution)/shard_map/all_to_all | solution.py:200
  173.7 0.6 output.1
  (4 shorter events, 0.1 us)
Async XLA Ops:
  1.2 24.0 %collective-permute-start.4 = (bf16[704,512]{1,0:T(8,128)(2,1)S(1)}, bf16[704,512]{1,0:T(8,128)(2,1)S(1)}, u32[]{:S(2)}, u32[]{:S(2)}) collective-permute-start(bf16[704,512]{1,0:T(8,128)(2,1)S(1)} %slice_bitcast_fusion), channel_id=1, source_target_pairs={{0,16},{16,0},{1,17},{17,1},{2,18},{18,2},{3,19},{19,3},{4,20},{20... | collective-permute-start | bytes 2162696 | tf_op jit(solution)/shard_map/ppermute | solution.py:186
  1.3 21.5 %collective-permute-start.5 = (bf16[512]{0:T(512)(128)(2,1)}, bf16[512]{0:T(512)(128)(2,1)S(1)}, u32[]{:S(2)}, u32[]{:S(2)}) collective-permute-start(bf16[512]{0:T(512)(128)(2,1)} %param.17), channel_id=1, source_target_pairs={{0,1},{1,0},{2,3},{3,2},{4,5},{5,4},{6,7},{7,6},{8,9},{9,8},{10,11... | collective-permute-start | bytes 3080 | tf_op jit(solution)/shard_map/ppermute | solution.py:186
  10.7 29.5 %copy-start.1 = (bf16[1,1024,512]{2,1,0:T(8,128)(2,1)S(1)}, bf16[1,1024,512]{2,1,0:T(8,128)(2,1)}, u32[]{:S(2)}) copy-start(bf16[1,1024,512]{2,1,0:T(8,128)(2,1)} %own_ref.1) | copy-start | bytes 3145732
  10.7 13.4 %collective-permute-start = (bf16[8,1024]{1,0:T(8,128)(2,1)}, bf16[8,1024]{1,0:T(8,128)(2,1)S(1)}, u32[]{:S(2)}, u32[]{:S(2)}) collective-permute-start(bf16[8,1024]{1,0:T(8,128)(2,1)} %get-tuple-element.15), channel_id=1, source_target_pairs={{0,128},{32,160},{64,192},{96,224},{1,129},{33,161},{65,193},{97,2... | collective-permute-start | bytes 49160 | tf_op jit(solution)/shard_map/ppermute | solution.py:196
  14.0 10.2 %collective-permute-start.1 = (bf16[8,1024]{1,0:T(8,128)(2,1)}, bf16[8,1024]{1,0:T(8,128)(2,1)S(1)}, u32[]{:S(2)}, u32[]{:S(2)}) collective-permute-start(bf16[8,1024]{1,0:T(8,128)(2,1)} %get-tuple-element.16), channel_id=1, source_target_pairs={{0,160},{32,192},{64,224},{96,128},{1,161},{33,193},{65,225},{97,1... | collective-permute-start | bytes 49160 | tf_op jit(solution)/shard_map/ppermute | solution.py:196
  18.1 6.0 %collective-permute-start.2 = (bf16[8,1024]{1,0:T(8,128)(2,1)}, bf16[8,1024]{1,0:T(8,128)(2,1)S(1)}, u32[]{:S(2)}, u32[]{:S(2)}) collective-permute-start(bf16[8,1024]{1,0:T(8,128)(2,1)} %get-tuple-element.17), channel_id=1, source_target_pairs={{0,192},{32,224},{64,128},{96,160},{1,193},{33,225},{65,129},{97,1... | collective-permute-start | bytes 49160 | tf_op jit(solution)/shard_map/ppermute | solution.py:196
  22.8 2.4 %collective-permute-start.3 = (bf16[8,1024]{1,0:T(8,128)(2,1)}, bf16[8,1024]{1,0:T(8,128)(2,1)S(1)}, u32[]{:S(2)}, u32[]{:S(2)}) collective-permute-start(bf16[8,1024]{1,0:T(8,128)(2,1)} %get-tuple-element.18), channel_id=1, source_target_pairs={{0,224},{32,128},{64,160},{96,192},{1,225},{33,129},{65,161},{97,1... | collective-permute-start | bytes 49160 | tf_op jit(solution)/shard_map/ppermute | solution.py:196
  38.1 17.8 %copy-start.3 = (bf16[512]{0:T(512)(128)(2,1)S(1)}, bf16[512]{0:T(512)(128)(2,1)}, u32[]{:S(2)}) copy-start(bf16[512]{0:T(512)(128)(2,1)} %param.17) | copy-start | bytes 3076
  38.1 22.1 %copy-start.2 = (bf16[512,512]{1,0:T(8,128)(2,1)S(1)}, bf16[512,512]{1,0:T(8,128)(2,1)}, u32[]{:S(2)}) copy-start(bf16[512,512]{1,0:T(8,128)(2,1)} %refs_4_.1) | copy-start | bytes 1572868
  38.1 11.6 %collective-permute-start.6 = (bf16[256,1024]{1,0:T(8,128)(2,1)S(1)}, bf16[256,1024]{1,0:T(8,128)(2,1)S(1)}, u32[]{:S(2)}, u32[]{:S(2)}) collective-permute-start(bf16[256,1024]{1,0:T(8,128)(2,1)S(1)} %bitcast.27), channel_id=1, source_target_pairs={{0,1},{1,0},{2,3},{3,2},{4,5},{5,4},{6,7},{7,6},{8,9},{9,8},{10,11... | collective-permute-start | bytes 1572872 | tf_op jit(solution)/shard_map/ppermute | solution.py:186
  40.3 9.4 %collective-permute-start.7 = (bf16[320,512]{1,0:T(8,128)(2,1)S(1)}, bf16[320,512]{1,0:T(8,128)(2,1)S(1)}, u32[]{:S(2)}, u32[]{:S(2)}) collective-permute-start(bf16[320,512]{1,0:T(8,128)(2,1)S(1)} %slice_bitcast_fusion.1), channel_id=1, source_target_pairs={{0,16},{16,0},{1,17},{17,1},{2,18},{18,2},{3,19},{19,3},{4,20},{20... | collective-permute-start | bytes 983048 | tf_op jit(solution)/shard_map/ppermute | solution.py:186
  50.9 5.4 %collective-permute-start.8 = (bf16[2,32,512]{2,1,0:T(8,128)(2,1)S(1)}, bf16[2,32,512]{2,1,0:T(8,128)(2,1)S(1)}, u32[]{:S(2)}, u32[]{:S(2)}) collective-permute-start(bf16[2,32,512]{2,1,0:T(8,128)(2,1)S(1)} %get-tuple-element.20), channel_id=1, source_target_pairs={{0,32},{32,64},{64,96},{96,0},{1,33},{33,65},{65,97},{97,1},{2,34}... | collective-permute-start | bytes 196616 | tf_op jit(solution)/shard_map/ppermute | solution.py:191
  52.3 7.9 %collective-permute-start.9 = (bf16[2,32,512]{2,1,0:T(8,128)(2,1)S(1)}, bf16[2,32,512]{2,1,0:T(8,128)(2,1)S(1)}, u32[]{:S(2)}, u32[]{:S(2)}) collective-permute-start(bf16[2,32,512]{2,1,0:T(8,128)(2,1)S(1)} %get-tuple-element.21), channel_id=1, source_target_pairs={{0,64},{32,96},{64,0},{96,32},{1,65},{33,97},{65,1},{97,33},{2,66}... | collective-permute-start | bytes 196616 | tf_op jit(solution)/shard_map/ppermute | solution.py:191
  53.2 7.0 %collective-permute-start.10 = (bf16[2,32,512]{2,1,0:T(8,128)(2,1)S(1)}, bf16[2,32,512]{2,1,0:T(8,128)(2,1)S(1)}, u32[]{:S(2)}, u32[]{:S(2)}) collective-permute-start(bf16[2,32,512]{2,1,0:T(8,128)(2,1)S(1)} %get-tuple-element.22), channel_id=1, source_target_pairs={{0,96},{32,0},{64,32},{96,64},{1,97},{33,1},{65,33},{97,65},{2,98}... | collective-permute-start | bytes 196616 | tf_op jit(solution)/shard_map/ppermute | solution.py:191
  61.2 22.5 %all-to-all-start.1 = ((bf16[8,64,512]{2,1,0:T(8,128)(2,1)}), bf16[8,64,512]{2,1,0:T(8,128)(2,1)S(1)}, u32[]{:S(2)}, u32[]{:S(2)}) async-start(bf16[8,64,512]{2,1,0:T(8,128)(2,1)} %get-tuple-element.23), calls=%async_computation.1 | async-start | bytes 1048576 | tf_op jit(solution)/shard_map/all_to_all | solution.py:200
  71.1 16.0 %collective-permute-start.12 = (bf16[512,896]{1,0:T(8,128)(2,1)}, bf16[512,896]{1,0:T(8,128)(2,1)S(1)}, u32[]{:S(2)}, u32[]{:S(2)}) collective-permute-start(bf16[512,896]{1,0:T(8,128)(2,1)} %get-tuple-element.28), channel_id=1, source_target_pairs={{0,1},{1,0},{2,3},{3,2},{4,5},{5,4},{6,7},{7,6},{8,9},{9,8},{10,11... | collective-permute-start | bytes 2752520 | tf_op jit(solution)/shard_map/ppermute | solution.py:186
  74.7 12.3 %collective-permute-start.13 = (bf16[512,896]{1,0:T(8,128)(2,1)}, bf16[512,896]{1,0:T(8,128)(2,1)}, u32[]{:S(2)}, u32[]{:S(2)}) collective-permute-start(bf16[512,896]{1,0:T(8,128)(2,1)} %get-tuple-element.26), channel_id=1, source_target_pairs={{0,1},{1,0},{2,3},{3,2},{4,5},{5,4},{6,7},{7,6},{8,9},{9,8},{10,11... | collective-permute-start | bytes 2752520 | tf_op jit(solution)/shard_map/ppermute | solution.py:186
  83.7 3.6 %collective-permute-start.11 = (bf16[512,512]{1,0:T(8,128)(2,1)S(1)}, bf16[512,512]{1,0:T(8,128)(2,1)S(1)}, u32[]{:S(2)}, u32[]{:S(2)}) collective-permute-start(bf16[512,512]{1,0:T(8,128)(2,1)S(1)} %bitcast.24), channel_id=1, source_target_pairs={{0,1},{1,0},{2,3},{3,2},{4,5},{5,4},{6,7},{7,6},{8,9},{9,8},{10,11... | collective-permute-start | bytes 1572872 | tf_op jit(solution)/shard_map/ppermute | solution.py:186
  116.8 18.4 %copy-start = (bf16[1,1792,512]{2,1,0:T(8,128)(2,1)S(1)}, bf16[1,1792,512]{2,1,0:T(8,128)(2,1)}, u32[]{:S(2)}) copy-start(bf16[1,1792,512]{2,1,0:T(8,128)(2,1)} %weight_ref.3) | copy-start | bytes 5505028
  132.2 5.2 %collective-permute-start.14 = (bf16[512,896]{1,0:T(8,128)(2,1)S(1)}, bf16[512,896]{1,0:T(8,128)(2,1)S(1)}, u32[]{:S(2)}, u32[]{:S(2)}) collective-permute-start(bf16[512,896]{1,0:T(8,128)(2,1)S(1)} %bitcast.22), channel_id=1, source_target_pairs={{0,1},{1,0},{2,3},{3,2},{4,5},{5,4},{6,7},{7,6},{8,9},{9,8},{10,11... | collective-permute-start | bytes 2752520 | tf_op jit(solution)/shard_map/ppermute | solution.py:186

commit v11 on v10

--- a/solution.py
+++ b/solution.py
@@ -217,10 +217,11 @@
             o_ref[i, k * rows:(k + 1) * rows] = block[...]
 
 
-def project_kernel(near_ref, far_ref, own_ref, pair_a_ref, pair_b_ref, *o_refs):
+def project_kernel(pairs, left_ref, own_ref, pair_a_ref, pair_b_ref, *refs):
+    near_refs, o_refs = (refs[:pairs], refs[pairs:]) if len(refs) == 2 * pairs else ((), refs[:pairs])
     core, low = lax.axis_index("core"), lax.axis_index("rl")
-    pairs, group = len(o_refs), o_refs[0].shape[1]
-    slots = near_ref.shape[0] // (2 * pairs * (group // 4))
+    group = left_ref.shape[0] // (2 * pairs)
+    slots = 4
     rows = pairs * group
     cut = pair_a_ref.shape[0]
     to = lax.broadcasted_iota(jnp.int32, (rows, 2 * rows), 0)
@@ -229,12 +230,15 @@
     first = ((to % group) // slots) * (2 * slots * pairs) + block * (2 * slots) + (to % slots) * 2
     pick_own = (source == first + low).astype(jnp.bfloat16)
     pick_pair = (source == first + 1 - low).astype(jnp.bfloat16)
-    for left_ref, place in ((near_ref, core), (far_ref, 1 - core)):
-        part = matmul(matmul(pick_own, left_ref[...]).astype(jnp.bfloat16), own_ref[0])
-        theirs = matmul(pick_pair, left_ref[...]).astype(jnp.bfloat16)
-        part = part + matmul(theirs[:, :cut], pair_a_ref[...]) + matmul(theirs[:, cut:], pair_b_ref[...])
-        for k in range(pairs):
-            o_refs[k][place] = part[k * group:(k + 1) * group].astype(jnp.bfloat16)
+    part = matmul(matmul(pick_own, left_ref[...]).astype(jnp.bfloat16), own_ref[0])
+    theirs = matmul(pick_pair, left_ref[...]).astype(jnp.bfloat16)
+    part = (part + matmul(theirs[:, :cut], pair_a_ref[...]) + matmul(theirs[:, cut:], pair_b_ref[...])).astype(jnp.bfloat16)
+    for k in range(pairs):
+        if near_refs:
+            o_refs[k][core] = near_refs[k][...]
+            o_refs[k][1 - core] = part[k * group:(k + 1) * group]
+        else:
+            o_refs[k][...] = part[k * group:(k + 1) * group]
 
 
 def stream_kernel(*refs):
@@ -344,8 +348,12 @@
     blocks = [to_ffn(block, k) for k, block in enumerate(blocks)]
     fanned = call(fan_kernel, "fan", jax.ShapeDtypeStruct((chips, pairs * 2 * slots, heads), bf16), in_specs=[WHOLE] * pairs + [HELD, HELD], out_specs=WHOLE)(*blocks, pair_a, gain_theirs)
     near = exchange(fanned, CHIPS).reshape(chips * pairs * 2 * slots, heads)
+    near_parts = call(functools.partial(project_kernel, pairs), "project_near", [jax.ShapeDtypeStruct((group // 2, width), bf16)] * pairs + [jax.ShapeDtypeStruct(near.shape, bf16)], in_specs=[WHOLE] * 4, out_specs=[WHOLE] * pairs + [HELD],
+        input_output_aliases={0: pairs})(near, out_weight, pair_a, pair_b)
+    *near_parts, near = near_parts
     far = flip(near, "core")
-    own, *parts = call(project_kernel, "project", [jax.ShapeDtypeStruct((2, group // 2, width), bf16)] * pairs, in_specs=[WHOLE] * 5, out_specs=[WHOLE] * pairs)(near, far, out_weight, pair_a, pair_b)
+    own, *parts = call(functools.partial(project_kernel, pairs), "project", [jax.ShapeDtypeStruct((2, group // 2, width), bf16)] * pairs, in_specs=[WHOLE] * (4 + pairs), out_specs=[WHOLE] * pairs)(
+        far, out_weight, pair_a, pair_b, *near_parts)
     parts = [own] + [turn(part, k + 1) for k, part in enumerate(parts)]
     parts = [part.reshape(group, width) for part in parts]
     stream, copies = call(stream_kernel, "stream", (jax.ShapeDtypeStruct((group, width), jnp.float32), jax.ShapeDtypeStruct((rows, group, width), bf16)), in_specs=[WHOLE] * (pairs + 2), out_specs=(WHOLE, WHOLE))(

time: 175 us -> 171 us (0.977)
  blocking collectives: 90.2 us -> 80.1 us
  waiting for transfers between devices: 24.3 us -> 26.9 us
  starting transfers between devices: 37.7 us -> 40.1 us
    all_to_all x5 -> x4, blocking collectives: 90.2 us -> 80.1 us  [exchange(): return lax.all_to_all(value, axes, split_axis=0, concat_axis=0, tiled=True)]
    all_to_all x1 -> x2, starting transfers between devices: 7.33 us -> 11.2 us  [exchange(): return lax.all_to_all(value, axes, split_axis=0, concat_axis=0, tiled=True)]
    all_to_all x1 -> x2, waiting for transfers between devices: 8.96 us -> 9.66 us  [exchange(): return lax.all_to_all(value, axes, split_axis=0, concat_axis=0, tiled=True)]
  transfers between devices with their start and end apart: 16 -> 17, of which waited for: 7 -> 10; matrix products, arithmetic and copies ran while one was open for 3% -> 3% of each run, Pallas kernels for 5% -> 5%
where the time goes in v11:
time: 171 us; the launch traced here: 170 us
  blocking collectives  80.1 us (47%)
  starting transfers between devices  40.1 us (23%)
  waiting for transfers between devices  26.9 us (16%)
  Pallas kernels  16.6 us (10%)
  local copies, waits for them, and re-layouts  6.3 us (4%)
    all_to_all x4, blocking collectives, exchange(): return lax.all_to_all(value, axes, split_axis=0, concat_axis=0, tiled=True)  80.1 us
    ppermute x4, starting transfers between devices, to_ffn(): lax.ppermute(value, ('side', 'rp'), [(i, count + (i + steps) % count) for...  13.3 us
    all_to_all x2, starting transfers between devices, exchange(): return lax.all_to_all(value, axes, split_axis=0, concat_axis=0, tiled=True)  11.2 us
    ppermute x8, waiting for transfers between devices, flip(): return lax.ppermute(value, axis, [(0, 1), (1, 0)])  10.9 us
    ppermute x8, starting transfers between devices, flip(): return lax.ppermute(value, axis, [(0, 1), (1, 0)])  10.9 us
    all_to_all x2, waiting for transfers between devices, exchange(): return lax.all_to_all(value, axes, split_axis=0, concat_axis=0, tiled=True)  9.66 us
    pallas_call x1, Pallas kernels, attention(): pl.pallas_call(attend_kernel, grid_spec=grid_spec, out_shape=[jax.ShapeDt...  6.94 us
    ppermute x3, waiting for transfers between devices, turn(): lax.ppermute(value, 'rp', [(i, (i + steps) % count) for i in range(count)])  5.24 us
  transfers between devices with their start and end apart: 17, of which 10 were waited for; matrix products, arithmetic and copies ran while one was open for 3% of the time, Pallas kernels for 5%

profile of v11, /device:TPU:33, one launch (start us, length us, event | category | flops | bytes accessed | tf_op | source)
XLA Modules:
  0.0 170.2 jit_solution(14613084959499077709)
XLA Ops:
  0.0 1.2 slice_bitcast_fusion
  1.2 0.1 collective-permute-start.4
  1.3 2.5 %collective-permute-start.5 = (bf16[512]{0:T(512)(128)(2,1)}, bf16[512]{0:T(512)(128)(2,1)S(1)}, u32[]{:S(2)}, u32[]{:S(2)}) collective-permute-start(bf16[512]{0:T(512)(128)(2,1)} %param.17), channel_id=1, source_target_pairs={{0,1},{1,0},{2,3},{3,2},{4,5},{5,4},{6,7},{7,6},{8,9},{9,8},{10,11... | collective-permute-start | bytes 3080 | tf_op jit(solution)/shard_map/ppermute | solution.py:186
  3.8 6.9 %attend.1 = (bf16[8,1024]{1,0:T(8,128)(2,1)}, bf16[8,1024]{1,0:T(8,128)(2,1)}, bf16[8,1024]{1,0:T(8,128)(2,1)}, bf16[8,1024]{1,0:T(8,128)(2,1)}) custom-call(s32[4]{0:T(128)} %len_ref.1, bf16[4,8192]{1,0:T(4,128)(2,1)} %q_ref.1, bf16[4,2048]{1,0:T(4,128)(2,1)} %new_ref.1, bf16[1,4,256,1024]{3,2,1,0:T(8,128)(2,1)} %k_hi_ref.1, ...), custom_call_target="tpu_custom_call" | custom-call | tf_op jit(solution)/shard_map/attend/pallas_call | solution.py:178
  10.7 0.0 copy-start
  10.7 3.2 %collective-permute-start = (bf16[8,1024]{1,0:T(8,128)(2,1)}, bf16[8,1024]{1,0:T(8,128)(2,1)S(1)}, u32[]{:S(2)}, u32[]{:S(2)}) collective-permute-start(bf16[8,1024]{1,0:T(8,128)(2,1)} %get-tuple-element.20), channel_id=1, source_target_pairs={{0,128},{32,160},{64,192},{96,224},{1,129},{33,161},{65,193},{97,2... | collective-permute-start | bytes 49160 | tf_op jit(solution)/shard_map/ppermute | solution.py:196
  13.9 4.1 %collective-permute-start.1 = (bf16[8,1024]{1,0:T(8,128)(2,1)}, bf16[8,1024]{1,0:T(8,128)(2,1)S(1)}, u32[]{:S(2)}, u32[]{:S(2)}) collective-permute-start(bf16[8,1024]{1,0:T(8,128)(2,1)} %get-tuple-element.21), channel_id=1, source_target_pairs={{0,160},{32,192},{64,224},{96,128},{1,161},{33,193},{65,225},{97,1... | collective-permute-start | bytes 49160 | tf_op jit(solution)/shard_map/ppermute | solution.py:196
  18.1 4.7 %collective-permute-start.2 = (bf16[8,1024]{1,0:T(8,128)(2,1)}, bf16[8,1024]{1,0:T(8,128)(2,1)S(1)}, u32[]{:S(2)}, u32[]{:S(2)}) collective-permute-start(bf16[8,1024]{1,0:T(8,128)(2,1)} %get-tuple-element.22), channel_id=1, source_target_pairs={{0,192},{32,224},{64,128},{96,160},{1,193},{33,225},{65,129},{97,1... | collective-permute-start | bytes 49160 | tf_op jit(solution)/shard_map/ppermute | solution.py:196
  22.8 0.0 collective-permute-done.5.refs_5_
  22.8 1.3 collective-permute-start.3
  24.1 0.0 collective-permute-done.refs_0_
  24.1 0.0 collective-permute-done.1.refs_1_
  24.1 0.0 collective-permute-done.2.refs_2_
  24.1 1.0 collective-permute-done.3.refs_3_
  25.2 0.0 collective-permute-done.4.refs_4_.pair_a_ref
  25.2 0.8 fan.1
  26.0 4.8 %all-to-all-start = ((bf16[8,32,1024]{2,1,0:T(8,128)(2,1)}), bf16[8,32,1024]{2,1,0:T(8,128)(2,1)S(1)}, u32[]{:S(2)}, u32[]{:S(2)}) async-start(bf16[8,32,1024]{2,1,0:T(8,128)(2,1)} %fan.1), calls=%async_computation | async-start | bytes 1048576 | tf_op jit(solution)/shard_map/all_to_all | solution.py:200
  30.8 0.0 copy-done
  30.8 0.7 collective-permute-start.6
  31.5 7.8 %collective-permute-done.6.pair_b_ref = bf16[320,512]{1,0:T(8,128)(2,1)S(1)} collective-permute-done((bf16[320,512]{1,0:T(8,128)(2,1)S(1)}, bf16[320,512]{1,0:T(8,128)(2,1)S(1)}, u32[]{:S(2)}, u32[]{:S(2)}) %collective-permute-start.6) | collective-permute-done | bytes 327712 | tf_op jit(solution)/shard_map/ppermute | solution.py:186
  39.3 0.5 all-to-all-done
  39.8 0.7 project_near.1
  40.5 0.0 copy-start.3
  40.5 0.0 copy-start.2
  40.5 1.6 collective-permute-start.7
  42.1 1.5 collective-permute-done.7.left_ref
  43.6 0.7 project.1
  44.3 1.1 collective-permute-start.8
  45.4 1.3 collective-permute-start.9
  46.7 2.2 %collective-permute-start.10 = (bf16[2,32,512]{2,1,0:T(8,128)(2,1)S(1)}, bf16[2,32,512]{2,1,0:T(8,128)(2,1)S(1)}, u32[]{:S(2)}, u32[]{:S(2)}) collective-permute-start(bf16[2,32,512]{2,1,0:T(8,128)(2,1)S(1)} %get-tuple-element.32), channel_id=1, source_target_pairs={{0,96},{32,0},{64,32},{96,64},{1,97},{33,1},{65,33},{97,65},{2,98}... | collective-permute-start | bytes 196616 | tf_op jit(solution)/shard_map/ppermute | solution.py:191
  49.0 0.0 copy-done.3
  49.0 1.6 collective-permute-done.8
  50.6 3.1 %collective-permute-done.9 = bf16[2,32,512]{2,1,0:T(8,128)(2,1)S(1)} collective-permute-done((bf16[2,32,512]{2,1,0:T(8,128)(2,1)S(1)}, bf16[2,32,512]{2,1,0:T(8,128)(2,1)S(1)}, u32[]{:S(2)}, u32[]{:S(2)}) %collective-permute-start.9) | collective-permute-done | bytes 65568 | tf_op jit(solution)/shard_map/ppermute | solution.py:191
  53.8 0.4 collective-permute-done.10
  54.2 0.0 copy-done.2
  54.2 1.0 stream.1
  55.2 6.4 %all-to-all-start.1 = ((bf16[8,64,512]{2,1,0:T(8,128)(2,1)}), bf16[8,64,512]{2,1,0:T(8,128)(2,1)S(1)}, u32[]{:S(2)}, u32[]{:S(2)}) async-start(bf16[8,64,512]{2,1,0:T(8,128)(2,1)} %get-tuple-element.33), calls=%async_computation.1 | async-start | bytes 1048576 | tf_op jit(solution)/shard_map/all_to_all | solution.py:200
  61.6 2.6 %dynamic-slice_bitcast_fusion.1 = (bf16[512,896]{1,0:T(8,128)(2,1)S(1)}, bf16[512,896]{1,0:T(8,128)(2,1)}) fusion(bf16[1,512,1792]{2,1,0:T(8,128)(2,1)} %param.19, s32[]{:T(128)S(6)} %select_n.9, s32[]{:T(128)S(6)} %select_n.8), kind=kLoop, calls=%fused_computation.1 | loop fusion | bytes 3670024 | tf_op jit(solution)/shard_map/dynamic_slice | solution.py:345
  64.2 1.1 collective-permute-start.12
  65.2 2.5 %dynamic-slice_bitcast_fusion = (bf16[512,896]{1,0:T(8,128)(2,1)S(1)}, bf16[512,896]{1,0:T(8,128)(2,1)}) fusion(bf16[1,512,1792]{2,1,0:T(8,128)(2,1)} %param.20, s32[]{:T(128)S(6)} %select_n.9, s32[]{:T(128)S(6)} %select_n.8), kind=kLoop, calls=%fused_computation | loop fusion | bytes 3670024 | tf_op jit(solution)/shard_map/dynamic_slice | solution.py:346
  67.8 0.0 collective-permute-start.13
  67.8 9.2 %all-to-all-done.1 = bf16[8,64,512]{2,1,0:T(8,128)(2,1)S(1)} async-done(((bf16[8,64,512]{2,1,0:T(8,128)(2,1)}), bf16[8,64,512]{2,1,0:T(8,128)(2,1)S(1)}, u32[]{:S(2)}, u32[]{:S(2)}) %all-to-all-start.1) | async-done | bytes 524320 | tf_op jit(solution)/shard_map/all_to_all | solution.py:200
  76.9 1.9 %collective-permute-start.11 = (bf16[512,512]{1,0:T(8,128)(2,1)S(1)}, bf16[512,512]{1,0:T(8,128)(2,1)S(1)}, u32[]{:S(2)}, u32[]{:S(2)}) collective-permute-start(bf16[512,512]{1,0:T(8,128)(2,1)S(1)} %bitcast.24), channel_id=1, source_target_pairs={{0,1},{1,0},{2,3},{3,2},{4,5},{5,4},{6,7},{7,6},{8,9},{9,8},{10,11... | collective-permute-start | bytes 1572872 | tf_op jit(solution)/shard_map/ppermute | solution.py:186
  78.9 1.3 gate_up_own.1.rest_0_
  80.2 0.0 collective-permute-done.12.gate_ref
  80.2 0.0 collective-permute-done.13.up_ref
  80.2 0.3 collective-permute-done.11.x_ref
  80.4 2.5 %gate_up.1 = bf16[512,1920]{1,0:T(8,128)(2,1)S(1)} custom-call(bf16[512,512]{1,0:T(8,128)(2,1)S(1)} %collective-permute-done.11.x_ref, bf16[1,512]{1,0:T(2,128)(2,1)S(1)} %broadcast_in_dim.7.gain_ref, bf16[512,896]{1,0:T(8,128)(2,1)S(1)} %collective-permute-done.12.gate_ref, bf16[512,896]{1,0:T(8,128)(2,1)} %collective-permute-done.13.up_ref, ...), custom_call_target="tpu_custom_call" | custom-call | tf_op jit(solution)/shard_map/gate_up/pallas_call | solution.py:365
  82.9 29.2 %all_to_all.30.parts_ref = bf16[8,64,1920]{2,1,0:T(8,128)(2,1)S(1)} all-to-all(bf16[8,64,1920]{2,1,0:T(8,128)(2,1)S(1)} %bitcast.21), channel_id=1, replica_groups=mesh['side'=2,'rp'=4,'rl'=2,'x'=4,'yl'=2,'core'=2] {'x','yl'}, dimensions={0} | all-to-all | bytes 3932160 | tf_op jit(solution)/shard_map/all_to_all | solution.py:200
  112.1 0.0 copy-start.1
  112.1 0.6 hidden.1
  112.7 14.8 %all_to_all.31 = bf16[8,64,896]{2,1,0:T(8,128)(2,1)S(1)} all-to-all(bf16[8,64,896]{2,1,0:T(8,128)(2,1)S(1)} %hidden.1), channel_id=1, replica_groups=mesh['side'=2,'rp'=4,'rl'=2,'x'=4,'yl'=2,'core'=2] {'x','yl'}, dimensions={0} | all-to-all | bytes 1835008 | tf_op jit(solution)/shard_map/all_to_all | solution.py:200
  127.5 3.1 %collective-permute-start.14 = (bf16[512,896]{1,0:T(8,128)(2,1)S(1)}, bf16[512,896]{1,0:T(8,128)(2,1)S(1)}, u32[]{:S(2)}, u32[]{:S(2)}) collective-permute-start(bf16[512,896]{1,0:T(8,128)(2,1)S(1)} %bitcast.22), channel_id=1, source_target_pairs={{0,1},{1,0},{2,3},{3,2},{4,5},{5,4},{6,7},{7,6},{8,9},{9,8},{10,11... | collective-permute-start | bytes 2752520 | tf_op jit(solution)/shard_map/ppermute | solution.py:186
  130.5 0.0 copy-done.1
  130.5 0.7 down_own.1.rest_0_
  131.2 1.4 collective-permute-done.14.x_ref
  132.6 0.7 down.1
  133.3 17.3 %all_to_all.32.parts_ref = bf16[8,64,512]{2,1,0:T(8,128)(2,1)S(1)} all-to-all(bf16[8,64,512]{2,1,0:T(8,128)(2,1)S(1)} %bitcast.27), channel_id=1, replica_groups=mesh['side'=2,'rp'=4,'rl'=2,'x'=4,'yl'=2,'core'=2] {'rl','rp'}, dimensions={0} | all-to-all | bytes 1048576 | tf_op jit(solution)/shard_map/all_to_all | solution.py:200
  150.7 0.1 final.1
  150.8 18.8 %all_to_all.33.back_ref = bf16[32,4,512]{2,1,0:T(4,128)(2,1)S(1)} all-to-all(bf16[32,4,512]{2,1,0:T(4,128)(2,1)S(1)} %final.1), channel_id=1, replica_groups=mesh['side'=2,'rp'=4,'rl'=2,'x'=4,'yl'=2,'core'=2] {'side','core','x','yl'}, dimensions={0} | all-to-all | bytes 262144 | tf_op jit(solution)/shard_map/all_to_all | solution.py:200
  169.6 0.6 output.1
  (3 shorter events, 0.0 us)
Async XLA Ops:
  1.2 24.0 %collective-permute-start.4 = (bf16[704,512]{1,0:T(8,128)(2,1)S(1)}, bf16[704,512]{1,0:T(8,128)(2,1)S(1)}, u32[]{:S(2)}, u32[]{:S(2)}) collective-permute-start(bf16[704,512]{1,0:T(8,128)(2,1)S(1)} %slice_bitcast_fusion), channel_id=1, source_target_pairs={{0,16},{16,0},{1,17},{17,1},{2,18},{18,2},{3,19},{19,3},{4,20},{20... | collective-permute-start | bytes 2162696 | tf_op jit(solution)/shard_map/ppermute | solution.py:186
  1.3 21.5 %collective-permute-start.5 = (bf16[512]{0:T(512)(128)(2,1)}, bf16[512]{0:T(512)(128)(2,1)S(1)}, u32[]{:S(2)}, u32[]{:S(2)}) collective-permute-start(bf16[512]{0:T(512)(128)(2,1)} %param.17), channel_id=1, source_target_pairs={{0,1},{1,0},{2,3},{3,2},{4,5},{5,4},{6,7},{7,6},{8,9},{9,8},{10,11... | collective-permute-start | bytes 3080 | tf_op jit(solution)/shard_map/ppermute | solution.py:186
  10.7 20.1 %copy-start = (bf16[1,1024,512]{2,1,0:T(8,128)(2,1)S(1)}, bf16[1,1024,512]{2,1,0:T(8,128)(2,1)}, u32[]{:S(2)}) copy-start(bf16[1,1024,512]{2,1,0:T(8,128)(2,1)} %own_ref.3) | copy-start | bytes 3145732
  10.7 13.4 %collective-permute-start = (bf16[8,1024]{1,0:T(8,128)(2,1)}, bf16[8,1024]{1,0:T(8,128)(2,1)S(1)}, u32[]{:S(2)}, u32[]{:S(2)}) collective-permute-start(bf16[8,1024]{1,0:T(8,128)(2,1)} %get-tuple-element.20), channel_id=1, source_target_pairs={{0,128},{32,160},{64,192},{96,224},{1,129},{33,161},{65,193},{97,2... | collective-permute-start | bytes 49160 | tf_op jit(solution)/shard_map/ppermute | solution.py:196
  13.9 10.2 %collective-permute-start.1 = (bf16[8,1024]{1,0:T(8,128)(2,1)}, bf16[8,1024]{1,0:T(8,128)(2,1)S(1)}, u32[]{:S(2)}, u32[]{:S(2)}) collective-permute-start(bf16[8,1024]{1,0:T(8,128)(2,1)} %get-tuple-element.21), channel_id=1, source_target_pairs={{0,160},{32,192},{64,224},{96,128},{1,161},{33,193},{65,225},{97,1... | collective-permute-start | bytes 49160 | tf_op jit(solution)/shard_map/ppermute | solution.py:196
  18.1 6.0 %collective-permute-start.2 = (bf16[8,1024]{1,0:T(8,128)(2,1)}, bf16[8,1024]{1,0:T(8,128)(2,1)S(1)}, u32[]{:S(2)}, u32[]{:S(2)}) collective-permute-start(bf16[8,1024]{1,0:T(8,128)(2,1)} %get-tuple-element.22), channel_id=1, source_target_pairs={{0,192},{32,224},{64,128},{96,160},{1,193},{33,225},{65,129},{97,1... | collective-permute-start | bytes 49160 | tf_op jit(solution)/shard_map/ppermute | solution.py:196
  22.8 2.4 %collective-permute-start.3 = (bf16[8,1024]{1,0:T(8,128)(2,1)}, bf16[8,1024]{1,0:T(8,128)(2,1)S(1)}, u32[]{:S(2)}, u32[]{:S(2)}) collective-permute-start(bf16[8,1024]{1,0:T(8,128)(2,1)} %get-tuple-element.23), channel_id=1, source_target_pairs={{0,224},{32,128},{64,160},{96,192},{1,225},{33,129},{65,161},{97,1... | collective-permute-start | bytes 49160 | tf_op jit(solution)/shard_map/ppermute | solution.py:196
  26.0 13.8 %all-to-all-start = ((bf16[8,32,1024]{2,1,0:T(8,128)(2,1)}), bf16[8,32,1024]{2,1,0:T(8,128)(2,1)S(1)}, u32[]{:S(2)}, u32[]{:S(2)}) async-start(bf16[8,32,1024]{2,1,0:T(8,128)(2,1)} %fan.1), calls=%async_computation | async-start | bytes 1048576 | tf_op jit(solution)/shard_map/all_to_all | solution.py:200
  30.8 8.4 %collective-permute-start.6 = (bf16[320,512]{1,0:T(8,128)(2,1)S(1)}, bf16[320,512]{1,0:T(8,128)(2,1)S(1)}, u32[]{:S(2)}, u32[]{:S(2)}) collective-permute-start(bf16[320,512]{1,0:T(8,128)(2,1)S(1)} %slice_bitcast_fusion.1), channel_id=1, source_target_pairs={{0,16},{16,0},{1,17},{17,1},{2,18},{18,2},{3,19},{19,3},{4,20},{20... | collective-permute-start | bytes 983048 | tf_op jit(solution)/shard_map/ppermute | solution.py:186
  40.5 8.5 %copy-start.3 = (bf16[512]{0:T(512)(128)(2,1)S(1)}, bf16[512]{0:T(512)(128)(2,1)}, u32[]{:S(2)}) copy-start(bf16[512]{0:T(512)(128)(2,1)} %param.17) | copy-start | bytes 3076
  40.5 13.7 %copy-start.2 = (bf16[512,512]{1,0:T(8,128)(2,1)S(1)}, bf16[512,512]{1,0:T(8,128)(2,1)}, u32[]{:S(2)}) copy-start(bf16[512,512]{1,0:T(8,128)(2,1)} %refs_4_.1) | copy-start | bytes 1572868
  40.5 3.1 %collective-permute-start.7 = (bf16[256,1024]{1,0:T(8,128)(2,1)S(1)}, bf16[256,1024]{1,0:T(8,128)(2,1)S(1)}, u32[]{:S(2)}, u32[]{:S(2)}) collective-permute-start(bf16[256,1024]{1,0:T(8,128)(2,1)S(1)} %get-tuple-element.24), channel_id=1, source_target_pairs={{0,1},{1,0},{2,3},{3,2},{4,5},{5,4},{6,7},{7,6},{8,9},{9,8},{10,11... | collective-permute-start | bytes 1572872 | tf_op jit(solution)/shard_map/ppermute | solution.py:186
  44.3 6.3 %collective-permute-start.8 = (bf16[2,32,512]{2,1,0:T(8,128)(2,1)S(1)}, bf16[2,32,512]{2,1,0:T(8,128)(2,1)S(1)}, u32[]{:S(2)}, u32[]{:S(2)}) collective-permute-start(bf16[2,32,512]{2,1,0:T(8,128)(2,1)S(1)} %get-tuple-element.30), channel_id=1, source_target_pairs={{0,32},{32,64},{64,96},{96,0},{1,33},{33,65},{65,97},{97,1},{2,34}... | collective-permute-start | bytes 196616 | tf_op jit(solution)/shard_map/ppermute | solution.py:191
  45.4 8.4 %collective-permute-start.9 = (bf16[2,32,512]{2,1,0:T(8,128)(2,1)S(1)}, bf16[2,32,512]{2,1,0:T(8,128)(2,1)S(1)}, u32[]{:S(2)}, u32[]{:S(2)}) collective-permute-start(bf16[2,32,512]{2,1,0:T(8,128)(2,1)S(1)} %get-tuple-element.31), channel_id=1, source_target_pairs={{0,64},{32,96},{64,0},{96,32},{1,65},{33,97},{65,1},{97,33},{2,66}... | collective-permute-start | bytes 196616 | tf_op jit(solution)/shard_map/ppermute | solution.py:191
  46.7 7.5 %collective-permute-start.10 = (bf16[2,32,512]{2,1,0:T(8,128)(2,1)S(1)}, bf16[2,32,512]{2,1,0:T(8,128)(2,1)S(1)}, u32[]{:S(2)}, u32[]{:S(2)}) collective-permute-start(bf16[2,32,512]{2,1,0:T(8,128)(2,1)S(1)} %get-tuple-element.32), channel_id=1, source_target_pairs={{0,96},{32,0},{64,32},{96,64},{1,97},{33,1},{65,33},{97,65},{2,98}... | collective-permute-start | bytes 196616 | tf_op jit(solution)/shard_map/ppermute | solution.py:191
  55.2 21.7 %all-to-all-start.1 = ((bf16[8,64,512]{2,1,0:T(8,128)(2,1)}), bf16[8,64,512]{2,1,0:T(8,128)(2,1)S(1)}, u32[]{:S(2)}, u32[]{:S(2)}) async-start(bf16[8,64,512]{2,1,0:T(8,128)(2,1)} %get-tuple-element.33), calls=%async_computation.1 | async-start | bytes 1048576 | tf_op jit(solution)/shard_map/all_to_all | solution.py:200
  64.2 16.0 %collective-permute-start.12 = (bf16[512,896]{1,0:T(8,128)(2,1)}, bf16[512,896]{1,0:T(8,128)(2,1)S(1)}, u32[]{:S(2)}, u32[]{:S(2)}) collective-permute-start(bf16[512,896]{1,0:T(8,128)(2,1)} %get-tuple-element.38), channel_id=1, source_target_pairs={{0,1},{1,0},{2,3},{3,2},{4,5},{5,4},{6,7},{7,6},{8,9},{9,8},{10,11... | collective-permute-start | bytes 2752520 | tf_op jit(solution)/shard_map/ppermute | solution.py:186
  67.8 12.4 %collective-permute-start.13 = (bf16[512,896]{1,0:T(8,128)(2,1)}, bf16[512,896]{1,0:T(8,128)(2,1)}, u32[]{:S(2)}, u32[]{:S(2)}) collective-permute-start(bf16[512,896]{1,0:T(8,128)(2,1)} %get-tuple-element.36), channel_id=1, source_target_pairs={{0,1},{1,0},{2,3},{3,2},{4,5},{5,4},{6,7},{7,6},{8,9},{9,8},{10,11... | collective-permute-start | bytes 2752520 | tf_op jit(solution)/shard_map/ppermute | solution.py:186
  76.9 3.5 %collective-permute-start.11 = (bf16[512,512]{1,0:T(8,128)(2,1)S(1)}, bf16[512,512]{1,0:T(8,128)(2,1)S(1)}, u32[]{:S(2)}, u32[]{:S(2)}) collective-permute-start(bf16[512,512]{1,0:T(8,128)(2,1)S(1)} %bitcast.24), channel_id=1, source_target_pairs={{0,1},{1,0},{2,3},{3,2},{4,5},{5,4},{6,7},{7,6},{8,9},{9,8},{10,11... | collective-permute-start | bytes 1572872 | tf_op jit(solution)/shard_map/ppermute | solution.py:186
  112.1 18.4 %copy-start.1 = (bf16[1,1792,512]{2,1,0:T(8,128)(2,1)S(1)}, bf16[1,1792,512]{2,1,0:T(8,128)(2,1)}, u32[]{:S(2)}) copy-start(bf16[1,1792,512]{2,1,0:T(8,128)(2,1)} %weight_ref.3) | copy-start | bytes 5505028
  127.5 5.2 %collective-permute-start.14 = (bf16[512,896]{1,0:T(8,128)(2,1)S(1)}, bf16[512,896]{1,0:T(8,128)(2,1)S(1)}, u32[]{:S(2)}, u32[]{:S(2)}) collective-permute-start(bf16[512,896]{1,0:T(8,128)(2,1)S(1)} %bitcast.22), channel_id=1, source_target_pairs={{0,1},{1,0},{2,3},{3,2},{4,5},{5,4},{6,7},{7,6},{8,9},{9,8},{10,11... | collective-permute-start | bytes 2752520 | tf_op jit(solution)/shard_map/ppermute | solution.py:186

commit v12 on v11

--- a/solution.py
+++ b/solution.py
@@ -32,7 +32,7 @@
 
 
 def attend_kernel(len_ref, q_ref, new_ref, k_lo_ref, k_hi_ref, v_lo_ref, v_hi_ref, *rest):
-    o_refs, (q_all, new_all, s_all, acc, out_all, fine_all, coarse_all, at_all) = rest[:-8], rest[-8:]
+    o_ref, q_all, new_all, s_all, acc, out_all, fine_all, coarse_all, at_all = rest
     slot = pl.program_id(0)
     slots = q_ref.shape[0]
     length = len_ref[slot]
@@ -140,7 +140,7 @@
         acc[...] += mix(v_hi_ref, w16[:, half:])
 
     out = acc[...] / total
-    pairs = len(o_refs)
+    pairs = o_ref.shape[0]
     per_row = H // (2 * pairs)
     for h in range(H):
         at, q_at = h // per_row, h % per_row
@@ -149,8 +149,7 @@
     @pl.when(slot == slots - 1)
     def _():
         for k in range(pairs):
-            home = lax.rem(lax.axis_index("rp") + k, pairs)
-            o_refs[k][...] = jnp.concatenate([out_all[home, j] for j in range(slots)], axis=0).astype(jnp.bfloat16)
+            o_ref[k] = jnp.concatenate([out_all[k, j] for j in range(slots)], axis=0).astype(jnp.bfloat16)
 
 
 def attention(queries, new_entries, cache_keys, cache_values, lengths, pairs):
@@ -170,14 +169,14 @@
     grid_spec = pltpu.PrefetchScalarGridSpec(
         num_scalar_prefetch=1, grid=(slots,),
         in_specs=[pl.BlockSpec((slots, H * HD), lambda s, n: (0, 0)), pl.BlockSpec((slots, 2 * width), lambda s, n: (0, 0)), low, high, low, high],
-        out_specs=[pl.BlockSpec((2 * slots, heads), lambda s, n: (0, 0))] * pairs,
+        out_specs=pl.BlockSpec((pairs, 2 * slots, heads), lambda s, n: (0, 0, 0)),
         scratch_shapes=[
             pltpu.VMEM((slots, H, HD), jnp.float32), pltpu.VMEM((slots, 2 * KVH, HD), jnp.float32),
             pltpu.VMEM((H, 2 * half), jnp.float32), pltpu.VMEM((H, HD), jnp.float32), pltpu.VMEM((pairs, slots, 2, heads), jnp.float32),
             pltpu.VMEM((slots, 2, 16, HD), jnp.float32), pltpu.VMEM((slots, 2, 2 * half // 16, HD), jnp.float32), pltpu.VMEM((slots, 2, 8, HD), jnp.float32)])
     return pl.pallas_call(
         attend_kernel, grid_spec=grid_spec,
-        out_shape=[jax.ShapeDtypeStruct((2 * slots, heads), jnp.bfloat16)] * pairs,
+        out_shape=jax.ShapeDtypeStruct((pairs, 2 * slots, heads), jnp.bfloat16),
         compiler_params=pltpu.CompilerParams(vmem_limit_bytes=60 << 20), name="attend",
     )(lengths, queries, new_entries, cache_keys, cache_keys, cache_values, cache_values)
 
@@ -209,12 +208,11 @@
     return pl.pallas_call(kernel, out_shape=out_shape, name=name, compiler_params=pltpu.CompilerParams(vmem_limit_bytes=limit << 20), **options)
 
 
-def fan_kernel(*refs):
-    blocks, o_ref = refs[:-3], refs[-1]
-    rows = blocks[0].shape[0]
+def fan_kernel(block_ref, held_ref, also_held_ref, o_ref):
+    rows = block_ref.shape[1]
     for i in range(o_ref.shape[0]):
-        for k, block in enumerate(blocks):
-            o_ref[i, k * rows:(k + 1) * rows] = block[...]
+        for k in range(block_ref.shape[0]):
+            o_ref[i, k * rows:(k + 1) * rows] = block_ref[k]
 
 
 def project_kernel(pairs, left_ref, own_ref, pair_a_ref, pair_b_ref, *refs):
@@ -226,7 +224,7 @@
     cut = pair_a_ref.shape[0]
     to = lax.broadcasted_iota(jnp.int32, (rows, 2 * rows), 0)
     source = lax.broadcasted_iota(jnp.int32, (rows, 2 * rows), 1)
-    block = (pairs - to // group) % pairs
+    block = (lax.axis_index("rp") + to // group) % pairs
     first = ((to % group) // slots) * (2 * slots * pairs) + block * (2 * slots) + (to % slots) * 2
     pick_own = (source == first + low).astype(jnp.bfloat16)
     pick_pair = (source == first + 1 - low).astype(jnp.bfloat16)
@@ -345,8 +343,8 @@
     gate_mine = lax.dynamic_slice_in_dim(gate_weight[0], core * half, half, 1)
     up_mine = lax.dynamic_slice_in_dim(up_weight[0], core * half, half, 1)
     blocks = attention(queries, new_entries, cache_keys, cache_values, lengths, pairs)
-    blocks = [to_ffn(block, k) for k, block in enumerate(blocks)]
-    fanned = call(fan_kernel, "fan", jax.ShapeDtypeStruct((chips, pairs * 2 * slots, heads), bf16), in_specs=[WHOLE] * pairs + [HELD, HELD], out_specs=WHOLE)(*blocks, pair_a, gain_theirs)
+    blocks = exchange(lax.ppermute(blocks, "side", [(0, 1)]), "rp")
+    fanned = call(fan_kernel, "fan", jax.ShapeDtypeStruct((chips, pairs * 2 * slots, heads), bf16), in_specs=[WHOLE, HELD, HELD], out_specs=WHOLE)(blocks, pair_a, gain_theirs)
     near = exchange(fanned, CHIPS).reshape(chips * pairs * 2 * slots, heads)
     near_parts = call(functools.partial(project_kernel, pairs), "project_near", [jax.ShapeDtypeStruct((group // 2, width), bf16)] * pairs + [jax.ShapeDtypeStruct(near.shape, bf16)], in_specs=[WHOLE] * 4, out_specs=[WHOLE] * pairs + [HELD],
         input_output_aliases={0: pairs})(near, out_weight, pair_a, pair_b)

time: 171 us -> 173 us (1.012)
  starting transfers between devices: 40.1 us -> 43.5 us
  blocking collectives: 80.1 us -> 77.9 us
    ppermute x4 -> x1, starting transfers between devices: 13.3 us -> 5.57 us  [local(): blocks = exchange(lax.ppermute(blocks, 'side', [(0, 1)]), 'rp')]
    ppermute x8, starting transfers between devices: 10.9 us -> 17.1 us  [flip(): return lax.ppermute(value, axis, [(0, 1), (1, 0)])]
    all_to_all x2 -> x3, starting transfers between devices: 11.2 us -> 16.7 us  [exchange(): return lax.all_to_all(value, axes, split_axis=0, concat_axis=0, tiled=True)]
    all_to_all x4, blocking collectives: 80.1 us -> 77.9 us  [exchange(): return lax.all_to_all(value, axes, split_axis=0, concat_axis=0, tiled=True)]
    ppermute x8, waiting for transfers between devices: 10.9 us -> 9.08 us  [flip(): return lax.ppermute(value, axis, [(0, 1), (1, 0)])]
    all_to_all x2 -> x3, waiting for transfers between devices: 9.66 us -> 11.5 us  [exchange(): return lax.all_to_all(value, axes, split_axis=0, concat_axis=0, tiled=True)]
  transfers between devices with their start and end apart: 17 -> 15, of which waited for: 10 -> 12; matrix products, arithmetic and copies ran while one was open for 3% -> 3% of each run, Pallas kernels for 5% -> 5%
where the time goes in v12:
time: 173 us; the launch traced here: 172 us
  blocking collectives  77.9 us (45%)
  starting transfers between devices  43.5 us (25%)
  waiting for transfers between devices  27.8 us (16%)
  Pallas kernels  16.2 us (9%)
  local copies, waits for them, and re-layouts  6.31 us (4%)
    all_to_all x4, blocking collectives, exchange(): return lax.all_to_all(value, axes, split_axis=0, concat_axis=0, tiled=True)  77.9 us
    ppermute x8, starting transfers between devices, flip(): return lax.ppermute(value, axis, [(0, 1), (1, 0)])  17.1 us
    all_to_all x3, starting transfers between devices, exchange(): return lax.all_to_all(value, axes, split_axis=0, concat_axis=0, tiled=True)  16.7 us
    all_to_all x3, waiting for transfers between devices, exchange(): return lax.all_to_all(value, axes, split_axis=0, concat_axis=0, tiled=True)  11.5 us
    ppermute x8, waiting for transfers between devices, flip(): return lax.ppermute(value, axis, [(0, 1), (1, 0)])  9.08 us
    pallas_call x1, Pallas kernels, attention(): pl.pallas_call(attend_kernel, grid_spec=grid_spec, out_shape=jax.ShapeDty...  6.56 us
    ppermute x3, waiting for transfers between devices, turn(): lax.ppermute(value, 'rp', [(i, (i + steps) % count) for i in range(count)])  6.27 us
    ppermute x1, starting transfers between devices, local(): blocks = exchange(lax.ppermute(blocks, 'side', [(0, 1)]), 'rp')  5.57 us
  transfers between devices with their start and end apart: 15, of which 12 were waited for; matrix products, arithmetic and copies ran while one was open for 3% of the time, Pallas kernels for 5%

profile of v12, /device:TPU:33, one launch (start us, length us, event | category | flops | bytes accessed | tf_op | source)
XLA Modules:
  0.0 171.9 jit_solution(1023254069378055863)
XLA Ops:
  0.0 1.2 slice_bitcast_fusion
  1.2 0.0 copy-start.3
  1.2 0.1 collective-permute-start.1
  1.3 6.6 %attend.1 = bf16[4,8,1024]{2,1,0:T(8,128)(2,1)} custom-call(s32[4]{0:T(128)} %len_ref.1, bf16[4,8192]{1,0:T(4,128)(2,1)} %q_ref.1, bf16[4,2048]{1,0:T(4,128)(2,1)} %new_ref.1, bf16[1,4,256,1024]{3,2,1,0:T(8,128)(2,1)} %k_hi_ref.1, bf16[1,4,256,1024]{3,2,1,0:T(8,128)(2,1)} %k_hi_ref.1, bf16[1,4,256,1024]{3,2,1,0:T(8,128)(2,1)} %v_hi_ref.1, ...), custom_call_target="tpu_custom_call" | custom-call | tf_op jit(solution)/shard_map/attend/pallas_call | solution.py:177
  7.8 0.0 copy-start
  7.8 5.6 %collective-permute-start = (bf16[4,8,1024]{2,1,0:T(8,128)(2,1)}, bf16[4,8,1024]{2,1,0:T(8,128)(2,1)}, u32[]{:S(2)}, u32[]{:S(2)}) collective-permute-start(bf16[4,8,1024]{2,1,0:T(8,128)(2,1)} %attend.1), channel_id=1, source_target_pairs={{0,128},{1,129},{2,130},{3,131},{4,132},{5,133},{6,134},{7,135},{8... | collective-permute-start | bytes 196616 | tf_op jit(solution)/shard_map/ppermute | solution.py:346
  13.4 1.0 collective-permute-done
  14.4 8.5 %all-to-all-start = ((bf16[4,8,1024]{2,1,0:T(8,128)(2,1)}), bf16[4,8,1024]{2,1,0:T(8,128)(2,1)S(1)}, u32[]{:S(2)}, u32[]{:S(2)}) async-start(bf16[4,8,1024]{2,1,0:T(8,128)(2,1)} %collective-permute-done), calls=%async_computation | async-start | bytes 131072 | tf_op jit(solution)/shard_map/all_to_all | solution.py:199
  22.9 0.0 copy-done.3
  22.9 2.1 %collective-permute-start.2 = (bf16[512]{0:T(512)(128)(2,1)S(1)}, bf16[512]{0:T(512)(128)(2,1)S(1)}, u32[]{:S(2)}, u32[]{:S(2)}) collective-permute-start(bf16[512]{0:T(512)(128)(2,1)S(1)} %copy-done.3), channel_id=1, source_target_pairs={{0,1},{1,0},{2,3},{3,2},{4,5},{5,4},{6,7},{7,6},{8,9},{9,8},{10,11... | collective-permute-start | bytes 3080 | tf_op jit(solution)/shard_map/ppermute | solution.py:185
  25.0 0.8 collective-permute-done.2.also_held_ref
  25.8 4.2 %all-to-all-done.block_ref = bf16[4,8,1024]{2,1,0:T(8,128)(2,1)S(1)} async-done(((bf16[4,8,1024]{2,1,0:T(8,128)(2,1)}), bf16[4,8,1024]{2,1,0:T(8,128)(2,1)S(1)}, u32[]{:S(2)}, u32[]{:S(2)}) %all-to-all-start) | async-done | bytes 65568 | tf_op jit(solution)/shard_map/all_to_all | solution.py:199
  30.0 0.0 collective-permute-done.1.held_ref.pair_a_ref
  30.0 0.8 fan.1
  30.8 4.0 %all-to-all-start.1 = ((bf16[8,32,1024]{2,1,0:T(8,128)(2,1)}), bf16[8,32,1024]{2,1,0:T(8,128)(2,1)S(1)}, u32[]{:S(2)}, u32[]{:S(2)}) async-start(bf16[8,32,1024]{2,1,0:T(8,128)(2,1)} %fan.1), calls=%async_computation.1 | async-start | bytes 1048576 | tf_op jit(solution)/shard_map/all_to_all | solution.py:199
  34.8 0.0 copy-done
  34.8 0.9 collective-permute-start.3
  35.8 5.1 %collective-permute-done.3.pair_b_ref = bf16[320,512]{1,0:T(8,128)(2,1)S(1)} collective-permute-done((bf16[320,512]{1,0:T(8,128)(2,1)S(1)}, bf16[320,512]{1,0:T(8,128)(2,1)S(1)}, u32[]{:S(2)}, u32[]{:S(2)}) %collective-permute-start.3) | collective-permute-done | bytes 327712 | tf_op jit(solution)/shard_map/ppermute | solution.py:185
  40.9 1.0 all-to-all-done.1
  41.8 0.7 project_near.1
  42.6 0.0 copy-start.2
  42.6 5.1 %collective-permute-start.4 = (bf16[256,1024]{1,0:T(8,128)(2,1)S(1)}, bf16[256,1024]{1,0:T(8,128)(2,1)S(1)}, u32[]{:S(2)}, u32[]{:S(2)}) collective-permute-start(bf16[256,1024]{1,0:T(8,128)(2,1)S(1)} %get-tuple-element.16), channel_id=1, source_target_pairs={{0,1},{1,0},{2,3},{3,2},{4,5},{5,4},{6,7},{7,6},{8,9},{9,8},{10,11... | collective-permute-start | bytes 1572872 | tf_op jit(solution)/shard_map/ppermute | solution.py:185
  47.7 1.5 collective-permute-done.4.left_ref
  49.3 0.7 project.1
  50.0 0.3 collective-permute-start.5
  50.3 2.1 %collective-permute-start.6 = (bf16[2,32,512]{2,1,0:T(8,128)(2,1)S(1)}, bf16[2,32,512]{2,1,0:T(8,128)(2,1)S(1)}, u32[]{:S(2)}, u32[]{:S(2)}) collective-permute-start(bf16[2,32,512]{2,1,0:T(8,128)(2,1)S(1)} %get-tuple-element.23), channel_id=1, source_target_pairs={{0,64},{32,96},{64,0},{96,32},{1,65},{33,97},{65,1},{97,33},{2,66}... | collective-permute-start | bytes 196616 | tf_op jit(solution)/shard_map/ppermute | solution.py:190
  52.4 1.7 collective-permute-start.7
  54.1 1.9 %collective-permute-done.5 = bf16[2,32,512]{2,1,0:T(8,128)(2,1)S(1)} collective-permute-done((bf16[2,32,512]{2,1,0:T(8,128)(2,1)S(1)}, bf16[2,32,512]{2,1,0:T(8,128)(2,1)S(1)}, u32[]{:S(2)}, u32[]{:S(2)}) %collective-permute-start.5) | collective-permute-done | bytes 65568 | tf_op jit(solution)/shard_map/ppermute | solution.py:190
  56.0 3.5 %collective-permute-done.6 = bf16[2,32,512]{2,1,0:T(8,128)(2,1)S(1)} collective-permute-done((bf16[2,32,512]{2,1,0:T(8,128)(2,1)S(1)}, bf16[2,32,512]{2,1,0:T(8,128)(2,1)S(1)}, u32[]{:S(2)}, u32[]{:S(2)}) %collective-permute-start.6) | collective-permute-done | bytes 65568 | tf_op jit(solution)/shard_map/ppermute | solution.py:190
  59.5 0.9 collective-permute-done.7
  60.4 0.0 copy-done.2
  60.4 1.0 stream.1
  61.4 4.2 %all-to-all-start.2 = ((bf16[8,64,512]{2,1,0:T(8,128)(2,1)}), bf16[8,64,512]{2,1,0:T(8,128)(2,1)S(1)}, u32[]{:S(2)}, u32[]{:S(2)}) async-start(bf16[8,64,512]{2,1,0:T(8,128)(2,1)} %get-tuple-element.25), calls=%async_computation.2 | async-start | bytes 1048576 | tf_op jit(solution)/shard_map/all_to_all | solution.py:199
  65.6 2.6 %dynamic-slice_bitcast_fusion = (bf16[512,896]{1,0:T(8,128)(2,1)S(1)}, bf16[512,896]{1,0:T(8,128)(2,1)}) fusion(bf16[1,512,1792]{2,1,0:T(8,128)(2,1)} %param.20, s32[]{:T(128)S(6)} %select_n.9, s32[]{:T(128)S(6)} %select_n.8), kind=kLoop, calls=%fused_computation | loop fusion | bytes 3670024 | tf_op jit(solution)/shard_map/dynamic_slice | solution.py:344
  68.1 2.2 %collective-permute-start.10 = (bf16[512,896]{1,0:T(8,128)(2,1)}, bf16[512,896]{1,0:T(8,128)(2,1)S(1)}, u32[]{:S(2)}, u32[]{:S(2)}) collective-permute-start(bf16[512,896]{1,0:T(8,128)(2,1)} %get-tuple-element.28), channel_id=1, source_target_pairs={{0,1},{1,0},{2,3},{3,2},{4,5},{5,4},{6,7},{7,6},{8,9},{9,8},{10,11... | collective-permute-start | bytes 2752520 | tf_op jit(solution)/shard_map/ppermute | solution.py:185
  70.3 2.5 %dynamic-slice_bitcast_fusion.1 = (bf16[512,896]{1,0:T(8,128)(2,1)S(1)}, bf16[512,896]{1,0:T(8,128)(2,1)}) fusion(bf16[1,512,1792]{2,1,0:T(8,128)(2,1)} %param.19, s32[]{:T(128)S(6)} %select_n.9, s32[]{:T(128)S(6)} %select_n.8), kind=kLoop, calls=%fused_computation.1 | loop fusion | bytes 3670024 | tf_op jit(solution)/shard_map/dynamic_slice | solution.py:343
  72.9 0.0 collective-permute-start.9
  72.9 6.3 %all-to-all-done.2 = bf16[8,64,512]{2,1,0:T(8,128)(2,1)S(1)} async-done(((bf16[8,64,512]{2,1,0:T(8,128)(2,1)}), bf16[8,64,512]{2,1,0:T(8,128)(2,1)S(1)}, u32[]{:S(2)}, u32[]{:S(2)}) %all-to-all-start.2) | async-done | bytes 524320 | tf_op jit(solution)/shard_map/all_to_all | solution.py:199
  79.2 3.7 %collective-permute-start.8 = (bf16[512,512]{1,0:T(8,128)(2,1)S(1)}, bf16[512,512]{1,0:T(8,128)(2,1)S(1)}, u32[]{:S(2)}, u32[]{:S(2)}) collective-permute-start(bf16[512,512]{1,0:T(8,128)(2,1)S(1)} %bitcast.24), channel_id=1, source_target_pairs={{0,1},{1,0},{2,3},{3,2},{4,5},{5,4},{6,7},{7,6},{8,9},{9,8},{10,11... | collective-permute-start | bytes 1572872 | tf_op jit(solution)/shard_map/ppermute | solution.py:185
  82.9 1.3 gate_up_own.1.rest_0_
  84.1 0.0 collective-permute-done.10.up_ref
  84.1 0.0 collective-permute-done.9.gate_ref
  84.1 0.3 collective-permute-done.8.x_ref
  84.4 2.5 %gate_up.1 = bf16[512,1920]{1,0:T(8,128)(2,1)S(1)} custom-call(bf16[512,512]{1,0:T(8,128)(2,1)S(1)} %collective-permute-done.8.x_ref, bf16[1,512]{1,0:T(2,128)(2,1)S(1)} %broadcast_in_dim.7.gain_ref, bf16[512,896]{1,0:T(8,128)(2,1)} %collective-permute-done.9.gate_ref, bf16[512,896]{1,0:T(8,128)(2,1)S(1)} %collective-permute-done.10.up_ref, ...), custom_call_target="tpu_custom_call" | custom-call | tf_op jit(solution)/shard_map/gate_up/pallas_call | solution.py:363
  86.9 29.1 %all_to_all.35.parts_ref = bf16[8,64,1920]{2,1,0:T(8,128)(2,1)S(1)} all-to-all(bf16[8,64,1920]{2,1,0:T(8,128)(2,1)S(1)} %bitcast.21), channel_id=1, replica_groups=mesh['side'=2,'rp'=4,'rl'=2,'x'=4,'yl'=2,'core'=2] {'x','yl'}, dimensions={0} | all-to-all | bytes 3932160 | tf_op jit(solution)/shard_map/all_to_all | solution.py:199
  116.0 0.0 copy-start.1
  116.0 0.6 hidden.1
  116.6 14.8 %all_to_all.36 = bf16[8,64,896]{2,1,0:T(8,128)(2,1)S(1)} all-to-all(bf16[8,64,896]{2,1,0:T(8,128)(2,1)S(1)} %hidden.1), channel_id=1, replica_groups=mesh['side'=2,'rp'=4,'rl'=2,'x'=4,'yl'=2,'core'=2] {'x','yl'}, dimensions={0} | all-to-all | bytes 1835008 | tf_op jit(solution)/shard_map/all_to_all | solution.py:199
  131.3 3.1 %collective-permute-start.11 = (bf16[512,896]{1,0:T(8,128)(2,1)S(1)}, bf16[512,896]{1,0:T(8,128)(2,1)S(1)}, u32[]{:S(2)}, u32[]{:S(2)}) collective-permute-start(bf16[512,896]{1,0:T(8,128)(2,1)S(1)} %bitcast.22), channel_id=1, source_target_pairs={{0,1},{1,0},{2,3},{3,2},{4,5},{5,4},{6,7},{7,6},{8,9},{9,8},{10,11... | collective-permute-start | bytes 2752520 | tf_op jit(solution)/shard_map/ppermute | solution.py:185
  134.4 0.0 copy-done.1
  134.4 0.7 down_own.1.rest_0_
  135.1 1.4 collective-permute-done.11.x_ref
  136.5 0.7 down.1
  137.2 17.4 %all_to_all.37.parts_ref = bf16[8,64,512]{2,1,0:T(8,128)(2,1)S(1)} all-to-all(bf16[8,64,512]{2,1,0:T(8,128)(2,1)S(1)} %bitcast.27), channel_id=1, replica_groups=mesh['side'=2,'rp'=4,'rl'=2,'x'=4,'yl'=2,'core'=2] {'rl','rp'}, dimensions={0} | all-to-all | bytes 1048576 | tf_op jit(solution)/shard_map/all_to_all | solution.py:199
  154.6 0.1 final.1
  154.7 16.6 %all_to_all.38.back_ref = bf16[32,4,512]{2,1,0:T(4,128)(2,1)S(1)} all-to-all(bf16[32,4,512]{2,1,0:T(4,128)(2,1)S(1)} %final.1), channel_id=1, replica_groups=mesh['side'=2,'rp'=4,'rl'=2,'x'=4,'yl'=2,'core'=2] {'side','core','x','yl'}, dimensions={0} | all-to-all | bytes 262144 | tf_op jit(solution)/shard_map/all_to_all | solution.py:199
  171.3 0.6 output.1
  (3 shorter events, 0.0 us)
Async XLA Ops:
  1.2 21.8 %copy-start.3 = (bf16[512]{0:T(512)(128)(2,1)S(1)}, bf16[512]{0:T(512)(128)(2,1)}, u32[]{:S(2)}) copy-start(bf16[512]{0:T(512)(128)(2,1)} %param.17) | copy-start | bytes 3076
  1.2 28.8 %collective-permute-start.1 = (bf16[704,512]{1,0:T(8,128)(2,1)S(1)}, bf16[704,512]{1,0:T(8,128)(2,1)S(1)}, u32[]{:S(2)}, u32[]{:S(2)}) collective-permute-start(bf16[704,512]{1,0:T(8,128)(2,1)S(1)} %slice_bitcast_fusion), channel_id=1, source_target_pairs={{0,16},{16,0},{1,17},{17,1},{2,18},{18,2},{3,19},{19,3},{4,20},{20... | collective-permute-start | bytes 2162696 | tf_op jit(solution)/shard_map/ppermute | solution.py:185
  7.8 27.0 %copy-start = (bf16[1,1024,512]{2,1,0:T(8,128)(2,1)S(1)}, bf16[1,1024,512]{2,1,0:T(8,128)(2,1)}, u32[]{:S(2)}) copy-start(bf16[1,1024,512]{2,1,0:T(8,128)(2,1)} %own_ref.3) | copy-start | bytes 3145732
  7.8 6.6 %collective-permute-start = (bf16[4,8,1024]{2,1,0:T(8,128)(2,1)}, bf16[4,8,1024]{2,1,0:T(8,128)(2,1)}, u32[]{:S(2)}, u32[]{:S(2)}) collective-permute-start(bf16[4,8,1024]{2,1,0:T(8,128)(2,1)} %attend.1), channel_id=1, source_target_pairs={{0,128},{1,129},{2,130},{3,131},{4,132},{5,133},{6,134},{7,135},{8... | collective-permute-start | bytes 196616 | tf_op jit(solution)/shard_map/ppermute | solution.py:346
  14.4 15.6 %all-to-all-start = ((bf16[4,8,1024]{2,1,0:T(8,128)(2,1)}), bf16[4,8,1024]{2,1,0:T(8,128)(2,1)S(1)}, u32[]{:S(2)}, u32[]{:S(2)}) async-start(bf16[4,8,1024]{2,1,0:T(8,128)(2,1)} %collective-permute-done), calls=%async_computation | async-start | bytes 131072 | tf_op jit(solution)/shard_map/all_to_all | solution.py:199
  22.9 2.9 %collective-permute-start.2 = (bf16[512]{0:T(512)(128)(2,1)S(1)}, bf16[512]{0:T(512)(128)(2,1)S(1)}, u32[]{:S(2)}, u32[]{:S(2)}) collective-permute-start(bf16[512]{0:T(512)(128)(2,1)S(1)} %copy-done.3), channel_id=1, source_target_pairs={{0,1},{1,0},{2,3},{3,2},{4,5},{5,4},{6,7},{7,6},{8,9},{9,8},{10,11... | collective-permute-start | bytes 3080 | tf_op jit(solution)/shard_map/ppermute | solution.py:185
  30.8 11.0 %all-to-all-start.1 = ((bf16[8,32,1024]{2,1,0:T(8,128)(2,1)}), bf16[8,32,1024]{2,1,0:T(8,128)(2,1)S(1)}, u32[]{:S(2)}, u32[]{:S(2)}) async-start(bf16[8,32,1024]{2,1,0:T(8,128)(2,1)} %fan.1), calls=%async_computation.1 | async-start | bytes 1048576 | tf_op jit(solution)/shard_map/all_to_all | solution.py:199
  34.8 6.0 %collective-permute-start.3 = (bf16[320,512]{1,0:T(8,128)(2,1)S(1)}, bf16[320,512]{1,0:T(8,128)(2,1)S(1)}, u32[]{:S(2)}, u32[]{:S(2)}) collective-permute-start(bf16[320,512]{1,0:T(8,128)(2,1)S(1)} %slice_bitcast_fusion.1), channel_id=1, source_target_pairs={{0,16},{16,0},{1,17},{17,1},{2,18},{18,2},{3,19},{19,3},{4,20},{20... | collective-permute-start | bytes 983048 | tf_op jit(solution)/shard_map/ppermute | solution.py:185
  42.6 17.8 %copy-start.2 = (bf16[512,512]{1,0:T(8,128)(2,1)S(1)}, bf16[512,512]{1,0:T(8,128)(2,1)}, u32[]{:S(2)}) copy-start(bf16[512,512]{1,0:T(8,128)(2,1)} %refs_4_.1) | copy-start | bytes 1572868
  42.6 6.7 %collective-permute-start.4 = (bf16[256,1024]{1,0:T(8,128)(2,1)S(1)}, bf16[256,1024]{1,0:T(8,128)(2,1)S(1)}, u32[]{:S(2)}, u32[]{:S(2)}) collective-permute-start(bf16[256,1024]{1,0:T(8,128)(2,1)S(1)} %get-tuple-element.16), channel_id=1, source_target_pairs={{0,1},{1,0},{2,3},{3,2},{4,5},{5,4},{6,7},{7,6},{8,9},{9,8},{10,11... | collective-permute-start | bytes 1572872 | tf_op jit(solution)/shard_map/ppermute | solution.py:185
  50.0 6.0 %collective-permute-start.5 = (bf16[2,32,512]{2,1,0:T(8,128)(2,1)S(1)}, bf16[2,32,512]{2,1,0:T(8,128)(2,1)S(1)}, u32[]{:S(2)}, u32[]{:S(2)}) collective-permute-start(bf16[2,32,512]{2,1,0:T(8,128)(2,1)S(1)} %get-tuple-element.22), channel_id=1, source_target_pairs={{0,32},{32,64},{64,96},{96,0},{1,33},{33,65},{65,97},{97,1},{2,34}... | collective-permute-start | bytes 196616 | tf_op jit(solution)/shard_map/ppermute | solution.py:190
  50.3 9.2 %collective-permute-start.6 = (bf16[2,32,512]{2,1,0:T(8,128)(2,1)S(1)}, bf16[2,32,512]{2,1,0:T(8,128)(2,1)S(1)}, u32[]{:S(2)}, u32[]{:S(2)}) collective-permute-start(bf16[2,32,512]{2,1,0:T(8,128)(2,1)S(1)} %get-tuple-element.23), channel_id=1, source_target_pairs={{0,64},{32,96},{64,0},{96,32},{1,65},{33,97},{65,1},{97,33},{2,66}... | collective-permute-start | bytes 196616 | tf_op jit(solution)/shard_map/ppermute | solution.py:190
  52.4 7.9 %collective-permute-start.7 = (bf16[2,32,512]{2,1,0:T(8,128)(2,1)S(1)}, bf16[2,32,512]{2,1,0:T(8,128)(2,1)S(1)}, u32[]{:S(2)}, u32[]{:S(2)}) collective-permute-start(bf16[2,32,512]{2,1,0:T(8,128)(2,1)S(1)} %get-tuple-element.24), channel_id=1, source_target_pairs={{0,96},{32,0},{64,32},{96,64},{1,97},{33,1},{65,33},{97,65},{2,98}... | collective-permute-start | bytes 196616 | tf_op jit(solution)/shard_map/ppermute | solution.py:190
  61.4 17.8 %all-to-all-start.2 = ((bf16[8,64,512]{2,1,0:T(8,128)(2,1)}), bf16[8,64,512]{2,1,0:T(8,128)(2,1)S(1)}, u32[]{:S(2)}, u32[]{:S(2)}) async-start(bf16[8,64,512]{2,1,0:T(8,128)(2,1)} %get-tuple-element.25), calls=%async_computation.2 | async-start | bytes 1048576 | tf_op jit(solution)/shard_map/all_to_all | solution.py:199
  68.1 16.0 %collective-permute-start.10 = (bf16[512,896]{1,0:T(8,128)(2,1)}, bf16[512,896]{1,0:T(8,128)(2,1)S(1)}, u32[]{:S(2)}, u32[]{:S(2)}) collective-permute-start(bf16[512,896]{1,0:T(8,128)(2,1)} %get-tuple-element.28), channel_id=1, source_target_pairs={{0,1},{1,0},{2,3},{3,2},{4,5},{5,4},{6,7},{7,6},{8,9},{9,8},{10,11... | collective-permute-start | bytes 2752520 | tf_op jit(solution)/shard_map/ppermute | solution.py:185
  72.9 11.3 %collective-permute-start.9 = (bf16[512,896]{1,0:T(8,128)(2,1)}, bf16[512,896]{1,0:T(8,128)(2,1)}, u32[]{:S(2)}, u32[]{:S(2)}) collective-permute-start(bf16[512,896]{1,0:T(8,128)(2,1)} %get-tuple-element.30), channel_id=1, source_target_pairs={{0,1},{1,0},{2,3},{3,2},{4,5},{5,4},{6,7},{7,6},{8,9},{9,8},{10,11... | collective-permute-start | bytes 2752520 | tf_op jit(solution)/shard_map/ppermute | solution.py:185
  79.2 5.2 %collective-permute-start.8 = (bf16[512,512]{1,0:T(8,128)(2,1)S(1)}, bf16[512,512]{1,0:T(8,128)(2,1)S(1)}, u32[]{:S(2)}, u32[]{:S(2)}) collective-permute-start(bf16[512,512]{1,0:T(8,128)(2,1)S(1)} %bitcast.24), channel_id=1, source_target_pairs={{0,1},{1,0},{2,3},{3,2},{4,5},{5,4},{6,7},{7,6},{8,9},{9,8},{10,11... | collective-permute-start | bytes 1572872 | tf_op jit(solution)/shard_map/ppermute | solution.py:185
  116.0 18.4 %copy-start.1 = (bf16[1,1792,512]{2,1,0:T(8,128)(2,1)S(1)}, bf16[1,1792,512]{2,1,0:T(8,128)(2,1)}, u32[]{:S(2)}) copy-start(bf16[1,1792,512]{2,1,0:T(8,128)(2,1)} %weight_ref.3) | copy-start | bytes 5505028
  131.3 5.2 %collective-permute-start.11 = (bf16[512,896]{1,0:T(8,128)(2,1)S(1)}, bf16[512,896]{1,0:T(8,128)(2,1)S(1)}, u32[]{:S(2)}, u32[]{:S(2)}) collective-permute-start(bf16[512,896]{1,0:T(8,128)(2,1)S(1)} %bitcast.22), channel_id=1, source_target_pairs={{0,1},{1,0},{2,3},{3,2},{4,5},{5,4},{6,7},{7,6},{8,9},{9,8},{10,11... | collective-permute-start | bytes 2752520 | tf_op jit(solution)/shard_map/ppermute | solution.py:185
